TPU v7x, 128 devices: a whole 4x4x4 slice. The times are simulated.
128 devices in a mesh: seq: 32 (over x, y, core), mp: 4 (over z).
Axes of the slice: x: 4, y: 4, z: 4, core: 2. Of those that a mesh axis runs over, the one named last changes fastest.
Arguments:
- q_in: bfloat16 [12288, 8192], P('seq', 'mp'), may hold values from -6 to 6
- k_in: bfloat16 [12288, 8192], P('seq', 'mp'), may hold values from -6 to 6
- v_in: bfloat16 [12288, 8192], P('seq', 'mp'), may hold values from -6 to 6
- dest_pos: int32 [12288], replicated, may hold values from -1 to 8191, as said below
- doc_ids: int32 [8192], replicated, may hold values from 0 to 63, never falling along the last dimension, each value on 1 to 512 neighbouring positions
- mr_filter: float32 [128, 8192], P(None, 'mp')
- norm_gain: float32 [8192], P('mp'), may hold values from 0.5 to 1.5
- residual: bfloat16 [8192, 8192], P('seq', 'mp')
- cotangent: bfloat16 [8192, 8192], P('seq', 'mp'), may hold values from -6 to 6
Outputs:
- normed: bfloat16 [8192, 8192], P('seq', 'mp')
- d_residual: bfloat16 [8192, 8192], P('seq', 'mp')
- d_q_in: bfloat16 [12288, 8192], P('seq', 'mp')
- d_k_in: bfloat16 [12288, 8192], P('seq', 'mp')
- d_v_in: bfloat16 [12288, 8192], P('seq', 'mp')
- d_filter: float32 [128, 8192], P(None, 'mp')
- d_gain: float32 [8192], P('mp')
Inputs may be any that keep to these rules, and one draw needn't show every extreme that they name: `dest_pos`: every position 0 .. 8191 stands in exactly one slot; all other slots hold -1. The 384 slots of one index of seq hold at most 16 positions of the 256 positions owned by any one index of seq; that bound is reached in every draw, and some index of seq has no slot holding -1. `doc_ids`: ids never fall along the positions; every document covers 1 to 512 positions, one exactly 512.
All inputs are finite; a program needn't handle non-finite values.
Results may differ from a plain program's by a relative error of at most 0.012.
Values may be sent and summed in bfloat16 or wider, within the bound.
No kernel may reach another device: no remote copies, remote signals or barrier semaphores. Data moves between devices by JAX's collectives and lax.ppermute only.
A program may use at most 256 MiB of HBM per device.

v0:
```python
import jax
import jax.numpy as jnp
from jax import lax
from jax.sharding import PartitionSpec as P

D = 8192


NORM_EPS = 1e-06


def from_behind(value, axis, steps):
    count = lax.axis_size(axis)
    leading, last = (max(0, -steps), min(count, count - steps))
    return lax.ppermute(value, axis, [(source, source + steps) for source in range(leading, last)])


def pack_rows(block, slot_index, slot_total):
    empty = jnp.zeros((slot_total, block.shape[1]), block.dtype)
    return empty.at[slot_index].set(block, mode="drop")


def forward_mix(window, mr_filter, docs_window, tap_count, row_count):
    own_docs = docs_window[tap_count : tap_count + row_count]
    running = jnp.zeros((row_count, window.shape[1]), jnp.float32)
    for offset in range(tap_count):
        lower = tap_count - offset
        kept_mask = (docs_window[lower : lower + row_count] == own_docs)[:, None]
        running = running + jnp.where(
            kept_mask,
            mr_filter[offset][None, :] * window[lower : lower + row_count].astype(jnp.float32),
            0.0,
        )
    return running


def backward_mix(grad_window, mr_filter, docs_window, tap_count, first_row, row_count):
    own_docs = docs_window[first_row : first_row + row_count]
    running = jnp.zeros((row_count, grad_window.shape[1]), jnp.float32)
    for offset in range(tap_count):
        upper = first_row + offset
        kept_mask = (docs_window[upper : upper + row_count] == own_docs)[:, None]
        running = running + jnp.where(
            kept_mask,
            mr_filter[offset][None, :] * grad_window[upper : upper + row_count].astype(jnp.float32),
            0.0,
        )
    return running


def filter_grad(d_mixture, window, docs_window, tap_count, row_count):
    own_docs = docs_window[tap_count : tap_count + row_count]
    tap_terms = []
    for offset in range(tap_count):
        lower = tap_count - offset
        kept_mask = (docs_window[lower : lower + row_count] == own_docs)[:, None]
        tap_terms.append(
            jnp.sum(
                jnp.where(
                    kept_mask,
                    d_mixture.astype(jnp.float32)
                    * window[lower : lower + row_count].astype(jnp.float32),
                    0.0,
                ),
                axis=0,
            )
        )
    return jnp.stack(tap_terms)


def body(q_in, k_in, v_in, dest_pos, doc_ids, mr_filter, norm_gain, residual, cotangent):
    shard_count = lax.axis_size("seq")
    my_index = lax.axis_index("seq")
    slot_count = q_in.shape[0]
    row_count = residual.shape[0]
    tap_count = mr_filter.shape[0]
    width_local = q_in.shape[1]
    pair_slots = 2 * row_count // shard_count
    slot_total = shard_count * pair_slots
    shard_range = jnp.arange(shard_count, dtype=jnp.int32)
    dest_table = dest_pos.reshape(shard_count, slot_count)
    own_plan = lax.dynamic_index_in_dim(dest_table, my_index, 0, keepdims=False)
    own_owner = jnp.where(own_plan >= 0, own_plan // row_count, shard_count)
    own_onehot = (own_owner[:, None] == shard_range[None, :]).astype(jnp.int32)
    own_rank = jnp.sum((jnp.cumsum(own_onehot, axis=0) - own_onehot) * own_onehot, axis=1)
    send_slot = jnp.where(own_plan >= 0, own_owner * pair_slots + own_rank, slot_total)
    arriving = (dest_table >= 0) & (dest_table // row_count == my_index)
    arriving_int = arriving.astype(jnp.int32)
    arrive_rank = jnp.cumsum(arriving_int, axis=1) - arriving_int
    arrive_slot = shard_range[:, None] * pair_slots + arrive_rank
    local_target = jnp.where(arriving, dest_table - my_index * row_count, row_count)
    source_row = (
        jnp.zeros((row_count,), jnp.int32)
        .at[local_target.reshape(-1)]
        .set(arrive_slot.reshape(-1), mode="drop")
    )
    slot_home = (
        jnp.full((slot_total,), row_count, jnp.int32)
        .at[source_row]
        .set(jnp.arange(row_count, dtype=jnp.int32))
    )

    def outgoing(block):
        return pack_rows(block, send_slot, slot_total).reshape(shard_count, pair_slots, width_local)

    def incoming(received):
        return received.reshape(slot_total, width_local)[source_row]

    def returning(block):
        return jnp.take(block, slot_home, axis=0, mode="fill", fill_value=0).reshape(
            shard_count, pair_slots, width_local
        )

    def homecoming(received):
        return jnp.take(
            received.reshape(slot_total, width_local), send_slot, axis=0, mode="fill", fill_value=0
        )

    moved_rows = (
        lax.all_to_all(outgoing(q_in), "seq", split_axis=0, concat_axis=0, tiled=True),
        lax.all_to_all(outgoing(k_in), "seq", split_axis=0, concat_axis=0, tiled=True),
        lax.all_to_all(outgoing(v_in), "seq", split_axis=0, concat_axis=0, tiled=True),
    )
    q_pos = incoming(moved_rows[0])
    k_pos = incoming(moved_rows[1])
    v_pos = incoming(moved_rows[2])
    product = (k_pos.astype(jnp.float32) * v_pos.astype(jnp.float32)).astype(jnp.bfloat16)
    doc_all = jnp.concatenate(
        [jnp.full((tap_count,), -1, jnp.int32), doc_ids, jnp.full((tap_count,), -2, jnp.int32)]
    )
    docs_window = lax.dynamic_slice_in_dim(doc_all, my_index * row_count, row_count + 2 * tap_count)
    tail_rows = from_behind(product[row_count - tap_count :], "seq", 1)
    window = jnp.concatenate([tail_rows, product], axis=0)
    mixture = forward_mix(window, mr_filter, docs_window, tap_count, row_count)
    summed = residual.astype(jnp.float32) + q_pos.astype(jnp.float32) * mixture
    cot_value = cotangent.astype(jnp.float32)
    scaled_cot = cot_value * norm_gain[None, :]
    local_squares = jnp.sum(summed * summed, axis=1)
    local_dot = jnp.sum(scaled_cot * summed, axis=1)
    square_sum = lax.psum(local_squares, "mp")
    dot_sum = lax.psum(local_dot, "mp")
    inv_rms = lax.rsqrt(square_sum / D + NORM_EPS)[:, None]
    row_dot = dot_sum[:, None]
    normed = (summed * inv_rms * norm_gain[None, :]).astype(jnp.bfloat16)
    gain_part = jnp.sum(cot_value * summed * inv_rms, axis=0)
    d_summed = inv_rms * scaled_cot - summed * (inv_rms * inv_rms * inv_rms) * row_dot / D
    d_residual = d_summed.astype(jnp.bfloat16)
    d_q_pos = (d_summed * mixture).astype(jnp.bfloat16)
    d_mixture = (d_summed * q_pos.astype(jnp.float32)).astype(jnp.bfloat16)
    filter_part = filter_grad(d_mixture, window, docs_window, tap_count, row_count)
    zero_rim = jnp.zeros((tap_count, width_local), jnp.bfloat16)
    head_rows = from_behind(d_mixture[:tap_count], "seq", -1)
    grad_window = jnp.concatenate([zero_rim, d_mixture, head_rows], axis=0)
    d_product_sum = backward_mix(
        grad_window, mr_filter, docs_window, tap_count, tap_count, row_count
    )
    d_product = d_product_sum.astype(jnp.bfloat16)
    d_filter, d_gain = lax.psum((filter_part, gain_part), "seq")
    d_k_pos = (d_product.astype(jnp.float32) * v_pos.astype(jnp.float32)).astype(jnp.bfloat16)
    d_v_pos = (d_product.astype(jnp.float32) * k_pos.astype(jnp.float32)).astype(jnp.bfloat16)
    back_rows = (
        lax.all_to_all(returning(d_q_pos), "seq", split_axis=0, concat_axis=0, tiled=True),
        lax.all_to_all(returning(d_k_pos), "seq", split_axis=0, concat_axis=0, tiled=True),
        lax.all_to_all(returning(d_v_pos), "seq", split_axis=0, concat_axis=0, tiled=True),
    )
    d_q_in = homecoming(back_rows[0])
    d_k_in = homecoming(back_rows[1])
    d_v_in = homecoming(back_rows[2])
    return (normed, d_residual, d_q_in, d_k_in, d_v_in, d_filter, d_gain)


def solution(mesh):
    return jax.shard_map(
        body,
        mesh=mesh,
        in_specs=(
            P("seq", "mp"),
            P("seq", "mp"),
            P("seq", "mp"),
            P(),
            P(),
            P(None, "mp"),
            P("mp"),
            P("seq", "mp"),
            P("seq", "mp"),
        ),
        out_specs=(
            P("seq", "mp"),
            P("seq", "mp"),
            P("seq", "mp"),
            P("seq", "mp"),
            P("seq", "mp"),
            P(None, "mp"),
            P("mp"),
        ),
        check_vma=False,
    )
```

profile of v0, /device:TPU:1, one launch (start us, length us, event | category | flops | bytes accessed | tf_op | source)
XLA Modules:
  0.0 1648.0 jit_solution(6610974850343305835)
XLA Ops:
  9.3 5.3 scatter_custom_fusion.2
  14.6 8.7 all-to-all-start.1
  39.4 45.4 %scatter_custom_fusion.1 = s32[256]{0:T(256)S(1)} fusion(s32[12288]{0:T(1024)S(1)} %get-tuple-element.364, s32[12288]{0:T(1024)S(1)} %get-tuple-element.363, s32[]{:T(128)} %constant.46.clone.1), kind=kCustom, calls=%fused_computation.1934 | custom fusion | bytes 1028 | tf_op jit(solution)/shard_map/scatter | solution.py:95
  87.4 5.8 scatter_custom_fusion.3
  93.2 5.2 scatter_custom_fusion
  104.5 7.6 all-to-all-start.2
  114.3 26.1 %all-to-all-done.2 = bf16[32,16,2048]{2,1,0:T(8,128)(2,1)} async-done(((bf16[32,16,2048]{2,1,0:T(8,128)(2,1)}), bf16[32,16,2048]{2,1,0:T(8,128)(2,1)}, u32[]{:S(2)}, u32[]{:S(2)}) %all-to-all-start.2) | async-done | bytes 2097184 | tf_op jit(solution)/shard_map/all_to_all | solution.py:122
  140.4 5.2 all-to-all-start
  150.9 4.4 gather_fusion.2
  156.7 3.7 collective-permute-start
  162.9 11.2 all-to-all-done
  174.5 4.4 gather_fusion
  179.5 181.1 %multiply_reduce_fusion = (f32[256]{0:T(256)S(1)}, f32[256,2048]{1,0:T(8,128)}, f32[256,2048]{1,0:T(8,128)}) fusion(bf16[256,2048]{1,0:T(8,128)(2,1)S(1)} %gather_fusion, bf16[256,2048]{1,0:T(8,128)(2,1)} %param.20, bf16[256,2048]{1,0:T(8,128)(2,1)S(1)} %fusion.6, bf16[128,2048]{1,0:T(8,128)(2,1)S(1)} %collective-permute-done, f32[2048]{0:T(1024)S(1)} %bitcast.349, ...), kind=kLoop, calls=%fused_computation.1332 | loop fusion | flops 470286080 | bytes 8946432 | tf_op jit(solution)/shard_map/reduce_sum | solution.py:138
  360.6 9.8 psum.28
  374.7 6.5 psum.29
  381.2 6.0 fusion.502
  388.0 6.7 collective-permute-start.1
  394.7 3.5 gather_fusion.3
  398.3 7.0 fusion.542
  405.5 6.2 fusion.538
  411.8 6.3 fusion.536
  418.2 6.1 fusion.534
  424.4 6.9 fusion.532
  431.4 6.0 fusion.530
  437.4 7.3 fusion.528
  444.8 7.4 fusion.526
  452.3 7.0 fusion.524
  459.4 6.4 fusion.522
  465.8 6.7 fusion.520
  472.5 6.5 fusion.518
  479.0 6.1 fusion.589
  485.1 6.4 fusion.590
  491.5 6.4 fusion.591
  497.9 6.3 fusion.592
  504.2 6.2 fusion.593
  510.4 6.4 fusion.594
  516.8 6.2 fusion.600
  523.0 6.6 fusion.595
  529.6 6.4 fusion.596
  539.7 3.6 fusion.290
  543.7 790.5 %fusion.264 = (bf16[256,2048]{1,0:T(8,128)(2,1)S(1)}, bf16[256,2048]{1,0:T(8,128)(2,1)}) fusion(bf16[256,2048]{1,0:T(8,128)(2,1)S(1)} %copy-done.4, bf16[256,2048]{1,0:T(8,128)(2,1)} %get-tuple-element.231, f32[2048]{0:T(1024)S(1)} %bitcast.350, pred[256]{0:T(512)(128)(4,1)} %get-tuple-element.500, bf16[256,2048]{1,0:T(8,128)(2,1)} %get-tuple-element.232, ...), kind=kLoop, calls=%fused_computation.1046 | loop fusion | flops 334495744 | bytes 95968768 | tf_op jit(solution)/shard_map/convert_element_type | solution.py:160
  1337.1 6.6 gather_fusion.5
  1347.0 5.7 broadcast_select_fusion
  1352.7 5.1 all-to-all-start.3
  1358.0 6.2 fusion.516
  1364.2 6.1 fusion.514
  1370.4 6.7 fusion.512
  1377.1 8.3 all-to-all-done.3
  1385.5 5.6 all-to-all-start.4
  1391.3 7.4 fusion.510
  1398.8 6.7 fusion.508
  1405.5 7.0 fusion.506
  1412.5 6.8 all-to-all-done.4
  1419.4 5.2 all-to-all-start.5
  1424.8 4.6 fusion.544
  1429.4 79.6 %psum.31 = f32[2048]{0:T(1024)} all-reduce(f32[2048]{0:T(1024)S(1)} %copy-done.147), channel_id=1, replica_groups=mesh['seq'=32,'mp'=4] {'seq'}, use_global_device_ids=true, to_apply=%region_144.147 | all-reduce | flops 2048 | bytes 16384 | tf_op jit(solution)/shard_map/psum | solution.py:158
  1509.1 6.5 fusion.504
  1516.0 5.7 fusion.540
  1522.1 16.9 %stack.515 = f32[128,2048]{1,0:T(8,128)} concatenate(f32[1,2048]{1,0:T(1,128)} %bitcast.653, f32[1,2048]{1,0:T(1,128)S(1)} %bitcast.693, f32[1,2048]{1,0:T(1,128)S(1)} %bitcast.691, f32[1,2048]{1,0:T(1,128)S(1)} %bitcast.692, f32[1,2048]{1,0:T(1,128)S(1)} %bitcast.694, f32[1,2048]{1,0:T(1,128)S(1)} %bitcast.695, f32[1,2048]{1,0:T(1,128)S(1)} %bitcast.582, ...), dimensions={0} | concatenate | bytes 2097152 | tf_op jit(solution)/shard_map/stack | solution.py:68
  1539.1 6.4 gather_fusion.4
  1545.5 6.9 gather_fusion.6
  1552.4 7.2 gather_fusion.8
  1559.6 4.2 broadcast_select_fusion.3
  1563.8 74.7 %all-reduce.2.cloned.1.call-done = f32[128,2048]{1,0:T(8,128)} async-done(((f32[128,2048]{1,0:T(8,128)}), f32[128,2048]{1,0:T(8,128)}) %all-reduce.2.cloned.1.call-update) | async-done | bytes 1048592 | tf_op jit(solution)/shard_map/psum | solution.py:158
  (625 shorter events, 55.9 us)
Async XLA Ops:
  14.6 89.8 %all-to-all-start.1 = ((bf16[32,16,2048]{2,1,0:T(8,128)(2,1)}), bf16[32,16,2048]{2,1,0:T(8,128)(2,1)S(1)}, u32[]{:S(2)}, u32[]{:S(2)}) async-start(bf16[32,16,2048]{2,1,0:T(8,128)(2,1)} %bitcast.322), calls=%async_computation.1 | async-start | bytes 4194304 | tf_op jit(solution)/shard_map/all_to_all | solution.py:121
  104.5 35.9 %all-to-all-start.2 = ((bf16[32,16,2048]{2,1,0:T(8,128)(2,1)}), bf16[32,16,2048]{2,1,0:T(8,128)(2,1)}, u32[]{:S(2)}, u32[]{:S(2)}) async-start(bf16[32,16,2048]{2,1,0:T(8,128)(2,1)} %bitcast.324), calls=%async_computation.2 | async-start | bytes 4194304 | tf_op jit(solution)/shard_map/all_to_all | solution.py:122
  140.4 33.7 %all-to-all-start = ((bf16[32,16,2048]{2,1,0:T(8,128)(2,1)}), bf16[32,16,2048]{2,1,0:T(8,128)(2,1)}, u32[]{:S(2)}, u32[]{:S(2)}) async-start(bf16[32,16,2048]{2,1,0:T(8,128)(2,1)} %bitcast.323), calls=%async_computation | async-start | bytes 4194304 | tf_op jit(solution)/shard_map/all_to_all | solution.py:120
  156.7 22.3 %collective-permute-start = (bf16[128,2048]{1,0:T(8,128)(2,1)}, bf16[128,2048]{1,0:T(8,128)(2,1)S(1)}, u32[]{:S(2)}, u32[]{:S(2)}) collective-permute-start(bf16[128,2048]{1,0:T(8,128)(2,1)} %slice.3106), channel_id=1, source_target_pairs={{0,4},{4,8},{8,12},{12,16},{16,20},{20,24},{24,28},{28,32},{32,36}... | collective-permute-start | bytes 1572872 | tf_op jit(solution)/shard_map/ppermute | solution.py:15
  162.7 16.3 copy-start.88
  162.7 16.3 copy-start.89
  162.7 16.3 copy-start.90
  162.7 16.3 copy-start.91
  162.7 16.3 copy-start.92
  162.7 16.3 copy-start.93
  162.7 16.3 copy-start.94
  162.7 16.3 copy-start.95
  162.7 16.3 copy-start.96
  162.8 16.3 copy-start.97
  162.8 16.3 copy-start.98
  162.8 16.3 copy-start.99
  162.8 16.3 copy-start.100
  162.8 16.3 copy-start.101
  162.8 16.3 copy-start.102
  162.8 16.3 copy-start.103
  162.8 16.3 copy-start.104
  162.8 16.3 copy-start.105
  162.8 16.3 copy-start.106
  178.9 181.7 %copy-start.6 = (bf16[256,2048]{1,0:T(8,128)(2,1)}, bf16[256,2048]{1,0:T(8,128)(2,1)S(1)}, u32[]{:S(2)}) copy-start(bf16[256,2048]{1,0:T(8,128)(2,1)S(1)} %gather_fusion) | copy-start | bytes 3145732
  178.9 181.7 %copy-start = (bf16[128,2048]{1,0:T(8,128)(2,1)}, bf16[128,2048]{1,0:T(8,128)(2,1)S(1)}, u32[]{:S(2)}) copy-start(bf16[128,2048]{1,0:T(8,128)(2,1)S(1)} %collective-permute-done) | copy-start | bytes 1572868
  388.0 91.0 %collective-permute-start.1 = (bf16[128,2048]{1,0:T(8,128)(2,1)}, bf16[128,2048]{1,0:T(8,128)(2,1)}, u32[]{:S(2)}, u32[]{:S(2)}) collective-permute-start(bf16[128,2048]{1,0:T(8,128)(2,1)} %slice.3359), channel_id=1, source_target_pairs={{4,0},{8,4},{12,8},{16,12},{20,16},{24,20},{28,24},{32,28},{36,32}... | collective-permute-start | bytes 1572872 | tf_op jit(solution)/shard_map/ppermute | solution.py:15
  398.3 13.4 copy-start.226
  398.3 13.4 copy-start.257
  398.3 13.4 copy-start.258
  431.3 13.4 copy-start.205
  437.4 14.8 copy-start.204
  437.4 14.8 copy-start.227
  437.4 14.8 copy-start.229
  437.4 14.8 copy-start.230
  437.4 14.8 copy-start.231
  437.4 14.8 copy-start.232
  444.7 14.5 copy-start.203
  444.7 14.5 copy-start.221
  444.8 14.5 copy-start.222
  444.8 14.5 copy-start.223
  444.8 14.5 copy-start.224
  444.8 14.5 copy-start.225
  452.2 13.6 copy-start.202
  452.2 13.6 copy-start.214
  452.2 13.6 copy-start.215
  452.2 13.6 copy-start.216
  452.3 13.6 copy-start.218
  452.3 13.6 copy-start.219
  1352.7 32.8 %all-to-all-start.3 = ((bf16[32,16,2048]{2,1,0:T(8,128)(2,1)}), bf16[32,16,2048]{2,1,0:T(8,128)(2,1)}, u32[]{:S(2)}, u32[]{:S(2)}) async-start(bf16[32,16,2048]{2,1,0:T(8,128)(2,1)} %bitcast.321), calls=%async_computation.3 | async-start | bytes 4194304 | tf_op jit(solution)/shard_map/all_to_all | solution.py:162
  1385.5 33.9 %all-to-all-start.4 = ((bf16[32,16,2048]{2,1,0:T(8,128)(2,1)}), bf16[32,16,2048]{2,1,0:T(8,128)(2,1)}, u32[]{:S(2)}, u32[]{:S(2)}) async-start(bf16[32,16,2048]{2,1,0:T(8,128)(2,1)} %bitcast.320), calls=%async_computation.4 | async-start | bytes 4194304 | tf_op jit(solution)/shard_map/all_to_all | solution.py:163
  1391.2 14.3 copy-start.162
  1391.2 14.3 copy-start.164
  1391.2 14.3 copy-start.165
  1391.2 14.3 copy-start.166
  1391.3 14.3 copy-start.167
  1391.3 14.3 copy-start.168
  1419.4 133.0 %all-to-all-start.5 = ((bf16[32,16,2048]{2,1,0:T(8,128)(2,1)}), bf16[32,16,2048]{2,1,0:T(8,128)(2,1)}, u32[]{:S(2)}, u32[]{:S(2)}) async-start(bf16[32,16,2048]{2,1,0:T(8,128)(2,1)} %bitcast.319), calls=%async_computation.5 | async-start | bytes 4194304 | tf_op jit(solution)/shard_map/all_to_all | solution.py:164
  1424.6 84.4 %copy-start.154 = (pred[256]{0:T(512)(128)(4,1)S(1)}, pred[256]{0:T(512)(128)(4,1)}, u32[]{:S(2)}) copy-start(pred[256]{0:T(512)(128)(4,1)} %get-tuple-element.513) | copy-start | bytes 772
  1424.6 84.4 %copy-start.155 = (pred[256]{0:T(512)(128)(4,1)S(1)}, pred[256]{0:T(512)(128)(4,1)}, u32[]{:S(2)}) copy-start(pred[256]{0:T(512)(128)(4,1)} %get-tuple-element.515) | copy-start | bytes 772
  1424.6 84.4 %copy-start.156 = (pred[256]{0:T(512)(128)(4,1)S(1)}, pred[256]{0:T(512)(128)(4,1)}, u32[]{:S(2)}) copy-start(pred[256]{0:T(512)(128)(4,1)} %get-tuple-element.516) | copy-start | bytes 772
  1424.6 84.4 %copy-start.157 = (pred[256]{0:T(512)(128)(4,1)S(1)}, pred[256]{0:T(512)(128)(4,1)}, u32[]{:S(2)}) copy-start(pred[256]{0:T(512)(128)(4,1)} %get-tuple-element.517) | copy-start | bytes 772
  1424.6 84.4 %copy-start.158 = (pred[256]{0:T(512)(128)(4,1)S(1)}, pred[256]{0:T(512)(128)(4,1)}, u32[]{:S(2)}) copy-start(pred[256]{0:T(512)(128)(4,1)} %get-tuple-element.519) | copy-start | bytes 772
  1424.6 84.4 %copy-start.159 = (pred[256]{0:T(512)(128)(4,1)S(1)}, pred[256]{0:T(512)(128)(4,1)}, u32[]{:S(2)}) copy-start(pred[256]{0:T(512)(128)(4,1)} %get-tuple-element.520) | copy-start | bytes 772
  1424.7 213.9 %all-reduce.2.cloned.1.call-start = ((), (), s32[]{:S(2)}) async-start(), calls=%async_computation.6 | async-start | bytes 2097152 | tf_op jit(solution)/shard_map/psum | solution.py:158
  (214 other events, 1473.2 us)
Sparse Core Ops, SparseCore 0:
  1539.2 99.3 all-reduce.1
where the time goes:
time: 1660 us; the launch traced here: 1650 us
  other arithmetic  1220 us (73%)
  local copies, waits for them, and re-layouts  137 us (8%)
  waiting for transfers between devices  127 us (8%)
  blocking collectives  95.9 us (6%)
  starting transfers between devices  47.9 us (3%)
  between operations  18.4 us (1%)
    convert_element_type x1, other arithmetic, body(): (d_product.astype(jnp.float32) * k_pos.astype(jnp.float32)).astype(jnp.bf...  790 us
    reduce_sum x1, other arithmetic, body(): local_squares = jnp.sum(summed * summed, axis=1)  181 us
    reduce_sum x23, other arithmetic, filter_grad(): jnp.sum(jnp.where(kept_mask, d_mixture.astype(jnp.float32) * window[lower...  146 us
    psum x1, blocking collectives, body(): d_filter, d_gain = lax.psum((filter_part, gain_part), 'seq')  79.6 us
    psum x1, waiting for transfers between devices, body(): d_filter, d_gain = lax.psum((filter_part, gain_part), 'seq')  74.7 us
    concatenate x10, other arithmetic, body(): grad_window = jnp.concatenate([zero_rim, d_mixture, head_rows], axis=0)  60.3 us
    scatter x1, local copies, waits for them, and re-layouts, body(): source_row = jnp.zeros((row_count,), jnp.int32).at[local_target.reshape(-...  45.4 us
  transfers between devices with their start and end apart: 9, of which 5 were waited for; matrix products, arithmetic and copies ran while one was open for 17% of the time, Pallas kernels for 0%

commit v1 on v0

v1 whole, which is shorter than its diff:
```python
import functools

import jax
import jax.numpy as jnp
from jax import lax
from jax.experimental import pallas as pl
from jax.experimental.pallas import tpu as pltpu
from jax.sharding import PartitionSpec as P

D = 8192
NORM_EPS = 1e-06
NDOCS = 64
BF = jnp.bfloat16
F32 = jnp.float32
I32 = jnp.int32

ROWS = 256
SLOTS = 384
TAPS = 128
SHARDS = 32
PAIR = 16
SENT = SHARDS * PAIR
WIN = TAPS + ROWS
FREQ = 320
CB = 512


def dot(a, b):
    return jnp.dot(a, b, preferred_element_type=F32)


def iota(shape, dim):
    return lax.broadcasted_iota(I32, shape, dim)


def onehot(match):
    return jnp.where(match, 1.0, 0.0).astype(BF)


def params():
    return pltpu.CompilerParams(
        dimension_semantics=("arbitrary",), vmem_limit_bytes=48 * 1024 * 1024
    )


def cols(rows, width=CB, last=None):
    if last is None:
        return pl.BlockSpec((rows, width), lambda j: (0, j))
    return pl.BlockSpec((rows, width), lambda j: (0, jnp.minimum(j, last)))


def whole(shape):
    return pl.BlockSpec(shape, lambda j: (0,) * len(shape))


def cost(flops, nbytes):
    return pl.CostEstimate(flops=int(flops), transcendentals=0, bytes_accessed=int(nbytes))


def sds(shape, dtype):
    return jax.ShapeDtypeStruct(shape, dtype)


def build_pack(owner_col, owner_row, pack):
    same = (owner_col == owner_row) & (iota((SLOTS, SLOTS), 0) < iota((SLOTS, SLOTS), 1))
    rank = jnp.sum(jnp.where(same, 1, 0), axis=0, keepdims=True)
    slot = jnp.where(owner_row >= 0, owner_row * PAIR + rank, -1)
    pack[...] = onehot(iota((SENT, SLOTS), 0) == slot)


def pack_product_kernel(owner_col, owner_row, k_ref, v_ref, out_ref, pack):
    @pl.when(pl.program_id(0) == 0)
    def _():
        build_pack(owner_col[...], owner_row[...], pack)

    product = (k_ref[...].astype(F32) * v_ref[...].astype(F32)).astype(BF)
    out_ref[...] = dot(pack[...], product).astype(BF)


def pack_rows_kernel(owner_col, owner_row, q_ref, out_ref, pack):
    @pl.when(pl.program_id(0) == 0)
    def _():
        build_pack(owner_col[...], owner_row[...], pack)

    out_ref[...] = dot(pack[...], q_ref[...]).astype(BF)


def pack_arrivals(kernel, owner_col, owner_row, blocks, width):
    return pl.pallas_call(
        kernel,
        grid=(width // CB,),
        in_specs=[whole((SLOTS, 1)), whole((1, SLOTS))] + [cols(SLOTS)] * len(blocks),
        out_specs=cols(SENT),
        out_shape=sds((SENT, width), BF),
        scratch_shapes=[pltpu.VMEM((SENT, SLOTS), BF)],
        compiler_params=params(),
        cost_estimate=cost(
            2 * SENT * SLOTS * width, 2 * width * (SENT + SLOTS * len(blocks))
        ),
    )(owner_col, owner_row, *blocks)


def place_product_kernel(pos_row, recv_ref, out_ref, tail_ref, place):
    @pl.when(pl.program_id(0) == 0)
    def _():
        place[...] = onehot(iota((ROWS, SENT), 0) == pos_row[...])

    rows = dot(place[...], recv_ref[...]).astype(BF)
    out_ref[...] = rows
    tail_ref[...] = rows[ROWS - TAPS :]


def place_product(pos_row, received):
    width = received.shape[1]
    return pl.pallas_call(
        place_product_kernel,
        grid=(width // CB,),
        in_specs=[whole((1, SENT)), cols(SENT)],
        out_specs=[cols(ROWS), cols(TAPS)],
        out_shape=[sds((ROWS, width), BF), sds((TAPS, width), BF)],
        scratch_shapes=[pltpu.VMEM((ROWS, SENT), BF)],
        compiler_params=params(),
        cost_estimate=cost(2 * SENT * ROWS * width, 2 * width * (SENT + ROWS + TAPS)),
    )(pos_row, received)


def segment_dft(docs_window):
    place = jnp.arange(WIN, dtype=I32)
    docs = jnp.where(place >= 1, docs_window, -1)
    ids = jnp.arange(NDOCS, dtype=I32)
    inside = docs[None, :] == ids[:, None]
    span = jnp.sum(inside.astype(I32), axis=1)
    own = jnp.sum((inside & (place >= TAPS)[None, :]).astype(I32), axis=1)
    first = jnp.min(jnp.where(inside, place[None, :], 2 * WIN), axis=1)
    taps = jnp.minimum(TAPS, span)
    length = jnp.maximum(span, own + taps - 1)
    length = length + 1 - length % 2
    slots = jnp.where(own > 0, (length + 1) // 2, 0)
    start = jnp.sum(jnp.where(ids[None, :] < ids[:, None], slots[None, :], 0), axis=1)
    slot = jnp.arange(FREQ, dtype=I32)[:, None]
    member = (slot >= start[None, :]) & (slot < (start + slots)[None, :])

    def pick(value):
        return jnp.sum(jnp.where(member, value[None, :], 0), axis=1, keepdims=True)

    live = pick(jnp.ones_like(ids)) > 0
    doc = jnp.where(live, pick(ids), -9)
    wave = slot - pick(start)
    size = jnp.where(live, pick(length), 1)
    size_f = size.astype(F32)
    inverse = 1.0 / size_f

    def angles(steps):
        turns = (wave * steps).astype(F32)
        turns = turns - jnp.floor(turns * inverse) * size_f
        return turns * (inverse * (2.0 * jnp.pi))

    turn = angles(place[None, :] - pick(first))
    mask = docs[None, :] == doc
    spectrum = jnp.concatenate(
        [jnp.where(mask, jnp.cos(turn), 0.0), jnp.where(mask, -jnp.sin(turn), 0.0)], axis=0
    ).astype(BF)
    lag = jnp.arange(TAPS, dtype=I32)[None, :]
    turn = angles(lag)
    weight = jnp.where(
        live & (lag < pick(taps)), jnp.where(wave == 0, inverse, 2.0 * inverse), 0.0
    )
    taps_spectrum = jnp.concatenate(
        [weight * jnp.cos(turn), -weight * jnp.sin(turn)], axis=0
    ).astype(BF)
    return spectrum, taps_spectrum


def mixture_kernel(cc, cc_own_t, bb, product, halo, filt, mix_ref, x_ref, f_ref):
    window = jnp.concatenate([halo[...], product[...]], axis=0)
    x = dot(cc[...], window)
    f = dot(bb[...], filt[...].astype(BF))
    xr, xi, fr, fi = x[:FREQ], x[FREQ:], f[:FREQ], f[FREQ:]
    y = jnp.concatenate(
        [(xr * fr - xi * fi).astype(BF), (xr * fi + xi * fr).astype(BF)], axis=0
    )
    mix_ref[...] = dot(cc_own_t[...], y)
    x_ref[...] = x.astype(BF)
    f_ref[...] = f.astype(BF)


def forward_mixture(spectrum, spectrum_t, taps_spectrum, product, halo, filt):
    width = product.shape[1]
    return pl.pallas_call(
        mixture_kernel,
        grid=(width // CB,),
        in_specs=[
            whole((2 * FREQ, WIN)),
            whole((ROWS, 2 * FREQ)),
            whole((2 * FREQ, TAPS)),
            cols(ROWS),
            cols(TAPS),
            cols(TAPS),
        ],
        out_specs=[cols(ROWS), cols(2 * FREQ), cols(2 * FREQ)],
        out_shape=[
            sds((ROWS, width), F32),
            sds((2 * FREQ, width), BF),
            sds((2 * FREQ, width), BF),
        ],
        compiler_params=params(),
        cost_estimate=cost(2 * 2 * FREQ * (WIN + TAPS + ROWS) * width, width * 8000),
    )(spectrum, spectrum_t[TAPS:], taps_spectrum, product, halo, filt)


def row_sums_kernel(pos_row, recv, mix, residual, cot, gain, q_ref, sums_ref, place, acc):
    step = pl.program_id(0)

    @pl.when(step == 0)
    def _():
        place[...] = onehot(iota((ROWS, SENT), 0) == pos_row[...])
        acc[...] = jnp.zeros_like(acc)

    q = dot(place[...], recv[...])
    q_ref[...] = q.astype(BF)
    summed = residual[...].astype(F32) + q * mix[...]
    scaled = cot[...].astype(F32) * gain[...]
    squares = jnp.sum(summed * summed, axis=1, keepdims=True)
    dots = jnp.sum(scaled * summed, axis=1, keepdims=True)
    lane = iota((ROWS, 128), 1)
    acc[...] += jnp.where(lane == 0, squares, jnp.where(lane == 1, dots, 0.0))

    @pl.when(step == pl.num_programs(0) - 1)
    def _():
        sums_ref[...] = jnp.transpose(acc[...])[:8]


def row_sums(pos_row, received, mix, residual, cot, gain):
    width = mix.shape[1]
    return pl.pallas_call(
        row_sums_kernel,
        grid=(width // CB,),
        in_specs=[whole((1, SENT)), cols(SENT), cols(ROWS), cols(ROWS), cols(ROWS), cols(1)],
        out_specs=[cols(ROWS), whole((8, ROWS))],
        out_shape=[sds((ROWS, width), BF), sds((8, ROWS), F32)],
        scratch_shapes=[pltpu.VMEM((ROWS, SENT), BF), pltpu.VMEM((ROWS, 128), F32)],
        compiler_params=params(),
        cost_estimate=cost(2 * SENT * ROWS * width, width * 4000),
    )(pos_row, received, mix, residual, cot, gain)


def tap_rows(shape, tap_dim, step):
    tap = iota(shape, tap_dim)
    return (tap // 4) * PAIR + tap % 4 + 4 * step


def backward_kernel(
    blocks,
    s0, s1, s2, s3, pos_col, cc_own, bb_t, q_ref, mix_ref, res_ref, cot_ref, gain_ref, x_ref, f_ref,
    normed_ref, dres_ref, z_ref, out_ref,
    give, stats, taps_acc, gain_acc,
):
    step = pl.program_id(0)

    @pl.when(step == 0)
    def _():
        give[...] = onehot(pos_col[...] == iota((SENT, ROWS), 1))
        sums = s0[...] + s1[...] + s2[...] + s3[...]
        tall = jnp.concatenate([sums, jnp.zeros((120, ROWS), F32)], axis=0)
        sums = jnp.transpose(tall)
        inv = lax.rsqrt(sums[:, 0:1] / D + NORM_EPS)
        lane = iota((ROWS, 128), 1)
        stats[...] = jnp.where(lane == 0, inv, sums)
        taps_acc[...] = jnp.zeros_like(taps_acc)
        gain_acc[...] = jnp.zeros_like(gain_acc)

    @pl.when(step < blocks)
    def _():
        inv = stats[:, 0:1]
        row_dot = stats[:, 1:2]
        gain = gain_ref[...]
        q = q_ref[...].astype(F32)
        mix = mix_ref[...]
        summed = res_ref[...].astype(F32) + q * mix
        cot = cot_ref[...].astype(F32)
        scaled = cot * gain
        unit = summed * inv
        normed_ref[...] = (unit * gain).astype(BF)
        gain_part = jnp.sum(cot * unit, axis=0, keepdims=True)
        d_summed = inv * scaled - summed * (inv * inv * inv) * row_dot / D
        dres_ref[...] = d_summed.astype(BF)
        out_ref[...] = dot(give[...], (d_summed * mix).astype(BF)).astype(BF)
        g = dot(cc_own[...], (d_summed * q).astype(BF))
        gr, gi = g[:FREQ], g[FREQ:]
        xr, xi = x_ref[:FREQ].astype(F32), x_ref[FREQ:].astype(F32)
        v = jnp.concatenate(
            [(gr * xr + gi * xi).astype(BF), (gi * xr - gr * xi).astype(BF)], axis=0
        )
        taps = dot(bb_t[...], v)
        fr, fi = f_ref[:FREQ].astype(F32), f_ref[FREQ:].astype(F32)
        z_ref[:FREQ] = (gr * fr + gi * fi).astype(BF)
        z_ref[FREQ:] = (gi * fr - gr * fi).astype(BF)
        spread = onehot(iota((SENT, TAPS), 0) == tap_rows((SENT, TAPS), 1, step))
        taps_acc[...] += dot(spread, taps.astype(BF))
        for i in range(CB // 128):
            row = iota((PAIR, 128), 0) == step * (CB // 128) + i
            gain_acc[...] += jnp.where(row, gain_part[:, 128 * i : 128 * (i + 1)], 0.0)

    @pl.when(step == blocks)
    def _():
        out_ref[...] = taps_acc[...].astype(BF)

    @pl.when(step == blocks + 1)
    def _():
        rows = jnp.broadcast_to(gain_acc[...][None], (SHARDS, PAIR, 128)).reshape(SENT, 128)
        out_ref[:, :128] = rows.astype(BF)


def backward(sums, pos_col, cc_own, bb_t, q, mix, residual, cot, gain, x, f):
    width = q.shape[1]
    blocks = width // CB
    last = blocks - 1
    return pl.pallas_call(
        functools.partial(backward_kernel, blocks),
        grid=(blocks + 2,),
        in_specs=[whole((8, ROWS))] * 4
        + [
            whole((SENT, 1)),
            whole((2 * FREQ, ROWS)),
            whole((TAPS, 2 * FREQ)),
            cols(ROWS, last=last),
            cols(ROWS, last=last),
            cols(ROWS, last=last),
            cols(ROWS, last=last),
            cols(1, last=last),
            cols(2 * FREQ, last=last),
            cols(2 * FREQ, last=last),
        ],
        out_specs=[
            cols(ROWS, last=last),
            cols(ROWS, last=last),
            cols(2 * FREQ, last=last),
            cols(SENT),
        ],
        out_shape=[
            sds((ROWS, width), BF),
            sds((ROWS, width), BF),
            sds((2 * FREQ, width), BF),
            sds((SENT, width + CB + 128), BF),
        ],
        scratch_shapes=[
            pltpu.VMEM((SENT, ROWS), BF),
            pltpu.VMEM((ROWS, 128), F32),
            pltpu.VMEM((SENT, CB), F32),
            pltpu.VMEM((PAIR, 128), F32),
        ],
        compiler_params=params(),
        cost_estimate=cost(3e9, width * 9000),
    )(*sums, pos_col, cc_own, bb_t, q, mix, residual, cot, gain, x, f)


def product_grad_kernel(cc_t, z_ref, own_ref, head_ref):
    grad = dot(cc_t[...], z_ref[...])
    head_ref[...] = grad[:TAPS].astype(BF)
    own_ref[...] = grad[TAPS:]


def product_grad(spectrum_t, z):
    width = z.shape[1]
    return pl.pallas_call(
        product_grad_kernel,
        grid=(width // CB,),
        in_specs=[whole((WIN, 2 * FREQ)), cols(2 * FREQ)],
        out_specs=[cols(ROWS), cols(TAPS)],
        out_shape=[sds((ROWS, width), F32), sds((TAPS, width), BF)],
        compiler_params=params(),
        cost_estimate=cost(2 * WIN * 2 * FREQ * width, width * 2600),
    )(spectrum_t, z)


def give_back_kernel(blocks, pos_col, own_ref, next_ref, out_ref, give):
    step = pl.program_id(0)

    @pl.when(step == 0)
    def _():
        give[...] = onehot(pos_col[...] == iota((SENT, ROWS), 1))

    own = own_ref[...]
    grad = jnp.concatenate(
        [own[: ROWS - TAPS], own[ROWS - TAPS :] + next_ref[...].astype(F32)], axis=0
    )
    out_ref[...] = dot(give[...], grad.astype(BF)).astype(BF)


def give_back(pos_col, own, from_next):
    width = own.shape[1]
    blocks = width // CB
    return pl.pallas_call(
        functools.partial(give_back_kernel, blocks),
        grid=(blocks,),
        in_specs=[whole((SENT, 1)), cols(ROWS), cols(TAPS)],
        out_specs=cols(SENT),
        out_shape=sds((SENT, width + CB), BF),
        scratch_shapes=[pltpu.VMEM((SENT, ROWS), BF)],
        compiler_params=params(),
        cost_estimate=cost(2 * SENT * ROWS * width, width * 2400),
    )(pos_col, own, from_next)


def reduce_kernel(taps_ref, gain_ref, rows_ref, out_ref, d_gain_ref):
    total = jnp.sum(taps_ref[...].astype(F32).reshape(SHARDS, PAIR, CB), axis=0)
    out_ref[...] = (
        jnp.broadcast_to(total[None], (SHARDS, PAIR, CB)).reshape(SENT, CB).astype(BF)
    )
    d_gain_ref[...] = jnp.sum(gain_ref[...].astype(F32).reshape(SHARDS, PAIR, 128), axis=0)


def reduce_parts(received, rows):
    width = rows.shape[1] - CB
    blocks = width // CB
    return pl.pallas_call(
        reduce_kernel,
        grid=(1,),
        in_specs=[
            pl.BlockSpec((SENT, CB), lambda j: (0, blocks)),
            pl.BlockSpec((SENT, 128), lambda j: (0, (width + CB) // 128)),
            pl.BlockSpec(memory_space=pl.ANY),
        ],
        out_specs=[
            pl.BlockSpec((SENT, CB), lambda j: (0, blocks)),
            whole((PAIR, 128)),
        ],
        out_shape=[sds(rows.shape, BF), sds((PAIR, 128), F32)],
        input_output_aliases={2: 0},
        compiler_params=params(),
        cost_estimate=cost(SENT * CB, SENT * CB * 4),
    )(received, received, rows)


def build_home(owner_col, owner_row, home):
    same = (owner_col == owner_row) & (iota((SLOTS, SLOTS), 1) < iota((SLOTS, SLOTS), 0))
    rank = jnp.sum(jnp.where(same, 1, 0), axis=1, keepdims=True)
    slot = jnp.where(owner_col >= 0, owner_col * PAIR + rank, -1)
    home[...] = onehot(iota((SLOTS, SENT), 1) == slot)


def home_rows_kernel(owner_col, owner_row, back_ref, out_ref, home):
    @pl.when(pl.program_id(0) == 0)
    def _():
        build_home(owner_col[...], owner_row[...], home)

    out_ref[...] = dot(home[...], back_ref[...]).astype(BF)


def home_rows(owner_col, owner_row, back, width):
    return pl.pallas_call(
        home_rows_kernel,
        grid=(width // CB,),
        in_specs=[whole((SLOTS, 1)), whole((1, SLOTS)), cols(SENT)],
        out_specs=cols(SLOTS),
        out_shape=sds((SLOTS, width), BF),
        scratch_shapes=[pltpu.VMEM((SLOTS, SENT), BF)],
        compiler_params=params(),
        cost_estimate=cost(2 * SENT * SLOTS * width, 2 * width * (SENT + SLOTS)),
    )(owner_col, owner_row, back)


def home_product_kernel(
    owner_col, owner_row, back_ref, taps_ref, k_ref, v_ref, dk_ref, dv_ref, filt_ref, home
):
    step = pl.program_id(0)

    @pl.when(step == 0)
    def _():
        build_home(owner_col[...], owner_row[...], home)

    grad = dot(home[...], back_ref[...])
    dk_ref[...] = (grad * v_ref[...].astype(F32)).astype(BF)
    dv_ref[...] = (grad * k_ref[...].astype(F32)).astype(BF)
    gather = onehot(iota((TAPS, SENT), 1) == tap_rows((TAPS, SENT), 0, step))
    filt_ref[...] = dot(gather, taps_ref[...])


def home_product(owner_col, owner_row, back, k, v):
    width = k.shape[1]
    blocks = width // CB
    return pl.pallas_call(
        home_product_kernel,
        grid=(blocks,),
        in_specs=[
            whole((SLOTS, 1)),
            whole((1, SLOTS)),
            cols(SENT),
            pl.BlockSpec((SENT, CB), lambda j: (0, blocks)),
            cols(SLOTS),
            cols(SLOTS),
        ],
        out_specs=[cols(SLOTS), cols(SLOTS), cols(TAPS)],
        out_shape=[sds((SLOTS, width), BF), sds((SLOTS, width), BF), sds((TAPS, width), F32)],
        scratch_shapes=[pltpu.VMEM((SLOTS, SENT), BF)],
        compiler_params=params(),
        cost_estimate=cost(2 * SENT * SLOTS * width, 2 * width * (SENT + 5 * SLOTS)),
    )(owner_col, owner_row, back, back, k, v)


def exchange(rows):
    shards = rows.reshape(SHARDS, PAIR, rows.shape[1])
    return lax.all_to_all(shards, "seq", split_axis=0, concat_axis=0, tiled=True).reshape(
        rows.shape
    )


def shift(value, steps):
    pairs = [(i, i + steps) for i in range(SHARDS) if 0 <= i + steps < SHARDS]
    return lax.ppermute(value, "seq", pairs)


def slot_positions(dest_table, my_index):
    arriving = (dest_table >= 0) & (dest_table // ROWS == my_index)
    before = (jnp.arange(SLOTS)[:, None] < jnp.arange(SLOTS)[None, :]).astype(BF)
    rank = jnp.dot(arriving.astype(BF), before, preferred_element_type=F32).astype(I32)
    rank = jnp.where(arriving, rank, -1)
    target = dest_table - my_index * ROWS + 1
    hit = rank[:, None, :] == jnp.arange(PAIR, dtype=I32)[None, :, None]
    return (jnp.sum(jnp.where(hit, target[:, None, :], 0), axis=2) - 1).reshape(SENT)


def body(q_in, k_in, v_in, dest_pos, doc_ids, mr_filter, norm_gain, residual, cotangent):
    my_index = lax.axis_index("seq")
    width = q_in.shape[1]
    gain = norm_gain[None, :]

    own_plan = lax.dynamic_slice_in_dim(dest_pos, my_index * SLOTS, SLOTS)
    own_owner = jnp.where(own_plan >= 0, own_plan // ROWS, -1)
    owner_col, owner_row = own_owner[:, None], own_owner[None, :]

    sent_product = pack_arrivals(pack_product_kernel, owner_col, owner_row, [k_in, v_in], width)
    sent_product, dest_later, docs_later, owner_col, owner_row = lax.optimization_barrier(
        (sent_product, dest_pos, doc_ids, owner_col, owner_row)
    )
    recv_product = exchange(sent_product)
    sent_q = pack_arrivals(pack_rows_kernel, owner_col, owner_row, [q_in], width)

    pos = slot_positions(dest_later.reshape(SHARDS, SLOTS), my_index)
    pos_row, pos_col = pos[None, :], pos[:, None]
    docs_all = jnp.concatenate([jnp.full((TAPS,), -1, I32), docs_later])
    docs_window = lax.dynamic_slice_in_dim(docs_all, my_index * ROWS, WIN)
    spectrum, taps_spectrum = segment_dft(docs_window)
    spectrum_t = spectrum.T
    taps_spectrum_t = taps_spectrum.T

    sent_q, recv_product, pos_row, pos_col, spectrum, spectrum_t, taps_spectrum, taps_spectrum_t = (
        lax.optimization_barrier(
            (sent_q, recv_product, pos_row, pos_col, spectrum, spectrum_t, taps_spectrum, taps_spectrum_t)
        )
    )
    recv_q = exchange(sent_q)
    product, tail = place_product(pos_row, recv_product)
    halo = shift(tail, 1)
    mix, x, f = forward_mixture(
        spectrum, spectrum_t, taps_spectrum, product, halo, mr_filter
    )
    recv_q, mix = lax.optimization_barrier((recv_q, mix))
    q_pos, sums = row_sums(pos_row, recv_q, mix, residual, cotangent, gain)
    all_sums = [sums] + [
        lax.ppermute(sums, "mp", [(i, (i + k) % 4) for i in range(4)]) for k in (1, 2, 3)
    ]
    normed, d_residual, z, sent_dq = backward(
        all_sums, pos_col, spectrum[:, TAPS:], taps_spectrum_t,
        q_pos, mix, residual, cotangent, gain, x, f,
    )
    back_q = exchange(sent_dq)
    own_grad, head_grad = product_grad(spectrum_t, z)
    from_next = shift(head_grad, -1)
    rows = give_back(pos_col, own_grad, from_next)
    sent_dp, d_gain = reduce_parts(back_q, rows)
    back_p = exchange(sent_dp)
    d_q_in = home_rows(owner_col, owner_row, back_q, width)
    d_k_in, d_v_in, d_filter = home_product(owner_col, owner_row, back_p, k_in, v_in)
    return (normed, d_residual, d_q_in, d_k_in, d_v_in, d_filter, d_gain.reshape(width))


def solution(mesh):
    return jax.shard_map(
        body,
        mesh=mesh,
        in_specs=(
            P("seq", "mp"),
            P("seq", "mp"),
            P("seq", "mp"),
            P(),
            P(),
            P(None, "mp"),
            P("mp"),
            P("seq", "mp"),
            P("seq", "mp"),
        ),
        out_specs=(
            P("seq", "mp"),
            P("seq", "mp"),
            P("seq", "mp"),
            P("seq", "mp"),
            P("seq", "mp"),
            P(None, "mp"),
            P("mp"),
        ),
        check_vma=False,
    )
```

time: 1660 us -> 231 us (0.14)
  other arithmetic: 1220 us -> 7.18 us
  blocking collectives: 95.9 us -> 0 us
  local copies, waits for them, and re-layouts: 137 us -> 44.6 us
  Pallas kernels: 0 us -> 42 us
  waiting for transfers between devices: 127 us -> 95.1 us
  between operations: 18.4 us -> 1 us
    convert_element_type x5 -> x0, other arithmetic: 794 us -> none  [the longest x1 790 us: body(): (d_product.astype(jnp.float32) * k_pos.astype(jnp.float32)).astype(jnp.bf...]
    reduce_sum x26 -> x3, other arithmetic: 331 us -> 0.88 us  [the longest x1 0.62 us: slot_positions(): jnp.sum(jnp.where(hit, target[:, None, :], 0), axis=2) - 1]
    psum x3 -> x0, blocking collectives: 95.9 us -> none  [the longest x1 79.6 us: body(): d_filter, d_gain = lax.psum((filter_part, gain_part), 'seq')]
    psum x1 -> x0, waiting for transfers between devices: 74.7 us -> none  [body(): d_filter, d_gain = lax.psum((filter_part, gain_part), 'seq')]
    scatter x5 -> x0, local copies, waits for them, and re-layouts: 63.1 us -> none  [the longest x1 45.4 us: body(): source_row = jnp.zeros((row_count,), jnp.int32).at[local_target.reshape(-...]
    concatenate x11 -> x2, other arithmetic: 60.4 us -> 1.7 us  [the longest x1 0.94 us: segment_dft(): jnp.concatenate([jnp.where(mask, jnp.cos(turn), 0.0), jnp.where(mask, -jn...]
    ppermute x2 -> x5, waiting for transfers between devices: 0.01 us -> 47.3 us  [the longest x2 47.3 us: shift(): return lax.ppermute(value, 'seq', pairs)]
    gather x9 -> x0, local copies, waits for them, and re-layouts: 45.3 us -> none  [the longest x3 20.5 us: homecoming(): jnp.take(received.reshape(slot_total, width_local), send_slot, axis=0, mo...]
  transfers between devices with their start and end apart: 9 -> 9, of which waited for: 5 -> 4; matrix products, arithmetic and copies ran while one was open for 17% -> 7% of each run, Pallas kernels for 0% -> 8%
where the time goes in v1:
time: 231 us; the launch traced here: 229 us
  waiting for transfers between devices  95.1 us (41%)
  local copies, waits for them, and re-layouts  44.6 us (19%)
  Pallas kernels  42 us (18%)
  starting transfers between devices  39 us (17%)
  other arithmetic  7.18 us (3%)
    all_to_all x4, waiting for transfers between devices, exchange(): lax.all_to_all(shards, 'seq', split_axis=0, concat_axis=0, tiled=True)  47.7 us
    ppermute x2, waiting for transfers between devices, shift(): return lax.ppermute(value, 'seq', pairs)  47.3 us
    unnamed x74, local copies, waits for them, and re-layouts  35.6 us
    all_to_all x4, starting transfers between devices, exchange(): lax.all_to_all(shards, 'seq', split_axis=0, concat_axis=0, tiled=True)  28.7 us
    pallas_call x1, Pallas kernels, backward(): pl.pallas_call(functools.partial(backward_kernel, blocks), grid=(blocks +...  10.7 us
    pallas_call x2, Pallas kernels, pack_arrivals(): pl.pallas_call(kernel, grid=(width // CB,), in_specs=[whole((SLOTS, 1)),...  5.89 us
    ppermute x2, starting transfers between devices, shift(): return lax.ppermute(value, 'seq', pairs)  5.86 us
    pallas_call x1, Pallas kernels, forward_mixture(): pl.pallas_call(mixture_kernel, grid=(width // CB,), in_specs=[whole((2 *...  5.73 us
  transfers between devices with their start and end apart: 9, of which 4 were waited for; matrix products, arithmetic and copies ran while one was open for 7% of the time, Pallas kernels for 8%

profile of v1, /device:TPU:1, one launch (start us, length us, event | category | flops | bytes accessed | tf_op | source)
XLA Modules:
  0.0 229.0 jit_solution(1147568502467059862)
XLA Ops:
  0.6 0.8 fusion.22
  1.6 1.4 copy-done.10
  3.0 1.4 copy-done.12
  4.4 3.6 %shard_map.144 = bf16[512,2048]{1,0:T(8,128)(2,1)} custom-call(s32[384,1]{1,0:T(8,128)S(1)} %copy.29.owner_col, s32[1,384]{1,0:T(1,128)S(1)} %broadcast_in_dim.147.owner_row, bf16[384,2048]{1,0:T(8,128)(2,1)S(1)} %copy-done.10, bf16[384,2048]{1,0:T(8,128)(2,1)S(1)} %copy-done.12), custom_call_target="tpu_custom_call" | custom-call | flops 805306368 | bytes 5242880 | tf_op jit(solution)/shard_map/pallas_call | solution.py:89
  8.0 8.7 %all-to-all-start = ((bf16[32,16,2048]{2,1,0:T(8,128)(2,1)}), bf16[32,16,2048]{2,1,0:T(8,128)(2,1)S(1)}, u32[]{:S(2)}, u32[]{:S(2)}) async-start(bf16[32,16,2048]{2,1,0:T(8,128)(2,1)} %bitcast), calls=%async_computation | async-start | bytes 4194304 | tf_op jit(solution)/shard_map/all_to_all | solution.py:503
  16.8 0.2 fusion
  17.0 0.6 select_reduce_fusion
  17.9 0.7 sub.88
  18.9 1.4 copy-done.19
  20.3 2.3 %shard_map.145 = bf16[512,2048]{1,0:T(8,128)(2,1)S(1)} custom-call(s32[384,1]{1,0:T(8,128)S(1)} %copy.30.owner_col, s32[1,384]{1,0:T(1,128)S(1)} %broadcast_in_dim.147.owner_row, bf16[384,2048]{1,0:T(8,128)(2,1)S(1)} %copy-done.19), custom_call_target="tpu_custom_call" | custom-call | flops 805306368 | bytes 3670016 | tf_op jit(solution)/shard_map/pallas_call | solution.py:89
  22.8 0.8 fusion.3
  23.8 0.8 pad_maximum_fusion.1
  24.5 2.4 %fusion.1 = (bf16[320,384]{0,1:T(8,128)(2,1)S(1)}, bf16[320,384]{0,1:T(8,128)(2,1)S(1)}) fusion(f32[320]{0:T(512)S(1)} %broadcast_multiply_fusion, f32[320]{0:T(512)S(1)} %get-tuple-element.84, f32[320]{0:T(512)S(1)} %get-tuple-element.83, s32[320]{0:T(512)S(1)} %get-tuple-element.79, s32[320]{0:T(512)S(1)} %get-tuple-element.93, ...), kind=kLoop, calls=%fused_computation.6 | loop fusion | flops 1720320 | bytes 500736 | tf_op jit(solution)/shard_map/convert.2
  27.2 0.9 pad_maximum_fusion
  28.1 16.9 %all-to-all-done = bf16[32,16,2048]{2,1,0:T(8,128)(2,1)S(1)} async-done(((bf16[32,16,2048]{2,1,0:T(8,128)(2,1)}), bf16[32,16,2048]{2,1,0:T(8,128)(2,1)S(1)}, u32[]{:S(2)}, u32[]{:S(2)}) %all-to-all-start) | async-done | bytes 2097184 | tf_op jit(solution)/shard_map/all_to_all | solution.py:503
  45.0 1.3 copy-done.7
  46.3 4.5 %all-to-all-start.1 = ((bf16[32,16,2048]{2,1,0:T(8,128)(2,1)}), bf16[32,16,2048]{2,1,0:T(8,128)(2,1)S(1)}, u32[]{:S(2)}, u32[]{:S(2)}) async-start(bf16[32,16,2048]{2,1,0:T(8,128)(2,1)} %bitcast.20), calls=%async_computation.1 | async-start | bytes 4194304 | tf_op jit(solution)/shard_map/all_to_all | solution.py:503
  50.9 1.6 copy-done.8
  52.5 2.5 %shard_map.146 = (bf16[256,2048]{1,0:T(8,128)(2,1)S(1)}, bf16[128,2048]{1,0:T(8,128)(2,1)}) custom-call(s32[1,512]{1,0:T(1,128)S(1)} %sub.87.pos_row, bf16[512,2048]{1,0:T(8,128)(2,1)S(1)} %bitcast.19), custom_call_target="tpu_custom_call" | custom-call | flops 536870912 | bytes 3670016 | tf_op jit(solution)/shard_map/pallas_call | solution.py:115
  54.9 1.0 copy-done.30
  55.9 3.5 %collective-permute-start = (bf16[128,2048]{1,0:T(8,128)(2,1)}, bf16[128,2048]{1,0:T(8,128)(2,1)S(1)}, u32[]{:S(2)}, u32[]{:S(2)}) collective-permute-start(bf16[128,2048]{1,0:T(8,128)(2,1)} %get-tuple-element.52), channel_id=1, source_target_pairs={{0,4},{4,8},{8,12},{12,16},{16,20},{20,24},{24,28},{28,32},{32,36}... | collective-permute-start | bytes 1572872 | tf_op jit(solution)/shard_map/ppermute | solution.py:510
  59.4 1.7 copy.32.bb
  61.1 2.0 copy.31.cc
  63.2 16.6 %collective-permute-done.halo = bf16[128,2048]{1,0:T(8,128)(2,1)S(1)} collective-permute-done((bf16[128,2048]{1,0:T(8,128)(2,1)}, bf16[128,2048]{1,0:T(8,128)(2,1)S(1)}, u32[]{:S(2)}, u32[]{:S(2)}) %collective-permute-start) | collective-permute-done | bytes 524320 | tf_op jit(solution)/shard_map/ppermute | solution.py:510
  79.8 0.8 copy-done.32
  80.6 1.0 copy-done.25
  81.6 0.9 copy-done.26
  82.5 1.2 copy-done.29
  83.7 1.2 copy-done.31
  85.0 1.0 copy-done.33
  86.0 5.7 %shard_map.147 = (f32[256,2048]{1,0:T(8,128)S(1)}, bf16[640,2048]{1,0:T(8,128)(2,1)}, bf16[640,2048]{1,0:T(8,128)(2,1)}) custom-call(bf16[640,384]{1,0:T(8,128)(2,1)S(1)} %copy-done.25, bf16[256,640]{1,0:T(8,128)(2,1)S(1)} %slice.6.cc_own_t, bf16[640,128]{1,0:T(8,128)(2,1)S(1)} %copy-done.26, bf16[256,2048]{1,0:T(8,128)(2,1)S(1)} %copy-done.31, ...), custom_call_target="tpu_custom_call" | custom-call | flops 2013265920 | bytes 16384000 | tf_op jit(solution)/shard_map/pallas_call | solution.py:189
  91.8 1.4 copy-done.3
  93.1 1.3 copy-done.5
  94.5 1.6 copy-done.6
  96.1 1.2 copy-done.15
  97.3 4.0 %shard_map.148 = (bf16[256,2048]{1,0:T(8,128)(2,1)S(1)}, f32[8,256]{1,0:T(8,128)S(1)}) custom-call(s32[1,512]{1,0:T(1,128)S(1)} %sub.87.pos_row, bf16[512,2048]{1,0:T(8,128)(2,1)S(1)} %bitcast.18, f32[256,2048]{1,0:T(8,128)} %copy-done.3, bf16[256,2048]{1,0:T(8,128)(2,1)S(1)} %copy-done.14, bf16[256,2048]{1,0:T(8,128)(2,1)S(1)} %copy-done.15, ...), custom_call_target="tpu_custom_call" | custom-call | flops 536870912 | bytes 8192000 | tf_op jit(solution)/shard_map/pallas_call | solution.py:235
  101.3 1.0 copy-done.23
  102.2 3.8 %collective-permute-start.3 = (f32[8,256]{1,0:T(8,128)S(1)}, f32[8,256]{1,0:T(8,128)S(1)}, u32[]{:S(2)}, u32[]{:S(2)}) collective-permute-start(f32[8,256]{1,0:T(8,128)S(1)} %get-tuple-element.56.s0), channel_id=1, source_target_pairs={{0,3},{1,0},{2,1},{3,2},{4,7},{5,4},{6,5},{7,6},{8,11},{9,8},{10,9... | collective-permute-start | bytes 24584 | tf_op jit(solution)/shard_map/ppermute | solution.py:561
  106.0 0.7 collective-permute-start.1
  106.7 0.8 slice.7
  107.5 1.5 copy.33.pos_col
  109.0 1.9 copy.34.cc_own
  110.9 1.2 copy-done.16
  112.1 0.9 copy-done.17
  113.1 1.0 copy-done.22
  114.1 1.2 copy-done.24
  115.3 10.7 %shard_map.149 = (bf16[256,2048]{1,0:T(8,128)(2,1)}, bf16[256,2048]{1,0:T(8,128)(2,1)}, bf16[640,2048]{1,0:T(8,128)(2,1)}, bf16[512,2688]{1,0:T(8,128)(2,1)}) custom-call(f32[8,256]{1,0:T(8,128)S(1)} %get-tuple-element.56.s0, f32[8,256]{1,0:T(8,128)S(1)} %collective-permute-done.1.s1, f32[8,256]{1,0:T(8,128)S(1)} %collective-permute-done.2.s2, ...), custom_call_target="tpu_custom_call" | custom-call | flops 3000000000 | bytes 18432000 | tf_op jit(solution)/shard_map/pallas_call | solution.py:318
  125.9 9.1 %all-to-all-start.2 = ((bf16[32,16,2688]{2,1,0:T(8,128)(2,1)}), bf16[32,16,2688]{2,1,0:T(8,128)(2,1)S(1)}, u32[]{:S(2)}, u32[]{:S(2)}) async-start(bf16[32,16,2688]{2,1,0:T(8,128)(2,1)} %bitcast.23), calls=%async_computation.2 | async-start | bytes 5505024 | tf_op jit(solution)/shard_map/all_to_all | solution.py:503
  135.1 1.1 copy-done.21
  136.2 1.7 copy-done.28
  137.9 2.3 %shard_map.151 = (f32[256,2048]{1,0:T(8,128)S(1)}, bf16[128,2048]{1,0:T(8,128)(2,1)S(1)}) custom-call(bf16[384,640]{1,0:T(8,128)(2,1)S(1)} %copy-done.21, bf16[640,2048]{1,0:T(8,128)(2,1)S(1)} %copy-done.28), custom_call_target="tpu_custom_call" | custom-call | flops 1006632960 | bytes 5324800 | tf_op jit(solution)/shard_map/pallas_call | solution.py:365
  140.2 2.3 %collective-permute-start.4 = (bf16[128,2048]{1,0:T(8,128)(2,1)S(1)}, bf16[128,2048]{1,0:T(8,128)(2,1)S(1)}, u32[]{:S(2)}, u32[]{:S(2)}) collective-permute-start(bf16[128,2048]{1,0:T(8,128)(2,1)S(1)} %get-tuple-element.67), channel_id=1, source_target_pairs={{4,0},{8,4},{12,8},{16,12},{20,16},{24,20},{28,24},{32,28},{36,32}... | collective-permute-start | bytes 1572872 | tf_op jit(solution)/shard_map/ppermute | solution.py:510
  142.6 30.7 %collective-permute-done.4.next_ref = bf16[128,2048]{1,0:T(8,128)(2,1)S(1)} collective-permute-done((bf16[128,2048]{1,0:T(8,128)(2,1)S(1)}, bf16[128,2048]{1,0:T(8,128)(2,1)S(1)}, u32[]{:S(2)}, u32[]{:S(2)}) %collective-permute-start.4) | collective-permute-done | bytes 524320 | tf_op jit(solution)/shard_map/ppermute | solution.py:510
  173.3 1.7 shard_map.152.rows_ref
  175.0 1.5 copy-done
  176.5 1.7 copy-done.1
  178.2 0.8 shard_map.153
  179.0 1.5 copy-done.2
  180.5 6.3 %all-to-all-start.3 = ((bf16[32,16,2560]{2,1,0:T(8,128)(2,1)}), bf16[32,16,2560]{2,1,0:T(8,128)(2,1)}, u32[]{:S(2)}, u32[]{:S(2)}) async-start(bf16[32,16,2560]{2,1,0:T(8,128)(2,1)} %bitcast.17), calls=%async_computation.3 | async-start | bytes 5242880 | tf_op jit(solution)/shard_map/all_to_all | solution.py:503
  186.8 3.1 %shard_map.150 = bf16[384,2048]{1,0:T(8,128)(2,1)} custom-call(s32[384,1]{1,0:T(8,128)S(1)} %copy.30.owner_col, s32[1,384]{1,0:T(1,128)S(1)} %broadcast_in_dim.147.owner_row, bf16[512,2688]{1,0:T(8,128)(2,1)S(1)} %bitcast.16), custom_call_target="tpu_custom_call" | custom-call | flops 805306368 | bytes 3670016 | tf_op jit(solution)/shard_map/pallas_call | solution.py:451
  190.0 30.8 %all-to-all-done.3 = bf16[32,16,2560]{2,1,0:T(8,128)(2,1)} async-done(((bf16[32,16,2560]{2,1,0:T(8,128)(2,1)}), bf16[32,16,2560]{2,1,0:T(8,128)(2,1)}, u32[]{:S(2)}, u32[]{:S(2)}) %all-to-all-start.3) | async-done | bytes 2621472 | tf_op jit(solution)/shard_map/all_to_all | solution.py:503
  220.8 1.4 copy-done.11
  222.2 1.4 copy-done.13
  223.6 5.4 %shard_map.154 = (bf16[384,2048]{1,0:T(8,128)(2,1)}, bf16[384,2048]{1,0:T(8,128)(2,1)}, f32[128,2048]{1,0:T(8,128)}) custom-call(s32[384,1]{1,0:T(8,128)S(1)} %copy.30.owner_col, s32[1,384]{1,0:T(1,128)S(1)} %broadcast_in_dim.147.owner_row, bf16[512,2560]{1,0:T(8,128)(2,1)} %bitcast.10.back_ref.taps_ref, bf16[512,2560]{1,0:T(8,128)(2,1)} %bitcast.10.back_ref.taps_ref, ...), custom_call_target="tpu_custom_call" | custom-call | flops 805306368 | bytes 9961472 | tf_op jit(solution)/shard_map/pallas_call | solution.py:482
  (73 shorter events, 1.3 us)
Async XLA Ops:
  1.6 1.4 copy-start.10
  3.0 1.4 copy-start.12
  8.0 8.7 %copy-start.35 = (s32[12288]{0:T(1024)S(1)}, s32[12288]{0:T(1024)}, u32[]{:S(2)}) copy-start(s32[12288]{0:T(1024)} %param.12) | copy-start | bytes 147460
  8.0 9.6 %copy-start.36 = (s32[8192]{0:T(1024)S(1)}, s32[8192]{0:T(1024)}, u32[]{:S(2)}) copy-start(s32[8192]{0:T(1024)} %param.13) | copy-start | bytes 98308
  8.0 37.0 %all-to-all-start = ((bf16[32,16,2048]{2,1,0:T(8,128)(2,1)}), bf16[32,16,2048]{2,1,0:T(8,128)(2,1)S(1)}, u32[]{:S(2)}, u32[]{:S(2)}) async-start(bf16[32,16,2048]{2,1,0:T(8,128)(2,1)} %bitcast), calls=%async_computation | async-start | bytes 4194304 | tf_op jit(solution)/shard_map/all_to_all | solution.py:503
  18.9 1.4 copy-start.19
  22.6 4.5 %copy-start.9 = (bf16[512,2048]{1,0:T(8,128)(2,1)}, bf16[512,2048]{1,0:T(8,128)(2,1)S(1)}, u32[]{:S(2)}) copy-start(bf16[512,2048]{1,0:T(8,128)(2,1)S(1)} %shard_map.145) | copy-start | bytes 6291460
  27.1 36.0 %copy-start.20 = (bf16[384,640]{1,0:T(8,128)(2,1)}, bf16[384,640]{1,0:T(8,128)(2,1)S(1)}, u32[]{:S(2)}) copy-start(bf16[384,640]{1,0:T(8,128)(2,1)S(1)} %fusion.34.cc_t) | copy-start | bytes 1474564
  45.0 1.3 copy-start.7
  46.3 46.8 %all-to-all-start.1 = ((bf16[32,16,2048]{2,1,0:T(8,128)(2,1)}), bf16[32,16,2048]{2,1,0:T(8,128)(2,1)S(1)}, u32[]{:S(2)}, u32[]{:S(2)}) async-start(bf16[32,16,2048]{2,1,0:T(8,128)(2,1)} %bitcast.20), calls=%async_computation.1 | async-start | bytes 4194304 | tf_op jit(solution)/shard_map/all_to_all | solution.py:503
  50.9 1.6 copy-start.8
  54.9 1.0 copy-start.30
  55.9 23.9 %collective-permute-start = (bf16[128,2048]{1,0:T(8,128)(2,1)}, bf16[128,2048]{1,0:T(8,128)(2,1)S(1)}, u32[]{:S(2)}, u32[]{:S(2)}) collective-permute-start(bf16[128,2048]{1,0:T(8,128)(2,1)} %get-tuple-element.52), channel_id=1, source_target_pairs={{0,4},{4,8},{8,12},{12,16},{16,20},{20,24},{24,28},{28,32},{32,36}... | collective-permute-start | bytes 1572872 | tf_op jit(solution)/shard_map/ppermute | solution.py:510
  79.8 0.8 copy-start.32
  80.6 1.0 copy-start.25
  81.6 0.9 copy-start.26
  82.5 1.2 copy-start.29
  83.7 1.2 copy-start.31
  85.0 1.0 copy-start.33
  86.0 8.4 %copy-start.14 = (bf16[256,2048]{1,0:T(8,128)(2,1)S(1)}, bf16[256,2048]{1,0:T(8,128)(2,1)}, u32[]{:S(2)}) copy-start(bf16[256,2048]{1,0:T(8,128)(2,1)} %res_ref.1) | copy-start | bytes 3145732
  86.0 8.4 %copy-start.27 = (f32[2048]{0:T(1024)S(1)}, f32[2048]{0:T(1024)}, u32[]{:S(2)}) copy-start(f32[2048]{0:T(1024)} %param.15) | copy-start | bytes 24580
  91.8 1.4 copy-start.3
  93.1 1.3 copy-start.5
  94.5 1.6 copy-start.6
  96.1 1.2 copy-start.15
  97.3 9.4 %copy-start.34 = (bf16[640,384]{0,1:T(8,128)(2,1)S(1)}, bf16[640,384]{0,1:T(8,128)(2,1)}, u32[]{:S(2)}) copy-start(bf16[640,384]{0,1:T(8,128)(2,1)} %pad_maximum_fusion) | copy-start | bytes 1474564
  97.3 13.6 %copy-start.4 = (f32[256,2048]{1,0:T(8,128)S(1)}, f32[256,2048]{1,0:T(8,128)}, u32[]{:S(2)}) copy-start(f32[256,2048]{1,0:T(8,128)} %copy-done.3) | copy-start | bytes 6291460
  101.3 1.0 copy-start.23
  102.2 8.6 %collective-permute-start.3 = (f32[8,256]{1,0:T(8,128)S(1)}, f32[8,256]{1,0:T(8,128)S(1)}, u32[]{:S(2)}, u32[]{:S(2)}) collective-permute-start(f32[8,256]{1,0:T(8,128)S(1)} %get-tuple-element.56.s0), channel_id=1, source_target_pairs={{0,3},{1,0},{2,1},{3,2},{4,7},{5,4},{6,5},{7,6},{8,11},{9,8},{10,9... | collective-permute-start | bytes 24584 | tf_op jit(solution)/shard_map/ppermute | solution.py:561
  106.0 4.9 %collective-permute-start.2 = (f32[8,256]{1,0:T(8,128)S(1)}, f32[8,256]{1,0:T(8,128)S(1)}, u32[]{:S(2)}, u32[]{:S(2)}) collective-permute-start(f32[8,256]{1,0:T(8,128)S(1)} %get-tuple-element.56.s0), channel_id=1, source_target_pairs={{0,2},{1,3},{2,0},{3,1},{4,6},{5,7},{6,4},{7,5},{8,10},{9,11},{10,... | collective-permute-start | bytes 24584 | tf_op jit(solution)/shard_map/ppermute | solution.py:561
  106.0 4.9 %collective-permute-start.1 = (f32[8,256]{1,0:T(8,128)S(1)}, f32[8,256]{1,0:T(8,128)S(1)}, u32[]{:S(2)}, u32[]{:S(2)}) collective-permute-start(f32[8,256]{1,0:T(8,128)S(1)} %get-tuple-element.56.s0), channel_id=1, source_target_pairs={{0,1},{1,2},{2,3},{3,0},{4,5},{5,6},{6,7},{7,4},{8,9},{9,10},{10,1... | collective-permute-start | bytes 24584 | tf_op jit(solution)/shard_map/ppermute | solution.py:561
  110.9 1.2 copy-start.16
  112.1 0.9 copy-start.17
  113.1 1.0 copy-start.22
  114.1 1.2 copy-start.24
  125.9 50.5 %all-to-all-start.2 = ((bf16[32,16,2688]{2,1,0:T(8,128)(2,1)}), bf16[32,16,2688]{2,1,0:T(8,128)(2,1)S(1)}, u32[]{:S(2)}, u32[]{:S(2)}) async-start(bf16[32,16,2688]{2,1,0:T(8,128)(2,1)} %bitcast.23), calls=%async_computation.2 | async-start | bytes 5505024 | tf_op jit(solution)/shard_map/all_to_all | solution.py:503
  135.1 38.2 %copy-start.18 = (s32[512,1]{1,0:T(8,128)S(1)}, s32[512,1]{1,0:T(8,128)}, u32[]{:S(2)}) copy-start(s32[512,1]{1,0:T(8,128)} %copy.33.pos_col) | copy-start | bytes 6148
  135.1 1.1 copy-start.21
  136.2 1.7 copy-start.28
  140.2 33.0 %collective-permute-start.4 = (bf16[128,2048]{1,0:T(8,128)(2,1)S(1)}, bf16[128,2048]{1,0:T(8,128)(2,1)S(1)}, u32[]{:S(2)}, u32[]{:S(2)}) collective-permute-start(bf16[128,2048]{1,0:T(8,128)(2,1)S(1)} %get-tuple-element.67), channel_id=1, source_target_pairs={{4,0},{8,4},{12,8},{16,12},{20,16},{24,20},{28,24},{32,28},{36,32}... | collective-permute-start | bytes 1572872 | tf_op jit(solution)/shard_map/ppermute | solution.py:510
  174.9 1.5 copy-start
  176.5 1.7 copy-start.1
  179.0 1.5 copy-start.2
  180.5 40.3 %all-to-all-start.3 = ((bf16[32,16,2560]{2,1,0:T(8,128)(2,1)}), bf16[32,16,2560]{2,1,0:T(8,128)(2,1)}, u32[]{:S(2)}, u32[]{:S(2)}) async-start(bf16[32,16,2560]{2,1,0:T(8,128)(2,1)} %bitcast.17), calls=%async_computation.3 | async-start | bytes 5242880 | tf_op jit(solution)/shard_map/all_to_all | solution.py:503
  220.8 1.4 copy-start.11
  222.2 1.4 copy-start.13

commit v2 on v1

v2 whole, which is shorter than its diff:
```python
import functools

import jax
import jax.numpy as jnp
from jax import lax
from jax.experimental import pallas as pl
from jax.experimental.pallas import tpu as pltpu
from jax.sharding import PartitionSpec as P

D = 8192
NORM_EPS = 1e-06
NDOCS = 64
BF = jnp.bfloat16
F32 = jnp.float32
I32 = jnp.int32

ROWS = 256
SLOTS = 384
TAPS = 128
SHARDS = 32
PAIR = 16
WIN = TAPS + ROWS
FREQ = 320
CB = 512


def dot(a, b):
    return jnp.dot(a, b, preferred_element_type=F32)


def iota(shape, dim):
    return lax.broadcasted_iota(I32, shape, dim)


def onehot(match):
    return jnp.where(match, 1.0, 0.0).astype(BF)


def params():
    return pltpu.CompilerParams(
        dimension_semantics=("arbitrary",), vmem_limit_bytes=24 * 1024 * 1024
    )


def cols(rows, width=CB, last=None):
    if last is None:
        return pl.BlockSpec((rows, width), lambda j: (0, j))
    return pl.BlockSpec((rows, width), lambda j: (0, jnp.minimum(j, last)))


def whole(shape):
    return pl.BlockSpec(shape, lambda j: (0,) * len(shape))


def cost(flops, nbytes):
    return pl.CostEstimate(flops=int(flops), transcendentals=0, bytes_accessed=int(nbytes))


def hbm(*values):
    return [pltpu.with_memory_space_constraint(v, pltpu.HBM) for v in values]


def sds(shape, dtype):
    return pltpu.HBM(shape, dtype)


def owners_of(table_ref, index):
    rows = [table_ref[pl.ds(3 * index + i, 1), :] for i in range(3)]
    plan = jnp.concatenate(rows, axis=1)
    return jnp.where(plan >= 0, plan // ROWS, -1)


def as_column(row):
    return jnp.transpose(jnp.broadcast_to(row, (128, SLOTS)))[:, 0:1]


def slots_of(pair, core, half, owner, owner_col, sibling_col):
    early = iota((SLOTS, SLOTS), 0) < iota((SLOTS, SLOTS), 1)
    same = jnp.where((owner_col == owner) & early, 1, 0)
    rank = jnp.sum(same, axis=0, keepdims=True)
    if pair == PAIR:
        return jnp.where(owner >= 0, owner * pair + rank, -1)
    before = jnp.sum(jnp.where(sibling_col == owner, 1, 0), axis=0, keepdims=True)
    mine = core if half == 0 else 1 - core
    rank = rank + mine * before
    return jnp.where((owner >= 0) & (rank % 2 == core), owner * pair + rank // 2, -1)


def plan_kernel(pair, index_ref, table_ref, slots_ref):
    index = index_ref[0]
    core = index % 2
    own = owners_of(table_ref, index)
    own_col = as_column(own)
    if pair == PAIR:
        slots_ref[...] = jnp.broadcast_to(
            slots_of(pair, core, 0, own, own_col, None), (8, SLOTS)
        )
        return
    other = owners_of(table_ref, index + 1 - 2 * core)
    other_col = as_column(other)
    first = slots_of(pair, core, 0, own, own_col, other_col)
    second = slots_of(pair, core, 1, other, other_col, own_col)
    theirs = slots_of(pair, 1 - core, 1, own, own_col, other_col)
    slots_ref[...] = jnp.concatenate(
        [first, second, theirs, jnp.full((5, SLOTS), -1, I32)], axis=0
    )


def send_plan(pair, my_index, dest_pos):
    return pl.pallas_call(
        functools.partial(plan_kernel, pair),
        grid_spec=pltpu.PrefetchScalarGridSpec(
            num_scalar_prefetch=1,
            grid=(1,),
            in_specs=[pl.BlockSpec((SHARDS * SLOTS // 128, 128), lambda j, ref: (0, 0))],
            out_specs=pl.BlockSpec((8, SLOTS), lambda j, ref: (0, 0)),
        ),
        out_shape=jax.ShapeDtypeStruct((8, SLOTS), I32),
        compiler_params=params(),
    )(my_index.reshape(1), dest_pos.reshape(SHARDS * SLOTS // 128, 128))


def build_pack(slots_ref, packs):
    for half, pack in enumerate(packs):
        pack[...] = onehot(iota(pack.shape, 0) == slots_ref[half : half + 1, :])


def pack_product_kernel(slots_ref, k_ref, v_ref, out_ref, pack):
    @pl.when(pl.program_id(0) == 0)
    def _():
        build_pack(slots_ref, [pack])

    product = (k_ref[...].astype(F32) * v_ref[...].astype(F32)).astype(BF)
    out_ref[...] = dot(pack[...], product).astype(BF)


def pack_rows_kernel(halves, slots_ref, *refs):
    blocks, out_ref, packs = refs[:halves], refs[halves], refs[halves + 1 :]

    @pl.when(pl.program_id(0) == 0)
    def _():
        build_pack(slots_ref, packs)

    total = dot(packs[0][...], blocks[0][...])
    for half in range(1, halves):
        total = total + dot(packs[half][...], blocks[half][...])
    out_ref[...] = total.astype(BF)


def pack_arrivals(kernel, pair, slots, blocks, halves):
    width = blocks[0].shape[1]
    sent = SHARDS * pair
    return pl.pallas_call(
        kernel,
        grid=(width // CB,),
        in_specs=[whole((8, SLOTS))] + [cols(SLOTS)] * len(blocks),
        out_specs=cols(sent),
        out_shape=sds((sent, width), BF),
        scratch_shapes=[pltpu.VMEM((sent, SLOTS), BF)] * halves,
        compiler_params=params(),
        cost_estimate=cost(
            2 * sent * SLOTS * width * halves, 2 * width * (sent + SLOTS * len(blocks))
        ),
    )(slots, *blocks)


def product_kernel(k_ref, v_ref, out_ref):
    out_ref[...] = (k_ref[...].astype(F32) * v_ref[...].astype(F32)).astype(BF)


def slot_product(k, v):
    width = k.shape[1]
    return pl.pallas_call(
        product_kernel,
        grid=(width // CB,),
        in_specs=[cols(SLOTS)] * 2,
        out_specs=cols(SLOTS),
        out_shape=sds((SLOTS, width), BF),
        compiler_params=params(),
        cost_estimate=cost(SLOTS * width, 6 * width * SLOTS),
    )(*hbm(k, v))


def place_product_kernel(pos_row, recv_ref, out_ref, tail_ref, place):
    @pl.when(pl.program_id(0) == 0)
    def _():
        place[...] = onehot(iota(place.shape, 0) == pos_row[...])

    rows = dot(place[...], recv_ref[...]).astype(BF)
    out_ref[...] = rows
    tail_ref[...] = rows[ROWS - TAPS :]


def place_product(pos_row, received):
    sent, width = received.shape
    return pl.pallas_call(
        place_product_kernel,
        grid=(width // CB,),
        in_specs=[whole((1, sent)), cols(sent)],
        out_specs=[cols(ROWS), cols(TAPS)],
        out_shape=[sds((ROWS, width), BF), sds((TAPS, width), BF)],
        scratch_shapes=[pltpu.VMEM((ROWS, sent), BF)],
        compiler_params=params(),
        cost_estimate=cost(2 * sent * ROWS * width, 2 * width * (sent + ROWS + TAPS)),
    )(pos_row, received)


def segment_dft(docs_window):
    place = jnp.arange(WIN, dtype=I32)
    docs = jnp.where(place >= 1, docs_window, -1)
    ids = jnp.arange(NDOCS, dtype=I32)
    inside = docs[None, :] == ids[:, None]
    span = jnp.sum(inside.astype(I32), axis=1)
    own = jnp.sum((inside & (place >= TAPS)[None, :]).astype(I32), axis=1)
    first = jnp.min(jnp.where(inside, place[None, :], 2 * WIN), axis=1)
    taps = jnp.minimum(TAPS, span)
    length = jnp.maximum(span, own + taps - 1)
    length = length + 1 - length % 2
    slots = jnp.where(own > 0, (length + 1) // 2, 0)
    start = jnp.sum(jnp.where(ids[None, :] < ids[:, None], slots[None, :], 0), axis=1)
    slot = jnp.arange(FREQ, dtype=I32)[:, None]
    member = (slot >= start[None, :]) & (slot < (start + slots)[None, :])

    def pick(value):
        return jnp.sum(jnp.where(member, value[None, :], 0), axis=1, keepdims=True)

    live = pick(jnp.ones_like(ids)) > 0
    doc = jnp.where(live, pick(ids), -9)
    wave = slot - pick(start)
    size = jnp.where(live, pick(length), 1)
    size_f = size.astype(F32)
    inverse = 1.0 / size_f

    def angles(steps):
        turns = (wave * steps).astype(F32)
        turns = turns - jnp.floor(turns * inverse) * size_f
        return turns * (inverse * (2.0 * jnp.pi))

    turn = angles(place[None, :] - pick(first))
    mask = docs[None, :] == doc
    spectrum = jnp.concatenate(
        [jnp.where(mask, jnp.cos(turn), 0.0), jnp.where(mask, -jnp.sin(turn), 0.0)], axis=0
    ).astype(BF)
    lag = jnp.arange(TAPS, dtype=I32)[None, :]
    turn = angles(lag)
    weight = jnp.where(
        live & (lag < pick(taps)), jnp.where(wave == 0, inverse, 2.0 * inverse), 0.0
    )
    taps_spectrum = jnp.concatenate(
        [weight * jnp.cos(turn), -weight * jnp.sin(turn)], axis=0
    ).astype(BF)
    return spectrum, taps_spectrum


CROSS = TAPS + ROWS - 1
CROSS_FREQ = (CROSS + 1) // 2


def crossing_dft(own_docs, next_docs):
    wave = jnp.arange(CROSS_FREQ, dtype=I32)[:, None]
    place = jnp.arange(TAPS, dtype=I32)[None, :]

    def waves(steps):
        turn = ((wave * steps) % CROSS).astype(F32) * (2.0 * jnp.pi / CROSS)
        return jnp.concatenate([jnp.cos(turn), -jnp.sin(turn)], axis=0)

    document = own_docs[ROWS - 1]
    head = jnp.where((next_docs == document)[None, :], waves(place + TAPS), 0.0)
    tail = jnp.where((own_docs[ROWS - TAPS :] == document)[None, :], waves(place), 0.0)
    weight = jnp.where(wave == 0, 1.0, 2.0) / CROSS
    taps = jnp.concatenate([weight, weight], axis=0) * waves(place)
    return head.astype(BF), tail.T.astype(BF), taps.astype(BF)


def mixture_kernel(cc, cc_own_t, bb, product, halo, filt, mix_ref, x_ref, f_ref):
    window = jnp.concatenate([halo[...], product[...]], axis=0)
    x = dot(cc[...], window)
    f = dot(bb[...], filt[...].astype(BF))
    xr, xi, fr, fi = x[:FREQ], x[FREQ:], f[:FREQ], f[FREQ:]
    y = jnp.concatenate(
        [(xr * fr - xi * fi).astype(BF), (xr * fi + xi * fr).astype(BF)], axis=0
    )
    mix_ref[...] = dot(cc_own_t[...], y)
    x_ref[...] = x.astype(BF)
    f_ref[...] = f.astype(BF)


def forward_mixture(spectrum, cc_own_t, taps_spectrum, product, halo, filt):
    width = product.shape[1]
    return pl.pallas_call(
        mixture_kernel,
        grid=(width // CB,),
        in_specs=[
            whole((2 * FREQ, WIN)),
            whole((ROWS, 2 * FREQ)),
            whole((2 * FREQ, TAPS)),
            cols(ROWS),
            cols(TAPS),
            cols(TAPS),
        ],
        out_specs=[cols(ROWS), cols(2 * FREQ), cols(2 * FREQ)],
        out_shape=[
            sds((ROWS, width), F32),
            sds((2 * FREQ, width), BF),
            sds((2 * FREQ, width), BF),
        ],
        compiler_params=params(),
        cost_estimate=cost(2 * 2 * FREQ * (WIN + TAPS + ROWS) * width, width * 8000),
    )(spectrum, cc_own_t, taps_spectrum, *hbm(product), halo, *hbm(filt))


def row_sums_kernel(pos_row, recv, mix, residual, cot, gain, q_ref, sums_ref, place, acc):
    step = pl.program_id(0)

    @pl.when(step == 0)
    def _():
        place[...] = onehot(iota(place.shape, 0) == pos_row[...])
        acc[...] = jnp.zeros_like(acc)

    q = dot(place[...], recv[...])
    q_ref[...] = q.astype(BF)
    summed = residual[...].astype(F32) + q * mix[...]
    scaled = cot[...].astype(F32) * gain[...]
    squares = jnp.sum(summed * summed, axis=1, keepdims=True)
    dots = jnp.sum(scaled * summed, axis=1, keepdims=True)
    lane = iota((ROWS, 128), 1)
    acc[...] += jnp.where(lane == 0, squares, jnp.where(lane == 1, dots, 0.0))

    @pl.when(step == pl.num_programs(0) - 1)
    def _():
        sums_ref[...] = jnp.transpose(acc[...])[:8]


def row_sums(pos_row, received, mix, residual, cot, gain):
    sent = received.shape[0]
    width = mix.shape[1]
    return pl.pallas_call(
        row_sums_kernel,
        grid=(width // CB,),
        in_specs=[whole((1, sent)), cols(sent), cols(ROWS), cols(ROWS), cols(ROWS), cols(1)],
        out_specs=[cols(ROWS), whole((8, ROWS))],
        out_shape=[sds((ROWS, width), BF), jax.ShapeDtypeStruct((8, ROWS), F32)],
        scratch_shapes=[pltpu.VMEM((ROWS, sent), BF), pltpu.VMEM((ROWS, 128), F32)],
        compiler_params=params(),
        cost_estimate=cost(2 * sent * ROWS * width, width * 4000),
    )(pos_row, received, *hbm(mix, residual, cot), gain)


def tap_rows(pair, shape, tap_dim, step):
    tap = iota(shape, tap_dim)
    return (tap // 4) * pair + tap % 4 + 4 * (step % (pair // 4))


def extra_cols(pair, width):
    return (width // CB) * 4 // pair * CB, width // pair


def row_stats(s0, s1, s2, s3, stats):
    sums = s0[...] + s1[...] + s2[...] + s3[...]
    sums = jnp.transpose(jnp.concatenate([sums, jnp.zeros((120, ROWS), F32)], axis=0))
    inv = lax.rsqrt(sums[:, 0:1] / D + NORM_EPS)
    stats[...] = jnp.where(iota((ROWS, 128), 1) == 0, inv, sums)


def d_summed_of(stats, summed, scaled):
    inv = stats[:, 0:1]
    return inv * scaled - summed * (inv * inv * inv) * stats[:, 1:2] / D


def backward_kernel(
    pair, blocks,
    s0, s1, s2, s3, pos_col, cc_own, bb_t, q_ref, mix_ref, res_ref, cot_ref, gain_ref, x_ref,
    dmix_ref, head_ref, out_ref,
    give, stats, taps_acc, gain_acc,
):
    step = pl.program_id(0)
    per = pair // 4
    parts = blocks // per
    sent = SHARDS * pair

    @pl.when(step == 0)
    def _():
        give[...] = onehot(pos_col[...] == iota(give.shape, 1))
        row_stats(s0, s1, s2, s3, stats)
        taps_acc[...] = jnp.zeros_like(taps_acc)
        gain_acc[...] = jnp.zeros_like(gain_acc)

    @pl.when(step < blocks)
    def _():
        q = q_ref[...].astype(F32)
        mix = mix_ref[...]
        summed = res_ref[...].astype(F32) + q * mix
        cot = cot_ref[...].astype(F32)
        gain_part = jnp.sum(cot * summed * stats[:, 0:1], axis=0, keepdims=True)
        d_summed = d_summed_of(stats, summed, cot * gain_ref[...])
        out_ref[...] = dot(give[...], (d_summed * mix).astype(BF)).astype(BF)
        d_mix = (d_summed * q).astype(BF)
        dmix_ref[...] = d_mix
        head_ref[...] = d_mix[:TAPS]
        g = dot(cc_own[...], d_mix)
        gr, gi = g[:FREQ], g[FREQ:]
        xr, xi = x_ref[:FREQ].astype(F32), x_ref[FREQ:].astype(F32)
        v = jnp.concatenate(
            [(gr * xr + gi * xi).astype(BF), (gi * xr - gr * xi).astype(BF)], axis=0
        )
        taps = dot(bb_t[...], v).astype(BF)
        spread = onehot(iota((sent, TAPS), 0) == tap_rows(pair, (sent, TAPS), 1, step))
        taps_acc[step // per] += dot(spread, taps)
        wide = gain_acc.shape[1]
        for i in range(CB // wide):
            row = iota(gain_acc.shape, 0) == step * (CB // wide) + i
            gain_acc[...] += jnp.where(row, gain_part[:, wide * i : wide * (i + 1)], 0.0)

    @pl.when((step >= blocks) & (step < blocks + parts))
    def _():
        out_ref[...] = taps_acc[jnp.minimum(step - blocks, parts - 1)].astype(BF)

    @pl.when(step == blocks + parts)
    def _():
        wide = gain_acc.shape[1]
        rows = jnp.broadcast_to(gain_acc[...][None], (SHARDS, pair, wide)).reshape(sent, wide)
        out_ref[:, :wide] = rows.astype(BF)


def backward(pair, sums, pos_col, cc_own, bb_t, q, mix, residual, cot, gain, x):
    width = q.shape[1]
    blocks = width // CB
    last = blocks - 1
    sent = SHARDS * pair
    part_cols, gain_cols = extra_cols(pair, width)
    parts = part_cols // CB
    row_block = cols(ROWS, last=last)
    return pl.pallas_call(
        functools.partial(backward_kernel, pair, blocks),
        grid=(blocks + parts + 1,),
        in_specs=[whole((8, ROWS))] * 4
        + [
            whole((sent, 1)),
            whole((2 * FREQ, ROWS)),
            whole((TAPS, 2 * FREQ)),
            row_block,
            row_block,
            row_block,
            row_block,
            cols(1, last=last),
            cols(2 * FREQ, last=last),
        ],
        out_specs=[row_block, cols(TAPS, last=last), cols(sent)],
        out_shape=[
            sds((ROWS, width), BF),
            sds((TAPS, width), BF),
            sds((sent, width + part_cols + gain_cols), BF),
        ],
        scratch_shapes=[
            pltpu.VMEM((sent, ROWS), BF),
            pltpu.VMEM((ROWS, 128), F32),
            pltpu.VMEM((parts, sent, CB), F32),
            pltpu.VMEM((pair, gain_cols), F32),
        ],
        compiler_params=params(),
        cost_estimate=cost(2e9, width * 6000),
    )(*sums, *hbm(pos_col, cc_own, bb_t, q, mix, residual, cot), gain, *hbm(x))


def finish_kernel(
    s0, s1, s2, s3, cc_own, cc_own_t, q_ref, mix_ref, res_ref, cot_ref, gain_ref, f_ref, dmix_ref,
    normed_ref, dres_ref, own_ref,
    stats,
):
    @pl.when(pl.program_id(0) == 0)
    def _():
        row_stats(s0, s1, s2, s3, stats)

    gain = gain_ref[...]
    summed = res_ref[...].astype(F32) + q_ref[...].astype(F32) * mix_ref[...]
    normed_ref[...] = (summed * stats[:, 0:1] * gain).astype(BF)
    dres_ref[...] = d_summed_of(stats, summed, cot_ref[...].astype(F32) * gain).astype(BF)
    g = dot(cc_own[...], dmix_ref[...])
    gr, gi = g[:FREQ], g[FREQ:]
    fr, fi = f_ref[:FREQ].astype(F32), f_ref[FREQ:].astype(F32)
    z = jnp.concatenate(
        [(gr * fr + gi * fi).astype(BF), (gi * fr - gr * fi).astype(BF)], axis=0
    )
    own_ref[...] = dot(cc_own_t[...], z)


def finish(sums, cc_own, cc_own_t, q, mix, residual, cot, gain, f, d_mix):
    width = q.shape[1]
    return pl.pallas_call(
        finish_kernel,
        grid=(width // CB,),
        in_specs=[whole((8, ROWS))] * 4
        + [whole((2 * FREQ, ROWS)), whole((ROWS, 2 * FREQ))]
        + [cols(ROWS)] * 4
        + [cols(1), cols(2 * FREQ), cols(ROWS)],
        out_specs=[cols(ROWS)] * 3,
        out_shape=[sds((ROWS, width), BF), sds((ROWS, width), BF), sds((ROWS, width), F32)],
        scratch_shapes=[pltpu.VMEM((ROWS, 128), F32)],
        compiler_params=params(),
        cost_estimate=cost(2 * 2 * 2 * FREQ * ROWS * width, width * 6000),
    )(*sums, *hbm(cc_own, cc_own_t, q, mix, residual, cot), gain, *hbm(f, d_mix))


def give_back_kernel(pos_col, head, tail_t, taps, own_ref, next_ref, filt, out_ref, give):
    @pl.when(pl.program_id(0) == 0)
    def _():
        give[...] = onehot(pos_col[...] == iota(give.shape, 1))

    g = dot(head[...], next_ref[...])
    f = dot(taps[...], filt[...].astype(BF))
    gr, gi, fr, fi = g[:CROSS_FREQ], g[CROSS_FREQ:], f[:CROSS_FREQ], f[CROSS_FREQ:]
    z = jnp.concatenate(
        [(gr * fr + gi * fi).astype(BF), (gi * fr - gr * fi).astype(BF)], axis=0
    )
    own = own_ref[...]
    grad = jnp.concatenate(
        [own[: ROWS - TAPS], own[ROWS - TAPS :] + dot(tail_t[...], z)], axis=0
    )
    out_ref[...] = dot(give[...], grad.astype(BF)).astype(BF)


def give_back(pair, pos_col, crossing, own, from_next, filt):
    width = own.shape[1]
    sent = SHARDS * pair
    return pl.pallas_call(
        give_back_kernel,
        grid=(width // CB,),
        in_specs=[
            whole((sent, 1)),
            whole((2 * CROSS_FREQ, TAPS)),
            whole((TAPS, 2 * CROSS_FREQ)),
            whole((2 * CROSS_FREQ, TAPS)),
            cols(ROWS),
            cols(TAPS),
            cols(TAPS),
        ],
        out_specs=cols(sent),
        out_shape=sds((sent, width + extra_cols(pair, width)[0]), BF),
        scratch_shapes=[pltpu.VMEM((sent, ROWS), BF)],
        compiler_params=params(),
        cost_estimate=cost(2 * sent * ROWS * width, width * 2400),
    )(*hbm(pos_col, *crossing, own), from_next, *hbm(filt))


def reduce_kernel(pair, taps_ref, gain_ref, rows_ref, out_ref, d_gain_ref):
    def over_sources(ref):
        value = ref[...].astype(F32)
        return jnp.sum(value.reshape(SHARDS, pair, value.shape[1]), axis=0)

    total = over_sources(taps_ref)
    out_ref[...] = (
        jnp.broadcast_to(total[None], (SHARDS, pair, CB)).reshape(SHARDS * pair, CB).astype(BF)
    )
    d_gain_ref[...] = over_sources(gain_ref)


def reduce_parts(pair, received, rows, width):
    part_cols, gain_cols = extra_cols(pair, width)
    blocks = width // CB
    sent = SHARDS * pair
    return pl.pallas_call(
        functools.partial(reduce_kernel, pair),
        grid=(part_cols // CB,),
        in_specs=[
            pl.BlockSpec((sent, CB), lambda j: (0, blocks + j)),
            pl.BlockSpec((sent, gain_cols), lambda j: (0, (width + part_cols) // gain_cols)),
            pl.BlockSpec(memory_space=pl.ANY),
        ],
        out_specs=[
            pl.BlockSpec((sent, CB), lambda j: (0, blocks + j)),
            whole((pair, gain_cols)),
        ],
        out_shape=[sds(rows.shape, BF), jax.ShapeDtypeStruct((pair, gain_cols), F32)],
        input_output_aliases={2: 0},
        compiler_params=params(),
        cost_estimate=cost(sent * part_cols, sent * part_cols * 4),
    )(received, received, *hbm(rows))


def build_home(pair, slots_ref, homes):
    for half, home in enumerate(homes):
        slot = as_column(slots_ref[2 * half : 2 * half + 1, :])
        home[...] = onehot(iota(home.shape, 1) == slot)


def homecoming(backs, homes):
    total = dot(homes[0][...], backs[0][...])
    for back, home in zip(backs[1:], homes[1:]):
        total = total + dot(home[...], back[...])
    return total


def home_rows_kernel(pair, halves, slots_ref, *refs):
    backs, out_ref, homes = refs[:halves], refs[halves], refs[halves + 1 :]

    @pl.when(pl.program_id(0) == 0)
    def _():
        build_home(pair, slots_ref, homes)

    out_ref[...] = homecoming(backs, homes).astype(BF)


def home_rows(pair, slots, backs, width):
    sent = SHARDS * pair
    halves = len(backs)
    return pl.pallas_call(
        functools.partial(home_rows_kernel, pair, halves),
        grid=(width // CB,),
        in_specs=[whole((8, SLOTS))] + [cols(sent)] * halves,
        out_specs=cols(SLOTS),
        out_shape=sds((SLOTS, width), BF),
        scratch_shapes=[pltpu.VMEM((SLOTS, sent), BF)] * halves,
        compiler_params=params(),
        cost_estimate=cost(
            2 * sent * SLOTS * width * halves, 2 * width * (sent * halves + SLOTS)
        ),
    )(slots, *backs)


def home_product_kernel(pair, halves, slots_ref, taps_ref, k_ref, v_ref, *refs):
    backs, (dk_ref, dv_ref, filt_ref), homes = refs[:halves], refs[halves : halves + 3], refs[halves + 3 :]
    step = pl.program_id(0)

    @pl.when(step == 0)
    def _():
        build_home(pair, slots_ref, homes)

    grad = homecoming(backs, homes)
    dk_ref[...] = (grad * v_ref[...].astype(F32)).astype(BF)
    dv_ref[...] = (grad * k_ref[...].astype(F32)).astype(BF)
    shape = (TAPS, SHARDS * pair)
    filt_ref[...] = dot(onehot(iota(shape, 1) == tap_rows(pair, shape, 0, step)), taps_ref[...])


def home_product(pair, slots, back, backs, k, v):
    width = k.shape[1]
    blocks = width // CB
    sent = SHARDS * pair
    halves = len(backs)
    per = pair // 4
    return pl.pallas_call(
        functools.partial(home_product_kernel, pair, halves),
        grid=(blocks,),
        in_specs=[
            whole((8, SLOTS)),
            pl.BlockSpec((sent, CB), lambda j: (0, blocks + j // per)),
            cols(SLOTS),
            cols(SLOTS),
        ]
        + [cols(sent)] * halves,
        out_specs=[cols(SLOTS), cols(SLOTS), cols(TAPS)],
        out_shape=[sds((SLOTS, width), BF), sds((SLOTS, width), BF), sds((TAPS, width), F32)],
        scratch_shapes=[pltpu.VMEM((SLOTS, sent), BF)] * halves,
        compiler_params=params(),
        cost_estimate=cost(2 * sent * SLOTS * width, 2 * width * (sent + 5 * SLOTS)),
    )(slots, back, *hbm(k, v), *backs)


def exchange(pair, rows):
    shards = rows.reshape(SHARDS, pair, rows.shape[1])
    return lax.all_to_all(shards, "seq", split_axis=0, concat_axis=0, tiled=True).reshape(
        rows.shape
    )


def shift(value, steps):
    pairs = [(i, i + steps) for i in range(SHARDS) if 0 <= i + steps < SHARDS]
    return lax.ppermute(value, "seq", pairs)


def swap(value):
    return lax.ppermute(value, "seq", [(i, i ^ 1) for i in range(SHARDS)])


def slot_positions(pair, dest_pos, my_index):
    holders = SHARDS * pair // PAIR
    table = dest_pos.reshape(holders, -1)
    arriving = (table >= 0) & (table // ROWS == my_index)
    row = jnp.arange(table.shape[1], dtype=I32)
    before = (row[:, None] < row[None, :]).astype(BF)
    rank = jnp.dot(arriving.astype(BF), before, preferred_element_type=F32).astype(I32)
    rank = jnp.where(arriving, rank, -1)
    target = table - my_index * ROWS + 1
    order = jnp.arange(PAIR, dtype=I32)
    if pair != PAIR:
        order = (order % pair) * 2 + order // pair
    hit = rank[:, None, :] == order[None, :, None]
    return (jnp.sum(jnp.where(hit, target[:, None, :], 0), axis=2) - 1).reshape(SHARDS * pair)


def layer(pair, q_in, k_in, v_in, dest_pos, doc_ids, mr_filter, norm_gain, residual, cotangent):
    my_index = lax.axis_index("seq")
    width = q_in.shape[1]
    gain = norm_gain[None, :]
    shared = pair != PAIR

    if shared:
        product_in = slot_product(k_in, v_in)
        product_other = swap(product_in)
        slots = send_plan(pair, my_index, dest_pos)
        q_other = swap(q_in)
        sent_product = pack_arrivals(
            functools.partial(pack_rows_kernel, 2), pair, slots, [product_in, product_other], 2
        )
        q_blocks = [q_in, q_other]
    else:
        slots = send_plan(pair, my_index, dest_pos)
        sent_product = pack_arrivals(pack_product_kernel, pair, slots, hbm(k_in, v_in), 1)
        q_blocks = hbm(q_in)
    sent_product, dest_later, docs_later, slots = lax.optimization_barrier(
        (sent_product, dest_pos, doc_ids, slots)
    )
    recv_product = exchange(pair, sent_product)
    halves = len(q_blocks)
    sent_q = pack_arrivals(
        functools.partial(pack_rows_kernel, halves), pair, slots, q_blocks, halves
    )

    pos = slot_positions(pair, dest_later, my_index)
    pos_row, pos_col = pos[None, :], pos[:, None]
    docs_all = jnp.concatenate(
        [jnp.full((TAPS,), -1, I32), docs_later, jnp.full((TAPS,), -2, I32)]
    )
    docs = lax.dynamic_slice_in_dim(docs_all, my_index * ROWS, WIN + TAPS)
    spectrum, taps_spectrum = segment_dft(docs[:WIN])
    spectrum_t = spectrum.T
    prepared = (
        pos_row,
        pos_col,
        spectrum,
        spectrum[:, TAPS:],
        spectrum_t[TAPS:],
        taps_spectrum,
        taps_spectrum.T,
        crossing_dft(docs[TAPS:WIN], docs[WIN:]),
    )
    sent_q, recv_product, prepared = lax.optimization_barrier((sent_q, recv_product, prepared))
    pos_row, pos_col, cc, cc_own, cc_own_t, bb, bb_t, crossing = prepared

    product, tail = place_product(pos_row, recv_product)
    sent_q, halo = lax.optimization_barrier((sent_q, shift(tail, 1)))
    recv_q = exchange(pair, sent_q)
    mix, x, f = forward_mixture(cc, cc_own_t, bb, product, halo, mr_filter)
    q_pos, sums = row_sums(pos_row, recv_q, mix, residual, cotangent, gain)
    all_sums = [sums] + [
        lax.ppermute(sums, "mp", [(i, (i + k) % 4) for i in range(4)]) for k in (1, 2, 3)
    ]
    d_mix, head, sent_dq = backward(
        pair, all_sums, pos_col, cc_own, bb_t, q_pos, mix, residual, cotangent, gain, x
    )
    from_next = shift(head, -1)
    back_q = exchange(pair, sent_dq)
    normed, d_residual, own_grad = finish(
        all_sums, cc_own, cc_own_t, q_pos, mix, residual, cotangent, gain, f, d_mix
    )
    rows = give_back(pair, pos_col, crossing, own_grad, from_next, mr_filter)
    sent_dp, d_gain = reduce_parts(pair, back_q, rows, width)
    back_p = exchange(pair, sent_dp)
    backs_q, backs_p = [back_q], [back_p]
    if shared:
        backs_q.append(swap(back_q[:, :width]))
        backs_p.append(swap(back_p[:, :width]))
    d_q_in = home_rows(pair, slots, backs_q, width)
    d_k_in, d_v_in, d_filter = home_product(pair, slots, back_p, backs_p, k_in, v_in)
    return (normed, d_residual, d_q_in, d_k_in, d_v_in, d_filter, d_gain.reshape(width))


def body(*args):
    return layer(PAIR, *args)


def solution(mesh):
    return jax.shard_map(
        body,
        mesh=mesh,
        in_specs=(
            P("seq", "mp"),
            P("seq", "mp"),
            P("seq", "mp"),
            P(),
            P(),
            P(None, "mp"),
            P("mp"),
            P("seq", "mp"),
            P("seq", "mp"),
        ),
        out_specs=(
            P("seq", "mp"),
            P("seq", "mp"),
            P("seq", "mp"),
            P("seq", "mp"),
            P("seq", "mp"),
            P(None, "mp"),
            P("mp"),
        ),
        check_vma=False,
    )
```

time: 231 us -> 213 us (0.922)
  local copies, waits for them, and re-layouts: 44.6 us -> 8.39 us
  Pallas kernels: 42 us -> 58.6 us
  other arithmetic: 7.18 us -> 11.5 us
    unnamed x74 -> x16, local copies, waits for them, and re-layouts: 35.6 us -> 2.64 us
    pallas_call x8 -> x9, Pallas kernels: 29.8 us -> 44.6 us  [the longest x1 10.2 us: backward(): pl.pallas_call(functools.partial(backward_kernel, pair, blocks), grid=(bl...]
    ppermute x2, waiting for transfers between devices: 47.3 us -> 33.5 us  [shift(): return lax.ppermute(value, 'seq', pairs)]
    all_to_all x4, waiting for transfers between devices: 47.7 us -> 60.4 us  [exchange(): lax.all_to_all(shards, 'seq', split_axis=0, concat_axis=0, tiled=True)]
    optimization_barrier x4 -> x5, local copies, waits for them, and re-layouts: 5.41 us -> 3.99 us  [layer(): lax.optimization_barrier((sent_q, recv_product, prepared))]
  transfers between devices with their start and end apart: 9 -> 9, of which waited for: 4 -> 6; matrix products, arithmetic and copies ran while one was open for 7% -> 8% of each run, Pallas kernels for 8% -> 13%
where the time goes in v2:
time: 213 us; the launch traced here: 212 us
  waiting for transfers between devices  95.4 us (45%)
  Pallas kernels  58.6 us (28%)
  starting transfers between devices  37 us (17%)
  other arithmetic  11.5 us (5%)
  local copies, waits for them, and re-layouts  8.39 us (4%)
    all_to_all x4, waiting for transfers between devices, exchange(): lax.all_to_all(shards, 'seq', split_axis=0, concat_axis=0, tiled=True)  60.4 us
    ppermute x2, waiting for transfers between devices, shift(): return lax.ppermute(value, 'seq', pairs)  33.5 us
    all_to_all x4, starting transfers between devices, exchange(): lax.all_to_all(shards, 'seq', split_axis=0, concat_axis=0, tiled=True)  28.2 us
    pallas_call x1, Pallas kernels, backward(): pl.pallas_call(functools.partial(backward_kernel, pair, blocks), grid=(bl...  10.2 us
    pallas_call x2, Pallas kernels, pack_arrivals(): pl.pallas_call(kernel, grid=(width // CB,), in_specs=[whole((8, SLOTS))]...  9.66 us
    pallas_call x1, Pallas kernels, finish(): pl.pallas_call(finish_kernel, grid=(width // CB,), in_specs=[whole((8, RO...  8.17 us
    pallas_call x1, Pallas kernels, forward_mixture(): pl.pallas_call(mixture_kernel, grid=(width // CB,), in_specs=[whole((2 *...  6.39 us
    pallas_call x1, Pallas kernels, give_back(): pl.pallas_call(give_back_kernel, grid=(width // CB,), in_specs=[whole((se...  6.29 us
  transfers between devices with their start and end apart: 9, of which 6 were waited for; matrix products, arithmetic and copies ran while one was open for 8% of the time, Pallas kernels for 13%

profile of v2, /device:TPU:1, one launch (start us, length us, event | category | flops | bytes accessed | tf_op | source)
XLA Modules:
  0.0 211.9 jit_solution(3239100378189703259)
XLA Ops:
  0.6 0.0 copy-start.1
  0.6 0.8 copy-done.1
  1.4 0.2 shard_map.144.slots_ref
  1.7 5.0 %shard_map.145 = bf16[512,2048]{1,0:T(8,128)(2,1)} custom-call(s32[8,384]{1,0:T(8,128)S(1)} %shard_map.144.slots_ref, bf16[384,2048]{1,0:T(8,128)(2,1)} %k_ref.3, bf16[384,2048]{1,0:T(8,128)(2,1)} %v_ref.3), custom_call_target="tpu_custom_call" | custom-call | flops 805306368 | bytes 5242880 | tf_op jit(solution)/shard_map/pallas_call | solution.py:153
  6.7 8.7 %all-to-all-start = ((bf16[32,16,2048]{2,1,0:T(8,128)(2,1)}), bf16[32,16,2048]{2,1,0:T(8,128)(2,1)S(1)}, u32[]{:S(2)}, u32[]{:S(2)}) async-start(bf16[32,16,2048]{2,1,0:T(8,128)(2,1)} %bitcast.29), calls=%async_computation | async-start | bytes 4194304 | tf_op jit(solution)/shard_map/all_to_all | solution.py:661
  15.5 0.2 fusion
  15.7 0.1 fusion.37
  15.8 0.2 select_reduce_fusion.4
  16.0 0.1 select_reduce_fusion.8
  16.1 0.2 select_reduce_fusion.1
  16.3 0.6 select_reduce_fusion
  17.0 2.5 %fusion.1 = (bf16[320,384]{0,1:T(8,128)(2,1)S(1)}, bf16[320,384]{0,1:T(8,128)(2,1)S(1)}) fusion(f32[320]{0:T(512)S(1)} %broadcast_multiply_fusion, f32[320]{0:T(512)S(1)} %get-tuple-element.90, f32[320]{0:T(512)S(1)} %get-tuple-element.89, s32[320]{0:T(512)S(1)} %get-tuple-element.85, s32[320]{0:T(512)S(1)} %get-tuple-element.103, ...), kind=kLoop, calls=%fused_computation.6 | loop fusion | flops 1720320 | bytes 500736 | tf_op jit(solution)/shard_map/convert.2
  19.4 0.9 fusion.48
  20.4 0.6 slice.25
  20.9 0.1 sub.81
  21.0 0.1 sub.80.pos_row
  21.1 1.0 slice.29.cc_own_t
  22.1 0.1 maximum_reduce_fusion
  22.2 4.7 %shard_map.146 = bf16[512,2048]{1,0:T(8,128)(2,1)} custom-call(s32[8,384]{1,0:T(8,128)S(1)} %shard_map.144.slots_ref, bf16[384,2048]{1,0:T(8,128)(2,1)} %refs_0_.1), custom_call_target="tpu_custom_call" | custom-call | flops 805306368 | bytes 3670016 | tf_op jit(solution)/shard_map/pallas_call | solution.py:153
  26.9 0.4 fusion.16
  27.3 0.4 sine_negate_fusion
  27.7 0.8 fusion.4
  28.5 0.8 fusion.47.bb_t
  29.3 0.1 pad_maximum_fusion.2
  29.4 0.8 fusion.3
  30.2 0.9 pad_maximum_fusion
  31.1 0.7 slice_compare_fusion
  31.8 0.4 fusion.19
  32.2 0.8 multiply_convert_fusion.taps
  33.0 0.7 fusion.7
  33.7 10.0 %all-to-all-done = bf16[32,16,2048]{2,1,0:T(8,128)(2,1)S(1)} async-done(((bf16[32,16,2048]{2,1,0:T(8,128)(2,1)}), bf16[32,16,2048]{2,1,0:T(8,128)(2,1)S(1)}, u32[]{:S(2)}, u32[]{:S(2)}) %all-to-all-start) | async-done | bytes 2097184 | tf_op jit(solution)/shard_map/all_to_all | solution.py:661
  43.7 2.6 %shard_map.147 = (bf16[256,2048]{1,0:T(8,128)(2,1)}, bf16[128,2048]{1,0:T(8,128)(2,1)}) custom-call(s32[1,512]{1,0:T(1,128)S(1)} %sub.80.pos_row, bf16[512,2048]{1,0:T(8,128)(2,1)S(1)} %bitcast.23), custom_call_target="tpu_custom_call" | custom-call | flops 536870912 | bytes 3670016 | tf_op jit(solution)/shard_map/pallas_call | solution.py:196
  46.3 2.1 %collective-permute-start = (bf16[128,2048]{1,0:T(8,128)(2,1)}, bf16[128,2048]{1,0:T(8,128)(2,1)S(1)}, u32[]{:S(2)}, u32[]{:S(2)}) collective-permute-start(bf16[128,2048]{1,0:T(8,128)(2,1)} %get-tuple-element.50), channel_id=1, source_target_pairs={{0,4},{4,8},{8,12},{12,16},{16,20},{20,24},{24,28},{28,32},{32,36}... | collective-permute-start | bytes 1572872 | tf_op jit(solution)/shard_map/ppermute | solution.py:668
  48.5 6.4 %collective-permute-done.halo = bf16[128,2048]{1,0:T(8,128)(2,1)S(1)} collective-permute-done((bf16[128,2048]{1,0:T(8,128)(2,1)}, bf16[128,2048]{1,0:T(8,128)(2,1)S(1)}, u32[]{:S(2)}, u32[]{:S(2)}) %collective-permute-start) | collective-permute-done | bytes 524320 | tf_op jit(solution)/shard_map/ppermute | solution.py:668
  54.9 0.8 copy-done.4
  55.7 7.0 %all-to-all-start.1 = ((bf16[32,16,2048]{2,1,0:T(8,128)(2,1)}), bf16[32,16,2048]{2,1,0:T(8,128)(2,1)S(1)}, u32[]{:S(2)}, u32[]{:S(2)}) async-start(bf16[32,16,2048]{2,1,0:T(8,128)(2,1)} %bitcast.30), calls=%async_computation.1 | async-start | bytes 4194304 | tf_op jit(solution)/shard_map/all_to_all | solution.py:661
  62.7 0.2 copy.30.bb
  62.8 1.3 copy.29.cc
  64.1 0.0 copy-start.5
  64.2 1.0 copy-done.5
  65.2 6.4 %shard_map.148 = (f32[256,2048]{1,0:T(8,128)}, bf16[640,2048]{1,0:T(8,128)(2,1)}, bf16[640,2048]{1,0:T(8,128)(2,1)}) custom-call(bf16[640,384]{1,0:T(8,128)(2,1)S(1)} %copy.29.cc, bf16[256,640]{1,0:T(8,128)(2,1)S(1)} %slice.29.cc_own_t, bf16[640,128]{1,0:T(8,128)(2,1)S(1)} %copy.30.bb, bf16[256,2048]{1,0:T(8,128)(2,1)} %get-tuple-element.55.product, ...), custom_call_target="tpu_custom_call" | custom-call | flops 2013265920 | bytes 16384000 | tf_op jit(solution)/shard_map/pallas_call | solution.py:290
  71.6 19.4 %all-to-all-done.1 = bf16[32,16,2048]{2,1,0:T(8,128)(2,1)S(1)} async-done(((bf16[32,16,2048]{2,1,0:T(8,128)(2,1)}), bf16[32,16,2048]{2,1,0:T(8,128)(2,1)S(1)}, u32[]{:S(2)}, u32[]{:S(2)}) %all-to-all-start.1) | async-done | bytes 2097184 | tf_op jit(solution)/shard_map/all_to_all | solution.py:661
  91.0 5.0 %shard_map.149 = (bf16[256,2048]{1,0:T(8,128)(2,1)}, f32[8,256]{1,0:T(8,128)S(1)}) custom-call(s32[1,512]{1,0:T(1,128)S(1)} %sub.80.pos_row, bf16[512,2048]{1,0:T(8,128)(2,1)S(1)} %bitcast.22, f32[256,2048]{1,0:T(8,128)} %get-tuple-element.57.mix.mix_ref, bf16[256,2048]{1,0:T(8,128)(2,1)} %res_ref.3, bf16[256,2048]{1,0:T(8,128)(2,1)} %cot_ref.3, ...), custom_call_target="tpu_custom_call" | custom-call | flops 536870912 | bytes 8192000 | tf_op jit(solution)/shard_map/pallas_call | solution.py:337
  96.0 3.8 %collective-permute-start.3 = (f32[8,256]{1,0:T(8,128)S(1)}, f32[8,256]{1,0:T(8,128)S(1)}, u32[]{:S(2)}, u32[]{:S(2)}) collective-permute-start(f32[8,256]{1,0:T(8,128)S(1)} %get-tuple-element.58.s0), channel_id=1, source_target_pairs={{0,3},{1,0},{2,1},{3,2},{4,7},{5,4},{6,5},{7,6},{8,11},{9,8},{10,9... | collective-permute-start | bytes 24584 | tf_op jit(solution)/shard_map/ppermute | solution.py:746
  99.7 0.0 collective-permute-start.2
  99.7 0.7 collective-permute-start.1
  100.4 0.9 copy.31.pos_col
  101.3 0.9 copy.33.cc_own
  102.2 0.0 collective-permute-done.3.s3
  102.2 1.5 collective-permute-done.2.s2
  103.7 0.0 collective-permute-done.1.s1
  103.7 10.2 %shard_map.150 = (bf16[256,2048]{1,0:T(8,128)(2,1)}, bf16[128,2048]{1,0:T(8,128)(2,1)}, bf16[512,2688]{1,0:T(8,128)(2,1)}) custom-call(f32[8,256]{1,0:T(8,128)S(1)} %get-tuple-element.58.s0, f32[8,256]{1,0:T(8,128)S(1)} %collective-permute-done.1.s1, f32[8,256]{1,0:T(8,128)S(1)} %collective-permute-done.2.s2, f32[8,256]{1,0:T(8,128)S(1)} %collective-permute-done.3.s3, ...), custom_call_target="tpu_custom_call" | custom-call | flops 2000000000 | bytes 12288000 | tf_op jit(solution)/shard_map/pallas_call | solution.py:433
  113.9 6.2 %all-to-all-start.2 = ((bf16[32,16,2688]{2,1,0:T(8,128)(2,1)}), bf16[32,16,2688]{2,1,0:T(8,128)(2,1)S(1)}, u32[]{:S(2)}, u32[]{:S(2)}) async-start(bf16[32,16,2688]{2,1,0:T(8,128)(2,1)} %bitcast.31), calls=%async_computation.2 | async-start | bytes 5505024 | tf_op jit(solution)/shard_map/all_to_all | solution.py:661
  120.1 2.3 %collective-permute-start.4 = (bf16[128,2048]{1,0:T(8,128)(2,1)}, bf16[128,2048]{1,0:T(8,128)(2,1)S(1)}, u32[]{:S(2)}, u32[]{:S(2)}) collective-permute-start(bf16[128,2048]{1,0:T(8,128)(2,1)} %get-tuple-element.73), channel_id=1, source_target_pairs={{4,0},{8,4},{12,8},{16,12},{20,16},{24,20},{28,24},{32,28},{36,32}... | collective-permute-start | bytes 1572872 | tf_op jit(solution)/shard_map/ppermute | solution.py:668
  122.4 0.8 copy.35.tail_t
  123.1 8.2 %shard_map.151 = (bf16[256,2048]{1,0:T(8,128)(2,1)}, bf16[256,2048]{1,0:T(8,128)(2,1)}, f32[256,2048]{1,0:T(8,128)}) custom-call(f32[8,256]{1,0:T(8,128)S(1)} %get-tuple-element.58.s0, f32[8,256]{1,0:T(8,128)S(1)} %collective-permute-done.1.s1, f32[8,256]{1,0:T(8,128)S(1)} %collective-permute-done.2.s2, f32[8,256]{1,0:T(8,128)S(1)} %collective-permute-done.3.s3, ...), custom_call_target="tpu_custom_call" | custom-call | flops 1342177280 | bytes 12288000 | tf_op jit(solution)/shard_map/pallas_call | solution.py:489
  131.3 27.0 %collective-permute-done.4.next_ref = bf16[128,2048]{1,0:T(8,128)(2,1)S(1)} collective-permute-done((bf16[128,2048]{1,0:T(8,128)(2,1)}, bf16[128,2048]{1,0:T(8,128)(2,1)S(1)}, u32[]{:S(2)}, u32[]{:S(2)}) %collective-permute-start.4) | collective-permute-done | bytes 524320 | tf_op jit(solution)/shard_map/ppermute | solution.py:668
  158.3 6.3 %shard_map.153.rows_ref = bf16[512,2560]{1,0:T(8,128)(2,1)} custom-call(s32[512,1]{1,0:T(8,128)} %copy.31.pos_col, bf16[384,128]{1,0:T(8,128)(2,1)} %get-tuple-element.69.head, bf16[128,384]{1,0:T(8,128)(2,1)} %copy.35.tail_t, bf16[384,128]{1,0:T(8,128)(2,1)} %multiply_convert_fusion.taps, f32[256,2048]{1,0:T(8,128)} %get-tuple-element.72.own_ref, ...), custom_call_target="tpu_custom_call" | custom-call | flops 536870912 | bytes 4915200 | tf_op jit(solution)/shard_map/pallas_call | solution.py:525
  164.6 0.0 all-to-all-done.2
  164.6 1.0 shard_map.154
  165.7 6.3 %all-to-all-start.3 = ((bf16[32,16,2560]{2,1,0:T(8,128)(2,1)}), bf16[32,16,2560]{2,1,0:T(8,128)(2,1)}, u32[]{:S(2)}, u32[]{:S(2)}) async-start(bf16[32,16,2560]{2,1,0:T(8,128)(2,1)} %bitcast.28), calls=%async_computation.3 | async-start | bytes 5242880 | tf_op jit(solution)/shard_map/all_to_all | solution.py:661
  172.0 3.0 %shard_map.152 = bf16[384,2048]{1,0:T(8,128)(2,1)} custom-call(s32[8,384]{1,0:T(8,128)S(1)} %shard_map.144.slots_ref, bf16[512,2688]{1,0:T(8,128)(2,1)S(1)} %bitcast.21), custom_call_target="tpu_custom_call" | custom-call | flops 805306368 | bytes 3670016 | tf_op jit(solution)/shard_map/pallas_call | solution.py:606
  175.0 30.9 %all-to-all-done.3 = bf16[32,16,2560]{2,1,0:T(8,128)(2,1)} async-done(((bf16[32,16,2560]{2,1,0:T(8,128)(2,1)}), bf16[32,16,2560]{2,1,0:T(8,128)(2,1)}, u32[]{:S(2)}, u32[]{:S(2)}) %all-to-all-start.3) | async-done | bytes 2621472 | tf_op jit(solution)/shard_map/all_to_all | solution.py:661
  205.9 6.0 %shard_map.155 = (bf16[384,2048]{1,0:T(8,128)(2,1)}, bf16[384,2048]{1,0:T(8,128)(2,1)}, f32[128,2048]{1,0:T(8,128)}) custom-call(s32[8,384]{1,0:T(8,128)S(1)} %shard_map.144.slots_ref, bf16[512,2560]{1,0:T(8,128)(2,1)} %bitcast.14.taps_ref.refs_0_, bf16[384,2048]{1,0:T(8,128)(2,1)} %k_ref.3, bf16[384,2048]{1,0:T(8,128)(2,1)} %v_ref.3, ...), custom_call_target="tpu_custom_call" | custom-call | flops 805306368 | bytes 9961472 | tf_op jit(solution)/shard_map/pallas_call | solution.py:641
  (25 shorter events, 0.1 us)
Async XLA Ops:
  0.6 0.8 copy-start.1
  6.7 8.7 %copy-start.2 = (s32[12288]{0:T(1024)S(1)}, s32[12288]{0:T(1024)}, u32[]{:S(2)}) copy-start(s32[12288]{0:T(1024)} %param.12) | copy-start | bytes 147460
  6.7 9.0 %copy-start.7 = (s32[8192]{0:T(1024)S(1)}, s32[8192]{0:T(1024)}, u32[]{:S(2)}) copy-start(s32[8192]{0:T(1024)} %param.13) | copy-start | bytes 98308
  6.7 37.0 %all-to-all-start = ((bf16[32,16,2048]{2,1,0:T(8,128)(2,1)}), bf16[32,16,2048]{2,1,0:T(8,128)(2,1)S(1)}, u32[]{:S(2)}, u32[]{:S(2)}) async-start(bf16[32,16,2048]{2,1,0:T(8,128)(2,1)} %bitcast.29), calls=%async_computation | async-start | bytes 4194304 | tf_op jit(solution)/shard_map/all_to_all | solution.py:661
  22.1 42.0 %copy-start = (bf16[256,640]{1,0:T(8,128)(2,1)}, bf16[256,640]{1,0:T(8,128)(2,1)S(1)}, u32[]{:S(2)}) copy-start(bf16[256,640]{1,0:T(8,128)(2,1)S(1)} %slice.29.cc_own_t) | copy-start | bytes 983044
  46.3 8.6 %collective-permute-start = (bf16[128,2048]{1,0:T(8,128)(2,1)}, bf16[128,2048]{1,0:T(8,128)(2,1)S(1)}, u32[]{:S(2)}, u32[]{:S(2)}) collective-permute-start(bf16[128,2048]{1,0:T(8,128)(2,1)} %get-tuple-element.50), channel_id=1, source_target_pairs={{0,4},{4,8},{8,12},{12,16},{16,20},{20,24},{24,28},{28,32},{32,36}... | collective-permute-start | bytes 1572872 | tf_op jit(solution)/shard_map/ppermute | solution.py:668
  54.9 0.8 copy-start.4
  55.7 35.3 %all-to-all-start.1 = ((bf16[32,16,2048]{2,1,0:T(8,128)(2,1)}), bf16[32,16,2048]{2,1,0:T(8,128)(2,1)S(1)}, u32[]{:S(2)}, u32[]{:S(2)}) async-start(bf16[32,16,2048]{2,1,0:T(8,128)(2,1)} %bitcast.30), calls=%async_computation.1 | async-start | bytes 4194304 | tf_op jit(solution)/shard_map/all_to_all | solution.py:661
  64.1 1.0 copy-start.5
  65.2 25.8 %copy-start.3 = (f32[2048]{0:T(1024)S(1)}, f32[2048]{0:T(1024)}, u32[]{:S(2)}) copy-start(f32[2048]{0:T(1024)} %param.15) | copy-start | bytes 24580
  91.0 10.3 %copy-start.6 = (bf16[640,256]{0,1:T(8,128)(2,1)S(1)}, bf16[640,256]{0,1:T(8,128)(2,1)}, u32[]{:S(2)}) copy-start(bf16[640,256]{0,1:T(8,128)(2,1)} %fusion.3) | copy-start | bytes 983044
  96.0 6.2 %collective-permute-start.3 = (f32[8,256]{1,0:T(8,128)S(1)}, f32[8,256]{1,0:T(8,128)S(1)}, u32[]{:S(2)}, u32[]{:S(2)}) collective-permute-start(f32[8,256]{1,0:T(8,128)S(1)} %get-tuple-element.58.s0), channel_id=1, source_target_pairs={{0,3},{1,0},{2,1},{3,2},{4,7},{5,4},{6,5},{7,6},{8,11},{9,8},{10,9... | collective-permute-start | bytes 24584 | tf_op jit(solution)/shard_map/ppermute | solution.py:746
  99.7 4.0 %collective-permute-start.2 = (f32[8,256]{1,0:T(8,128)S(1)}, f32[8,256]{1,0:T(8,128)S(1)}, u32[]{:S(2)}, u32[]{:S(2)}) collective-permute-start(f32[8,256]{1,0:T(8,128)S(1)} %get-tuple-element.58.s0), channel_id=1, source_target_pairs={{0,2},{1,3},{2,0},{3,1},{4,6},{5,7},{6,4},{7,5},{8,10},{9,11},{10,... | collective-permute-start | bytes 24584 | tf_op jit(solution)/shard_map/ppermute | solution.py:746
  99.7 4.0 %collective-permute-start.1 = (f32[8,256]{1,0:T(8,128)S(1)}, f32[8,256]{1,0:T(8,128)S(1)}, u32[]{:S(2)}, u32[]{:S(2)}) collective-permute-start(f32[8,256]{1,0:T(8,128)S(1)} %get-tuple-element.58.s0), channel_id=1, source_target_pairs={{0,1},{1,2},{2,3},{3,0},{4,5},{5,6},{6,7},{7,4},{8,9},{9,10},{10,1... | collective-permute-start | bytes 24584 | tf_op jit(solution)/shard_map/ppermute | solution.py:746
  113.9 50.7 %all-to-all-start.2 = ((bf16[32,16,2688]{2,1,0:T(8,128)(2,1)}), bf16[32,16,2688]{2,1,0:T(8,128)(2,1)S(1)}, u32[]{:S(2)}, u32[]{:S(2)}) async-start(bf16[32,16,2688]{2,1,0:T(8,128)(2,1)} %bitcast.31), calls=%async_computation.2 | async-start | bytes 5505024 | tf_op jit(solution)/shard_map/all_to_all | solution.py:661
  120.1 38.2 %collective-permute-start.4 = (bf16[128,2048]{1,0:T(8,128)(2,1)}, bf16[128,2048]{1,0:T(8,128)(2,1)S(1)}, u32[]{:S(2)}, u32[]{:S(2)}) collective-permute-start(bf16[128,2048]{1,0:T(8,128)(2,1)} %get-tuple-element.73), channel_id=1, source_target_pairs={{4,0},{8,4},{12,8},{16,12},{20,16},{24,20},{28,24},{32,28},{36,32}... | collective-permute-start | bytes 1572872 | tf_op jit(solution)/shard_map/ppermute | solution.py:668
  165.7 40.2 %all-to-all-start.3 = ((bf16[32,16,2560]{2,1,0:T(8,128)(2,1)}), bf16[32,16,2560]{2,1,0:T(8,128)(2,1)}, u32[]{:S(2)}, u32[]{:S(2)}) async-start(bf16[32,16,2560]{2,1,0:T(8,128)(2,1)} %bitcast.28), calls=%async_computation.3 | async-start | bytes 5242880 | tf_op jit(solution)/shard_map/all_to_all | solution.py:661

commit v3 on v2

--- a/solution.py
+++ b/solution.py
@@ -36,9 +36,9 @@
     return jnp.where(match, 1.0, 0.0).astype(BF)
 
 
-def params():
+def params(grid=True):
     return pltpu.CompilerParams(
-        dimension_semantics=("arbitrary",), vmem_limit_bytes=24 * 1024 * 1024
+        dimension_semantics=("arbitrary",) if grid else None, vmem_limit_bytes=24 * 1024 * 1024
     )
 
 
@@ -48,6 +48,13 @@
     return pl.BlockSpec((rows, width), lambda j: (0, jnp.minimum(j, last)))
 
 
+RESIDENT = pl.BlockSpec(memory_space=pltpu.VMEM)
+
+
+def block_of(step):
+    return pl.ds(pl.multiple_of(step * CB, CB), CB)
+
+
 def whole(shape):
     return pl.BlockSpec(shape, lambda j: (0,) * len(shape))
 
@@ -58,6 +65,10 @@
 
 def hbm(*values):
     return [pltpu.with_memory_space_constraint(v, pltpu.HBM) for v in values]
+
+
+def kept(*values):
+    return [pltpu.with_memory_space_constraint(v, pltpu.VMEM) for v in values]
 
 
 def sds(shape, dtype):
@@ -71,7 +82,7 @@
 
 
 def as_column(row):
-    return jnp.transpose(jnp.broadcast_to(row, (128, SLOTS)))[:, 0:1]
+    return jnp.transpose(jnp.broadcast_to(row, (128, row.shape[1])))[:, 0:1]
 
 
 def slots_of(pair, core, half, owner, owner_col, sibling_col):
@@ -125,43 +136,53 @@
         pack[...] = onehot(iota(pack.shape, 0) == slots_ref[half : half + 1, :])
 
 
-def pack_product_kernel(slots_ref, k_ref, v_ref, out_ref, pack):
-    @pl.when(pl.program_id(0) == 0)
-    def _():
-        build_pack(slots_ref, [pack])
-
-    product = (k_ref[...].astype(F32) * v_ref[...].astype(F32)).astype(BF)
-    out_ref[...] = dot(pack[...], product).astype(BF)
-
-
-def pack_rows_kernel(halves, slots_ref, *refs):
-    blocks, out_ref, packs = refs[:halves], refs[halves], refs[halves + 1 :]
-
-    @pl.when(pl.program_id(0) == 0)
+def pack_kernel(halves, blocks, slots_ref, *refs):
+    first, second = refs[: 2 * halves : 2], refs[1 : 2 * halves : 2]
+    q_refs, out_ref, packs = refs[2:3], refs[3], refs[4:]
+    if halves == 2:
+        first, second, q_refs, out_ref, packs = None, refs[:2], refs[2:4], refs[4], refs[5:]
+    step = pl.program_id(0)
+
+    @pl.when(step == 0)
     def _():
         build_pack(slots_ref, packs)
 
-    total = dot(packs[0][...], blocks[0][...])
-    for half in range(1, halves):
-        total = total + dot(packs[half][...], blocks[half][...])
-    out_ref[...] = total.astype(BF)
-
-
-def pack_arrivals(kernel, pair, slots, blocks, halves):
-    width = blocks[0].shape[1]
+    def packed(values):
+        total = dot(packs[0][...], values[0])
+        for value, pack in zip(values[1:], packs[1:]):
+            total = total + dot(pack[...], value)
+        return total.astype(BF)
+
+    @pl.when(step < blocks)
+    def _():
+        if first is None:
+            out_ref[...] = packed([ref[...] for ref in second])
+        else:
+            product = first[0][...].astype(F32) * second[0][...].astype(F32)
+            out_ref[...] = packed([product.astype(BF)])
+
+    @pl.when(step >= blocks)
+    def _():
+        out_ref[...] = packed([ref[...] for ref in q_refs])
+
+
+def pack_arrivals(pair, slots, early, late):
+    width = early[0].shape[1]
+    blocks = width // CB
+    halves = len(late)
     sent = SHARDS * pair
     return pl.pallas_call(
-        kernel,
-        grid=(width // CB,),
-        in_specs=[whole((8, SLOTS))] + [cols(SLOTS)] * len(blocks),
+        functools.partial(pack_kernel, halves, blocks),
+        grid=(2 * blocks,),
+        in_specs=[whole((8, SLOTS))]
+        + [cols(SLOTS, last=blocks - 1)] * len(early)
+        + [pl.BlockSpec((SLOTS, CB), lambda j: (0, jnp.maximum(j - blocks, 0)))] * halves,
         out_specs=cols(sent),
-        out_shape=sds((sent, width), BF),
+        out_shape=sds((sent, 2 * width), BF),
         scratch_shapes=[pltpu.VMEM((sent, SLOTS), BF)] * halves,
         compiler_params=params(),
-        cost_estimate=cost(
-            2 * sent * SLOTS * width * halves, 2 * width * (sent + SLOTS * len(blocks))
-        ),
-    )(slots, *blocks)
+        cost_estimate=cost(4 * sent * SLOTS * width * halves, 4 * width * (sent + SLOTS * 2)),
+    )(slots, *early, *late)
 
 
 def product_kernel(k_ref, v_ref, out_ref):
@@ -181,27 +202,25 @@
     )(*hbm(k, v))
 
 
-def place_product_kernel(pos_row, recv_ref, out_ref, tail_ref, place):
+def place_tail_kernel(pos_row, recv_ref, tail_ref, place):
     @pl.when(pl.program_id(0) == 0)
     def _():
-        place[...] = onehot(iota(place.shape, 0) == pos_row[...])
-
-    rows = dot(place[...], recv_ref[...]).astype(BF)
-    out_ref[...] = rows
-    tail_ref[...] = rows[ROWS - TAPS :]
-
-
-def place_product(pos_row, received):
-    sent, width = received.shape
-    return pl.pallas_call(
-        place_product_kernel,
+        place[...] = onehot(iota(place.shape, 0) + (ROWS - TAPS) == pos_row[...])
+
+    tail_ref[...] = dot(place[...], recv_ref[...]).astype(BF)
+
+
+def place_tail(pos_row, received, width):
+    sent = received.shape[0]
+    return pl.pallas_call(
+        place_tail_kernel,
         grid=(width // CB,),
         in_specs=[whole((1, sent)), cols(sent)],
-        out_specs=[cols(ROWS), cols(TAPS)],
-        out_shape=[sds((ROWS, width), BF), sds((TAPS, width), BF)],
-        scratch_shapes=[pltpu.VMEM((ROWS, sent), BF)],
-        compiler_params=params(),
-        cost_estimate=cost(2 * sent * ROWS * width, 2 * width * (sent + ROWS + TAPS)),
+        out_specs=cols(TAPS),
+        out_shape=sds((TAPS, width), BF),
+        scratch_shapes=[pltpu.VMEM((TAPS, sent), BF)],
+        compiler_params=params(),
+        cost_estimate=cost(2 * sent * TAPS * width, 2 * width * (sent + TAPS)),
     )(pos_row, received)
 
 
@@ -240,7 +259,7 @@
     mask = docs[None, :] == doc
     spectrum = jnp.concatenate(
         [jnp.where(mask, jnp.cos(turn), 0.0), jnp.where(mask, -jnp.sin(turn), 0.0)], axis=0
-    ).astype(BF)
+    )
     lag = jnp.arange(TAPS, dtype=I32)[None, :]
     turn = angles(lag)
     weight = jnp.where(
@@ -248,7 +267,7 @@
     )
     taps_spectrum = jnp.concatenate(
         [weight * jnp.cos(turn), -weight * jnp.sin(turn)], axis=0
-    ).astype(BF)
+    )
     return spectrum, taps_spectrum
 
 
@@ -269,81 +288,180 @@
     tail = jnp.where((own_docs[ROWS - TAPS :] == document)[None, :], waves(place), 0.0)
     weight = jnp.where(wave == 0, 1.0, 2.0) / CROSS
     taps = jnp.concatenate([weight, weight], axis=0) * waves(place)
-    return head.astype(BF), tail.T.astype(BF), taps.astype(BF)
-
-
-def mixture_kernel(cc, cc_own_t, bb, product, halo, filt, mix_ref, x_ref, f_ref):
-    window = jnp.concatenate([halo[...], product[...]], axis=0)
-    x = dot(cc[...], window)
+    return head, tail, taps
+
+
+def spectra_product(xr, xi, fr, fi):
+    return jnp.concatenate(
+        [(xr * fr - xi * fi).astype(BF), (xr * fi + xi * fr).astype(BF)], axis=0
+    )
+
+
+def conj_product(gr, gi, fr, fi):
+    return jnp.concatenate(
+        [(gr * fr + gi * fi).astype(BF), (gi * fr - gr * fi).astype(BF)], axis=0
+    )
+
+
+def sums_of(summed, scaled):
+    squares = jnp.sum(summed * summed, axis=1, keepdims=True)
+    dots = jnp.sum(scaled * summed, axis=1, keepdims=True)
+    lane = iota((summed.shape[0], 128), 1)
+    return jnp.where(lane == 0, squares, jnp.where(lane == 1, dots, 0.0))
+
+
+def conv_kernel(
+    pos_row, cc_own, cc_own_t, bb, recv_p, recv_q, filt, residual, cot, gain,
+    q_ref, mix_ref, x_ref, f_ref, sums_ref,
+    place, acc,
+):
+    step = pl.program_id(0)
+
+    @pl.when(step == 0)
+    def _():
+        place[...] = onehot(iota(place.shape, 0) == pos_row[...])
+        acc[...] = jnp.zeros_like(acc)
+
+    at = block_of(step)
+    product = dot(place[...], recv_p[...]).astype(BF)
+    q = dot(place[...], recv_q[...])
+    q_ref[:, at] = q.astype(BF)
+    x = dot(cc_own[...], product)
     f = dot(bb[...], filt[...].astype(BF))
-    xr, xi, fr, fi = x[:FREQ], x[FREQ:], f[:FREQ], f[FREQ:]
-    y = jnp.concatenate(
-        [(xr * fr - xi * fi).astype(BF), (xr * fi + xi * fr).astype(BF)], axis=0
-    )
-    mix_ref[...] = dot(cc_own_t[...], y)
-    x_ref[...] = x.astype(BF)
-    f_ref[...] = f.astype(BF)
-
-
-def forward_mixture(spectrum, cc_own_t, taps_spectrum, product, halo, filt):
-    width = product.shape[1]
-    return pl.pallas_call(
-        mixture_kernel,
+    x_ref[:, at] = x.astype(BF)
+    f_ref[:, at] = f.astype(BF)
+    mix = dot(cc_own_t[...], spectra_product(x[:FREQ], x[FREQ:], f[:FREQ], f[FREQ:]))
+    mix_ref[:, at] = mix
+    late = slice(TAPS, ROWS)
+    summed = residual[late].astype(F32) + q[late] * mix[late]
+    acc[...] += sums_of(summed, cot[late].astype(F32) * gain[...])
+
+    @pl.when(step == pl.num_programs(0) - 1)
+    def _():
+        sums_ref[...] = jnp.transpose(acc[...])[:8]
+
+
+def forward(pos_row, cc_own, cc_own_t, bb, received, filt, residual, cot, gain):
+    sent = received.shape[0]
+    width = received.shape[1] // 2
+    blocks = width // CB
+    return pl.pallas_call(
+        conv_kernel,
+        grid=(blocks,),
+        in_specs=[
+            whole((1, sent)),
+            whole((2 * FREQ, ROWS)),
+            whole((ROWS, 2 * FREQ)),
+            whole((2 * FREQ, TAPS)),
+            cols(sent),
+            pl.BlockSpec((sent, CB), lambda j: (0, blocks + j)),
+            cols(TAPS),
+            cols(ROWS),
+            cols(ROWS),
+            cols(1),
+        ],
+        out_specs=[RESIDENT] * 4 + [whole((8, TAPS))],
+        out_shape=[
+            pltpu.VMEM((ROWS, width), BF),
+            pltpu.VMEM((ROWS, width), F32),
+            pltpu.VMEM((2 * FREQ, width), BF),
+            pltpu.VMEM((2 * FREQ, width), BF),
+            jax.ShapeDtypeStruct((8, TAPS), F32),
+        ],
+        scratch_shapes=[pltpu.VMEM((ROWS, sent), BF), pltpu.VMEM((TAPS, 128), F32)],
+        compiler_params=params(),
+        cost_estimate=cost(4e9, width * 6000),
+    )(pos_row, *hbm(cc_own, cc_own_t, bb), received, received, *hbm(filt, residual, cot), gain)
+
+
+def crossing(value):
+    return value[:CROSS_FREQ], value[FREQ : FREQ + CROSS_FREQ]
+
+
+def head_kernel(
+    cc_halo, cc_head_t, halo, f_ref, q_ref, mix_ref, residual, cot, gain, sums_ref,
+    mix_head_ref, out_sums_ref,
+    acc,
+):
+    step = pl.program_id(0)
+
+    @pl.when(step == 0)
+    def _():
+        acc[...] = jnp.zeros_like(acc)
+
+    at = block_of(step)
+    x = dot(cc_halo[...], halo[...])
+    fr, fi = crossing(f_ref[:, at].astype(F32))
+    y = spectra_product(x[:CROSS_FREQ], x[CROSS_FREQ:], fr, fi)
+    mix = mix_ref[:TAPS, at] + dot(cc_head_t[...], y)
+    mix_head_ref[:, at] = mix
+    summed = residual[...].astype(F32) + q_ref[:TAPS, at].astype(F32) * mix
+    acc[...] += sums_of(summed, cot[...].astype(F32) * gain[...])
+
+    @pl.when(step == pl.num_programs(0) - 1)
+    def _():
+        out_sums_ref[:, :TAPS] = jnp.transpose(acc[...])[:8]
+        out_sums_ref[:, TAPS:] = sums_ref[...]
+
+
+def forward_head(cc_halo, cc_head_t, halo, f, q, mix, residual, cot, gain, sums):
+    width = q.shape[1]
+    return pl.pallas_call(
+        head_kernel,
         grid=(width // CB,),
         in_specs=[
-            whole((2 * FREQ, WIN)),
-            whole((ROWS, 2 * FREQ)),
-            whole((2 * FREQ, TAPS)),
-            cols(ROWS),
+            whole((2 * CROSS_FREQ, TAPS)),
+            whole((TAPS, 2 * CROSS_FREQ)),
+            cols(TAPS),
+            RESIDENT,
+            RESIDENT,
+            RESIDENT,
             cols(TAPS),
             cols(TAPS),
+            cols(1),
+            whole((8, TAPS)),
         ],
-        out_specs=[cols(ROWS), cols(2 * FREQ), cols(2 * FREQ)],
-        out_shape=[
-            sds((ROWS, width), F32),
-            sds((2 * FREQ, width), BF),
-            sds((2 * FREQ, width), BF),
-        ],
-        compiler_params=params(),
-        cost_estimate=cost(2 * 2 * FREQ * (WIN + TAPS + ROWS) * width, width * 8000),
-    )(spectrum, cc_own_t, taps_spectrum, *hbm(product), halo, *hbm(filt))
-
-
-def row_sums_kernel(pos_row, recv, mix, residual, cot, gain, q_ref, sums_ref, place, acc):
-    step = pl.program_id(0)
-
-    @pl.when(step == 0)
-    def _():
-        place[...] = onehot(iota(place.shape, 0) == pos_row[...])
-        acc[...] = jnp.zeros_like(acc)
-
-    q = dot(place[...], recv[...])
-    q_ref[...] = q.astype(BF)
-    summed = residual[...].astype(F32) + q * mix[...]
-    scaled = cot[...].astype(F32) * gain[...]
-    squares = jnp.sum(summed * summed, axis=1, keepdims=True)
-    dots = jnp.sum(scaled * summed, axis=1, keepdims=True)
-    lane = iota((ROWS, 128), 1)
-    acc[...] += jnp.where(lane == 0, squares, jnp.where(lane == 1, dots, 0.0))
-
-    @pl.when(step == pl.num_programs(0) - 1)
-    def _():
-        sums_ref[...] = jnp.transpose(acc[...])[:8]
-
-
-def row_sums(pos_row, received, mix, residual, cot, gain):
-    sent = received.shape[0]
-    width = mix.shape[1]
-    return pl.pallas_call(
-        row_sums_kernel,
-        grid=(width // CB,),
-        in_specs=[whole((1, sent)), cols(sent), cols(ROWS), cols(ROWS), cols(ROWS), cols(1)],
-        out_specs=[cols(ROWS), whole((8, ROWS))],
-        out_shape=[sds((ROWS, width), BF), jax.ShapeDtypeStruct((8, ROWS), F32)],
-        scratch_shapes=[pltpu.VMEM((ROWS, sent), BF), pltpu.VMEM((ROWS, 128), F32)],
-        compiler_params=params(),
-        cost_estimate=cost(2 * sent * ROWS * width, width * 4000),
-    )(pos_row, received, *hbm(mix, residual, cot), gain)
+        out_specs=[RESIDENT, whole((8, ROWS))],
+        out_shape=[pltpu.VMEM((TAPS, width), F32), jax.ShapeDtypeStruct((8, ROWS), F32)],
+        scratch_shapes=[pltpu.VMEM((TAPS, 128), F32)],
+        compiler_params=params(),
+        cost_estimate=cost(6e8, width * 3000),
+    )(*hbm(cc_halo, cc_head_t), halo, *kept(f, q, mix), *hbm(residual, cot), gain, sums)
+
+
+def prepare_kernel(
+    cc_ref, bb_ref, head_ref, tail_ref, taps_ref,
+    own, own_t, halo, head_t, bb, bb_t, onward_head, onward_tail_t, onward_taps,
+):
+    own[...] = cc_ref[:, TAPS:].astype(BF)
+    own_t[...] = jnp.transpose(cc_ref[:, TAPS:]).astype(BF)
+    bb[...] = bb_ref[...].astype(BF)
+    bb_t[...] = jnp.transpose(bb_ref[...]).astype(BF)
+    real, imag = crossing(cc_ref)
+    halo[:CROSS_FREQ] = real[:, :TAPS].astype(BF)
+    halo[CROSS_FREQ:] = imag[:, :TAPS].astype(BF)
+    head = jnp.concatenate([real[:, TAPS : 2 * TAPS], imag[:, TAPS : 2 * TAPS]], axis=0)
+    head_t[...] = jnp.transpose(head).astype(BF)
+    onward_head[...] = head_ref[...].astype(BF)
+    onward_tail_t[...] = jnp.transpose(tail_ref[...]).astype(BF)
+    onward_taps[...] = taps_ref[...].astype(BF)
+
+
+def prepare(cc, bb, head, tail, taps):
+    shapes = [
+        (2 * FREQ, ROWS),
+        (ROWS, 2 * FREQ),
+        (2 * CROSS_FREQ, TAPS),
+        (TAPS, 2 * CROSS_FREQ),
+        (2 * FREQ, TAPS),
+        (TAPS, 2 * FREQ),
+        (2 * CROSS_FREQ, TAPS),
+        (TAPS, 2 * CROSS_FREQ),
+        (2 * CROSS_FREQ, TAPS),
+    ]
+    return pl.pallas_call(
+        prepare_kernel, out_shape=[sds(shape, BF) for shape in shapes], compiler_params=params(False)
+    )(cc, bb, head, tail, taps)
 
 
 def tap_rows(pair, shape, tap_dim, step):
@@ -367,10 +485,46 @@
     return inv * scaled - summed * (inv * inv * inv) * stats[:, 1:2] / D
 
 
+def head_grad_kernel(
+    s0, s1, s2, s3, q_ref, mix_head_ref, res_ref, cot_ref, gain_ref, head_ref, stats
+):
+    step = pl.program_id(0)
+
+    @pl.when(step == 0)
+    def _():
+        row_stats(s0, s1, s2, s3, stats)
+
+    at = block_of(step)
+    q = q_ref[:TAPS, at].astype(F32)
+    summed = res_ref[...].astype(F32) + q * mix_head_ref[:, at]
+    d_summed = d_summed_of(stats[:TAPS], summed, cot_ref[...].astype(F32) * gain_ref[...])
+    head_ref[...] = (d_summed * q).astype(BF)
+
+
+def head_grad(sums, q, mix_head, residual, cot, gain):
+    width = q.shape[1]
+    return pl.pallas_call(
+        head_grad_kernel,
+        grid=(width // CB,),
+        in_specs=[whole((8, ROWS))] * 4
+        + [RESIDENT, RESIDENT, cols(TAPS), cols(TAPS), cols(1)],
+        out_specs=cols(TAPS),
+        out_shape=sds((TAPS, width), BF),
+        scratch_shapes=[pltpu.VMEM((ROWS, 128), F32)],
+        compiler_params=params(),
+        cost_estimate=cost(width * TAPS * 10, width * TAPS * 6),
+    )(*sums, *kept(q, mix_head), *hbm(residual, cot), gain)
+
+
+def mixture_block(mix_ref, mix_head_ref, at):
+    return jnp.concatenate([mix_head_ref[:, at], mix_ref[TAPS:, at]], axis=0)
+
+
 def backward_kernel(
     pair, blocks,
-    s0, s1, s2, s3, pos_col, cc_own, bb_t, q_ref, mix_ref, res_ref, cot_ref, gain_ref, x_ref,
-    dmix_ref, head_ref, out_ref,
+    s0, s1, s2, s3, pos_row, cc_own, cc_halo, bb_t, q_ref, mix_ref, mix_head_ref, x_ref,
+    halo_ref, res_ref, cot_ref, gain_ref,
+    dmix_ref, out_ref,
     give, stats, taps_acc, gain_acc,
 ):
     step = pl.program_id(0)
@@ -380,15 +534,16 @@
 
     @pl.when(step == 0)
     def _():
-        give[...] = onehot(pos_col[...] == iota(give.shape, 1))
+        give[...] = onehot(as_column(pos_row[...]) == iota(give.shape, 1))
         row_stats(s0, s1, s2, s3, stats)
         taps_acc[...] = jnp.zeros_like(taps_acc)
         gain_acc[...] = jnp.zeros_like(gain_acc)
 
     @pl.when(step < blocks)
     def _():
-        q = q_ref[...].astype(F32)
-        mix = mix_ref[...]
+        at = block_of(jnp.minimum(step, blocks - 1))
+        q = q_ref[:, at].astype(F32)
+        mix = mixture_block(mix_ref, mix_head_ref, at)
         summed = res_ref[...].astype(F32) + q * mix
         cot = cot_ref[...].astype(F32)
         gain_part = jnp.sum(cot * summed * stats[:, 0:1], axis=0, keepdims=True)
@@ -396,16 +551,17 @@
         out_ref[...] = dot(give[...], (d_summed * mix).astype(BF)).astype(BF)
         d_mix = (d_summed * q).astype(BF)
         dmix_ref[...] = d_mix
-        head_ref[...] = d_mix[:TAPS]
         g = dot(cc_own[...], d_mix)
-        gr, gi = g[:FREQ], g[FREQ:]
-        xr, xi = x_ref[:FREQ].astype(F32), x_ref[FREQ:].astype(F32)
-        v = jnp.concatenate(
-            [(gr * xr + gi * xi).astype(BF), (gi * xr - gr * xi).astype(BF)], axis=0
+        x = x_ref[:, at].astype(F32)
+        reach = dot(cc_halo[...], halo_ref[...])
+        xr = jnp.concatenate([x[:CROSS_FREQ] + reach[:CROSS_FREQ], x[CROSS_FREQ:FREQ]], axis=0)
+        xi = jnp.concatenate(
+            [x[FREQ : FREQ + CROSS_FREQ] + reach[CROSS_FREQ:], x[FREQ + CROSS_FREQ :]], axis=0
         )
-        taps = dot(bb_t[...], v).astype(BF)
+        taps = dot(bb_t[...], conj_product(g[:FREQ], g[FREQ:], xr, xi)).astype(BF)
         spread = onehot(iota((sent, TAPS), 0) == tap_rows(pair, (sent, TAPS), 1, step))
-        taps_acc[step // per] += dot(spread, taps)
+        part = jnp.minimum(step // per, parts - 1)
+        taps_acc[part] += dot(spread, taps)
         wide = gain_acc.shape[1]
         for i in range(CB // wide):
             row = iota(gain_acc.shape, 0) == step * (CB // wide) + i
@@ -413,7 +569,7 @@
 
     @pl.when((step >= blocks) & (step < blocks + parts))
     def _():
-        out_ref[...] = taps_acc[jnp.minimum(step - blocks, parts - 1)].astype(BF)
+        out_ref[...] = taps_acc[jnp.clip(step - blocks, 0, parts - 1)].astype(BF)
 
     @pl.when(step == blocks + parts)
     def _():
@@ -422,33 +578,33 @@
         out_ref[:, :wide] = rows.astype(BF)
 
 
-def backward(pair, sums, pos_col, cc_own, bb_t, q, mix, residual, cot, gain, x):
+def backward(pair, sums, pos_row, cc_own, cc_halo, bb_t, q, mix, mix_head, x, halo, residual, cot, gain):
     width = q.shape[1]
     blocks = width // CB
     last = blocks - 1
     sent = SHARDS * pair
     part_cols, gain_cols = extra_cols(pair, width)
     parts = part_cols // CB
-    row_block = cols(ROWS, last=last)
     return pl.pallas_call(
         functools.partial(backward_kernel, pair, blocks),
         grid=(blocks + parts + 1,),
         in_specs=[whole((8, ROWS))] * 4
         + [
-            whole((sent, 1)),
+            whole((1, sent)),
             whole((2 * FREQ, ROWS)),
+            whole((2 * CROSS_FREQ, TAPS)),
             whole((TAPS, 2 * FREQ)),
-            row_block,
-            row_block,
-            row_block,
-            row_block,
+        ]
+        + [RESIDENT] * 4
+        + [
+            cols(TAPS, last=last),
+            cols(ROWS, last=last),
+            cols(ROWS, last=last),
             cols(1, last=last),
-            cols(2 * FREQ, last=last),
         ],
-        out_specs=[row_block, cols(TAPS, last=last), cols(sent)],
+        out_specs=[cols(ROWS, last=last), cols(sent)],
         out_shape=[
             sds((ROWS, width), BF),
-            sds((TAPS, width), BF),
             sds((sent, width + part_cols + gain_cols), BF),
         ],
         scratch_shapes=[
@@ -459,59 +615,64 @@
         ],
         compiler_params=params(),
         cost_estimate=cost(2e9, width * 6000),
-    )(*sums, *hbm(pos_col, cc_own, bb_t, q, mix, residual, cot), gain, *hbm(x))
+    )(
+        *sums, *hbm(pos_row, cc_own, cc_halo, bb_t), *kept(q, mix, mix_head, x), halo,
+        *hbm(residual, cot), gain,
+    )
 
 
 def finish_kernel(
-    s0, s1, s2, s3, cc_own, cc_own_t, q_ref, mix_ref, res_ref, cot_ref, gain_ref, f_ref, dmix_ref,
+    s0, s1, s2, s3, cc_own, cc_own_t, q_ref, mix_ref, mix_head_ref, f_ref, res_ref, cot_ref,
+    gain_ref, dmix_ref,
     normed_ref, dres_ref, own_ref,
     stats,
 ):
-    @pl.when(pl.program_id(0) == 0)
+    step = pl.program_id(0)
+
+    @pl.when(step == 0)
     def _():
         row_stats(s0, s1, s2, s3, stats)
 
+    at = block_of(step)
     gain = gain_ref[...]
-    summed = res_ref[...].astype(F32) + q_ref[...].astype(F32) * mix_ref[...]
+    mix = mixture_block(mix_ref, mix_head_ref, at)
+    summed = res_ref[...].astype(F32) + q_ref[:, at].astype(F32) * mix
     normed_ref[...] = (summed * stats[:, 0:1] * gain).astype(BF)
     dres_ref[...] = d_summed_of(stats, summed, cot_ref[...].astype(F32) * gain).astype(BF)
     g = dot(cc_own[...], dmix_ref[...])
-    gr, gi = g[:FREQ], g[FREQ:]
-    fr, fi = f_ref[:FREQ].astype(F32), f_ref[FREQ:].astype(F32)
-    z = jnp.concatenate(
-        [(gr * fr + gi * fi).astype(BF), (gi * fr - gr * fi).astype(BF)], axis=0
-    )
-    own_ref[...] = dot(cc_own_t[...], z)
-
-
-def finish(sums, cc_own, cc_own_t, q, mix, residual, cot, gain, f, d_mix):
+    f = f_ref[:, at].astype(F32)
+    own_ref[...] = dot(cc_own_t[...], conj_product(g[:FREQ], g[FREQ:], f[:FREQ], f[FREQ:]))
+
+
+def finish(sums, cc_own, cc_own_t, q, mix, mix_head, f, residual, cot, gain, d_mix):
     width = q.shape[1]
     return pl.pallas_call(
         finish_kernel,
         grid=(width // CB,),
         in_specs=[whole((8, ROWS))] * 4
         + [whole((2 * FREQ, ROWS)), whole((ROWS, 2 * FREQ))]
-        + [cols(ROWS)] * 4
-        + [cols(1), cols(2 * FREQ), cols(ROWS)],
+        + [RESIDENT] * 4
+        + [cols(ROWS), cols(ROWS), cols(1), cols(ROWS)],
         out_specs=[cols(ROWS)] * 3,
         out_shape=[sds((ROWS, width), BF), sds((ROWS, width), BF), sds((ROWS, width), F32)],
         scratch_shapes=[pltpu.VMEM((ROWS, 128), F32)],
         compiler_params=params(),
         cost_estimate=cost(2 * 2 * 2 * FREQ * ROWS * width, width * 6000),
-    )(*sums, *hbm(cc_own, cc_own_t, q, mix, residual, cot), gain, *hbm(f, d_mix))
-
-
-def give_back_kernel(pos_col, head, tail_t, taps, own_ref, next_ref, filt, out_ref, give):
+    )(
+        *sums, *hbm(cc_own, cc_own_t), *kept(q, mix, mix_head, f), *hbm(residual, cot), gain,
+        *hbm(d_mix),
+    )
+
+
+def give_back_kernel(pos_row, head, tail_t, taps, own_ref, next_ref, filt, out_ref, give):
     @pl.when(pl.program_id(0) == 0)
     def _():
-        give[...] = onehot(pos_col[...] == iota(give.shape, 1))
+        give[...] = onehot(as_column(pos_row[...]) == iota(give.shape, 1))
 
     g = dot(head[...], next_ref[...])
     f = dot(taps[...], filt[...].astype(BF))
     gr, gi, fr, fi = g[:CROSS_FREQ], g[CROSS_FREQ:], f[:CROSS_FREQ], f[CROSS_FREQ:]
-    z = jnp.concatenate(
-        [(gr * fr + gi * fi).astype(BF), (gi * fr - gr * fi).astype(BF)], axis=0
-    )
+    z = conj_product(gr, gi, fr, fi)
     own = own_ref[...]
     grad = jnp.concatenate(
         [own[: ROWS - TAPS], own[ROWS - TAPS :] + dot(tail_t[...], z)], axis=0
@@ -519,14 +680,14 @@
     out_ref[...] = dot(give[...], grad.astype(BF)).astype(BF)
 
 
-def give_back(pair, pos_col, crossing, own, from_next, filt):
+def give_back(pair, pos_row, onward, own, from_next, filt):
     width = own.shape[1]
     sent = SHARDS * pair
     return pl.pallas_call(
         give_back_kernel,
         grid=(width // CB,),
         in_specs=[
-            whole((sent, 1)),
+            whole((1, sent)),
             whole((2 * CROSS_FREQ, TAPS)),
             whole((TAPS, 2 * CROSS_FREQ)),
             whole((2 * CROSS_FREQ, TAPS)),
@@ -539,7 +700,7 @@
         scratch_shapes=[pltpu.VMEM((sent, ROWS), BF)],
         compiler_params=params(),
         cost_estimate=cost(2 * sent * ROWS * width, width * 2400),
-    )(*hbm(pos_col, *crossing, own), from_next, *hbm(filt))
+    )(*hbm(pos_row, *onward, own), from_next, *hbm(filt))
 
 
 def reduce_kernel(pair, taps_ref, gain_ref, rows_ref, out_ref, d_gain_ref):
@@ -697,63 +858,52 @@
     if shared:
         product_in = slot_product(k_in, v_in)
         product_other = swap(product_in)
+        q_other = swap(q_in)
         slots = send_plan(pair, my_index, dest_pos)
-        q_other = swap(q_in)
-        sent_product = pack_arrivals(
-            functools.partial(pack_rows_kernel, 2), pair, slots, [product_in, product_other], 2
+        sent_rows = pack_arrivals(
+            pair, slots, [*hbm(product_in), product_other], [*hbm(q_in), q_other]
         )
-        q_blocks = [q_in, q_other]
     else:
         slots = send_plan(pair, my_index, dest_pos)
-        sent_product = pack_arrivals(pack_product_kernel, pair, slots, hbm(k_in, v_in), 1)
-        q_blocks = hbm(q_in)
-    sent_product, dest_later, docs_later, slots = lax.optimization_barrier(
-        (sent_product, dest_pos, doc_ids, slots)
-    )
-    recv_product = exchange(pair, sent_product)
-    halves = len(q_blocks)
-    sent_q = pack_arrivals(
-        functools.partial(pack_rows_kernel, halves), pair, slots, q_blocks, halves
-    )
+        sent_rows = pack_arrivals(pair, slots, hbm(k_in, v_in), hbm(q_in))
+    sent_rows, dest_later, docs_later, slots = lax.optimization_barrier(
+        (sent_rows, dest_pos, doc_ids, slots)
+    )
+    received = exchange(pair, sent_rows)
 
     pos = slot_positions(pair, dest_later, my_index)
-    pos_row, pos_col = pos[None, :], pos[:, None]
+    pos_row = pos[None, :]
     docs_all = jnp.concatenate(
         [jnp.full((TAPS,), -1, I32), docs_later, jnp.full((TAPS,), -2, I32)]
     )
     docs = lax.dynamic_slice_in_dim(docs_all, my_index * ROWS, WIN + TAPS)
-    spectrum, taps_spectrum = segment_dft(docs[:WIN])
-    spectrum_t = spectrum.T
-    prepared = (
-        pos_row,
-        pos_col,
-        spectrum,
-        spectrum[:, TAPS:],
-        spectrum_t[TAPS:],
-        taps_spectrum,
-        taps_spectrum.T,
-        crossing_dft(docs[TAPS:WIN], docs[WIN:]),
-    )
-    sent_q, recv_product, prepared = lax.optimization_barrier((sent_q, recv_product, prepared))
-    pos_row, pos_col, cc, cc_own, cc_own_t, bb, bb_t, crossing = prepared
-
-    product, tail = place_product(pos_row, recv_product)
-    sent_q, halo = lax.optimization_barrier((sent_q, shift(tail, 1)))
-    recv_q = exchange(pair, sent_q)
-    mix, x, f = forward_mixture(cc, cc_own_t, bb, product, halo, mr_filter)
-    q_pos, sums = row_sums(pos_row, recv_q, mix, residual, cotangent, gain)
+    cc, bb = segment_dft(docs[:WIN])
+    onward = crossing_dft(docs[TAPS:WIN], docs[WIN:])
+    prepared = prepare(cc, bb, *onward)
+    received, pos_row, prepared = lax.optimization_barrier((received, pos_row, prepared))
+    cc_own, cc_own_t, cc_halo, cc_head_t, bb, bb_t, *onward = prepared
+
+    halo = shift(place_tail(pos_row, received, width), 1)
+    q, mix, x, f, sums = forward(
+        pos_row, cc_own, cc_own_t, bb, received, mr_filter, residual, cotangent, gain
+    )
+    mix_head, sums = forward_head(
+        cc_halo, cc_head_t, halo, f, q, mix, residual, cotangent, gain, sums
+    )
     all_sums = [sums] + [
         lax.ppermute(sums, "mp", [(i, (i + k) % 4) for i in range(4)]) for k in (1, 2, 3)
     ]
-    d_mix, head, sent_dq = backward(
-        pair, all_sums, pos_col, cc_own, bb_t, q_pos, mix, residual, cotangent, gain, x
-    )
-    from_next = shift(head, -1)
+    head = head_grad(all_sums, q, mix_head, residual, cotangent, gain)
+    d_mix, sent_dq = backward(
+        pair, all_sums, pos_row, cc_own, cc_halo, bb_t, q, mix, mix_head, x, halo,
+        residual, cotangent, gain,
+    )
+    sent_dq, from_next = lax.optimization_barrier((sent_dq, shift(head, -1)))
     back_q = exchange(pair, sent_dq)
     normed, d_residual, own_grad = finish(
-        all_sums, cc_own, cc_own_t, q_pos, mix, residual, cotangent, gain, f, d_mix
-    )
-    rows = give_back(pair, pos_col, crossing, own_grad, from_next, mr_filter)
+        all_sums, cc_own, cc_own_t, q, mix, mix_head, f, residual, cotangent, gain, d_mix
+    )
+    rows = give_back(pair, pos_row, onward, own_grad, from_next, mr_filter)
     sent_dp, d_gain = reduce_parts(pair, back_q, rows, width)
     back_p = exchange(pair, sent_dp)
     backs_q, backs_p = [back_q], [back_p]

time: 213 us -> 206 us (0.967)
  other arithmetic: 11.5 us -> 6.17 us
  Pallas kernels: 58.6 us -> 63.1 us
  starting transfers between devices: 37 us -> 32.5 us
    ppermute x2, waiting for transfers between devices: 33.5 us -> 0.01 us  [shift(): return lax.ppermute(value, 'seq', pairs)]
    all_to_all x4 -> x3, waiting for transfers between devices: 60.4 us -> 91.1 us  [exchange(): lax.all_to_all(shards, 'seq', split_axis=0, concat_axis=0, tiled=True)]
    all_to_all x4 -> x3, starting transfers between devices: 28.2 us -> 20.1 us  [exchange(): lax.all_to_all(shards, 'seq', split_axis=0, concat_axis=0, tiled=True)]
    pallas_call x6 -> x7, Pallas kernels: 29.9 us -> 36 us  [the longest x1 8.43 us: pack_arrivals(): pl.pallas_call(functools.partial(pack_kernel, halves, blocks), grid=(2 *...]
    optimization_barrier x5 -> x0, local copies, waits for them, and re-layouts: 3.99 us -> none  [layer(): lax.optimization_barrier((sent_q, recv_product, prepared))]
    unnamed x16 -> x26, local copies, waits for them, and re-layouts: 2.64 us -> 6.6 us
    ppermute x2, starting transfers between devices: 4.39 us -> 7.94 us  [shift(): return lax.ppermute(value, 'seq', pairs)]
    another operation x2 -> x0, other arithmetic: 3.27 us -> none
  transfers between devices with their start and end apart: 9 -> 8, of which waited for: 6 -> 5; matrix products, arithmetic and copies ran while one was open for 8% -> 3% of each run, Pallas kernels for 13% -> 17%
where the time goes in v3:
time: 206 us; the launch traced here: 205 us
  waiting for transfers between devices  94.4 us (46%)
  Pallas kernels  63.1 us (31%)
  starting transfers between devices  32.5 us (16%)
  local copies, waits for them, and re-layouts  7.29 us (4%)
  other arithmetic  6.17 us (3%)
    all_to_all x3, waiting for transfers between devices, exchange(): lax.all_to_all(shards, 'seq', split_axis=0, concat_axis=0, tiled=True)  91.1 us
    all_to_all x3, starting transfers between devices, exchange(): lax.all_to_all(shards, 'seq', split_axis=0, concat_axis=0, tiled=True)  20.1 us
    pallas_call x1, Pallas kernels, backward(): pl.pallas_call(functools.partial(backward_kernel, pair, blocks), grid=(bl...  9.94 us
    pallas_call x1, Pallas kernels, pack_arrivals(): pl.pallas_call(functools.partial(pack_kernel, halves, blocks), grid=(2 *...  8.43 us
    ppermute x2, starting transfers between devices, shift(): return lax.ppermute(value, 'seq', pairs)  7.94 us
    pallas_call x1, Pallas kernels, forward(): pl.pallas_call(conv_kernel, grid=(blocks,), in_specs=[whole((1, sent)), w...  7.44 us
    pallas_call x1, Pallas kernels, finish(): pl.pallas_call(finish_kernel, grid=(width // CB,), in_specs=[whole((8, RO...  6.89 us
    unnamed x26, local copies, waits for them, and re-layouts  6.6 us
  transfers between devices with their start and end apart: 8, of which 5 were waited for; matrix products, arithmetic and copies ran while one was open for 3% of the time, Pallas kernels for 17%

profile of v3, /device:TPU:1, one launch (start us, length us, event | category | flops | bytes accessed | tf_op | source)
XLA Modules:
  0.0 204.7 jit_solution(5385073919402409520)
XLA Ops:
  0.6 0.0 copy-start.8
  0.6 0.8 copy-done.8
  1.4 0.2 shard_map.144.slots_ref
  1.7 8.4 %shard_map.145 = bf16[512,4096]{1,0:T(8,128)(2,1)} custom-call(s32[8,384]{1,0:T(8,128)S(1)} %shard_map.144.slots_ref, bf16[384,2048]{1,0:T(8,128)(2,1)} %k_ref.1, bf16[384,2048]{1,0:T(8,128)(2,1)} %v_ref.1, bf16[384,2048]{1,0:T(8,128)(2,1)} %refs_2_.1), custom_call_target="tpu_custom_call" | custom-call | flops 1610612736 | bytes 10485760 | tf_op jit(solution)/shard_map/pallas_call | solution.py:174
  10.1 8.8 %all-to-all-start = ((bf16[32,16,4096]{2,1,0:T(8,128)(2,1)}), bf16[32,16,4096]{2,1,0:T(8,128)(2,1)}, u32[]{:S(2)}, u32[]{:S(2)}) async-start(bf16[32,16,4096]{2,1,0:T(8,128)(2,1)} %bitcast.21), calls=%async_computation | async-start | bytes 8388608 | tf_op jit(solution)/shard_map/all_to_all | solution.py:822
  18.9 0.0 copy-done.12
  18.9 0.1 fusion.32
  19.0 0.6 slice.17
  19.6 0.2 select_reduce_fusion.4
  19.8 0.1 select_reduce_fusion.8
  19.9 0.0 copy-done.9
  20.0 0.2 fusion
  20.2 0.6 select_reduce_fusion
  20.8 0.1 sub.78.pos_row
  20.9 0.1 maximum_reduce_fusion
  21.0 0.4 fusion.11
  21.4 0.4 sine_negate_fusion
  21.8 0.2 select_reduce_fusion.1
  22.0 0.7 select_multiply_fusion
  22.8 2.1 %compare_select_fusion.1 = (f32[320,384]{1,0:T(8,128)S(1)}, f32[320,384]{1,0:T(8,128)S(1)}) fusion(f32[320]{0:T(512)S(1)} %broadcast_multiply_fusion, f32[320]{0:T(512)S(1)} %get-tuple-element.104, f32[320]{0:T(512)S(1)} %get-tuple-element.103, s32[320]{0:T(512)S(1)} %get-tuple-element.99, s32[320]{0:T(512)S(1)} %get-tuple-element.119, ...), kind=kLoop, calls=%fused_computation.6 | loop fusion | flops 1474560 | bytes 992256 | tf_op jit(solution)/shard_map/jit(_where)/select_n | solution.py:261
  24.9 0.1 pad_maximum_fusion.cc_ref
  24.9 0.7 slice_compare_fusion
  25.6 0.4 fusion.14
  26.0 0.1 fusion.3
  26.1 1.3 shard_map.146
  27.4 43.7 %all-to-all-done = bf16[32,16,4096]{2,1,0:T(8,128)(2,1)} async-done(((bf16[32,16,4096]{2,1,0:T(8,128)(2,1)}), bf16[32,16,4096]{2,1,0:T(8,128)(2,1)}, u32[]{:S(2)}, u32[]{:S(2)}) %all-to-all-start) | async-done | bytes 4194336 | tf_op jit(solution)/shard_map/all_to_all | solution.py:822
  71.1 3.9 %shard_map.147 = bf16[128,2048]{1,0:T(8,128)(2,1)} custom-call(s32[1,512]{1,0:T(1,128)S(1)} %sub.78.pos_row, bf16[512,4096]{1,0:T(8,128)(2,1)} %bitcast.3.recv_ref.recv_p.recv_q), custom_call_target="tpu_custom_call" | custom-call | flops 268435456 | bytes 2621440 | tf_op jit(solution)/shard_map/pallas_call | solution.py:215
  75.1 5.8 %collective-permute-start = (bf16[128,2048]{1,0:T(8,128)(2,1)}, bf16[128,2048]{1,0:T(8,128)(2,1)S(1)}, u32[]{:S(2)}, u32[]{:S(2)}) collective-permute-start(bf16[128,2048]{1,0:T(8,128)(2,1)} %shard_map.147), channel_id=1, source_target_pairs={{0,4},{4,8},{8,12},{12,16},{16,20},{20,24},{24,28},{28,32},{32,36}... | collective-permute-start | bytes 1572872 | tf_op jit(solution)/shard_map/ppermute | solution.py:829
  80.9 0.0 copy-done.11
  80.9 0.0 copy-done.10
  80.9 7.4 %shard_map.148 = (bf16[256,2048]{1,0:T(8,128)(2,1)S(1)}, f32[256,2048]{1,0:T(8,128)S(1)}, bf16[640,2048]{1,0:T(8,128)(2,1)S(1)}, bf16[640,2048]{1,0:T(8,128)(2,1)S(1)}, f32[8,128]{1,0:T(8,128)S(1)}) custom-call(s32[1,512]{1,0:T(1,128)S(1)} %sub.78.pos_row, bf16[640,256]{1,0:T(8,128)(2,1)} %get-tuple-element.66.cc_own, ...), custom_call_target="tpu_custom_call" | custom-call | flops 4000000000 | bytes 12288000 | tf_op jit(solution)/shard_map/pallas_call | solution.py:348
  88.4 0.0 copy-start.4
  88.4 0.0 copy-start
  88.4 0.0 copy-start.2
  88.4 0.0 collective-permute-done.halo.halo_ref
  88.4 4.8 %shard_map.149 = (f32[128,2048]{1,0:T(8,128)S(1)}, f32[8,256]{1,0:T(8,128)S(1)}) custom-call(bf16[384,128]{1,0:T(8,128)(2,1)} %get-tuple-element.62.cc_halo, bf16[128,384]{1,0:T(8,128)(2,1)} %get-tuple-element.63.cc_head_t, bf16[128,2048]{1,0:T(8,128)(2,1)S(1)} %collective-permute-done.halo.halo_ref, bf16[640,2048]{1,0:T(8,128)(2,1)S(1)} %get-tuple-element.69.f_ref, ...), custom_call_target="tpu_custom_call" | custom-call | flops 600000000 | bytes 6144000 | tf_op jit(solution)/shard_map/pallas_call | solution.py:409
  93.2 0.0 copy-done.4
  93.2 0.0 copy-start.6
  93.2 3.8 %collective-permute-start.3 = (f32[8,256]{1,0:T(8,128)S(1)}, f32[8,256]{1,0:T(8,128)S(1)}, u32[]{:S(2)}, u32[]{:S(2)}) collective-permute-start(f32[8,256]{1,0:T(8,128)S(1)} %get-tuple-element.73.s0), channel_id=1, source_target_pairs={{0,3},{1,0},{2,1},{3,2},{4,7},{5,4},{6,5},{7,6},{8,11},{9,8},{10,9... | collective-permute-start | bytes 24584 | tf_op jit(solution)/shard_map/ppermute | solution.py:894
  97.0 0.0 collective-permute-start.2
  97.0 0.7 collective-permute-start.1
  97.7 0.1 collective-permute-done.3.s3
  97.8 3.2 %collective-permute-done.2.s2 = f32[8,256]{1,0:T(8,128)S(1)} collective-permute-done((f32[8,256]{1,0:T(8,128)S(1)}, f32[8,256]{1,0:T(8,128)S(1)}, u32[]{:S(2)}, u32[]{:S(2)}) %collective-permute-start.2) | collective-permute-done | bytes 8224 | tf_op jit(solution)/shard_map/ppermute | solution.py:894
  101.0 0.0 collective-permute-done.1.s1
  101.0 3.9 %shard_map.152 = bf16[128,2048]{1,0:T(8,128)(2,1)} custom-call(f32[8,256]{1,0:T(8,128)S(1)} %get-tuple-element.73.s0, f32[8,256]{1,0:T(8,128)S(1)} %collective-permute-done.1.s1, f32[8,256]{1,0:T(8,128)S(1)} %collective-permute-done.2.s2, f32[8,256]{1,0:T(8,128)S(1)} %collective-permute-done.3.s3, bf16[256,2048]{1,0:T(8,128)(2,1)S(1)} %get-tuple-element.70.q_ref, ...), custom_call_target="tpu_custom_call" | custom-call | flops 2621440 | bytes 1572864 | tf_op jit(solution)/shard_map/pallas_call | solution.py:506
  104.9 2.1 %collective-permute-start.4 = (bf16[128,2048]{1,0:T(8,128)(2,1)}, bf16[128,2048]{1,0:T(8,128)(2,1)S(1)}, u32[]{:S(2)}, u32[]{:S(2)}) collective-permute-start(bf16[128,2048]{1,0:T(8,128)(2,1)} %shard_map.152), channel_id=1, source_target_pairs={{4,0},{8,4},{12,8},{16,12},{20,16},{24,20},{28,24},{32,28},{36,32}... | collective-permute-start | bytes 1572872 | tf_op jit(solution)/shard_map/ppermute | solution.py:829
  107.0 0.0 copy-done
  107.0 0.0 copy-done.2
  107.0 9.9 %shard_map.150 = (bf16[256,2048]{1,0:T(8,128)(2,1)}, bf16[512,2688]{1,0:T(8,128)(2,1)}) custom-call(f32[8,256]{1,0:T(8,128)S(1)} %get-tuple-element.73.s0, f32[8,256]{1,0:T(8,128)S(1)} %collective-permute-done.1.s1, f32[8,256]{1,0:T(8,128)S(1)} %collective-permute-done.2.s2, f32[8,256]{1,0:T(8,128)S(1)} %collective-permute-done.3.s3, s32[1,512]{1,0:T(1,128)} %copy-done.11, ...), custom_call_target="tpu_custom_call" | custom-call | flops 2000000000 | bytes 12288000 | tf_op jit(solution)/shard_map/pallas_call | solution.py:588
  117.0 0.0 copy-done.6
  117.0 0.0 collective-permute-done.4.next_ref
  117.0 5.9 %all-to-all-start.1 = ((bf16[32,16,2688]{2,1,0:T(8,128)(2,1)}), bf16[32,16,2688]{2,1,0:T(8,128)(2,1)S(1)}, u32[]{:S(2)}, u32[]{:S(2)}) async-start(bf16[32,16,2688]{2,1,0:T(8,128)(2,1)} %bitcast.22), calls=%async_computation.1 | async-start | bytes 5505024 | tf_op jit(solution)/shard_map/all_to_all | solution.py:822
  122.9 1.6 copy-done.1
  124.5 1.2 copy-done.3
  125.7 1.7 copy-done.5
  127.5 1.2 copy-done.7
  128.7 6.9 %shard_map.151 = (bf16[256,2048]{1,0:T(8,128)(2,1)}, bf16[256,2048]{1,0:T(8,128)(2,1)}, f32[256,2048]{1,0:T(8,128)}) custom-call(f32[8,256]{1,0:T(8,128)S(1)} %get-tuple-element.73.s0, f32[8,256]{1,0:T(8,128)S(1)} %collective-permute-done.1.s1, f32[8,256]{1,0:T(8,128)S(1)} %collective-permute-done.2.s2, f32[8,256]{1,0:T(8,128)S(1)} %collective-permute-done.3.s3, ...), custom_call_target="tpu_custom_call" | custom-call | flops 1342177280 | bytes 12288000 | tf_op jit(solution)/shard_map/pallas_call | solution.py:649
  135.6 6.3 %shard_map.154.rows_ref = bf16[512,2560]{1,0:T(8,128)(2,1)} custom-call(s32[1,512]{1,0:T(1,128)} %copy-done.11, bf16[384,128]{1,0:T(8,128)(2,1)} %get-tuple-element.83.head, bf16[128,384]{1,0:T(8,128)(2,1)} %get-tuple-element.84.tail_t, bf16[384,128]{1,0:T(8,128)(2,1)} %get-tuple-element.85.taps, f32[256,2048]{1,0:T(8,128)} %get-tuple-element.86.own_ref, ...), custom_call_target="tpu_custom_call" | custom-call | flops 536870912 | bytes 4915200 | tf_op jit(solution)/shard_map/pallas_call | solution.py:686
  141.9 16.3 %all-to-all-done.1 = bf16[32,16,2688]{2,1,0:T(8,128)(2,1)S(1)} async-done(((bf16[32,16,2688]{2,1,0:T(8,128)(2,1)}), bf16[32,16,2688]{2,1,0:T(8,128)(2,1)S(1)}, u32[]{:S(2)}, u32[]{:S(2)}) %all-to-all-start.1) | async-done | bytes 2752544 | tf_op jit(solution)/shard_map/all_to_all | solution.py:822
  158.2 1.0 shard_map.155
  159.2 5.4 %all-to-all-start.2 = ((bf16[32,16,2560]{2,1,0:T(8,128)(2,1)}), bf16[32,16,2560]{2,1,0:T(8,128)(2,1)}, u32[]{:S(2)}, u32[]{:S(2)}) async-start(bf16[32,16,2560]{2,1,0:T(8,128)(2,1)} %bitcast.20), calls=%async_computation.2 | async-start | bytes 5242880 | tf_op jit(solution)/shard_map/all_to_all | solution.py:822
  164.6 3.0 %shard_map.153 = bf16[384,2048]{1,0:T(8,128)(2,1)} custom-call(s32[8,384]{1,0:T(8,128)S(1)} %shard_map.144.slots_ref, bf16[512,2688]{1,0:T(8,128)(2,1)S(1)} %bitcast.13), custom_call_target="tpu_custom_call" | custom-call | flops 805306368 | bytes 3670016 | tf_op jit(solution)/shard_map/pallas_call | solution.py:767
  167.6 31.0 %all-to-all-done.2 = bf16[32,16,2560]{2,1,0:T(8,128)(2,1)} async-done(((bf16[32,16,2560]{2,1,0:T(8,128)(2,1)}), bf16[32,16,2560]{2,1,0:T(8,128)(2,1)}, u32[]{:S(2)}, u32[]{:S(2)}) %all-to-all-start.2) | async-done | bytes 2621472 | tf_op jit(solution)/shard_map/all_to_all | solution.py:822
  198.7 6.0 %shard_map.156 = (bf16[384,2048]{1,0:T(8,128)(2,1)}, bf16[384,2048]{1,0:T(8,128)(2,1)}, f32[128,2048]{1,0:T(8,128)}) custom-call(s32[8,384]{1,0:T(8,128)S(1)} %shard_map.144.slots_ref, bf16[512,2560]{1,0:T(8,128)(2,1)} %bitcast.9.taps_ref.refs_0_, bf16[384,2048]{1,0:T(8,128)(2,1)} %k_ref.1, bf16[384,2048]{1,0:T(8,128)(2,1)} %v_ref.1, ...), custom_call_target="tpu_custom_call" | custom-call | flops 805306368 | bytes 9961472 | tf_op jit(solution)/shard_map/pallas_call | solution.py:802
  (23 shorter events, 0.1 us)
Async XLA Ops:
  0.6 0.8 copy-start.8
  10.1 8.8 %copy-start.12 = (s32[8192]{0:T(1024)S(1)}, s32[8192]{0:T(1024)}, u32[]{:S(2)}) copy-start(s32[8192]{0:T(1024)} %param.13) | copy-start | bytes 98308
  10.1 9.8 %copy-start.9 = (s32[12288]{0:T(1024)S(1)}, s32[12288]{0:T(1024)}, u32[]{:S(2)}) copy-start(s32[12288]{0:T(1024)} %param.12) | copy-start | bytes 147460
  10.1 61.0 %all-to-all-start = ((bf16[32,16,4096]{2,1,0:T(8,128)(2,1)}), bf16[32,16,4096]{2,1,0:T(8,128)(2,1)}, u32[]{:S(2)}, u32[]{:S(2)}) async-start(bf16[32,16,4096]{2,1,0:T(8,128)(2,1)} %bitcast.21), calls=%async_computation | async-start | bytes 8388608 | tf_op jit(solution)/shard_map/all_to_all | solution.py:822
  20.9 60.0 %copy-start.11 = (s32[1,512]{1,0:T(1,128)}, s32[1,512]{1,0:T(1,128)S(1)}, u32[]{:S(2)}) copy-start(s32[1,512]{1,0:T(1,128)S(1)} %sub.78.pos_row) | copy-start | bytes 6148
  27.4 53.5 %copy-start.10 = (f32[2048]{0:T(1024)S(1)}, f32[2048]{0:T(1024)}, u32[]{:S(2)}) copy-start(f32[2048]{0:T(1024)} %param.15) | copy-start | bytes 24580
  75.1 13.4 %collective-permute-start = (bf16[128,2048]{1,0:T(8,128)(2,1)}, bf16[128,2048]{1,0:T(8,128)(2,1)S(1)}, u32[]{:S(2)}, u32[]{:S(2)}) collective-permute-start(bf16[128,2048]{1,0:T(8,128)(2,1)} %shard_map.147), channel_id=1, source_target_pairs={{0,4},{4,8},{8,12},{12,16},{16,20},{20,24},{24,28},{28,32},{32,36}... | collective-permute-start | bytes 1572872 | tf_op jit(solution)/shard_map/ppermute | solution.py:829
  88.4 4.8 %copy-start.4 = (bf16[640,2048]{1,0:T(8,128)(2,1)}, bf16[640,2048]{1,0:T(8,128)(2,1)S(1)}, u32[]{:S(2)}) copy-start(bf16[640,2048]{1,0:T(8,128)(2,1)S(1)} %get-tuple-element.69.f_ref) | copy-start | bytes 7864324
  88.4 18.6 %copy-start = (f32[256,2048]{1,0:T(8,128)}, f32[256,2048]{1,0:T(8,128)S(1)}, u32[]{:S(2)}) copy-start(f32[256,2048]{1,0:T(8,128)S(1)} %get-tuple-element.71.mix_ref) | copy-start | bytes 6291460
  88.4 18.6 %copy-start.2 = (bf16[256,2048]{1,0:T(8,128)(2,1)}, bf16[256,2048]{1,0:T(8,128)(2,1)S(1)}, u32[]{:S(2)}) copy-start(bf16[256,2048]{1,0:T(8,128)(2,1)S(1)} %get-tuple-element.70.q_ref) | copy-start | bytes 3145732
  93.2 23.8 %copy-start.6 = (f32[128,2048]{1,0:T(8,128)}, f32[128,2048]{1,0:T(8,128)S(1)}, u32[]{:S(2)}) copy-start(f32[128,2048]{1,0:T(8,128)S(1)} %get-tuple-element.74.mix_head_ref) | copy-start | bytes 3145732
  93.2 4.6 %collective-permute-start.3 = (f32[8,256]{1,0:T(8,128)S(1)}, f32[8,256]{1,0:T(8,128)S(1)}, u32[]{:S(2)}, u32[]{:S(2)}) collective-permute-start(f32[8,256]{1,0:T(8,128)S(1)} %get-tuple-element.73.s0), channel_id=1, source_target_pairs={{0,3},{1,0},{2,1},{3,2},{4,7},{5,4},{6,5},{7,6},{8,11},{9,8},{10,9... | collective-permute-start | bytes 24584 | tf_op jit(solution)/shard_map/ppermute | solution.py:894
  97.0 4.0 %collective-permute-start.2 = (f32[8,256]{1,0:T(8,128)S(1)}, f32[8,256]{1,0:T(8,128)S(1)}, u32[]{:S(2)}, u32[]{:S(2)}) collective-permute-start(f32[8,256]{1,0:T(8,128)S(1)} %get-tuple-element.73.s0), channel_id=1, source_target_pairs={{0,2},{1,3},{2,0},{3,1},{4,6},{5,7},{6,4},{7,5},{8,10},{9,11},{10,... | collective-permute-start | bytes 24584 | tf_op jit(solution)/shard_map/ppermute | solution.py:894
  97.0 4.0 %collective-permute-start.1 = (f32[8,256]{1,0:T(8,128)S(1)}, f32[8,256]{1,0:T(8,128)S(1)}, u32[]{:S(2)}, u32[]{:S(2)}) collective-permute-start(f32[8,256]{1,0:T(8,128)S(1)} %get-tuple-element.73.s0), channel_id=1, source_target_pairs={{0,1},{1,2},{2,3},{3,0},{4,5},{5,6},{6,7},{7,4},{8,9},{9,10},{10,1... | collective-permute-start | bytes 24584 | tf_op jit(solution)/shard_map/ppermute | solution.py:894
  104.9 12.1 %collective-permute-start.4 = (bf16[128,2048]{1,0:T(8,128)(2,1)}, bf16[128,2048]{1,0:T(8,128)(2,1)S(1)}, u32[]{:S(2)}, u32[]{:S(2)}) collective-permute-start(bf16[128,2048]{1,0:T(8,128)(2,1)} %shard_map.152), channel_id=1, source_target_pairs={{4,0},{8,4},{12,8},{16,12},{20,16},{24,20},{28,24},{32,28},{36,32}... | collective-permute-start | bytes 1572872 | tf_op jit(solution)/shard_map/ppermute | solution.py:829
  117.0 41.2 %all-to-all-start.1 = ((bf16[32,16,2688]{2,1,0:T(8,128)(2,1)}), bf16[32,16,2688]{2,1,0:T(8,128)(2,1)S(1)}, u32[]{:S(2)}, u32[]{:S(2)}) async-start(bf16[32,16,2688]{2,1,0:T(8,128)(2,1)} %bitcast.22), calls=%async_computation.1 | async-start | bytes 5505024 | tf_op jit(solution)/shard_map/all_to_all | solution.py:822
  122.9 1.6 copy-start.1
  124.5 1.2 copy-start.3
  125.7 1.7 copy-start.5
  127.5 1.2 copy-start.7
  159.2 39.4 %all-to-all-start.2 = ((bf16[32,16,2560]{2,1,0:T(8,128)(2,1)}), bf16[32,16,2560]{2,1,0:T(8,128)(2,1)}, u32[]{:S(2)}, u32[]{:S(2)}) async-start(bf16[32,16,2560]{2,1,0:T(8,128)(2,1)} %bitcast.20), calls=%async_computation.2 | async-start | bytes 5242880 | tf_op jit(solution)/shard_map/all_to_all | solution.py:822

commit v4 on v3

--- a/solution.py
+++ b/solution.py
@@ -22,6 +22,8 @@
 WIN = TAPS + ROWS
 FREQ = 320
 CB = 512
+PACK, PRODUCT, TAIL, CONV, HEAD = 1024, 1024, 2048, 1024, 1024
+HEAD_GRAD, BACK, FINISH, GIVE, HOME, HOME_P = 1024, 1024, 1024, 1024, 1024, 1024
 
 
 def dot(a, b):
@@ -38,7 +40,7 @@
 
 def params(grid=True):
     return pltpu.CompilerParams(
-        dimension_semantics=("arbitrary",) if grid else None, vmem_limit_bytes=24 * 1024 * 1024
+        dimension_semantics=("arbitrary",) if grid else None, vmem_limit_bytes=36 * 1024 * 1024
     )
 
 
@@ -51,8 +53,8 @@
 RESIDENT = pl.BlockSpec(memory_space=pltpu.VMEM)
 
 
-def block_of(step):
-    return pl.ds(pl.multiple_of(step * CB, CB), CB)
+def block_of(step, width=CB):
+    return pl.ds(pl.multiple_of(step * width, width), width)
 
 
 def whole(shape):
@@ -168,21 +170,21 @@
 
 def pack_arrivals(pair, slots, early, late):
     width = early[0].shape[1]
-    blocks = width // CB
+    blocks = width // PACK
     halves = len(late)
     sent = SHARDS * pair
     return pl.pallas_call(
         functools.partial(pack_kernel, halves, blocks),
         grid=(2 * blocks,),
-        in_specs=[whole((8, SLOTS))]
-        + [cols(SLOTS, last=blocks - 1)] * len(early)
-        + [pl.BlockSpec((SLOTS, CB), lambda j: (0, jnp.maximum(j - blocks, 0)))] * halves,
-        out_specs=cols(sent),
+        in_specs=[RESIDENT]
+        + [cols(SLOTS, PACK, last=blocks - 1)] * len(early)
+        + [pl.BlockSpec((SLOTS, PACK), lambda j: (0, jnp.maximum(j - blocks, 0)))] * halves,
+        out_specs=cols(sent, PACK),
         out_shape=sds((sent, 2 * width), BF),
         scratch_shapes=[pltpu.VMEM((sent, SLOTS), BF)] * halves,
         compiler_params=params(),
         cost_estimate=cost(4 * sent * SLOTS * width * halves, 4 * width * (sent + SLOTS * 2)),
-    )(slots, *early, *late)
+    )(*kept(slots), *early, *late)
 
 
 def product_kernel(k_ref, v_ref, out_ref):
@@ -193,9 +195,9 @@
     width = k.shape[1]
     return pl.pallas_call(
         product_kernel,
-        grid=(width // CB,),
-        in_specs=[cols(SLOTS)] * 2,
-        out_specs=cols(SLOTS),
+        grid=(width // PRODUCT,),
+        in_specs=[cols(SLOTS, PRODUCT)] * 2,
+        out_specs=cols(SLOTS, PRODUCT),
         out_shape=sds((SLOTS, width), BF),
         compiler_params=params(),
         cost_estimate=cost(SLOTS * width, 6 * width * SLOTS),
@@ -214,14 +216,14 @@
     sent = received.shape[0]
     return pl.pallas_call(
         place_tail_kernel,
-        grid=(width // CB,),
-        in_specs=[whole((1, sent)), cols(sent)],
-        out_specs=cols(TAPS),
+        grid=(width // TAIL,),
+        in_specs=[RESIDENT, cols(sent, TAIL)],
+        out_specs=cols(TAPS, TAIL),
         out_shape=sds((TAPS, width), BF),
         scratch_shapes=[pltpu.VMEM((TAPS, sent), BF)],
         compiler_params=params(),
         cost_estimate=cost(2 * sent * TAPS * width, 2 * width * (sent + TAPS)),
-    )(pos_row, received)
+    )(*kept(pos_row), received)
 
 
 def segment_dft(docs_window):
@@ -322,7 +324,7 @@
         place[...] = onehot(iota(place.shape, 0) == pos_row[...])
         acc[...] = jnp.zeros_like(acc)
 
-    at = block_of(step)
+    at = block_of(step, CONV)
     product = dot(place[...], recv_p[...]).astype(BF)
     q = dot(place[...], recv_q[...])
     q_ref[:, at] = q.astype(BF)
@@ -344,21 +346,21 @@
 def forward(pos_row, cc_own, cc_own_t, bb, received, filt, residual, cot, gain):
     sent = received.shape[0]
     width = received.shape[1] // 2
-    blocks = width // CB
+    blocks = width // CONV
     return pl.pallas_call(
         conv_kernel,
         grid=(blocks,),
         in_specs=[
-            whole((1, sent)),
-            whole((2 * FREQ, ROWS)),
-            whole((ROWS, 2 * FREQ)),
-            whole((2 * FREQ, TAPS)),
-            cols(sent),
-            pl.BlockSpec((sent, CB), lambda j: (0, blocks + j)),
-            cols(TAPS),
-            cols(ROWS),
-            cols(ROWS),
-            cols(1),
+            RESIDENT,
+            RESIDENT,
+            RESIDENT,
+            RESIDENT,
+            cols(sent, CONV),
+            pl.BlockSpec((sent, CONV), lambda j: (0, blocks + j)),
+            cols(TAPS, CONV),
+            cols(ROWS, CONV),
+            cols(ROWS, CONV),
+            cols(1, CONV),
         ],
         out_specs=[RESIDENT] * 4 + [whole((8, TAPS))],
         out_shape=[
@@ -371,7 +373,7 @@
         scratch_shapes=[pltpu.VMEM((ROWS, sent), BF), pltpu.VMEM((TAPS, 128), F32)],
         compiler_params=params(),
         cost_estimate=cost(4e9, width * 6000),
-    )(pos_row, *hbm(cc_own, cc_own_t, bb), received, received, *hbm(filt, residual, cot), gain)
+    )(*kept(pos_row, cc_own, cc_own_t, bb), received, received, *hbm(filt, residual, cot), gain)
 
 
 def crossing(value):
@@ -389,7 +391,7 @@
     def _():
         acc[...] = jnp.zeros_like(acc)
 
-    at = block_of(step)
+    at = block_of(step, HEAD)
     x = dot(cc_halo[...], halo[...])
     fr, fi = crossing(f_ref[:, at].astype(F32))
     y = spectra_product(x[:CROSS_FREQ], x[CROSS_FREQ:], fr, fi)
@@ -408,25 +410,25 @@
     width = q.shape[1]
     return pl.pallas_call(
         head_kernel,
-        grid=(width // CB,),
+        grid=(width // HEAD,),
         in_specs=[
-            whole((2 * CROSS_FREQ, TAPS)),
-            whole((TAPS, 2 * CROSS_FREQ)),
-            cols(TAPS),
-            RESIDENT,
-            RESIDENT,
-            RESIDENT,
-            cols(TAPS),
-            cols(TAPS),
-            cols(1),
-            whole((8, TAPS)),
+            RESIDENT,
+            RESIDENT,
+            cols(TAPS, HEAD),
+            RESIDENT,
+            RESIDENT,
+            RESIDENT,
+            cols(TAPS, HEAD),
+            cols(TAPS, HEAD),
+            cols(1, HEAD),
+            RESIDENT,
         ],
         out_specs=[RESIDENT, whole((8, ROWS))],
         out_shape=[pltpu.VMEM((TAPS, width), F32), jax.ShapeDtypeStruct((8, ROWS), F32)],
         scratch_shapes=[pltpu.VMEM((TAPS, 128), F32)],
         compiler_params=params(),
         cost_estimate=cost(6e8, width * 3000),
-    )(*hbm(cc_halo, cc_head_t), halo, *kept(f, q, mix), *hbm(residual, cot), gain, sums)
+    )(*kept(cc_halo, cc_head_t), halo, *kept(f, q, mix), *hbm(residual, cot), gain, *kept(sums))
 
 
 def prepare_kernel(
@@ -460,7 +462,7 @@
         (2 * CROSS_FREQ, TAPS),
     ]
     return pl.pallas_call(
-        prepare_kernel, out_shape=[sds(shape, BF) for shape in shapes], compiler_params=params(False)
+        prepare_kernel, out_shape=[pltpu.VMEM(shape, BF) for shape in shapes], compiler_params=params(False)
     )(cc, bb, head, tail, taps)
 
 
@@ -494,7 +496,7 @@
     def _():
         row_stats(s0, s1, s2, s3, stats)
 
-    at = block_of(step)
+    at = block_of(step, HEAD_GRAD)
     q = q_ref[:TAPS, at].astype(F32)
     summed = res_ref[...].astype(F32) + q * mix_head_ref[:, at]
     d_summed = d_summed_of(stats[:TAPS], summed, cot_ref[...].astype(F32) * gain_ref[...])
@@ -505,15 +507,15 @@
     width = q.shape[1]
     return pl.pallas_call(
         head_grad_kernel,
-        grid=(width // CB,),
-        in_specs=[whole((8, ROWS))] * 4
-        + [RESIDENT, RESIDENT, cols(TAPS), cols(TAPS), cols(1)],
-        out_specs=cols(TAPS),
+        grid=(width // HEAD_GRAD,),
+        in_specs=[RESIDENT] * 4
+        + [RESIDENT, RESIDENT, cols(TAPS, HEAD_GRAD), cols(TAPS, HEAD_GRAD), cols(1, HEAD_GRAD)],
+        out_specs=cols(TAPS, HEAD_GRAD),
         out_shape=sds((TAPS, width), BF),
         scratch_shapes=[pltpu.VMEM((ROWS, 128), F32)],
         compiler_params=params(),
         cost_estimate=cost(width * TAPS * 10, width * TAPS * 6),
-    )(*sums, *kept(q, mix_head), *hbm(residual, cot), gain)
+    )(*kept(*sums, q, mix_head), *hbm(residual, cot), gain)
 
 
 def mixture_block(mix_ref, mix_head_ref, at):
@@ -529,7 +531,7 @@
 ):
     step = pl.program_id(0)
     per = pair // 4
-    parts = blocks // per
+    parts = taps_acc.shape[0]
     sent = SHARDS * pair
 
     @pl.when(step == 0)
@@ -541,7 +543,7 @@
 
     @pl.when(step < blocks)
     def _():
-        at = block_of(jnp.minimum(step, blocks - 1))
+        at = block_of(jnp.minimum(step, blocks - 1), BACK)
         q = q_ref[:, at].astype(F32)
         mix = mixture_block(mix_ref, mix_head_ref, at)
         summed = res_ref[...].astype(F32) + q * mix
@@ -559,50 +561,57 @@
             [x[FREQ : FREQ + CROSS_FREQ] + reach[CROSS_FREQ:], x[FREQ + CROSS_FREQ :]], axis=0
         )
         taps = dot(bb_t[...], conj_product(g[:FREQ], g[FREQ:], xr, xi)).astype(BF)
-        spread = onehot(iota((sent, TAPS), 0) == tap_rows(pair, (sent, TAPS), 1, step))
-        part = jnp.minimum(step // per, parts - 1)
-        taps_acc[part] += dot(spread, taps)
+        for i in range(BACK // CB):
+            block = jnp.minimum(step, blocks - 1) * (BACK // CB) + i
+            spread = onehot(iota((sent, TAPS), 0) == tap_rows(pair, (sent, TAPS), 1, block))
+            taps_acc[block // per] += dot(spread, taps[:, CB * i : CB * (i + 1)])
         wide = gain_acc.shape[1]
-        for i in range(CB // wide):
-            row = iota(gain_acc.shape, 0) == step * (CB // wide) + i
+        for i in range(BACK // wide):
+            row = iota(gain_acc.shape, 0) == step * (BACK // wide) + i
             gain_acc[...] += jnp.where(row, gain_part[:, wide * i : wide * (i + 1)], 0.0)
 
-    @pl.when((step >= blocks) & (step < blocks + parts))
-    def _():
-        out_ref[...] = taps_acc[jnp.clip(step - blocks, 0, parts - 1)].astype(BF)
-
-    @pl.when(step == blocks + parts)
-    def _():
+    def extra(at):
+        if at < CB * parts:
+            return taps_acc[at // CB]
         wide = gain_acc.shape[1]
-        rows = jnp.broadcast_to(gain_acc[...][None], (SHARDS, pair, wide)).reshape(sent, wide)
-        out_ref[:, :wide] = rows.astype(BF)
+        return jnp.broadcast_to(gain_acc[...][None], (SHARDS, pair, wide)).reshape(sent, wide)
+
+    starts = [CB * part for part in range(parts + 1)]
+    for late in range(pl.cdiv(starts[-1] + 1, BACK)):
+
+        @pl.when(step == blocks + late)
+        def _(late=late):
+            for at in starts:
+                if at // BACK == late:
+                    value = extra(at).astype(BF)
+                    out_ref[:, at % BACK : at % BACK + value.shape[1]] = value
 
 
 def backward(pair, sums, pos_row, cc_own, cc_halo, bb_t, q, mix, mix_head, x, halo, residual, cot, gain):
     width = q.shape[1]
-    blocks = width // CB
+    blocks = width // BACK
     last = blocks - 1
     sent = SHARDS * pair
     part_cols, gain_cols = extra_cols(pair, width)
     parts = part_cols // CB
     return pl.pallas_call(
         functools.partial(backward_kernel, pair, blocks),
-        grid=(blocks + parts + 1,),
-        in_specs=[whole((8, ROWS))] * 4
+        grid=(blocks + pl.cdiv(part_cols + gain_cols, BACK),),
+        in_specs=[RESIDENT] * 4
         + [
-            whole((1, sent)),
-            whole((2 * FREQ, ROWS)),
-            whole((2 * CROSS_FREQ, TAPS)),
-            whole((TAPS, 2 * FREQ)),
+            RESIDENT,
+            RESIDENT,
+            RESIDENT,
+            RESIDENT,
         ]
         + [RESIDENT] * 4
         + [
-            cols(TAPS, last=last),
-            cols(ROWS, last=last),
-            cols(ROWS, last=last),
-            cols(1, last=last),
+            cols(TAPS, BACK, last=last),
+            cols(ROWS, BACK, last=last),
+            cols(ROWS, BACK, last=last),
+            cols(1, BACK, last=last),
         ],
-        out_specs=[cols(ROWS, last=last), cols(sent)],
+        out_specs=[cols(ROWS, BACK, last=last), cols(sent, BACK)],
         out_shape=[
             sds((ROWS, width), BF),
             sds((sent, width + part_cols + gain_cols), BF),
@@ -616,7 +625,7 @@
         compiler_params=params(),
         cost_estimate=cost(2e9, width * 6000),
     )(
-        *sums, *hbm(pos_row, cc_own, cc_halo, bb_t), *kept(q, mix, mix_head, x), halo,
+        *kept(*sums, pos_row, cc_own, cc_halo, bb_t, q, mix, mix_head, x), halo,
         *hbm(residual, cot), gain,
     )
 
@@ -633,7 +642,7 @@
     def _():
         row_stats(s0, s1, s2, s3, stats)
 
-    at = block_of(step)
+    at = block_of(step, FINISH)
     gain = gain_ref[...]
     mix = mixture_block(mix_ref, mix_head_ref, at)
     summed = res_ref[...].astype(F32) + q_ref[:, at].astype(F32) * mix
@@ -648,18 +657,18 @@
     width = q.shape[1]
     return pl.pallas_call(
         finish_kernel,
-        grid=(width // CB,),
-        in_specs=[whole((8, ROWS))] * 4
-        + [whole((2 * FREQ, ROWS)), whole((ROWS, 2 * FREQ))]
+        grid=(width // FINISH,),
+        in_specs=[RESIDENT] * 4
+        + [RESIDENT, RESIDENT]
         + [RESIDENT] * 4
-        + [cols(ROWS), cols(ROWS), cols(1), cols(ROWS)],
-        out_specs=[cols(ROWS)] * 3,
+        + [cols(ROWS, FINISH), cols(ROWS, FINISH), cols(1, FINISH), cols(ROWS, FINISH)],
+        out_specs=[cols(ROWS, FINISH)] * 3,
         out_shape=[sds((ROWS, width), BF), sds((ROWS, width), BF), sds((ROWS, width), F32)],
         scratch_shapes=[pltpu.VMEM((ROWS, 128), F32)],
         compiler_params=params(),
         cost_estimate=cost(2 * 2 * 2 * FREQ * ROWS * width, width * 6000),
     )(
-        *sums, *hbm(cc_own, cc_own_t), *kept(q, mix, mix_head, f), *hbm(residual, cot), gain,
+        *kept(*sums, cc_own, cc_own_t, q, mix, mix_head, f), *hbm(residual, cot), gain,
         *hbm(d_mix),
     )
 
@@ -685,22 +694,22 @@
     sent = SHARDS * pair
     return pl.pallas_call(
         give_back_kernel,
-        grid=(width // CB,),
+        grid=(width // GIVE,),
         in_specs=[
-            whole((1, sent)),
-            whole((2 * CROSS_FREQ, TAPS)),
-            whole((TAPS, 2 * CROSS_FREQ)),
-            whole((2 * CROSS_FREQ, TAPS)),
-            cols(ROWS),
-            cols(TAPS),
-            cols(TAPS),
+            RESIDENT,
+            RESIDENT,
+            RESIDENT,
+            RESIDENT,
+            cols(ROWS, GIVE),
+            cols(TAPS, GIVE),
+            cols(TAPS, GIVE),
         ],
-        out_specs=cols(sent),
+        out_specs=cols(sent, GIVE),
         out_shape=sds((sent, width + extra_cols(pair, width)[0]), BF),
         scratch_shapes=[pltpu.VMEM((sent, ROWS), BF)],
         compiler_params=params(),
         cost_estimate=cost(2 * sent * ROWS * width, width * 2400),
-    )(*hbm(pos_row, *onward, own), from_next, *hbm(filt))
+    )(*kept(pos_row, *onward), *hbm(own), from_next, *hbm(filt))
 
 
 def reduce_kernel(pair, taps_ref, gain_ref, rows_ref, out_ref, d_gain_ref):
@@ -766,16 +775,16 @@
     halves = len(backs)
     return pl.pallas_call(
         functools.partial(home_rows_kernel, pair, halves),
-        grid=(width // CB,),
-        in_specs=[whole((8, SLOTS))] + [cols(sent)] * halves,
-        out_specs=cols(SLOTS),
+        grid=(width // HOME,),
+        in_specs=[RESIDENT] + [cols(sent, HOME)] * halves,
+        out_specs=cols(SLOTS, HOME),
         out_shape=sds((SLOTS, width), BF),
         scratch_shapes=[pltpu.VMEM((SLOTS, sent), BF)] * halves,
         compiler_params=params(),
         cost_estimate=cost(
             2 * sent * SLOTS * width * halves, 2 * width * (sent * halves + SLOTS)
         ),
-    )(slots, *backs)
+    )(*kept(slots), *backs)
 
 
 def home_product_kernel(pair, halves, slots_ref, taps_ref, k_ref, v_ref, *refs):
@@ -790,31 +799,34 @@
     dk_ref[...] = (grad * v_ref[...].astype(F32)).astype(BF)
     dv_ref[...] = (grad * k_ref[...].astype(F32)).astype(BF)
     shape = (TAPS, SHARDS * pair)
-    filt_ref[...] = dot(onehot(iota(shape, 1) == tap_rows(pair, shape, 0, step)), taps_ref[...])
+    for i in range(HOME_P // CB):
+        block = step * (HOME_P // CB) + i
+        gather = onehot(iota(shape, 1) == tap_rows(pair, shape, 0, block))
+        part = taps_ref[:, block_of(block // (pair // 4))]
+        filt_ref[:, CB * i : CB * (i + 1)] = dot(gather, part)
 
 
 def home_product(pair, slots, back, backs, k, v):
     width = k.shape[1]
-    blocks = width // CB
+    part_cols = extra_cols(pair, width)[0]
     sent = SHARDS * pair
     halves = len(backs)
-    per = pair // 4
     return pl.pallas_call(
         functools.partial(home_product_kernel, pair, halves),
-        grid=(blocks,),
+        grid=(width // HOME_P,),
         in_specs=[
-            whole((8, SLOTS)),
-            pl.BlockSpec((sent, CB), lambda j: (0, blocks + j // per)),
-            cols(SLOTS),
-            cols(SLOTS),
+            RESIDENT,
+            pl.BlockSpec((sent, part_cols), lambda j: (0, width // part_cols)),
+            cols(SLOTS, HOME_P),
+            cols(SLOTS, HOME_P),
         ]
-        + [cols(sent)] * halves,
-        out_specs=[cols(SLOTS), cols(SLOTS), cols(TAPS)],
+        + [cols(sent, HOME_P)] * halves,
+        out_specs=[cols(SLOTS, HOME_P), cols(SLOTS, HOME_P), cols(TAPS, HOME_P)],
         out_shape=[sds((SLOTS, width), BF), sds((SLOTS, width), BF), sds((TAPS, width), F32)],
         scratch_shapes=[pltpu.VMEM((SLOTS, sent), BF)] * halves,
         compiler_params=params(),
         cost_estimate=cost(2 * sent * SLOTS * width, 2 * width * (sent + 5 * SLOTS)),
-    )(slots, back, *hbm(k, v), *backs)
+    )(*kept(slots), back, *hbm(k, v), *backs)
 
 
 def exchange(pair, rows):

time: 206 us -> 198 us (0.961)
  Pallas kernels: 63.1 us -> 49.7 us
  waiting for transfers between devices: 94.4 us -> 98.4 us
  local copies, waits for them, and re-layouts: 7.29 us -> 10.1 us
    pallas_call x7, Pallas kernels: 34.4 us -> 26.4 us  [the longest x1 6.47 us: forward(): pl.pallas_call(conv_kernel, grid=(blocks,), in_specs=[RESIDENT, RESIDENT,...]
    unnamed x26 -> x40, local copies, waits for them, and re-layouts: 6.6 us -> 9.37 us
    ppermute x2, waiting for transfers between devices: 0.01 us -> 2.36 us  [shift(): return lax.ppermute(value, 'seq', pairs)]
  transfers between devices with their start and end apart: 8 -> 8, of which waited for: 5 -> 6; matrix products, arithmetic and copies ran while one was open for 3% -> 4% of each run, Pallas kernels for 17% -> 14%
where the time goes in v4:
time: 198 us; the launch traced here: 197 us
  waiting for transfers between devices  98.4 us (50%)
  Pallas kernels  49.7 us (25%)
  starting transfers between devices  31.5 us (16%)
  local copies, waits for them, and re-layouts  10.1 us (5%)
  other arithmetic  6.17 us (3%)
    all_to_all x3, waiting for transfers between devices, exchange(): lax.all_to_all(shards, 'seq', split_axis=0, concat_axis=0, tiled=True)  92.7 us
    all_to_all x3, starting transfers between devices, exchange(): lax.all_to_all(shards, 'seq', split_axis=0, concat_axis=0, tiled=True)  19.2 us
    unnamed x40, local copies, waits for them, and re-layouts  9.37 us
    pallas_call x1, Pallas kernels, backward(): pl.pallas_call(functools.partial(backward_kernel, pair, blocks), grid=(bl...  7.94 us
    ppermute x2, starting transfers between devices, shift(): return lax.ppermute(value, 'seq', pairs)  7.76 us
    pallas_call x1, Pallas kernels, pack_arrivals(): pl.pallas_call(functools.partial(pack_kernel, halves, blocks), grid=(2 *...  6.57 us
    pallas_call x1, Pallas kernels, forward(): pl.pallas_call(conv_kernel, grid=(blocks,), in_specs=[RESIDENT, RESIDENT,...  6.47 us
    pallas_call x1, Pallas kernels, finish(): pl.pallas_call(finish_kernel, grid=(width // FINISH,), in_specs=[RESIDENT...  6.07 us
  transfers between devices with their start and end apart: 8, of which 6 were waited for; matrix products, arithmetic and copies ran while one was open for 4% of the time, Pallas kernels for 14%

profile of v4, /device:TPU:1, one launch (start us, length us, event | category | flops | bytes accessed | tf_op | source)
XLA Modules:
  0.0 197.0 jit_solution(7577486676639958646)
XLA Ops:
  0.6 0.0 copy-start.10
  0.6 0.8 copy-done.10
  1.4 0.2 shard_map.144.slots_ref
  1.7 6.6 %shard_map.145 = bf16[512,4096]{1,0:T(8,128)(2,1)} custom-call(s32[8,384]{1,0:T(8,128)S(1)} %shard_map.144.slots_ref, bf16[384,2048]{1,0:T(8,128)(2,1)} %k_ref.1, bf16[384,2048]{1,0:T(8,128)(2,1)} %v_ref.1, bf16[384,2048]{1,0:T(8,128)(2,1)} %refs_2_.1), custom_call_target="tpu_custom_call" | custom-call | flops 1610612736 | bytes 10485760 | tf_op jit(solution)/shard_map/pallas_call | solution.py:176
  8.3 8.8 %all-to-all-start = ((bf16[32,16,4096]{2,1,0:T(8,128)(2,1)}), bf16[32,16,4096]{2,1,0:T(8,128)(2,1)}, u32[]{:S(2)}, u32[]{:S(2)}) async-start(bf16[32,16,4096]{2,1,0:T(8,128)(2,1)} %bitcast.21), calls=%async_computation | async-start | bytes 8388608 | tf_op jit(solution)/shard_map/all_to_all | solution.py:834
  17.1 0.0 copy-done.19
  17.1 0.1 fusion.32
  17.2 0.6 slice.17
  17.8 0.2 select_reduce_fusion.4
  18.0 0.1 select_reduce_fusion.8
  18.1 0.0 copy-done.11
  18.1 0.2 fusion
  18.3 0.6 select_reduce_fusion
  19.0 0.1 sub.78.pos_row
  19.1 0.1 maximum_reduce_fusion
  19.2 0.4 fusion.11
  19.5 0.4 sine_negate_fusion
  19.9 0.2 select_reduce_fusion.1
  20.1 0.7 select_multiply_fusion
  20.9 2.1 %compare_select_fusion.1 = (f32[320,384]{1,0:T(8,128)S(1)}, f32[320,384]{1,0:T(8,128)S(1)}) fusion(f32[320]{0:T(512)S(1)} %broadcast_multiply_fusion, f32[320]{0:T(512)S(1)} %get-tuple-element.104, f32[320]{0:T(512)S(1)} %get-tuple-element.103, s32[320]{0:T(512)S(1)} %get-tuple-element.99, s32[320]{0:T(512)S(1)} %get-tuple-element.119, ...), kind=kLoop, calls=%fused_computation.6 | loop fusion | flops 1474560 | bytes 992256 | tf_op jit(solution)/shard_map/jit(_where)/select_n | solution.py:263
  23.0 0.1 pad_maximum_fusion.cc_ref
  23.1 0.7 slice_compare_fusion
  23.7 0.4 fusion.14
  24.1 0.1 fusion.3
  24.3 0.3 shard_map.146
  24.6 0.0 copy-start.13
  24.6 0.6 copy-done.13
  25.2 0.6 copy-done.15
  25.8 43.4 %all-to-all-done = bf16[32,16,4096]{2,1,0:T(8,128)(2,1)} async-done(((bf16[32,16,4096]{2,1,0:T(8,128)(2,1)}), bf16[32,16,4096]{2,1,0:T(8,128)(2,1)}, u32[]{:S(2)}, u32[]{:S(2)}) %all-to-all-start) | async-done | bytes 4194336 | tf_op jit(solution)/shard_map/all_to_all | solution.py:834
  69.3 2.8 %shard_map.147 = bf16[128,2048]{1,0:T(8,128)(2,1)} custom-call(s32[1,512]{1,0:T(1,128)S(1)} %sub.78.pos_row, bf16[512,4096]{1,0:T(8,128)(2,1)} %bitcast.3.recv_ref.recv_p.recv_q), custom_call_target="tpu_custom_call" | custom-call | flops 268435456 | bytes 2621440 | tf_op jit(solution)/shard_map/pallas_call | solution.py:217
  72.1 5.8 %collective-permute-start = (bf16[128,2048]{1,0:T(8,128)(2,1)}, bf16[128,2048]{1,0:T(8,128)(2,1)S(1)}, u32[]{:S(2)}, u32[]{:S(2)}) collective-permute-start(bf16[128,2048]{1,0:T(8,128)(2,1)} %shard_map.147), channel_id=1, source_target_pairs={{0,4},{4,8},{8,12},{12,16},{16,20},{20,24},{24,28},{28,32},{32,36}... | collective-permute-start | bytes 1572872 | tf_op jit(solution)/shard_map/ppermute | solution.py:841
  77.9 0.0 copy-done.12
  78.0 6.5 %shard_map.148 = (bf16[256,2048]{1,0:T(8,128)(2,1)S(1)}, f32[256,2048]{1,0:T(8,128)S(1)}, bf16[640,2048]{1,0:T(8,128)(2,1)S(1)}, bf16[640,2048]{1,0:T(8,128)(2,1)S(1)}, f32[8,128]{1,0:T(8,128)S(1)}) custom-call(s32[1,512]{1,0:T(1,128)S(1)} %sub.78.pos_row, bf16[640,256]{1,0:T(8,128)(2,1)S(1)} %get-tuple-element.66.cc_own, ...), custom_call_target="tpu_custom_call" | custom-call | flops 4000000000 | bytes 12288000 | tf_op jit(solution)/shard_map/pallas_call | solution.py:350
  84.5 0.0 copy-start.2
  84.5 0.0 collective-permute-done.halo.halo_ref
  84.5 3.3 %shard_map.149 = (f32[128,2048]{1,0:T(8,128)S(1)}, f32[8,256]{1,0:T(8,128)S(1)}) custom-call(bf16[384,128]{1,0:T(8,128)(2,1)S(1)} %get-tuple-element.62.cc_halo, bf16[128,384]{1,0:T(8,128)(2,1)S(1)} %get-tuple-element.63.cc_head_t, bf16[128,2048]{1,0:T(8,128)(2,1)S(1)} %collective-permute-done.halo.halo_ref, bf16[640,2048]{1,0:T(8,128)(2,1)S(1)} %get-tuple-element.69.f_ref, ...), custom_call_target="tpu_custom_call" | custom-call | flops 600000000 | bytes 6144000 | tf_op jit(solution)/shard_map/pallas_call | solution.py:411
  87.8 0.0 copy-start.6
  87.8 3.8 %collective-permute-start.3 = (f32[8,256]{1,0:T(8,128)S(1)}, f32[8,256]{1,0:T(8,128)S(1)}, u32[]{:S(2)}, u32[]{:S(2)}) collective-permute-start(f32[8,256]{1,0:T(8,128)S(1)} %get-tuple-element.73.s0), channel_id=1, source_target_pairs={{0,3},{1,0},{2,1},{3,2},{4,7},{5,4},{6,5},{7,6},{8,11},{9,8},{10,9... | collective-permute-start | bytes 24584 | tf_op jit(solution)/shard_map/ppermute | solution.py:906
  91.6 0.0 collective-permute-start.2
  91.7 0.7 collective-permute-start.1
  92.3 0.1 collective-permute-done.3.s3
  92.4 3.2 %collective-permute-done.2.s2 = f32[8,256]{1,0:T(8,128)S(1)} collective-permute-done((f32[8,256]{1,0:T(8,128)S(1)}, f32[8,256]{1,0:T(8,128)S(1)}, u32[]{:S(2)}, u32[]{:S(2)}) %collective-permute-start.2) | collective-permute-done | bytes 8224 | tf_op jit(solution)/shard_map/ppermute | solution.py:906
  95.7 0.0 collective-permute-done.1.s1
  95.7 2.6 %shard_map.152 = bf16[128,2048]{1,0:T(8,128)(2,1)} custom-call(f32[8,256]{1,0:T(8,128)S(1)} %get-tuple-element.73.s0, f32[8,256]{1,0:T(8,128)S(1)} %collective-permute-done.1.s1, f32[8,256]{1,0:T(8,128)S(1)} %collective-permute-done.2.s2, f32[8,256]{1,0:T(8,128)S(1)} %collective-permute-done.3.s3, bf16[256,2048]{1,0:T(8,128)(2,1)S(1)} %get-tuple-element.70.q_ref, ...), custom_call_target="tpu_custom_call" | custom-call | flops 2621440 | bytes 1572864 | tf_op jit(solution)/shard_map/pallas_call | solution.py:508
  98.2 1.9 collective-permute-start.4
  100.1 0.0 copy-done
  100.1 0.0 copy-done.2
  100.2 7.9 %shard_map.150 = (bf16[256,2048]{1,0:T(8,128)(2,1)}, bf16[512,2688]{1,0:T(8,128)(2,1)}) custom-call(f32[8,256]{1,0:T(8,128)S(1)} %get-tuple-element.73.s0, f32[8,256]{1,0:T(8,128)S(1)} %collective-permute-done.1.s1, f32[8,256]{1,0:T(8,128)S(1)} %collective-permute-done.2.s2, f32[8,256]{1,0:T(8,128)S(1)} %collective-permute-done.3.s3, ...), custom_call_target="tpu_custom_call" | custom-call | flops 2000000000 | bytes 12288000 | tf_op jit(solution)/shard_map/pallas_call | solution.py:597
  108.1 2.4 %collective-permute-done.4.next_ref = bf16[128,2048]{1,0:T(8,128)(2,1)S(1)} collective-permute-done((bf16[128,2048]{1,0:T(8,128)(2,1)}, bf16[128,2048]{1,0:T(8,128)(2,1)S(1)}, u32[]{:S(2)}, u32[]{:S(2)}) %collective-permute-start.4) | collective-permute-done | bytes 524320 | tf_op jit(solution)/shard_map/ppermute | solution.py:841
  110.5 0.8 copy-done.8
  111.3 5.1 %all-to-all-start.1 = ((bf16[32,16,2688]{2,1,0:T(8,128)(2,1)}), bf16[32,16,2688]{2,1,0:T(8,128)(2,1)S(1)}, u32[]{:S(2)}, u32[]{:S(2)}) async-start(bf16[32,16,2688]{2,1,0:T(8,128)(2,1)} %bitcast.22), calls=%async_computation.1 | async-start | bytes 5505024 | tf_op jit(solution)/shard_map/all_to_all | solution.py:834
  116.4 1.6 copy-done.1
  117.9 1.2 copy-done.3
  119.2 1.7 copy-done.5
  120.9 1.2 copy-done.7
  122.1 0.7 copy-done.18
  122.8 6.1 %shard_map.151 = (bf16[256,2048]{1,0:T(8,128)(2,1)}, bf16[256,2048]{1,0:T(8,128)(2,1)}, f32[256,2048]{1,0:T(8,128)}) custom-call(f32[8,256]{1,0:T(8,128)S(1)} %get-tuple-element.73.s0, f32[8,256]{1,0:T(8,128)S(1)} %copy-done.18, f32[8,256]{1,0:T(8,128)S(1)} %collective-permute-done.2.s2, f32[8,256]{1,0:T(8,128)S(1)} %collective-permute-done.3.s3, ...), custom_call_target="tpu_custom_call" | custom-call | flops 1342177280 | bytes 12288000 | tf_op jit(solution)/shard_map/pallas_call | solution.py:658
  128.9 4.9 %shard_map.154.rows_ref = bf16[512,2560]{1,0:T(8,128)(2,1)} custom-call(s32[1,512]{1,0:T(1,128)S(1)} %sub.78.pos_row, bf16[384,128]{1,0:T(8,128)(2,1)S(1)} %get-tuple-element.83.head, bf16[128,384]{1,0:T(8,128)(2,1)S(1)} %copy-done.14, bf16[384,128]{1,0:T(8,128)(2,1)S(1)} %copy-done.16, f32[256,2048]{1,0:T(8,128)} %get-tuple-element.86.own_ref, ...), custom_call_target="tpu_custom_call" | custom-call | flops 536870912 | bytes 4915200 | tf_op jit(solution)/shard_map/pallas_call | solution.py:695
  133.8 17.8 %all-to-all-done.1 = bf16[32,16,2688]{2,1,0:T(8,128)(2,1)S(1)} async-done(((bf16[32,16,2688]{2,1,0:T(8,128)(2,1)}), bf16[32,16,2688]{2,1,0:T(8,128)(2,1)S(1)}, u32[]{:S(2)}, u32[]{:S(2)}) %all-to-all-start.1) | async-done | bytes 2752544 | tf_op jit(solution)/shard_map/all_to_all | solution.py:834
  151.6 1.0 shard_map.155
  152.7 5.4 %all-to-all-start.2 = ((bf16[32,16,2560]{2,1,0:T(8,128)(2,1)}), bf16[32,16,2560]{2,1,0:T(8,128)(2,1)}, u32[]{:S(2)}, u32[]{:S(2)}) async-start(bf16[32,16,2560]{2,1,0:T(8,128)(2,1)} %bitcast.20), calls=%async_computation.2 | async-start | bytes 5242880 | tf_op jit(solution)/shard_map/all_to_all | solution.py:834
  158.0 2.6 %shard_map.153 = bf16[384,2048]{1,0:T(8,128)(2,1)} custom-call(s32[8,384]{1,0:T(8,128)S(1)} %shard_map.144.slots_ref, bf16[512,2688]{1,0:T(8,128)(2,1)S(1)} %bitcast.13), custom_call_target="tpu_custom_call" | custom-call | flops 805306368 | bytes 3670016 | tf_op jit(solution)/shard_map/pallas_call | solution.py:776
  160.6 31.4 %all-to-all-done.2 = bf16[32,16,2560]{2,1,0:T(8,128)(2,1)} async-done(((bf16[32,16,2560]{2,1,0:T(8,128)(2,1)}), bf16[32,16,2560]{2,1,0:T(8,128)(2,1)}, u32[]{:S(2)}, u32[]{:S(2)}) %all-to-all-start.2) | async-done | bytes 2621472 | tf_op jit(solution)/shard_map/all_to_all | solution.py:834
  192.1 4.9 %shard_map.156 = (bf16[384,2048]{1,0:T(8,128)(2,1)}, bf16[384,2048]{1,0:T(8,128)(2,1)}, f32[128,2048]{1,0:T(8,128)}) custom-call(s32[8,384]{1,0:T(8,128)S(1)} %shard_map.144.slots_ref, bf16[512,2560]{1,0:T(8,128)(2,1)} %bitcast.9.taps_ref.refs_0_, bf16[384,2048]{1,0:T(8,128)(2,1)} %k_ref.1, bf16[384,2048]{1,0:T(8,128)(2,1)} %v_ref.1, ...), custom_call_target="tpu_custom_call" | custom-call | flops 805306368 | bytes 9961472 | tf_op jit(solution)/shard_map/pallas_call | solution.py:814
  (37 shorter events, 0.2 us)
Async XLA Ops:
  0.6 0.8 copy-start.10
  8.3 8.8 %copy-start.19 = (s32[8192]{0:T(1024)S(1)}, s32[8192]{0:T(1024)}, u32[]{:S(2)}) copy-start(s32[8192]{0:T(1024)} %param.13) | copy-start | bytes 98308
  8.3 9.8 %copy-start.11 = (s32[12288]{0:T(1024)S(1)}, s32[12288]{0:T(1024)}, u32[]{:S(2)}) copy-start(s32[12288]{0:T(1024)} %param.12) | copy-start | bytes 147460
  8.3 61.0 %all-to-all-start = ((bf16[32,16,4096]{2,1,0:T(8,128)(2,1)}), bf16[32,16,4096]{2,1,0:T(8,128)(2,1)}, u32[]{:S(2)}, u32[]{:S(2)}) async-start(bf16[32,16,4096]{2,1,0:T(8,128)(2,1)} %bitcast.21), calls=%async_computation | async-start | bytes 8388608 | tf_op jit(solution)/shard_map/all_to_all | solution.py:834
  24.6 0.6 copy-start.13
  25.2 0.6 copy-start.15
  25.8 52.1 %copy-start.12 = (f32[2048]{0:T(1024)S(1)}, f32[2048]{0:T(1024)}, u32[]{:S(2)}) copy-start(f32[2048]{0:T(1024)} %param.15) | copy-start | bytes 24580
  72.1 12.4 %collective-permute-start = (bf16[128,2048]{1,0:T(8,128)(2,1)}, bf16[128,2048]{1,0:T(8,128)(2,1)S(1)}, u32[]{:S(2)}, u32[]{:S(2)}) collective-permute-start(bf16[128,2048]{1,0:T(8,128)(2,1)} %shard_map.147), channel_id=1, source_target_pairs={{0,4},{4,8},{8,12},{12,16},{16,20},{20,24},{24,28},{28,32},{32,36}... | collective-permute-start | bytes 1572872 | tf_op jit(solution)/shard_map/ppermute | solution.py:841
  84.4 3.3 %copy-start.4 = (bf16[640,2048]{1,0:T(8,128)(2,1)}, bf16[640,2048]{1,0:T(8,128)(2,1)S(1)}, u32[]{:S(2)}) copy-start(bf16[640,2048]{1,0:T(8,128)(2,1)S(1)} %get-tuple-element.69.f_ref) | copy-start | bytes 7864324
  84.4 15.7 %copy-start = (f32[256,2048]{1,0:T(8,128)}, f32[256,2048]{1,0:T(8,128)S(1)}, u32[]{:S(2)}) copy-start(f32[256,2048]{1,0:T(8,128)S(1)} %get-tuple-element.71.mix_ref) | copy-start | bytes 6291460
  84.5 15.7 %copy-start.2 = (bf16[256,2048]{1,0:T(8,128)(2,1)}, bf16[256,2048]{1,0:T(8,128)(2,1)S(1)}, u32[]{:S(2)}) copy-start(bf16[256,2048]{1,0:T(8,128)(2,1)S(1)} %get-tuple-element.70.q_ref) | copy-start | bytes 3145732
  87.8 20.3 %copy-start.6 = (f32[128,2048]{1,0:T(8,128)}, f32[128,2048]{1,0:T(8,128)S(1)}, u32[]{:S(2)}) copy-start(f32[128,2048]{1,0:T(8,128)S(1)} %get-tuple-element.74.mix_head_ref) | copy-start | bytes 3145732
  87.8 4.6 %collective-permute-start.3 = (f32[8,256]{1,0:T(8,128)S(1)}, f32[8,256]{1,0:T(8,128)S(1)}, u32[]{:S(2)}, u32[]{:S(2)}) collective-permute-start(f32[8,256]{1,0:T(8,128)S(1)} %get-tuple-element.73.s0), channel_id=1, source_target_pairs={{0,3},{1,0},{2,1},{3,2},{4,7},{5,4},{6,5},{7,6},{8,11},{9,8},{10,9... | collective-permute-start | bytes 24584 | tf_op jit(solution)/shard_map/ppermute | solution.py:906
  91.6 4.0 %collective-permute-start.2 = (f32[8,256]{1,0:T(8,128)S(1)}, f32[8,256]{1,0:T(8,128)S(1)}, u32[]{:S(2)}, u32[]{:S(2)}) collective-permute-start(f32[8,256]{1,0:T(8,128)S(1)} %get-tuple-element.73.s0), channel_id=1, source_target_pairs={{0,2},{1,3},{2,0},{3,1},{4,6},{5,7},{6,4},{7,5},{8,10},{9,11},{10,... | collective-permute-start | bytes 24584 | tf_op jit(solution)/shard_map/ppermute | solution.py:906
  91.7 4.0 %collective-permute-start.1 = (f32[8,256]{1,0:T(8,128)S(1)}, f32[8,256]{1,0:T(8,128)S(1)}, u32[]{:S(2)}, u32[]{:S(2)}) collective-permute-start(f32[8,256]{1,0:T(8,128)S(1)} %get-tuple-element.73.s0), channel_id=1, source_target_pairs={{0,1},{1,2},{2,3},{3,0},{4,5},{5,6},{6,7},{7,4},{8,9},{9,10},{10,1... | collective-permute-start | bytes 24584 | tf_op jit(solution)/shard_map/ppermute | solution.py:906
  95.7 12.4 %copy-start.17 = (f32[8,256]{1,0:T(8,128)}, f32[8,256]{1,0:T(8,128)S(1)}, u32[]{:S(2)}) copy-start(f32[8,256]{1,0:T(8,128)S(1)} %collective-permute-done.1.s1) | copy-start | bytes 24580
  98.2 12.2 %collective-permute-start.4 = (bf16[128,2048]{1,0:T(8,128)(2,1)}, bf16[128,2048]{1,0:T(8,128)(2,1)S(1)}, u32[]{:S(2)}, u32[]{:S(2)}) collective-permute-start(bf16[128,2048]{1,0:T(8,128)(2,1)} %shard_map.152), channel_id=1, source_target_pairs={{4,0},{8,4},{12,8},{16,12},{20,16},{24,20},{28,24},{32,28},{36,32}... | collective-permute-start | bytes 1572872 | tf_op jit(solution)/shard_map/ppermute | solution.py:841
  110.5 0.8 copy-start.8
  111.3 40.4 %all-to-all-start.1 = ((bf16[32,16,2688]{2,1,0:T(8,128)(2,1)}), bf16[32,16,2688]{2,1,0:T(8,128)(2,1)S(1)}, u32[]{:S(2)}, u32[]{:S(2)}) async-start(bf16[32,16,2688]{2,1,0:T(8,128)(2,1)} %bitcast.22), calls=%async_computation.1 | async-start | bytes 5505024 | tf_op jit(solution)/shard_map/all_to_all | solution.py:834
  116.3 1.6 copy-start.1
  117.9 1.2 copy-start.3
  119.2 1.7 copy-start.5
  120.9 1.2 copy-start.7
  122.1 0.7 copy-start.18
  122.8 6.1 %copy-start.9 = (bf16[128,2048]{1,0:T(8,128)(2,1)S(1)}, bf16[128,2048]{1,0:T(8,128)(2,1)}, u32[]{:S(2)}) copy-start(bf16[128,2048]{1,0:T(8,128)(2,1)} %copy-done.8) | copy-start | bytes 1572868
  122.8 6.1 %copy-start.14 = (bf16[128,384]{1,0:T(8,128)(2,1)S(1)}, bf16[128,384]{1,0:T(8,128)(2,1)}, u32[]{:S(2)}) copy-start(bf16[128,384]{1,0:T(8,128)(2,1)} %copy-done.13) | copy-start | bytes 294916
  122.8 6.1 %copy-start.16 = (bf16[384,128]{1,0:T(8,128)(2,1)S(1)}, bf16[384,128]{1,0:T(8,128)(2,1)}, u32[]{:S(2)}) copy-start(bf16[384,128]{1,0:T(8,128)(2,1)} %copy-done.15) | copy-start | bytes 294916
  152.7 39.4 %all-to-all-start.2 = ((bf16[32,16,2560]{2,1,0:T(8,128)(2,1)}), bf16[32,16,2560]{2,1,0:T(8,128)(2,1)}, u32[]{:S(2)}, u32[]{:S(2)}) async-start(bf16[32,16,2560]{2,1,0:T(8,128)(2,1)} %bitcast.20), calls=%async_computation.2 | async-start | bytes 5242880 | tf_op jit(solution)/shard_map/all_to_all | solution.py:834

commit v5 on v4

--- a/solution.py
+++ b/solution.py
@@ -1,4 +1,5 @@
 import functools
+import math
 
 import jax
 import jax.numpy as jnp
@@ -22,8 +23,11 @@
 WIN = TAPS + ROWS
 FREQ = 320
 CB = 512
-PACK, PRODUCT, TAIL, CONV, HEAD = 1024, 1024, 2048, 1024, 1024
-HEAD_GRAD, BACK, FINISH, GIVE, HOME, HOME_P = 1024, 1024, 1024, 1024, 1024, 1024
+WIDE, NARROW = 1024, 256
+
+
+def step_width(pair):
+    return NARROW if pair == PAIR else WIDE
 
 
 def dot(a, b):
@@ -169,17 +173,18 @@
 
 
 def pack_arrivals(pair, slots, early, late):
+    wide = step_width(pair)
     width = early[0].shape[1]
-    blocks = width // PACK
+    blocks = width // wide
     halves = len(late)
     sent = SHARDS * pair
     return pl.pallas_call(
         functools.partial(pack_kernel, halves, blocks),
         grid=(2 * blocks,),
         in_specs=[RESIDENT]
-        + [cols(SLOTS, PACK, last=blocks - 1)] * len(early)
-        + [pl.BlockSpec((SLOTS, PACK), lambda j: (0, jnp.maximum(j - blocks, 0)))] * halves,
-        out_specs=cols(sent, PACK),
+        + [cols(SLOTS, wide, last=blocks - 1)] * len(early)
+        + [pl.BlockSpec((SLOTS, wide), lambda j: (0, jnp.maximum(j - blocks, 0)))] * halves,
+        out_specs=cols(sent, wide),
         out_shape=sds((sent, 2 * width), BF),
         scratch_shapes=[pltpu.VMEM((sent, SLOTS), BF)] * halves,
         compiler_params=params(),
@@ -195,9 +200,9 @@
     width = k.shape[1]
     return pl.pallas_call(
         product_kernel,
-        grid=(width // PRODUCT,),
-        in_specs=[cols(SLOTS, PRODUCT)] * 2,
-        out_specs=cols(SLOTS, PRODUCT),
+        grid=(width // WIDE,),
+        in_specs=[cols(SLOTS, WIDE)] * 2,
+        out_specs=cols(SLOTS, WIDE),
         out_shape=sds((SLOTS, width), BF),
         compiler_params=params(),
         cost_estimate=cost(SLOTS * width, 6 * width * SLOTS),
@@ -212,18 +217,31 @@
     tail_ref[...] = dot(place[...], recv_ref[...]).astype(BF)
 
 
-def place_tail(pos_row, received, width):
+def place_tail(wide, pos_row, received, width):
     sent = received.shape[0]
     return pl.pallas_call(
         place_tail_kernel,
-        grid=(width // TAIL,),
-        in_specs=[RESIDENT, cols(sent, TAIL)],
-        out_specs=cols(TAPS, TAIL),
+        grid=(width // wide,),
+        in_specs=[RESIDENT, cols(sent, wide)],
+        out_specs=cols(TAPS, wide),
         out_shape=sds((TAPS, width), BF),
         scratch_shapes=[pltpu.VMEM((TAPS, sent), BF)],
         compiler_params=params(),
         cost_estimate=cost(2 * sent * TAPS * width, 2 * width * (sent + TAPS)),
     )(*kept(pos_row), received)
+
+
+def wave_of(turns):
+    square = (turns * turns) * (4.0 * math.pi * math.pi)
+
+    def series(first):
+        total = jnp.zeros_like(square)
+        for power in range(first + 18, first - 1, -2):
+            term = (-1.0) ** ((power - first) // 2) / math.factorial(power)
+            total = total * square + term
+        return total
+
+    return series(0), series(1) * (turns * (-2.0 * math.pi))
 
 
 def segment_dft(docs_window):
@@ -252,24 +270,22 @@
     size_f = size.astype(F32)
     inverse = 1.0 / size_f
 
-    def angles(steps):
+    def waves(steps):
         turns = (wave * steps).astype(F32)
-        turns = turns - jnp.floor(turns * inverse) * size_f
-        return turns * (inverse * (2.0 * jnp.pi))
-
-    turn = angles(place[None, :] - pick(first))
+        turns = turns - jnp.round(turns * inverse) * size_f
+        return wave_of(turns * inverse)
+
+    real, imag = waves(place[None, :] - pick(first))
     mask = docs[None, :] == doc
-    spectrum = jnp.concatenate(
-        [jnp.where(mask, jnp.cos(turn), 0.0), jnp.where(mask, -jnp.sin(turn), 0.0)], axis=0
+    spectrum = jnp.where(
+        jnp.concatenate([mask, mask], axis=0), jnp.concatenate([real, imag], axis=0), 0.0
     )
     lag = jnp.arange(TAPS, dtype=I32)[None, :]
-    turn = angles(lag)
+    real, imag = waves(lag)
     weight = jnp.where(
         live & (lag < pick(taps)), jnp.where(wave == 0, inverse, 2.0 * inverse), 0.0
     )
-    taps_spectrum = jnp.concatenate(
-        [weight * jnp.cos(turn), -weight * jnp.sin(turn)], axis=0
-    )
+    taps_spectrum = jnp.concatenate([weight * real, weight * imag], axis=0)
     return spectrum, taps_spectrum
 
 
@@ -282,8 +298,9 @@
     place = jnp.arange(TAPS, dtype=I32)[None, :]
 
     def waves(steps):
-        turn = ((wave * steps) % CROSS).astype(F32) * (2.0 * jnp.pi / CROSS)
-        return jnp.concatenate([jnp.cos(turn), -jnp.sin(turn)], axis=0)
+        turns = (wave * steps).astype(F32)
+        turns = turns - jnp.round(turns * (1.0 / CROSS)) * CROSS
+        return jnp.concatenate(wave_of(turns * (1.0 / CROSS)), axis=0)
 
     document = own_docs[ROWS - 1]
     head = jnp.where((next_docs == document)[None, :], waves(place + TAPS), 0.0)
@@ -324,7 +341,7 @@
         place[...] = onehot(iota(place.shape, 0) == pos_row[...])
         acc[...] = jnp.zeros_like(acc)
 
-    at = block_of(step, CONV)
+    at = block_of(step, recv_p.shape[1])
     product = dot(place[...], recv_p[...]).astype(BF)
     q = dot(place[...], recv_q[...])
     q_ref[:, at] = q.astype(BF)
@@ -343,10 +360,10 @@
         sums_ref[...] = jnp.transpose(acc[...])[:8]
 
 
-def forward(pos_row, cc_own, cc_own_t, bb, received, filt, residual, cot, gain):
+def forward(wide, pos_row, cc_own, cc_own_t, bb, received, filt, residual, cot, gain):
     sent = received.shape[0]
     width = received.shape[1] // 2
-    blocks = width // CONV
+    blocks = width // wide
     return pl.pallas_call(
         conv_kernel,
         grid=(blocks,),
@@ -355,12 +372,12 @@
             RESIDENT,
             RESIDENT,
             RESIDENT,
-            cols(sent, CONV),
-            pl.BlockSpec((sent, CONV), lambda j: (0, blocks + j)),
-            cols(TAPS, CONV),
-            cols(ROWS, CONV),
-            cols(ROWS, CONV),
-            cols(1, CONV),
+            cols(sent, wide),
+            pl.BlockSpec((sent, wide), lambda j: (0, blocks + j)),
+            cols(TAPS, wide),
+            cols(ROWS, wide),
+            cols(ROWS, wide),
+            cols(1, wide),
         ],
         out_specs=[RESIDENT] * 4 + [whole((8, TAPS))],
         out_shape=[
@@ -391,7 +408,7 @@
     def _():
         acc[...] = jnp.zeros_like(acc)
 
-    at = block_of(step, HEAD)
+    at = block_of(step, halo.shape[1])
     x = dot(cc_halo[...], halo[...])
     fr, fi = crossing(f_ref[:, at].astype(F32))
     y = spectra_product(x[:CROSS_FREQ], x[CROSS_FREQ:], fr, fi)
@@ -406,21 +423,21 @@
         out_sums_ref[:, TAPS:] = sums_ref[...]
 
 
-def forward_head(cc_halo, cc_head_t, halo, f, q, mix, residual, cot, gain, sums):
+def forward_head(wide, cc_halo, cc_head_t, halo, f, q, mix, residual, cot, gain, sums):
     width = q.shape[1]
     return pl.pallas_call(
         head_kernel,
-        grid=(width // HEAD,),
+        grid=(width // wide,),
         in_specs=[
             RESIDENT,
             RESIDENT,
-            cols(TAPS, HEAD),
-            RESIDENT,
-            RESIDENT,
-            RESIDENT,
-            cols(TAPS, HEAD),
-            cols(TAPS, HEAD),
-            cols(1, HEAD),
+            cols(TAPS, wide),
+            RESIDENT,
+            RESIDENT,
+            RESIDENT,
+            cols(TAPS, wide),
+            cols(TAPS, wide),
+            cols(1, wide),
             RESIDENT,
         ],
         out_specs=[RESIDENT, whole((8, ROWS))],
@@ -496,21 +513,21 @@
     def _():
         row_stats(s0, s1, s2, s3, stats)
 
-    at = block_of(step, HEAD_GRAD)
+    at = block_of(step, res_ref.shape[1])
     q = q_ref[:TAPS, at].astype(F32)
     summed = res_ref[...].astype(F32) + q * mix_head_ref[:, at]
     d_summed = d_summed_of(stats[:TAPS], summed, cot_ref[...].astype(F32) * gain_ref[...])
     head_ref[...] = (d_summed * q).astype(BF)
 
 
-def head_grad(sums, q, mix_head, residual, cot, gain):
+def head_grad(wide, sums, q, mix_head, residual, cot, gain):
     width = q.shape[1]
     return pl.pallas_call(
         head_grad_kernel,
-        grid=(width // HEAD_GRAD,),
+        grid=(width // wide,),
         in_specs=[RESIDENT] * 4
-        + [RESIDENT, RESIDENT, cols(TAPS, HEAD_GRAD), cols(TAPS, HEAD_GRAD), cols(1, HEAD_GRAD)],
-        out_specs=cols(TAPS, HEAD_GRAD),
+        + [RESIDENT, RESIDENT, cols(TAPS, wide), cols(TAPS, wide), cols(1, wide)],
+        out_specs=cols(TAPS, wide),
         out_shape=sds((TAPS, width), BF),
         scratch_shapes=[pltpu.VMEM((ROWS, 128), F32)],
         compiler_params=params(),
@@ -531,6 +548,7 @@
 ):
     step = pl.program_id(0)
     per = pair // 4
+    span = res_ref.shape[1]
     parts = taps_acc.shape[0]
     sent = SHARDS * pair
 
@@ -543,7 +561,7 @@
 
     @pl.when(step < blocks)
     def _():
-        at = block_of(jnp.minimum(step, blocks - 1), BACK)
+        at = block_of(jnp.minimum(step, blocks - 1), span)
         q = q_ref[:, at].astype(F32)
         mix = mixture_block(mix_ref, mix_head_ref, at)
         summed = res_ref[...].astype(F32) + q * mix
@@ -561,13 +579,13 @@
             [x[FREQ : FREQ + CROSS_FREQ] + reach[CROSS_FREQ:], x[FREQ + CROSS_FREQ :]], axis=0
         )
         taps = dot(bb_t[...], conj_product(g[:FREQ], g[FREQ:], xr, xi)).astype(BF)
-        for i in range(BACK // CB):
-            block = jnp.minimum(step, blocks - 1) * (BACK // CB) + i
+        for i in range(span // CB):
+            block = jnp.minimum(step, blocks - 1) * (span // CB) + i
             spread = onehot(iota((sent, TAPS), 0) == tap_rows(pair, (sent, TAPS), 1, block))
             taps_acc[block // per] += dot(spread, taps[:, CB * i : CB * (i + 1)])
         wide = gain_acc.shape[1]
-        for i in range(BACK // wide):
-            row = iota(gain_acc.shape, 0) == step * (BACK // wide) + i
+        for i in range(span // wide):
+            row = iota(gain_acc.shape, 0) == step * (span // wide) + i
             gain_acc[...] += jnp.where(row, gain_part[:, wide * i : wide * (i + 1)], 0.0)
 
     def extra(at):
@@ -577,26 +595,27 @@
         return jnp.broadcast_to(gain_acc[...][None], (SHARDS, pair, wide)).reshape(sent, wide)
 
     starts = [CB * part for part in range(parts + 1)]
-    for late in range(pl.cdiv(starts[-1] + 1, BACK)):
+    for late in range(pl.cdiv(starts[-1] + 1, span)):
 
         @pl.when(step == blocks + late)
         def _(late=late):
             for at in starts:
-                if at // BACK == late:
+                if at // span == late:
                     value = extra(at).astype(BF)
-                    out_ref[:, at % BACK : at % BACK + value.shape[1]] = value
+                    out_ref[:, at % span : at % span + value.shape[1]] = value
 
 
 def backward(pair, sums, pos_row, cc_own, cc_halo, bb_t, q, mix, mix_head, x, halo, residual, cot, gain):
+    wide = max(CB, step_width(pair))
     width = q.shape[1]
-    blocks = width // BACK
+    blocks = width // wide
     last = blocks - 1
     sent = SHARDS * pair
     part_cols, gain_cols = extra_cols(pair, width)
     parts = part_cols // CB
     return pl.pallas_call(
         functools.partial(backward_kernel, pair, blocks),
-        grid=(blocks + pl.cdiv(part_cols + gain_cols, BACK),),
+        grid=(blocks + pl.cdiv(part_cols + gain_cols, wide),),
         in_specs=[RESIDENT] * 4
         + [
             RESIDENT,
@@ -606,12 +625,12 @@
         ]
         + [RESIDENT] * 4
         + [
-            cols(TAPS, BACK, last=last),
-            cols(ROWS, BACK, last=last),
-            cols(ROWS, BACK, last=last),
-            cols(1, BACK, last=last),
+            cols(TAPS, wide, last=last),
+            cols(ROWS, wide, last=last),
+            cols(ROWS, wide, last=last),
+            cols(1, wide, last=last),
         ],
-        out_specs=[cols(ROWS, BACK, last=last), cols(sent, BACK)],
+        out_specs=[cols(ROWS, wide, last=last), cols(sent, wide)],
         out_shape=[
             sds((ROWS, width), BF),
             sds((sent, width + part_cols + gain_cols), BF),
@@ -642,7 +661,7 @@
     def _():
         row_stats(s0, s1, s2, s3, stats)
 
-    at = block_of(step, FINISH)
+    at = block_of(step, res_ref.shape[1])
     gain = gain_ref[...]
     mix = mixture_block(mix_ref, mix_head_ref, at)
     summed = res_ref[...].astype(F32) + q_ref[:, at].astype(F32) * mix
@@ -653,16 +672,16 @@
     own_ref[...] = dot(cc_own_t[...], conj_product(g[:FREQ], g[FREQ:], f[:FREQ], f[FREQ:]))
 
 
-def finish(sums, cc_own, cc_own_t, q, mix, mix_head, f, residual, cot, gain, d_mix):
+def finish(wide, sums, cc_own, cc_own_t, q, mix, mix_head, f, residual, cot, gain, d_mix):
     width = q.shape[1]
     return pl.pallas_call(
         finish_kernel,
-        grid=(width // FINISH,),
+        grid=(width // wide,),
         in_specs=[RESIDENT] * 4
         + [RESIDENT, RESIDENT]
         + [RESIDENT] * 4
-        + [cols(ROWS, FINISH), cols(ROWS, FINISH), cols(1, FINISH), cols(ROWS, FINISH)],
-        out_specs=[cols(ROWS, FINISH)] * 3,
+        + [cols(ROWS, wide), cols(ROWS, wide), cols(1, wide), cols(ROWS, wide)],
+        out_specs=[cols(ROWS, wide)] * 3,
         out_shape=[sds((ROWS, width), BF), sds((ROWS, width), BF), sds((ROWS, width), F32)],
         scratch_shapes=[pltpu.VMEM((ROWS, 128), F32)],
         compiler_params=params(),
@@ -690,21 +709,22 @@
 
 
 def give_back(pair, pos_row, onward, own, from_next, filt):
+    wide = step_width(pair)
     width = own.shape[1]
     sent = SHARDS * pair
     return pl.pallas_call(
         give_back_kernel,
-        grid=(width // GIVE,),
+        grid=(width // wide,),
         in_specs=[
             RESIDENT,
             RESIDENT,
             RESIDENT,
             RESIDENT,
-            cols(ROWS, GIVE),
-            cols(TAPS, GIVE),
-            cols(TAPS, GIVE),
+            cols(ROWS, wide),
+            cols(TAPS, wide),
+            cols(TAPS, wide),
         ],
-        out_specs=cols(sent, GIVE),
+        out_specs=cols(sent, wide),
         out_shape=sds((sent, width + extra_cols(pair, width)[0]), BF),
         scratch_shapes=[pltpu.VMEM((sent, ROWS), BF)],
         compiler_params=params(),
@@ -771,13 +791,14 @@
 
 
 def home_rows(pair, slots, backs, width):
+    wide = step_width(pair)
     sent = SHARDS * pair
     halves = len(backs)
     return pl.pallas_call(
         functools.partial(home_rows_kernel, pair, halves),
-        grid=(width // HOME,),
-        in_specs=[RESIDENT] + [cols(sent, HOME)] * halves,
-        out_specs=cols(SLOTS, HOME),
+        grid=(width // wide,),
+        in_specs=[RESIDENT] + [cols(sent, wide)] * halves,
+        out_specs=cols(SLOTS, wide),
         out_shape=sds((SLOTS, width), BF),
         scratch_shapes=[pltpu.VMEM((SLOTS, sent), BF)] * halves,
         compiler_params=params(),
@@ -799,29 +820,30 @@
     dk_ref[...] = (grad * v_ref[...].astype(F32)).astype(BF)
     dv_ref[...] = (grad * k_ref[...].astype(F32)).astype(BF)
     shape = (TAPS, SHARDS * pair)
-    for i in range(HOME_P // CB):
-        block = step * (HOME_P // CB) + i
+    for i in range(k_ref.shape[1] // CB):
+        block = step * (k_ref.shape[1] // CB) + i
         gather = onehot(iota(shape, 1) == tap_rows(pair, shape, 0, block))
         part = taps_ref[:, block_of(block // (pair // 4))]
         filt_ref[:, CB * i : CB * (i + 1)] = dot(gather, part)
 
 
 def home_product(pair, slots, back, backs, k, v):
+    wide = max(CB, step_width(pair))
     width = k.shape[1]
     part_cols = extra_cols(pair, width)[0]
     sent = SHARDS * pair
     halves = len(backs)
     return pl.pallas_call(
         functools.partial(home_product_kernel, pair, halves),
-        grid=(width // HOME_P,),
+        grid=(width // wide,),
         in_specs=[
             RESIDENT,
             pl.BlockSpec((sent, part_cols), lambda j: (0, width // part_cols)),
-            cols(SLOTS, HOME_P),
-            cols(SLOTS, HOME_P),
+            cols(SLOTS, wide),
+            cols(SLOTS, wide),
         ]
-        + [cols(sent, HOME_P)] * halves,
-        out_specs=[cols(SLOTS, HOME_P), cols(SLOTS, HOME_P), cols(TAPS, HOME_P)],
+        + [cols(sent, wide)] * halves,
+        out_specs=[cols(SLOTS, wide), cols(SLOTS, wide), cols(TAPS, wide)],
         out_shape=[sds((SLOTS, width), BF), sds((SLOTS, width), BF), sds((TAPS, width), F32)],
         scratch_shapes=[pltpu.VMEM((SLOTS, sent), BF)] * halves,
         compiler_params=params(),
@@ -861,23 +883,20 @@
     return (jnp.sum(jnp.where(hit, target[:, None, :], 0), axis=2) - 1).reshape(SHARDS * pair)
 
 
-def layer(pair, q_in, k_in, v_in, dest_pos, doc_ids, mr_filter, norm_gain, residual, cotangent):
+def layer(pair, others, q_in, k_in, v_in, dest_pos, doc_ids, mr_filter, norm_gain, residual, cotangent):
     my_index = lax.axis_index("seq")
     width = q_in.shape[1]
+    wide = step_width(pair)
     gain = norm_gain[None, :]
     shared = pair != PAIR
 
+    slots = send_plan(pair, my_index, dest_pos)
     if shared:
-        product_in = slot_product(k_in, v_in)
-        product_other = swap(product_in)
-        q_other = swap(q_in)
-        slots = send_plan(pair, my_index, dest_pos)
-        sent_rows = pack_arrivals(
-            pair, slots, [*hbm(product_in), product_other], [*hbm(q_in), q_other]
-        )
+        product_in, product_other, q_other = others
+        early, late = [*hbm(product_in), product_other], [*hbm(q_in), q_other]
     else:
-        slots = send_plan(pair, my_index, dest_pos)
-        sent_rows = pack_arrivals(pair, slots, hbm(k_in, v_in), hbm(q_in))
+        early, late = hbm(k_in, v_in), hbm(q_in)
+    sent_rows = pack_arrivals(pair, slots, early, late)
     sent_rows, dest_later, docs_later, slots = lax.optimization_barrier(
         (sent_rows, dest_pos, doc_ids, slots)
     )
@@ -895,17 +914,17 @@
     received, pos_row, prepared = lax.optimization_barrier((received, pos_row, prepared))
     cc_own, cc_own_t, cc_halo, cc_head_t, bb, bb_t, *onward = prepared
 
-    halo = shift(place_tail(pos_row, received, width), 1)
+    halo = shift(place_tail(wide, pos_row, received, width), 1)
     q, mix, x, f, sums = forward(
-        pos_row, cc_own, cc_own_t, bb, received, mr_filter, residual, cotangent, gain
+        wide, pos_row, cc_own, cc_own_t, bb, received, mr_filter, residual, cotangent, gain
     )
     mix_head, sums = forward_head(
-        cc_halo, cc_head_t, halo, f, q, mix, residual, cotangent, gain, sums
+        wide, cc_halo, cc_head_t, halo, f, q, mix, residual, cotangent, gain, sums
     )
     all_sums = [sums] + [
         lax.ppermute(sums, "mp", [(i, (i + k) % 4) for i in range(4)]) for k in (1, 2, 3)
     ]
-    head = head_grad(all_sums, q, mix_head, residual, cotangent, gain)
+    head = head_grad(wide, all_sums, q, mix_head, residual, cotangent, gain)
     d_mix, sent_dq = backward(
         pair, all_sums, pos_row, cc_own, cc_halo, bb_t, q, mix, mix_head, x, halo,
         residual, cotangent, gain,
@@ -913,7 +932,7 @@
     sent_dq, from_next = lax.optimization_barrier((sent_dq, shift(head, -1)))
     back_q = exchange(pair, sent_dq)
     normed, d_residual, own_grad = finish(
-        all_sums, cc_own, cc_own_t, q, mix, mix_head, f, residual, cotangent, gain, d_mix
+        wide, all_sums, cc_own, cc_own_t, q, mix, mix_head, f, residual, cotangent, gain, d_mix
     )
     rows = give_back(pair, pos_row, onward, own_grad, from_next, mr_filter)
     sent_dp, d_gain = reduce_parts(pair, back_q, rows, width)
@@ -927,8 +946,24 @@
     return (normed, d_residual, d_q_in, d_k_in, d_v_in, d_filter, d_gain.reshape(width))
 
 
-def body(*args):
-    return layer(PAIR, *args)
+def fits_shared(dest_pos):
+    chips = dest_pos.reshape(SHARDS // 2, 2 * SLOTS)
+    owner = jnp.where(chips >= 0, chips // ROWS, -1)
+    load = jnp.sum(
+        (owner[:, None, :] == jnp.arange(SHARDS, dtype=I32)[None, :, None]).astype(I32), axis=2
+    )
+    return jnp.max(load) <= PAIR
+
+
+def body(q_in, k_in, v_in, dest_pos, *rest):
+    product_in = slot_product(k_in, v_in)
+    others = (product_in, swap(product_in), swap(q_in))
+    return lax.cond(
+        fits_shared(dest_pos),
+        functools.partial(layer, PAIR // 2),
+        functools.partial(layer, PAIR),
+        others, q_in, k_in, v_in, dest_pos, *rest,
+    )
 
 
 def solution(mesh):

time: 198 us -> 160 us (0.81)
  waiting for transfers between devices: 98.4 us -> 57.9 us
  local copies, waits for them, and re-layouts: 10.1 us -> 12.3 us
    all_to_all x3, waiting for transfers between devices: 92.7 us -> 50.8 us  [exchange(): lax.all_to_all(shards, 'seq', split_axis=0, concat_axis=0, tiled=True)]
    cond x0 -> x53, local copies, waits for them, and re-layouts: none -> 10.5 us
    unnamed x40 -> x6, local copies, waits for them, and re-layouts: 9.37 us -> 0.01 us
    ppermute x0 -> x4, waiting for transfers between devices: none -> 3.78 us  [swap(): return lax.ppermute(value, 'seq', [(i, i ^ 1) for i in range(SHARDS)])]
    ppermute x0 -> x4, starting transfers between devices: none -> 2.54 us  [swap(): return lax.ppermute(value, 'seq', [(i, i ^ 1) for i in range(SHARDS)])]
    ppermute x2, waiting for transfers between devices: 2.36 us -> 0.01 us  [shift(): return lax.ppermute(value, 'seq', pairs)]
    pallas_call x5 -> x6, Pallas kernels: 19.7 us -> 20.9 us  [the longest x1 6.02 us: finish(): pl.pallas_call(finish_kernel, grid=(width // wide,), in_specs=[RESIDENT]...]
  transfers between devices with their start and end apart: 8 -> 12, of which waited for: 6 -> 7; matrix products, arithmetic and copies ran while one was open for 4% -> 5% of each run, Pallas kernels for 14% -> 17%
where the time goes in v5:
time: 160 us; the launch traced here: 159 us
  waiting for transfers between devices  57.9 us (36%)
  Pallas kernels  49.6 us (31%)
  starting transfers between devices  32 us (20%)
  local copies, waits for them, and re-layouts  12.3 us (8%)
  other arithmetic  5.44 us (3%)
    all_to_all x3, waiting for transfers between devices, exchange(): lax.all_to_all(shards, 'seq', split_axis=0, concat_axis=0, tiled=True)  50.8 us
    all_to_all x3, starting transfers between devices, exchange(): lax.all_to_all(shards, 'seq', split_axis=0, concat_axis=0, tiled=True)  18.9 us
    cond x53, local copies, waits for them, and re-layouts  10.5 us
    pallas_call x1, Pallas kernels, backward(): pl.pallas_call(functools.partial(backward_kernel, pair, blocks), grid=(bl...  7.98 us
    ppermute x2, starting transfers between devices, shift(): return lax.ppermute(value, 'seq', pairs)  6.04 us
    pallas_call x1, Pallas kernels, finish(): pl.pallas_call(finish_kernel, grid=(width // wide,), in_specs=[RESIDENT]...  6.02 us
    pallas_call x1, Pallas kernels, pack_arrivals(): pl.pallas_call(functools.partial(pack_kernel, halves, blocks), grid=(2 *...  5.84 us
    pallas_call x1, Pallas kernels, forward(): pl.pallas_call(conv_kernel, grid=(blocks,), in_specs=[RESIDENT, RESIDENT,...  5.32 us
  transfers between devices with their start and end apart: 12, of which 7 were waited for; matrix products, arithmetic and copies ran while one was open for 5% of the time, Pallas kernels for 17%

profile of v5, /device:TPU:1, one launch (start us, length us, event | category | flops | bytes accessed | tf_op | source)
XLA Modules:
  0.0 159.3 jit_solution(18009579253670320626)
XLA Ops:
  0.7 3.0 %shard_map.148 = bf16[384,2048]{1,0:T(8,128)(2,1)} custom-call(bf16[384,2048]{1,0:T(8,128)(2,1)} %k_ref.1, bf16[384,2048]{1,0:T(8,128)(2,1)} %v_ref.1), custom_call_target="tpu_custom_call" | custom-call | flops 786432 | bytes 4718592 | tf_op jit(solution)/shard_map/pallas_call | solution.py:201
  3.6 1.4 collective-permute-start.12
  5.1 0.4 convert_reduce_fusion.4
  5.5 0.6 reduce_max.9
  6.8 1.5 collective-permute-done.12
  8.3 2.2 %collective-permute-done.13 = bf16[384,2048]{1,0:T(8,128)(2,1)S(1)} collective-permute-done((bf16[384,2048]{1,0:T(8,128)(2,1)}, bf16[384,2048]{1,0:T(8,128)(2,1)S(1)}, u32[]{:S(2)}, u32[]{:S(2)}) %collective-permute-start.13) | collective-permute-done | bytes 1572896 | tf_op jit(solution)/shard_map/ppermute | solution.py:867
  10.6 148.7 %conditional.1 = (bf16[256,2048]{1,0:T(8,128)(2,1)}, bf16[256,2048]{1,0:T(8,128)(2,1)}, bf16[384,2048]{1,0:T(8,128)(2,1)}, bf16[384,2048]{1,0:T(8,128)(2,1)}, f3...) conditional(s32[]{:T(128)} %convert_element_type.91, (s32[12288]{0:T(1024)S(1)}, ...), branch_computations={%region_2.14_spmd, %region_14.26_spmd} | conditional | flops 11995193344 | bytes 185124192 | solution.py:961
  10.6 0.4 branch_1_fun.13.slots_ref
  11.0 5.8 %branch_1_fun.14 = bf16[256,4096]{1,0:T(8,128)(2,1)} custom-call(s32[8,384]{1,0:T(8,128)S(1)} %branch_1_fun.13.slots_ref, bf16[384,2048]{1,0:T(8,128)(2,1)} %get-tuple-element.95.refs_0_, bf16[384,2048]{1,0:T(8,128)(2,1)S(1)} %get-tuple-element.96.refs_1_, bf16[384,2048]{1,0:T(8,128)(2,1)} %get-tuple-element.97.refs_2_, ...), custom_call_target="tpu_custom_call" | custom-call | flops 1610612736 | bytes 8388608 | tf_op jit(solution)/shard_map/cond/branch_1_fun/pallas_call | solution.py:181
  16.8 7.5 %all-to-all-start.3 = ((bf16[32,8,4096]{2,1,0:T(8,128)(2,1)}), bf16[32,8,4096]{2,1,0:T(8,128)(2,1)S(1)}, u32[]{:S(2)}, u32[]{:S(2)}) async-start(bf16[32,8,4096]{2,1,0:T(8,128)(2,1)} %bitcast.40), calls=%async_computation.3 | async-start | bytes 4194304 | tf_op jit(solution)/shard_map/cond/branch_1_fun/all_to_all | solution.py:856
  24.4 0.1 multiply_add_fusion.4
  24.6 0.3 fusion.40
  24.9 0.1 fusion.69
  25.0 0.2 select_reduce_fusion.13
  25.1 0.1 select_reduce_fusion.17
  25.3 0.2 select_reduce_fusion.10
  25.5 0.4 select_reduce_fusion.9
  25.9 0.5 iota_add_fusion.1
  26.4 0.6 slice.32
  27.0 0.1 sub.159.pos_row
  27.1 0.1 maximum_reduce_fusion.1
  27.2 0.1 multiply_multiply_fusion.6
  27.3 0.4 select_multiply_fusion.3
  27.8 0.1 broadcast_compare_fusion.2
  27.9 0.9 multiply_add_fusion.3
  28.8 0.1 maximum_select_fusion.2.cc_ref
  28.9 0.7 slice_compare_fusion.2
  29.6 0.2 multiply_add_fusion.5
  29.8 0.1 fusion.48
  29.9 0.3 branch_1_fun.15
  30.2 0.7 copy-done.20
  30.9 0.6 copy-done.28
  31.5 0.6 copy-done.30
  32.2 20.5 %all-to-all-done.3 = bf16[32,8,4096]{2,1,0:T(8,128)(2,1)S(1)} async-done(((bf16[32,8,4096]{2,1,0:T(8,128)(2,1)}), bf16[32,8,4096]{2,1,0:T(8,128)(2,1)S(1)}, u32[]{:S(2)}, u32[]{:S(2)}) %all-to-all-start.3) | async-done | bytes 2097184 | tf_op jit(solution)/shard_map/cond/branch_1_fun/all_to_all | solution.py:856
  52.7 1.5 branch_1_fun.16
  54.2 2.1 %collective-permute-start.5 = (bf16[128,2048]{1,0:T(8,128)(2,1)}, bf16[128,2048]{1,0:T(8,128)(2,1)S(1)}, u32[]{:S(2)}, u32[]{:S(2)}) collective-permute-start(bf16[128,2048]{1,0:T(8,128)(2,1)} %branch_1_fun.16), channel_id=1, source_target_pairs={{0,4},{4,8},{8,12},{12,16},{16,20},{20,24},{24,28},{28,32},{32,36}... | collective-permute-start | bytes 1572872 | tf_op jit(solution)/shard_map/cond/branch_1_fun/ppermute | solution.py:863
  56.4 1.6 copy-done.15
  58.0 0.9 copy-done.35
  58.9 5.3 %branch_1_fun.17 = (bf16[256,2048]{1,0:T(8,128)(2,1)S(1)}, f32[256,2048]{1,0:T(8,128)S(1)}, bf16[640,2048]{1,0:T(8,128)(2,1)S(1)}, bf16[640,2048]{1,0:T(8,128)(2,1)S(1)}, f32[8,128]{1,0:T(8,128)S(1)}) custom-call(s32[1,256]{1,0:T(1,128)S(1)} %sub.159.pos_row, bf16[640,256]{1,0:T(8,128)(2,1)S(1)} %get-tuple-element.116.cc_own, ...), custom_call_target="tpu_custom_call" | custom-call | flops 4000000000 | bytes 12288000 | tf_op jit(solution)/shard_map/cond/branch_1_fun/pallas_call | solution.py:367
  64.2 3.3 %branch_1_fun.18 = (f32[128,2048]{1,0:T(8,128)S(1)}, f32[8,256]{1,0:T(8,128)S(1)}) custom-call(bf16[384,128]{1,0:T(8,128)(2,1)S(1)} %get-tuple-element.112.cc_halo, bf16[128,384]{1,0:T(8,128)(2,1)S(1)} %copy-done.23, bf16[128,2048]{1,0:T(8,128)(2,1)S(1)} %collective-permute-done.5.halo.halo_ref, bf16[640,2048]{1,0:T(8,128)(2,1)S(1)} %get-tuple-element.123.f_ref, ...), custom_call_target="tpu_custom_call" | custom-call | flops 600000000 | bytes 6144000 | tf_op jit(solution)/shard_map/cond/branch_1_fun/pallas_call | solution.py:428
  67.6 3.8 %collective-permute-start.8 = (f32[8,256]{1,0:T(8,128)S(1)}, f32[8,256]{1,0:T(8,128)S(1)}, u32[]{:S(2)}, u32[]{:S(2)}) collective-permute-start(f32[8,256]{1,0:T(8,128)S(1)} %get-tuple-element.127.s0), channel_id=1, source_target_pairs={{0,3},{1,0},{2,1},{3,2},{4,7},{5,4},{6,5},{7,6},{8,11},{9,8},{10,9... | collective-permute-start | bytes 24584 | tf_op jit(solution)/shard_map/cond/branch_1_fun/ppermute | solution.py:925
  71.4 0.7 collective-permute-start.6
  72.1 0.1 collective-permute-done.8.s3
  72.2 3.2 %collective-permute-done.7.s2 = f32[8,256]{1,0:T(8,128)S(1)} collective-permute-done((f32[8,256]{1,0:T(8,128)S(1)}, f32[8,256]{1,0:T(8,128)S(1)}, u32[]{:S(2)}, u32[]{:S(2)}) %collective-permute-start.7) | collective-permute-done | bytes 8224 | tf_op jit(solution)/shard_map/cond/branch_1_fun/ppermute | solution.py:925
  75.4 2.6 %branch_1_fun.21 = bf16[128,2048]{1,0:T(8,128)(2,1)} custom-call(f32[8,256]{1,0:T(8,128)S(1)} %get-tuple-element.127.s0, f32[8,256]{1,0:T(8,128)S(1)} %collective-permute-done.6.s1, f32[8,256]{1,0:T(8,128)S(1)} %collective-permute-done.7.s2, f32[8,256]{1,0:T(8,128)S(1)} %collective-permute-done.8.s3, bf16[256,2048]{1,0:T(8,128)(2,1)S(1)} %get-tuple-element.124.q_ref, ...), custom_call_target="tpu_custom_call" | custom-call | flops 2621440 | bytes 1572864 | tf_op jit(solution)/shard_map/cond/branch_1_fun/pallas_call | solution.py:525
  78.0 3.9 %collective-permute-start.9 = (bf16[128,2048]{1,0:T(8,128)(2,1)}, bf16[128,2048]{1,0:T(8,128)(2,1)S(1)}, u32[]{:S(2)}, u32[]{:S(2)}) collective-permute-start(bf16[128,2048]{1,0:T(8,128)(2,1)} %branch_1_fun.21), channel_id=1, source_target_pairs={{4,0},{8,4},{12,8},{16,12},{20,16},{24,20},{28,24},{32,28},{36,32}... | collective-permute-start | bytes 1572872 | tf_op jit(solution)/shard_map/cond/branch_1_fun/ppermute | solution.py:863
  82.0 8.0 %branch_1_fun.19 = (bf16[256,2048]{1,0:T(8,128)(2,1)}, bf16[256,3328]{1,0:T(8,128)(2,1)}) custom-call(f32[8,256]{1,0:T(8,128)S(1)} %get-tuple-element.127.s0, f32[8,256]{1,0:T(8,128)S(1)} %collective-permute-done.6.s1, f32[8,256]{1,0:T(8,128)S(1)} %collective-permute-done.7.s2, f32[8,256]{1,0:T(8,128)S(1)} %collective-permute-done.8.s3, ...), custom_call_target="tpu_custom_call" | custom-call | flops 2000000000 | bytes 12288000 | tf_op jit(solution)/shard_map/cond/branch_1_fun/pallas_call | solution.py:616
  90.0 0.8 copy-done.18
  90.8 7.0 %all-to-all-start.4 = ((bf16[32,8,3328]{2,1,0:T(8,128)(2,1)}), bf16[32,8,3328]{2,1,0:T(8,128)(2,1)S(1)}, u32[]{:S(2)}, u32[]{:S(2)}) async-start(bf16[32,8,3328]{2,1,0:T(8,128)(2,1)} %bitcast.42), calls=%async_computation.4 | async-start | bytes 3407872 | tf_op jit(solution)/shard_map/cond/branch_1_fun/all_to_all | solution.py:856
  97.8 1.6 copy-done.3
  99.4 1.7 %copy-done.9 = bf16[640,2048]{1,0:T(8,128)(2,1)S(1)} copy-done((bf16[640,2048]{1,0:T(8,128)(2,1)S(1)}, bf16[640,2048]{1,0:T(8,128)(2,1)}, u32[]{:S(2)}) %copy-start.9) | copy-done | bytes 2621464 | tf_op jit(solution)/shard_map/cond
  101.1 1.2 copy-done.13
  102.3 6.0 %branch_1_fun.20 = (bf16[256,2048]{1,0:T(8,128)(2,1)}, bf16[256,2048]{1,0:T(8,128)(2,1)}, f32[256,2048]{1,0:T(8,128)}) custom-call(f32[8,256]{1,0:T(8,128)S(1)} %get-tuple-element.127.s0, f32[8,256]{1,0:T(8,128)S(1)} %collective-permute-done.6.s1, f32[8,256]{1,0:T(8,128)S(1)} %collective-permute-done.7.s2, f32[8,256]{1,0:T(8,128)S(1)} %collective-permute-done.8.s3, ...), custom_call_target="tpu_custom_call" | custom-call | flops 1342177280 | bytes 12288000 | tf_op jit(solution)/shard_map/cond/branch_1_fun/pallas_call | solution.py:677
  108.4 4.5 %branch_1_fun.23.rows_ref = bf16[256,3072]{1,0:T(8,128)(2,1)} custom-call(s32[1,256]{1,0:T(1,128)S(1)} %sub.159.pos_row, bf16[384,128]{1,0:T(8,128)(2,1)S(1)} %copy-done.29, bf16[128,384]{1,0:T(8,128)(2,1)S(1)} %copy-done.31, bf16[384,128]{1,0:T(8,128)(2,1)S(1)} %copy-done.33, f32[256,2048]{1,0:T(8,128)} %get-tuple-element.140.own_ref, ...), custom_call_target="tpu_custom_call" | custom-call | flops 268435456 | bytes 4915200 | tf_op jit(solution)/shard_map/cond/branch_1_fun/pallas_call | solution.py:715
  112.9 9.0 %all-to-all-done.4 = bf16[32,8,3328]{2,1,0:T(8,128)(2,1)S(1)} async-done(((bf16[32,8,3328]{2,1,0:T(8,128)(2,1)}), bf16[32,8,3328]{2,1,0:T(8,128)(2,1)S(1)}, u32[]{:S(2)}, u32[]{:S(2)}) %all-to-all-start.4) | async-done | bytes 1703968 | tf_op jit(solution)/shard_map/cond/branch_1_fun/all_to_all | solution.py:856
  121.8 1.0 branch_1_fun.24
  122.8 4.4 %all-to-all-start.5 = ((bf16[32,8,3072]{2,1,0:T(8,128)(2,1)}), bf16[32,8,3072]{2,1,0:T(8,128)(2,1)S(1)}, u32[]{:S(2)}, u32[]{:S(2)}) async-start(bf16[32,8,3072]{2,1,0:T(8,128)(2,1)} %bitcast.39), calls=%async_computation.5 | async-start | bytes 3145728 | tf_op jit(solution)/shard_map/cond/branch_1_fun/all_to_all | solution.py:856
  127.2 1.1 slice.37
  128.3 0.3 collective-permute-start.10
  128.6 21.3 %all-to-all-done.5 = bf16[32,8,3072]{2,1,0:T(8,128)(2,1)S(1)} async-done(((bf16[32,8,3072]{2,1,0:T(8,128)(2,1)}), bf16[32,8,3072]{2,1,0:T(8,128)(2,1)S(1)}, u32[]{:S(2)}, u32[]{:S(2)}) %all-to-all-start.5) | async-done | bytes 1572896 | tf_op jit(solution)/shard_map/cond/branch_1_fun/all_to_all | solution.py:856
  150.0 0.8 collective-permute-start.11
  150.8 0.6 copy.22
  151.4 3.4 %branch_1_fun.22 = bf16[384,2048]{1,0:T(8,128)(2,1)} custom-call(s32[8,384]{1,0:T(8,128)S(1)} %branch_1_fun.13.slots_ref, bf16[256,3328]{1,0:T(8,128)(2,1)S(1)} %bitcast.29, bf16[256,2048]{1,0:T(8,128)(2,1)} %collective-permute-done.10.refs_1_), custom_call_target="tpu_custom_call" | custom-call | flops 805306368 | bytes 3670016 | tf_op jit(solution)/shard_map/cond/branch_1_fun/pallas_call | solution.py:797
  154.8 4.4 %branch_1_fun.25 = (bf16[384,2048]{1,0:T(8,128)(2,1)}, bf16[384,2048]{1,0:T(8,128)(2,1)}, f32[128,2048]{1,0:T(8,128)}) custom-call(s32[8,384]{1,0:T(8,128)S(1)} %branch_1_fun.13.slots_ref, bf16[256,3072]{1,0:T(8,128)(2,1)S(1)} %bitcast.31, bf16[384,2048]{1,0:T(8,128)(2,1)} %get-tuple-element.143.k_ref, bf16[384,2048]{1,0:T(8,128)(2,1)} %get-tuple-element.144.v_ref, ...), custom_call_target="tpu_custom_call" | custom-call | flops 402653184 | bytes 8912896 | tf_op jit(solution)/shard_map/cond/branch_1_fun/pallas_call | solution.py:836
  (74 shorter events, 0.4 us)
Async XLA Ops:
  0.6 4.4 %copy-start.36 = (s32[12288]{0:T(1024)S(1)}, s32[12288]{0:T(1024)}, u32[]{:S(2)}) copy-start(s32[12288]{0:T(1024)} %param.14) | copy-start | bytes 147460
  0.6 9.9 %copy-start.37 = (f32[2048]{0:T(1024)S(1)}, f32[2048]{0:T(1024)}, u32[]{:S(2)}) copy-start(f32[2048]{0:T(1024)} %param.17) | copy-start | bytes 24580
  0.7 9.9 %copy-start.43 = (s32[8192]{0:T(1024)S(1)}, s32[8192]{0:T(1024)}, u32[]{:S(2)}) copy-start(s32[8192]{0:T(1024)} %param.15) | copy-start | bytes 98308
  3.6 4.7 %collective-permute-start.12 = (bf16[384,2048]{1,0:T(8,128)(2,1)}, bf16[384,2048]{1,0:T(8,128)(2,1)S(1)}, u32[]{:S(2)}, u32[]{:S(2)}) collective-permute-start(bf16[384,2048]{1,0:T(8,128)(2,1)} %shard_map.148), channel_id=1, source_target_pairs={{0,4},{4,0},{8,12},{12,8},{16,20},{20,16},{24,28},{28,24},{32,36},... | collective-permute-start | bytes 4718600 | tf_op jit(solution)/shard_map/ppermute | solution.py:867
  5.1 5.5 %collective-permute-start.13 = (bf16[384,2048]{1,0:T(8,128)(2,1)}, bf16[384,2048]{1,0:T(8,128)(2,1)S(1)}, u32[]{:S(2)}, u32[]{:S(2)}) collective-permute-start(bf16[384,2048]{1,0:T(8,128)(2,1)} %param.11), channel_id=1, source_target_pairs={{0,4},{4,0},{8,12},{12,8},{16,20},{20,16},{24,28},{28,24},{32,36},... | collective-permute-start | bytes 4718600 | tf_op jit(solution)/shard_map/ppermute | solution.py:867
  10.6 53.7 %copy-start.40 = (f32[2048]{0:T(1024)}, f32[2048]{0:T(1024)S(1)}, u32[]{:S(2)}) copy-start(f32[2048]{0:T(1024)S(1)} %get-tuple-element.122) | copy-start | bytes 24580 | tf_op jit(solution)/shard_map/cond
  16.8 35.9 %all-to-all-start.3 = ((bf16[32,8,4096]{2,1,0:T(8,128)(2,1)}), bf16[32,8,4096]{2,1,0:T(8,128)(2,1)S(1)}, u32[]{:S(2)}, u32[]{:S(2)}) async-start(bf16[32,8,4096]{2,1,0:T(8,128)(2,1)} %bitcast.40), calls=%async_computation.3 | async-start | bytes 4194304 | tf_op jit(solution)/shard_map/cond/branch_1_fun/all_to_all | solution.py:856
  27.7 1.9 %copy-start.44 = (s32[128]{0:T(128)S(1)}, s32[128]{0:T(128)}, u32[]{:S(2)}) copy-start(s32[128]{0:T(128)} %iota_add_fusion.1) | copy-start | bytes 1540 | tf_op jit(solution)/shard_map/cond
  30.2 0.7 copy-start.20
  30.9 0.6 copy-start.28
  31.5 0.6 copy-start.30
  32.2 24.1 %copy-start.22 = (bf16[128,384]{1,0:T(8,128)(2,1)}, bf16[128,384]{1,0:T(8,128)(2,1)S(1)}, u32[]{:S(2)}) copy-start(bf16[128,384]{1,0:T(8,128)(2,1)S(1)} %get-tuple-element.113.cc_head_t) | copy-start | bytes 294916 | tf_op jit(solution)/shard_map/cond
  32.2 24.2 %copy-start.32 = (bf16[384,128]{1,0:T(8,128)(2,1)}, bf16[384,128]{1,0:T(8,128)(2,1)S(1)}, u32[]{:S(2)}) copy-start(bf16[384,128]{1,0:T(8,128)(2,1)S(1)} %get-tuple-element.139.taps) | copy-start | bytes 294916 | tf_op jit(solution)/shard_map/cond
  32.2 24.2 %copy-start.34 = (bf16[640,128]{1,0:T(8,128)(2,1)}, bf16[640,128]{1,0:T(8,128)(2,1)S(1)}, u32[]{:S(2)}) copy-start(bf16[640,128]{1,0:T(8,128)(2,1)S(1)} %get-tuple-element.118.bb) | copy-start | bytes 491524 | tf_op jit(solution)/shard_map/cond
  52.7 3.7 %copy-start.14 = (bf16[32,8,4096]{2,1,0:T(8,128)(2,1)}, bf16[32,8,4096]{2,1,0:T(8,128)(2,1)S(1)}, u32[]{:S(2)}) copy-start(bf16[32,8,4096]{2,1,0:T(8,128)(2,1)S(1)} %all-to-all-done.3) | copy-start | bytes 6291460 | tf_op jit(solution)/shard_map/cond
  54.2 10.0 %collective-permute-start.5 = (bf16[128,2048]{1,0:T(8,128)(2,1)}, bf16[128,2048]{1,0:T(8,128)(2,1)S(1)}, u32[]{:S(2)}, u32[]{:S(2)}) collective-permute-start(bf16[128,2048]{1,0:T(8,128)(2,1)} %branch_1_fun.16), channel_id=1, source_target_pairs={{0,4},{4,8},{8,12},{12,16},{16,20},{20,24},{24,28},{28,32},{32,36}... | collective-permute-start | bytes 1572872 | tf_op jit(solution)/shard_map/cond/branch_1_fun/ppermute | solution.py:863
  56.4 1.6 copy-start.15
  57.9 0.9 copy-start.35
  58.9 5.4 %copy-start.23 = (bf16[128,384]{1,0:T(8,128)(2,1)S(1)}, bf16[128,384]{1,0:T(8,128)(2,1)}, u32[]{:S(2)}) copy-start(bf16[128,384]{1,0:T(8,128)(2,1)} %copy-done.22) | copy-start | bytes 294916 | tf_op jit(solution)/shard_map/cond
  64.2 3.4 %copy-start.8 = (bf16[640,2048]{1,0:T(8,128)(2,1)}, bf16[640,2048]{1,0:T(8,128)(2,1)S(1)}, u32[]{:S(2)}) copy-start(bf16[640,2048]{1,0:T(8,128)(2,1)S(1)} %get-tuple-element.123.f_ref) | copy-start | bytes 7864324 | tf_op jit(solution)/shard_map/cond
  64.2 17.7 %copy-start.2 = (f32[256,2048]{1,0:T(8,128)}, f32[256,2048]{1,0:T(8,128)S(1)}, u32[]{:S(2)}) copy-start(f32[256,2048]{1,0:T(8,128)S(1)} %get-tuple-element.125.mix_ref) | copy-start | bytes 6291460 | tf_op jit(solution)/shard_map/cond
  67.6 14.4 %copy-start.12 = (f32[128,2048]{1,0:T(8,128)}, f32[128,2048]{1,0:T(8,128)S(1)}, u32[]{:S(2)}) copy-start(f32[128,2048]{1,0:T(8,128)S(1)} %get-tuple-element.128.mix_head_ref) | copy-start | bytes 3145732 | tf_op jit(solution)/shard_map/cond
  67.6 4.6 %collective-permute-start.8 = (f32[8,256]{1,0:T(8,128)S(1)}, f32[8,256]{1,0:T(8,128)S(1)}, u32[]{:S(2)}, u32[]{:S(2)}) collective-permute-start(f32[8,256]{1,0:T(8,128)S(1)} %get-tuple-element.127.s0), channel_id=1, source_target_pairs={{0,3},{1,0},{2,1},{3,2},{4,7},{5,4},{6,5},{7,6},{8,11},{9,8},{10,9... | collective-permute-start | bytes 24584 | tf_op jit(solution)/shard_map/cond/branch_1_fun/ppermute | solution.py:925
  71.4 4.0 %collective-permute-start.7 = (f32[8,256]{1,0:T(8,128)S(1)}, f32[8,256]{1,0:T(8,128)S(1)}, u32[]{:S(2)}, u32[]{:S(2)}) collective-permute-start(f32[8,256]{1,0:T(8,128)S(1)} %get-tuple-element.127.s0), channel_id=1, source_target_pairs={{0,2},{1,3},{2,0},{3,1},{4,6},{5,7},{6,4},{7,5},{8,10},{9,11},{10,... | collective-permute-start | bytes 24584 | tf_op jit(solution)/shard_map/cond/branch_1_fun/ppermute | solution.py:925
  71.4 4.0 %collective-permute-start.6 = (f32[8,256]{1,0:T(8,128)S(1)}, f32[8,256]{1,0:T(8,128)S(1)}, u32[]{:S(2)}, u32[]{:S(2)}) collective-permute-start(f32[8,256]{1,0:T(8,128)S(1)} %get-tuple-element.127.s0), channel_id=1, source_target_pairs={{0,1},{1,2},{2,3},{3,0},{4,5},{5,6},{6,7},{7,4},{8,9},{9,10},{10,1... | collective-permute-start | bytes 24584 | tf_op jit(solution)/shard_map/cond/branch_1_fun/ppermute | solution.py:925
  75.4 6.5 %copy-start.21 = (bf16[128,640]{1,0:T(8,128)(2,1)S(1)}, bf16[128,640]{1,0:T(8,128)(2,1)}, u32[]{:S(2)}) copy-start(bf16[128,640]{1,0:T(8,128)(2,1)} %copy-done.20) | copy-start | bytes 491524 | tf_op jit(solution)/shard_map/cond
  75.4 6.6 %copy-start.41 = (f32[2048]{0:T(1024)S(1)}, f32[2048]{0:T(1024)}, u32[]{:S(2)}) copy-start(f32[2048]{0:T(1024)} %copy-done.40) | copy-start | bytes 24580 | tf_op jit(solution)/shard_map/cond
  78.0 11.9 %collective-permute-start.9 = (bf16[128,2048]{1,0:T(8,128)(2,1)}, bf16[128,2048]{1,0:T(8,128)(2,1)S(1)}, u32[]{:S(2)}, u32[]{:S(2)}) collective-permute-start(bf16[128,2048]{1,0:T(8,128)(2,1)} %branch_1_fun.21), channel_id=1, source_target_pairs={{4,0},{8,4},{12,8},{16,12},{20,16},{24,20},{28,24},{32,28},{36,32}... | collective-permute-start | bytes 1572872 | tf_op jit(solution)/shard_map/cond/branch_1_fun/ppermute | solution.py:863
  90.0 0.8 copy-start.18
  90.8 7.0 %copy-start.42 = (f32[2048]{0:T(1024)S(1)}, f32[2048]{0:T(1024)}, u32[]{:S(2)}) copy-start(f32[2048]{0:T(1024)} %copy-done.40) | copy-start | bytes 24580 | tf_op jit(solution)/shard_map/cond
  90.8 31.1 %all-to-all-start.4 = ((bf16[32,8,3328]{2,1,0:T(8,128)(2,1)}), bf16[32,8,3328]{2,1,0:T(8,128)(2,1)S(1)}, u32[]{:S(2)}, u32[]{:S(2)}) async-start(bf16[32,8,3328]{2,1,0:T(8,128)(2,1)} %bitcast.42), calls=%async_computation.4 | async-start | bytes 3407872 | tf_op jit(solution)/shard_map/cond/branch_1_fun/all_to_all | solution.py:856
  97.8 1.6 copy-start.3
  99.4 1.7 %copy-start.9 = (bf16[640,2048]{1,0:T(8,128)(2,1)S(1)}, bf16[640,2048]{1,0:T(8,128)(2,1)}, u32[]{:S(2)}) copy-start(bf16[640,2048]{1,0:T(8,128)(2,1)} %copy-done.8) | copy-start | bytes 7864324 | tf_op jit(solution)/shard_map/cond
  101.1 1.2 copy-start.13
  102.3 6.0 %copy-start.19 = (bf16[128,2048]{1,0:T(8,128)(2,1)S(1)}, bf16[128,2048]{1,0:T(8,128)(2,1)}, u32[]{:S(2)}) copy-start(bf16[128,2048]{1,0:T(8,128)(2,1)} %copy-done.18) | copy-start | bytes 1572868 | tf_op jit(solution)/shard_map/cond
  102.3 6.0 %copy-start.29 = (bf16[384,128]{1,0:T(8,128)(2,1)S(1)}, bf16[384,128]{1,0:T(8,128)(2,1)}, u32[]{:S(2)}) copy-start(bf16[384,128]{1,0:T(8,128)(2,1)} %copy-done.28) | copy-start | bytes 294916 | tf_op jit(solution)/shard_map/cond
  102.3 6.0 %copy-start.31 = (bf16[128,384]{1,0:T(8,128)(2,1)S(1)}, bf16[128,384]{1,0:T(8,128)(2,1)}, u32[]{:S(2)}) copy-start(bf16[128,384]{1,0:T(8,128)(2,1)} %copy-done.30) | copy-start | bytes 294916 | tf_op jit(solution)/shard_map/cond
  102.3 6.0 %copy-start.33 = (bf16[384,128]{1,0:T(8,128)(2,1)S(1)}, bf16[384,128]{1,0:T(8,128)(2,1)}, u32[]{:S(2)}) copy-start(bf16[384,128]{1,0:T(8,128)(2,1)} %copy-done.32) | copy-start | bytes 294916 | tf_op jit(solution)/shard_map/cond
  122.8 27.1 %all-to-all-start.5 = ((bf16[32,8,3072]{2,1,0:T(8,128)(2,1)}), bf16[32,8,3072]{2,1,0:T(8,128)(2,1)S(1)}, u32[]{:S(2)}, u32[]{:S(2)}) async-start(bf16[32,8,3072]{2,1,0:T(8,128)(2,1)} %bitcast.39), calls=%async_computation.5 | async-start | bytes 3145728 | tf_op jit(solution)/shard_map/cond/branch_1_fun/all_to_all | solution.py:856
  128.3 23.1 %collective-permute-start.10 = (bf16[256,2048]{1,0:T(8,128)(2,1)}, bf16[256,2048]{1,0:T(8,128)(2,1)}, u32[]{:S(2)}, u32[]{:S(2)}) collective-permute-start(bf16[256,2048]{1,0:T(8,128)(2,1)} %slice.37), channel_id=1, source_target_pairs={{0,4},{4,0},{8,12},{12,8},{16,20},{20,16},{24,28},{28,24},{32,36},... | collective-permute-start | bytes 3145736 | tf_op jit(solution)/shard_map/cond/branch_1_fun/ppermute | solution.py:867
  150.0 4.8 %collective-permute-start.11 = (bf16[256,2048]{1,0:T(8,128)(2,1)S(1)}, bf16[256,2048]{1,0:T(8,128)(2,1)S(1)}, u32[]{:S(2)}, u32[]{:S(2)}) collective-permute-start(bf16[256,2048]{1,0:T(8,128)(2,1)S(1)} %slice.36), channel_id=1, source_target_pairs={{0,4},{4,0},{8,12},{12,8},{16,20},{20,16},{24,28},{28,24},{32,36},... | collective-permute-start | bytes 3145736 | tf_op jit(solution)/shard_map/cond/branch_1_fun/ppermute | solution.py:867

commit v6 on v5

--- a/solution.py
+++ b/solution.py
@@ -23,7 +23,7 @@
 WIN = TAPS + ROWS
 FREQ = 320
 CB = 512
-WIDE, NARROW = 1024, 256
+WIDE, NARROW = 1024, 128
 
 
 def step_width(pair):
@@ -148,6 +148,7 @@
     if halves == 2:
         first, second, q_refs, out_ref, packs = None, refs[:2], refs[2:4], refs[4], refs[5:]
     step = pl.program_id(0)
+    wide = out_ref.shape[1]
 
     @pl.when(step == 0)
     def _():
@@ -162,14 +163,17 @@
     @pl.when(step < blocks)
     def _():
         if first is None:
-            out_ref[...] = packed([ref[...] for ref in second])
+            out_ref[...] = packed([second[0][...], second[1][:, block_of(step, wide)]])
         else:
             product = first[0][...].astype(F32) * second[0][...].astype(F32)
             out_ref[...] = packed([product.astype(BF)])
 
     @pl.when(step >= blocks)
     def _():
-        out_ref[...] = packed([ref[...] for ref in q_refs])
+        rows = [q_refs[0][...]]
+        if halves == 2:
+            rows.append(q_refs[1][:, block_of(step - blocks, wide)])
+        out_ref[...] = packed(rows)
 
 
 def pack_arrivals(pair, slots, early, late):
@@ -182,8 +186,10 @@
         functools.partial(pack_kernel, halves, blocks),
         grid=(2 * blocks,),
         in_specs=[RESIDENT]
-        + [cols(SLOTS, wide, last=blocks - 1)] * len(early)
-        + [pl.BlockSpec((SLOTS, wide), lambda j: (0, jnp.maximum(j - blocks, 0)))] * halves,
+        + [cols(SLOTS, wide, last=blocks - 1)]
+        + [RESIDENT if halves == 2 else cols(SLOTS, wide, last=blocks - 1)]
+        + [pl.BlockSpec((SLOTS, wide), lambda j: (0, jnp.maximum(j - blocks, 0)))]
+        + [RESIDENT] * (halves - 1),
         out_specs=cols(sent, wide),
         out_shape=sds((sent, 2 * width), BF),
         scratch_shapes=[pltpu.VMEM((sent, SLOTS), BF)] * halves,
@@ -214,7 +220,7 @@
     def _():
         place[...] = onehot(iota(place.shape, 0) + (ROWS - TAPS) == pos_row[...])
 
-    tail_ref[...] = dot(place[...], recv_ref[...]).astype(BF)
+    tail_ref[...] = dot(place[...], recv_ref[:, block_of(pl.program_id(0), tail_ref.shape[1])]).astype(BF)
 
 
 def place_tail(wide, pos_row, received, width):
@@ -222,13 +228,13 @@
     return pl.pallas_call(
         place_tail_kernel,
         grid=(width // wide,),
-        in_specs=[RESIDENT, cols(sent, wide)],
+        in_specs=[RESIDENT, RESIDENT],
         out_specs=cols(TAPS, wide),
         out_shape=sds((TAPS, width), BF),
         scratch_shapes=[pltpu.VMEM((TAPS, sent), BF)],
         compiler_params=params(),
         cost_estimate=cost(2 * sent * TAPS * width, 2 * width * (sent + TAPS)),
-    )(*kept(pos_row), received)
+    )(*kept(pos_row, received))
 
 
 def wave_of(turns):
@@ -236,7 +242,7 @@
 
     def series(first):
         total = jnp.zeros_like(square)
-        for power in range(first + 18, first - 1, -2):
+        for power in range(first + 16, first - 1, -2):
             term = (-1.0) ** ((power - first) // 2) / math.factorial(power)
             total = total * square + term
         return total
@@ -330,7 +336,7 @@
 
 
 def conv_kernel(
-    pos_row, cc_own, cc_own_t, bb, recv_p, recv_q, filt, residual, cot, gain,
+    pos_row, cc_own, cc_own_t, bb, recv, filt, residual, cot, gain,
     q_ref, mix_ref, x_ref, f_ref, sums_ref,
     place, acc,
 ):
@@ -341,9 +347,9 @@
         place[...] = onehot(iota(place.shape, 0) == pos_row[...])
         acc[...] = jnp.zeros_like(acc)
 
-    at = block_of(step, recv_p.shape[1])
-    product = dot(place[...], recv_p[...]).astype(BF)
-    q = dot(place[...], recv_q[...])
+    at = block_of(step, filt.shape[1])
+    product = dot(place[...], recv[:, at]).astype(BF)
+    q = dot(place[...], recv[:, block_of(step + pl.num_programs(0), filt.shape[1])])
     q_ref[:, at] = q.astype(BF)
     x = dot(cc_own[...], product)
     f = dot(bb[...], filt[...].astype(BF))
@@ -372,8 +378,7 @@
             RESIDENT,
             RESIDENT,
             RESIDENT,
-            cols(sent, wide),
-            pl.BlockSpec((sent, wide), lambda j: (0, blocks + j)),
+            RESIDENT,
             cols(TAPS, wide),
             cols(ROWS, wide),
             cols(ROWS, wide),
@@ -390,7 +395,7 @@
         scratch_shapes=[pltpu.VMEM((ROWS, sent), BF), pltpu.VMEM((TAPS, 128), F32)],
         compiler_params=params(),
         cost_estimate=cost(4e9, width * 6000),
-    )(*kept(pos_row, cc_own, cc_own_t, bb), received, received, *hbm(filt, residual, cot), gain)
+    )(*kept(pos_row, cc_own, cc_own_t, bb, received), *hbm(filt, residual, cot), gain)
 
 
 def crossing(value):
@@ -399,7 +404,7 @@
 
 def head_kernel(
     cc_halo, cc_head_t, halo, f_ref, q_ref, mix_ref, residual, cot, gain, sums_ref,
-    mix_head_ref, out_sums_ref,
+    mix_head_ref, summed_ref, scaled_ref, out_sums_ref,
     acc,
 ):
     step = pl.program_id(0)
@@ -415,7 +420,10 @@
     mix = mix_ref[:TAPS, at] + dot(cc_head_t[...], y)
     mix_head_ref[:, at] = mix
     summed = residual[...].astype(F32) + q_ref[:TAPS, at].astype(F32) * mix
-    acc[...] += sums_of(summed, cot[...].astype(F32) * gain[...])
+    scaled = cot[...].astype(F32) * gain[...]
+    summed_ref[:, at] = summed
+    scaled_ref[:, at] = scaled
+    acc[...] += sums_of(summed, scaled)
 
     @pl.when(step == pl.num_programs(0) - 1)
     def _():
@@ -440,8 +448,8 @@
             cols(1, wide),
             RESIDENT,
         ],
-        out_specs=[RESIDENT, whole((8, ROWS))],
-        out_shape=[pltpu.VMEM((TAPS, width), F32), jax.ShapeDtypeStruct((8, ROWS), F32)],
+        out_specs=[RESIDENT] * 3 + [whole((8, ROWS))],
+        out_shape=[pltpu.VMEM((TAPS, width), F32)] * 3 + [jax.ShapeDtypeStruct((8, ROWS), F32)],
         scratch_shapes=[pltpu.VMEM((TAPS, 128), F32)],
         compiler_params=params(),
         cost_estimate=cost(6e8, width * 3000),
@@ -483,13 +491,17 @@
     )(cc, bb, head, tail, taps)
 
 
-def tap_rows(pair, shape, tap_dim, step):
+def tap_rows(pair, shape, tap_dim, block):
     tap = iota(shape, tap_dim)
-    return (tap // 4) * pair + tap % 4 + 4 * (step % (pair // 4))
-
-
-def extra_cols(pair, width):
-    return (width // CB) * 4 // pair * CB, width // pair
+    return (tap // 4) * pair + tap % 4 + 4 * block
+
+
+def part_cols(pair):
+    return 4 * WIDE // pair
+
+
+def piece_cols(pair):
+    return WIDE + part_cols(pair) + 128
 
 
 def row_stats(s0, s1, s2, s3, stats):
@@ -504,35 +516,30 @@
     return inv * scaled - summed * (inv * inv * inv) * stats[:, 1:2] / D
 
 
-def head_grad_kernel(
-    s0, s1, s2, s3, q_ref, mix_head_ref, res_ref, cot_ref, gain_ref, head_ref, stats
-):
+def head_grad_kernel(s0, s1, s2, s3, q_ref, summed_ref, scaled_ref, head_ref, stats):
     step = pl.program_id(0)
 
     @pl.when(step == 0)
     def _():
         row_stats(s0, s1, s2, s3, stats)
 
-    at = block_of(step, res_ref.shape[1])
-    q = q_ref[:TAPS, at].astype(F32)
-    summed = res_ref[...].astype(F32) + q * mix_head_ref[:, at]
-    d_summed = d_summed_of(stats[:TAPS], summed, cot_ref[...].astype(F32) * gain_ref[...])
-    head_ref[...] = (d_summed * q).astype(BF)
-
-
-def head_grad(wide, sums, q, mix_head, residual, cot, gain):
+    at = block_of(step, head_ref.shape[1])
+    d_summed = d_summed_of(stats[:TAPS], summed_ref[:, at], scaled_ref[:, at])
+    head_ref[...] = (d_summed * q_ref[:TAPS, at].astype(F32)).astype(BF)
+
+
+def head_grad(wide, sums, q, summed_head, scaled_head):
     width = q.shape[1]
     return pl.pallas_call(
         head_grad_kernel,
         grid=(width // wide,),
-        in_specs=[RESIDENT] * 4
-        + [RESIDENT, RESIDENT, cols(TAPS, wide), cols(TAPS, wide), cols(1, wide)],
+        in_specs=[RESIDENT] * 7,
         out_specs=cols(TAPS, wide),
         out_shape=sds((TAPS, width), BF),
         scratch_shapes=[pltpu.VMEM((ROWS, 128), F32)],
         compiler_params=params(),
         cost_estimate=cost(width * TAPS * 10, width * TAPS * 6),
-    )(*kept(*sums, q, mix_head), *hbm(residual, cot), gain)
+    )(*kept(*sums, q, summed_head, scaled_head))
 
 
 def mixture_block(mix_ref, mix_head_ref, at):
@@ -540,107 +547,62 @@
 
 
 def backward_kernel(
-    pair, blocks,
+    pair,
     s0, s1, s2, s3, pos_row, cc_own, cc_halo, bb_t, q_ref, mix_ref, mix_head_ref, x_ref,
     halo_ref, res_ref, cot_ref, gain_ref,
     dmix_ref, out_ref,
-    give, stats, taps_acc, gain_acc,
+    give, stats,
 ):
     step = pl.program_id(0)
-    per = pair // 4
-    span = res_ref.shape[1]
-    parts = taps_acc.shape[0]
+    part = part_cols(pair)
     sent = SHARDS * pair
 
     @pl.when(step == 0)
     def _():
         give[...] = onehot(as_column(pos_row[...]) == iota(give.shape, 1))
         row_stats(s0, s1, s2, s3, stats)
-        taps_acc[...] = jnp.zeros_like(taps_acc)
-        gain_acc[...] = jnp.zeros_like(gain_acc)
-
-    @pl.when(step < blocks)
-    def _():
-        at = block_of(jnp.minimum(step, blocks - 1), span)
-        q = q_ref[:, at].astype(F32)
-        mix = mixture_block(mix_ref, mix_head_ref, at)
-        summed = res_ref[...].astype(F32) + q * mix
-        cot = cot_ref[...].astype(F32)
-        gain_part = jnp.sum(cot * summed * stats[:, 0:1], axis=0, keepdims=True)
-        d_summed = d_summed_of(stats, summed, cot * gain_ref[...])
-        out_ref[...] = dot(give[...], (d_summed * mix).astype(BF)).astype(BF)
-        d_mix = (d_summed * q).astype(BF)
-        dmix_ref[...] = d_mix
-        g = dot(cc_own[...], d_mix)
-        x = x_ref[:, at].astype(F32)
-        reach = dot(cc_halo[...], halo_ref[...])
-        xr = jnp.concatenate([x[:CROSS_FREQ] + reach[:CROSS_FREQ], x[CROSS_FREQ:FREQ]], axis=0)
-        xi = jnp.concatenate(
-            [x[FREQ : FREQ + CROSS_FREQ] + reach[CROSS_FREQ:], x[FREQ + CROSS_FREQ :]], axis=0
-        )
-        taps = dot(bb_t[...], conj_product(g[:FREQ], g[FREQ:], xr, xi)).astype(BF)
-        for i in range(span // CB):
-            block = jnp.minimum(step, blocks - 1) * (span // CB) + i
-            spread = onehot(iota((sent, TAPS), 0) == tap_rows(pair, (sent, TAPS), 1, block))
-            taps_acc[block // per] += dot(spread, taps[:, CB * i : CB * (i + 1)])
-        wide = gain_acc.shape[1]
-        for i in range(span // wide):
-            row = iota(gain_acc.shape, 0) == step * (span // wide) + i
-            gain_acc[...] += jnp.where(row, gain_part[:, wide * i : wide * (i + 1)], 0.0)
-
-    def extra(at):
-        if at < CB * parts:
-            return taps_acc[at // CB]
-        wide = gain_acc.shape[1]
-        return jnp.broadcast_to(gain_acc[...][None], (SHARDS, pair, wide)).reshape(sent, wide)
-
-    starts = [CB * part for part in range(parts + 1)]
-    for late in range(pl.cdiv(starts[-1] + 1, span)):
-
-        @pl.when(step == blocks + late)
-        def _(late=late):
-            for at in starts:
-                if at // span == late:
-                    value = extra(at).astype(BF)
-                    out_ref[:, at % span : at % span + value.shape[1]] = value
+
+    at = block_of(step, WIDE)
+    q = q_ref[:, at].astype(F32)
+    mix = mixture_block(mix_ref, mix_head_ref, at)
+    summed = res_ref[...].astype(F32) + q * mix
+    cot = cot_ref[...].astype(F32)
+    gain_part = jnp.sum(cot * summed * stats[:, 0:1], axis=0, keepdims=True)
+    d_summed = d_summed_of(stats, summed, cot * gain_ref[...])
+    out_ref[:, :WIDE] = dot(give[...], (d_summed * mix).astype(BF)).astype(BF)
+    d_mix = (d_summed * q).astype(BF)
+    dmix_ref[...] = d_mix
+    g = dot(cc_own[...], d_mix)
+    x = x_ref[:, at].astype(F32)
+    reach = dot(cc_halo[...], halo_ref[...])
+    xr = jnp.concatenate([x[:CROSS_FREQ] + reach[:CROSS_FREQ], x[CROSS_FREQ:FREQ]], axis=0)
+    xi = jnp.concatenate(
+        [x[FREQ : FREQ + CROSS_FREQ] + reach[CROSS_FREQ:], x[FREQ + CROSS_FREQ :]], axis=0
+    )
+    taps = dot(bb_t[...], conj_product(g[:FREQ], g[FREQ:], xr, xi)).astype(BF)
+    total = jnp.zeros((sent, part), F32)
+    for block in range(WIDE // part):
+        spread = onehot(iota((sent, TAPS), 0) == tap_rows(pair, (sent, TAPS), 1, block))
+        total = total + dot(spread, taps[:, part * block : part * (block + 1)])
+    out_ref[:, WIDE : WIDE + part] = total.astype(BF)
+    rows = [gain_part[:, 128 * r : 128 * (r + 1)] for r in range(WIDE // 128)]
+    rows = jnp.concatenate(rows + [jnp.zeros((pair - len(rows), 128), F32)] * (pair > len(rows)), axis=0)
+    rows = jnp.broadcast_to(rows[None], (SHARDS, pair, 128)).reshape(sent, 128)
+    out_ref[:, WIDE + part :] = rows.astype(BF)
 
 
 def backward(pair, sums, pos_row, cc_own, cc_halo, bb_t, q, mix, mix_head, x, halo, residual, cot, gain):
-    wide = max(CB, step_width(pair))
     width = q.shape[1]
-    blocks = width // wide
-    last = blocks - 1
+    steps = width // WIDE
     sent = SHARDS * pair
-    part_cols, gain_cols = extra_cols(pair, width)
-    parts = part_cols // CB
-    return pl.pallas_call(
-        functools.partial(backward_kernel, pair, blocks),
-        grid=(blocks + pl.cdiv(part_cols + gain_cols, wide),),
-        in_specs=[RESIDENT] * 4
-        + [
-            RESIDENT,
-            RESIDENT,
-            RESIDENT,
-            RESIDENT,
-        ]
-        + [RESIDENT] * 4
-        + [
-            cols(TAPS, wide, last=last),
-            cols(ROWS, wide, last=last),
-            cols(ROWS, wide, last=last),
-            cols(1, wide, last=last),
-        ],
-        out_specs=[cols(ROWS, wide, last=last), cols(sent, wide)],
-        out_shape=[
-            sds((ROWS, width), BF),
-            sds((sent, width + part_cols + gain_cols), BF),
-        ],
-        scratch_shapes=[
-            pltpu.VMEM((sent, ROWS), BF),
-            pltpu.VMEM((ROWS, 128), F32),
-            pltpu.VMEM((parts, sent, CB), F32),
-            pltpu.VMEM((pair, gain_cols), F32),
-        ],
+    return pl.pallas_call(
+        functools.partial(backward_kernel, pair),
+        grid=(steps,),
+        in_specs=[RESIDENT] * 12
+        + [cols(TAPS, WIDE), cols(ROWS, WIDE), cols(ROWS, WIDE), cols(1, WIDE)],
+        out_specs=[cols(ROWS, WIDE), cols(sent, piece_cols(pair))],
+        out_shape=[sds((ROWS, width), BF), sds((sent, steps * piece_cols(pair)), BF)],
+        scratch_shapes=[pltpu.VMEM((sent, ROWS), BF), pltpu.VMEM((ROWS, 128), F32)],
         compiler_params=params(),
         cost_estimate=cost(2e9, width * 6000),
     )(
@@ -725,46 +687,48 @@
             cols(TAPS, wide),
         ],
         out_specs=cols(sent, wide),
-        out_shape=sds((sent, width + extra_cols(pair, width)[0]), BF),
+        out_shape=sds((sent, width + CB), BF),
         scratch_shapes=[pltpu.VMEM((sent, ROWS), BF)],
         compiler_params=params(),
         cost_estimate=cost(2 * sent * ROWS * width, width * 2400),
     )(*kept(pos_row, *onward), *hbm(own), from_next, *hbm(filt))
 
 
-def reduce_kernel(pair, taps_ref, gain_ref, rows_ref, out_ref, d_gain_ref):
-    def over_sources(ref):
-        value = ref[...].astype(F32)
-        return jnp.sum(value.reshape(SHARDS, pair, value.shape[1]), axis=0)
-
-    total = over_sources(taps_ref)
-    out_ref[...] = (
-        jnp.broadcast_to(total[None], (SHARDS, pair, CB)).reshape(SHARDS * pair, CB).astype(BF)
-    )
-    d_gain_ref[...] = over_sources(gain_ref)
+def reduce_kernel(pair, pieces, received_ref, rows_ref, out_ref, d_gain_ref):
+    def over_sources(at, size):
+        value = received_ref[:, at : at + size].astype(F32)
+        return jnp.sum(value.reshape(SHARDS, pair, size), axis=0)
+
+    part = part_cols(pair)
+    starts = [piece_cols(pair) * piece + WIDE for piece in range(pieces)]
+    totals = [over_sources(at, part) for at in starts]
+    if pair == PAIR:
+        both = jnp.broadcast_to(jnp.concatenate(totals, axis=1)[None], (SHARDS, pair, CB))
+    else:
+        both = jnp.broadcast_to(
+            jnp.concatenate(totals, axis=0)[None], (SHARDS // 2, 2 * pair, CB)
+        )
+    out_ref[...] = both.reshape(SHARDS * pair, CB).astype(BF)
+    for piece, at in enumerate(starts):
+        d_gain_ref[piece] = over_sources(at + part, 128)[:8]
 
 
 def reduce_parts(pair, received, rows, width):
-    part_cols, gain_cols = extra_cols(pair, width)
-    blocks = width // CB
     sent = SHARDS * pair
-    return pl.pallas_call(
-        functools.partial(reduce_kernel, pair),
-        grid=(part_cols // CB,),
-        in_specs=[
-            pl.BlockSpec((sent, CB), lambda j: (0, blocks + j)),
-            pl.BlockSpec((sent, gain_cols), lambda j: (0, (width + part_cols) // gain_cols)),
-            pl.BlockSpec(memory_space=pl.ANY),
+    pieces = width // WIDE
+    return pl.pallas_call(
+        functools.partial(reduce_kernel, pair, pieces),
+        grid=(1,),
+        in_specs=[RESIDENT, pl.BlockSpec(memory_space=pl.ANY)],
+        out_specs=[
+            pl.BlockSpec((sent, CB), lambda j: (0, width // CB)),
+            whole((pieces, 8, 128)),
         ],
-        out_specs=[
-            pl.BlockSpec((sent, CB), lambda j: (0, blocks + j)),
-            whole((pair, gain_cols)),
-        ],
-        out_shape=[sds(rows.shape, BF), jax.ShapeDtypeStruct((pair, gain_cols), F32)],
-        input_output_aliases={2: 0},
-        compiler_params=params(),
-        cost_estimate=cost(sent * part_cols, sent * part_cols * 4),
-    )(received, received, *hbm(rows))
+        out_shape=[sds(rows.shape, BF), jax.ShapeDtypeStruct((pieces, 8, 128), F32)],
+        input_output_aliases={1: 0},
+        compiler_params=params(),
+        cost_estimate=cost(sent * CB, sent * CB * 4),
+    )(*kept(received), *hbm(rows))
 
 
 def build_home(pair, slots_ref, homes):
@@ -787,68 +751,75 @@
     def _():
         build_home(pair, slots_ref, homes)
 
-    out_ref[...] = homecoming(backs, homes).astype(BF)
+    piece = piece_cols(pair)
+    at = pl.ds(pl.multiple_of(pl.program_id(0) * piece, 128), WIDE)
+    rows = [ref.at[:, at] for ref in backs]
+    out_ref[...] = homecoming(rows, homes).astype(BF)
 
 
 def home_rows(pair, slots, backs, width):
-    wide = step_width(pair)
     sent = SHARDS * pair
     halves = len(backs)
     return pl.pallas_call(
         functools.partial(home_rows_kernel, pair, halves),
-        grid=(width // wide,),
-        in_specs=[RESIDENT] + [cols(sent, wide)] * halves,
-        out_specs=cols(SLOTS, wide),
+        grid=(width // WIDE,),
+        in_specs=[RESIDENT] + [RESIDENT] * halves,
+        out_specs=cols(SLOTS, WIDE),
         out_shape=sds((SLOTS, width), BF),
         scratch_shapes=[pltpu.VMEM((SLOTS, sent), BF)] * halves,
         compiler_params=params(),
         cost_estimate=cost(
             2 * sent * SLOTS * width * halves, 2 * width * (sent * halves + SLOTS)
         ),
-    )(*kept(slots), *backs)
-
-
-def home_product_kernel(pair, halves, slots_ref, taps_ref, k_ref, v_ref, *refs):
-    backs, (dk_ref, dv_ref, filt_ref), homes = refs[:halves], refs[halves : halves + 3], refs[halves + 3 :]
+    )(*kept(slots, *backs))
+
+
+def home_product_kernel(pair, halves, index_ref, slots_ref, k_ref, v_ref, *refs):
+    backs, refs = refs[:halves], refs[halves:]
+    (dk_ref, dv_ref, filt_ref), homes = refs[:3], refs[3:]
     step = pl.program_id(0)
 
     @pl.when(step == 0)
     def _():
         build_home(pair, slots_ref, homes)
 
-    grad = homecoming(backs, homes)
+    grad = homecoming([ref.at[:, block_of(step, WIDE)] for ref in backs], homes)
     dk_ref[...] = (grad * v_ref[...].astype(F32)).astype(BF)
     dv_ref[...] = (grad * k_ref[...].astype(F32)).astype(BF)
+    part = part_cols(pair)
+    width = backs[0].shape[1] - CB
+    taps_refs = [ref.at[:, width:] for ref in backs]
+    if pair == PAIR:
+        taps = taps_refs[0][:, block_of(step, part)]
+    else:
+        core = lax.rem(index_ref[0], 2)
+        taps = jnp.where(core == step, taps_refs[0][...], taps_refs[1][...])
     shape = (TAPS, SHARDS * pair)
-    for i in range(k_ref.shape[1] // CB):
-        block = step * (k_ref.shape[1] // CB) + i
+    for block in range(WIDE // part):
         gather = onehot(iota(shape, 1) == tap_rows(pair, shape, 0, block))
-        part = taps_ref[:, block_of(block // (pair // 4))]
-        filt_ref[:, CB * i : CB * (i + 1)] = dot(gather, part)
-
-
-def home_product(pair, slots, back, backs, k, v):
-    wide = max(CB, step_width(pair))
+        filt_ref[:, part * block : part * (block + 1)] = dot(gather, taps)
+
+
+def home_product(pair, my_index, slots, backs, k, v):
     width = k.shape[1]
-    part_cols = extra_cols(pair, width)[0]
     sent = SHARDS * pair
     halves = len(backs)
     return pl.pallas_call(
         functools.partial(home_product_kernel, pair, halves),
-        grid=(width // wide,),
+        grid=(width // WIDE,),
         in_specs=[
-            RESIDENT,
-            pl.BlockSpec((sent, part_cols), lambda j: (0, width // part_cols)),
-            cols(SLOTS, wide),
-            cols(SLOTS, wide),
+            pl.BlockSpec(memory_space=pltpu.SMEM),
+            RESIDENT,
+            cols(SLOTS, WIDE),
+            cols(SLOTS, WIDE),
         ]
-        + [cols(sent, wide)] * halves,
-        out_specs=[cols(SLOTS, wide), cols(SLOTS, wide), cols(TAPS, wide)],
+        + [RESIDENT] * halves,
+        out_specs=[cols(SLOTS, WIDE), cols(SLOTS, WIDE), cols(TAPS, WIDE)],
         out_shape=[sds((SLOTS, width), BF), sds((SLOTS, width), BF), sds((TAPS, width), F32)],
         scratch_shapes=[pltpu.VMEM((SLOTS, sent), BF)] * halves,
         compiler_params=params(),
         cost_estimate=cost(2 * sent * SLOTS * width, 2 * width * (sent + 5 * SLOTS)),
-    )(*kept(slots), back, *hbm(k, v), *backs)
+    )(my_index.reshape(1), *kept(slots), *hbm(k, v), *kept(*backs))
 
 
 def exchange(pair, rows):
@@ -893,7 +864,8 @@
     slots = send_plan(pair, my_index, dest_pos)
     if shared:
         product_in, product_other, q_other = others
-        early, late = [*hbm(product_in), product_other], [*hbm(q_in), q_other]
+        early = [*hbm(product_in), *kept(product_other)]
+        late = [*hbm(q_in), *kept(q_other)]
     else:
         early, late = hbm(k_in, v_in), hbm(q_in)
     sent_rows = pack_arrivals(pair, slots, early, late)
@@ -918,13 +890,13 @@
     q, mix, x, f, sums = forward(
         wide, pos_row, cc_own, cc_own_t, bb, received, mr_filter, residual, cotangent, gain
     )
-    mix_head, sums = forward_head(
+    mix_head, summed_head, scaled_head, sums = forward_head(
         wide, cc_halo, cc_head_t, halo, f, q, mix, residual, cotangent, gain, sums
     )
     all_sums = [sums] + [
         lax.ppermute(sums, "mp", [(i, (i + k) % 4) for i in range(4)]) for k in (1, 2, 3)
     ]
-    head = head_grad(wide, all_sums, q, mix_head, residual, cotangent, gain)
+    head = head_grad(wide, all_sums, q, summed_head, scaled_head)
     d_mix, sent_dq = backward(
         pair, all_sums, pos_row, cc_own, cc_halo, bb_t, q, mix, mix_head, x, halo,
         residual, cotangent, gain,
@@ -939,10 +911,10 @@
     back_p = exchange(pair, sent_dp)
     backs_q, backs_p = [back_q], [back_p]
     if shared:
-        backs_q.append(swap(back_q[:, :width]))
-        backs_p.append(swap(back_p[:, :width]))
+        backs_q.append(swap(back_q))
+        backs_p.append(swap(back_p))
     d_q_in = home_rows(pair, slots, backs_q, width)
-    d_k_in, d_v_in, d_filter = home_product(pair, slots, back_p, backs_p, k_in, v_in)
+    d_k_in, d_v_in, d_filter = home_product(pair, my_index, slots, backs_p, k_in, v_in)
     return (normed, d_residual, d_q_in, d_k_in, d_v_in, d_filter, d_gain.reshape(width))
 
 

time: 160 us -> 156 us (0.975)
  waiting for transfers between devices: 57.9 us -> 55.1 us
    all_to_all x3, waiting for transfers between devices: 50.8 us -> 47 us  [exchange(): lax.all_to_all(shards, 'seq', split_axis=0, concat_axis=0, tiled=True)]
    cond x53 -> x56, local copies, waits for them, and re-layouts: 10.5 us -> 11.6 us
  transfers between devices with their start and end apart: 12 -> 12, of which waited for: 7 -> 8; matrix products, arithmetic and copies ran while one was open for 5% -> 4% of each run, Pallas kernels for 17% -> 17%
where the time goes in v6:
time: 156 us; the launch traced here: 155 us
  waiting for transfers between devices  55.1 us (35%)
  Pallas kernels  48.8 us (31%)
  starting transfers between devices  32.5 us (21%)
  local copies, waits for them, and re-layouts  12.3 us (8%)
  other arithmetic  4.81 us (3%)
    all_to_all x3, waiting for transfers between devices, exchange(): lax.all_to_all(shards, 'seq', split_axis=0, concat_axis=0, tiled=True)  47 us
    all_to_all x3, starting transfers between devices, exchange(): lax.all_to_all(shards, 'seq', split_axis=0, concat_axis=0, tiled=True)  20 us
    cond x56, local copies, waits for them, and re-layouts  11.6 us
    pallas_call x1, Pallas kernels, backward(): pl.pallas_call(functools.partial(backward_kernel, pair), grid=(steps,), i...  7.16 us
    pallas_call x1, Pallas kernels, finish(): pl.pallas_call(finish_kernel, grid=(width // wide,), in_specs=[RESIDENT]...  6 us
    pallas_call x1, Pallas kernels, pack_arrivals(): pl.pallas_call(functools.partial(pack_kernel, halves, blocks), grid=(2 *...  5.78 us
    ppermute x2, starting transfers between devices, shift(): return lax.ppermute(value, 'seq', pairs)  5.76 us
    pallas_call x1, Pallas kernels, forward(): pl.pallas_call(conv_kernel, grid=(blocks,), in_specs=[RESIDENT, RESIDENT,...  5.29 us
  transfers between devices with their start and end apart: 12, of which 8 were waited for; matrix products, arithmetic and copies ran while one was open for 4% of the time, Pallas kernels for 17%

profile of v6, /device:TPU:1, one launch (start us, length us, event | category | flops | bytes accessed | tf_op | source)
XLA Modules:
  0.0 155.5 jit_solution(11563967915150199471)
XLA Ops:
  0.7 2.9 %shard_map.148 = bf16[384,2048]{1,0:T(8,128)(2,1)} custom-call(bf16[384,2048]{1,0:T(8,128)(2,1)} %k_ref.1, bf16[384,2048]{1,0:T(8,128)(2,1)} %v_ref.1), custom_call_target="tpu_custom_call" | custom-call | flops 786432 | bytes 4718592 | tf_op jit(solution)/shard_map/pallas_call | solution.py:207
  3.6 1.4 collective-permute-start.12
  5.1 0.4 convert_reduce_fusion.4
  5.5 0.6 reduce_max.9
  6.7 1.5 collective-permute-done.12
  8.3 2.2 %collective-permute-done.13 = bf16[384,2048]{1,0:T(8,128)(2,1)S(1)} collective-permute-done((bf16[384,2048]{1,0:T(8,128)(2,1)}, bf16[384,2048]{1,0:T(8,128)(2,1)S(1)}, u32[]{:S(2)}, u32[]{:S(2)}) %collective-permute-start.13) | collective-permute-done | bytes 1572896 | tf_op jit(solution)/shard_map/ppermute | solution.py:838
  10.5 144.9 %conditional.1 = (bf16[256,2048]{1,0:T(8,128)(2,1)}, bf16[256,2048]{1,0:T(8,128)(2,1)}, bf16[384,2048]{1,0:T(8,128)(2,1)}, bf16[384,2048]{1,0:T(8,128)(2,1)}, f3...) conditional(s32[]{:T(128)} %convert_element_type.91, (s32[12288]{0:T(1024)S(1)}, ...), branch_computations={%region_2.14_spmd, %region_14.26_spmd} | conditional | flops 11994341376 | bytes 178098304 | solution.py:933
  10.5 0.4 branch_1_fun.13.slots_ref
  11.0 5.8 %branch_1_fun.14 = bf16[256,4096]{1,0:T(8,128)(2,1)} custom-call(s32[8,384]{1,0:T(8,128)S(1)} %branch_1_fun.13.slots_ref, bf16[384,2048]{1,0:T(8,128)(2,1)} %get-tuple-element.97.refs_0_, bf16[384,2048]{1,0:T(8,128)(2,1)S(1)} %get-tuple-element.98.refs_1_, bf16[384,2048]{1,0:T(8,128)(2,1)} %get-tuple-element.99.refs_2_, ...), custom_call_target="tpu_custom_call" | custom-call | flops 1610612736 | bytes 8388608 | tf_op jit(solution)/shard_map/cond/branch_1_fun/pallas_call | solution.py:185
  16.7 7.7 %all-to-all-start.3 = ((bf16[32,8,4096]{2,1,0:T(8,128)(2,1)}), bf16[32,8,4096]{2,1,0:T(8,128)(2,1)S(1)}, u32[]{:S(2)}, u32[]{:S(2)}) async-start(bf16[32,8,4096]{2,1,0:T(8,128)(2,1)} %bitcast.31), calls=%async_computation.3 | async-start | bytes 4194304 | tf_op jit(solution)/shard_map/cond/branch_1_fun/all_to_all | solution.py:827
  24.4 0.1 multiply_add_fusion.4
  24.6 0.3 fusion.40
  24.9 0.1 fusion.69
  25.0 0.2 select_reduce_fusion.13
  25.2 0.1 select_reduce_fusion.17
  25.3 0.2 select_reduce_fusion.10
  25.5 0.4 select_reduce_fusion.9
  25.9 0.6 slice.28
  26.6 0.1 maximum_reduce_fusion.1
  26.7 0.1 multiply_multiply_fusion.6
  26.8 0.4 select_multiply_fusion.3
  27.2 0.1 broadcast_compare_fusion.2
  27.4 0.9 multiply_add_fusion.3
  28.2 0.1 maximum_select_fusion.2.cc_ref
  28.4 0.7 slice_compare_fusion.2
  29.0 0.2 multiply_add_fusion.5
  29.2 0.1 fusion.48
  29.3 0.3 branch_1_fun.15
  29.6 0.6 copy-done.18
  30.2 0.7 copy-done.20
  31.0 0.7 copy-done.23
  31.6 0.6 copy-done.25
  32.3 0.6 copy-done.33
  32.9 0.6 copy-done.35
  33.6 0.6 copy-done.37
  34.2 0.7 copy-done.47
  34.9 17.8 %all-to-all-done.3 = bf16[32,8,4096]{2,1,0:T(8,128)(2,1)S(1)} async-done(((bf16[32,8,4096]{2,1,0:T(8,128)(2,1)}), bf16[32,8,4096]{2,1,0:T(8,128)(2,1)S(1)}, u32[]{:S(2)}, u32[]{:S(2)}) %all-to-all-start.3) | async-done | bytes 2097184 | tf_op jit(solution)/shard_map/cond/branch_1_fun/all_to_all | solution.py:827
  52.7 1.2 branch_1_fun.16
  53.9 2.1 %collective-permute-start.5 = (bf16[128,2048]{1,0:T(8,128)(2,1)}, bf16[128,2048]{1,0:T(8,128)(2,1)S(1)}, u32[]{:S(2)}, u32[]{:S(2)}) collective-permute-start(bf16[128,2048]{1,0:T(8,128)(2,1)} %branch_1_fun.16), channel_id=1, source_target_pairs={{0,4},{4,8},{8,12},{12,16},{16,20},{20,24},{24,28},{28,32},{32,36}... | collective-permute-start | bytes 1572872 | tf_op jit(solution)/shard_map/cond/branch_1_fun/ppermute | solution.py:834
  56.1 1.6 %copy-done.9 = bf16[32,8,4096]{2,1,0:T(8,128)(2,1)S(1)} copy-done((bf16[32,8,4096]{2,1,0:T(8,128)(2,1)S(1)}, bf16[32,8,4096]{2,1,0:T(8,128)(2,1)}, u32[]{:S(2)}) %copy-start.9) | copy-done | bytes 2097176 | tf_op jit(solution)/shard_map/cond
  57.7 5.3 %branch_1_fun.17 = (bf16[256,2048]{1,0:T(8,128)(2,1)S(1)}, f32[256,2048]{1,0:T(8,128)S(1)}, bf16[640,2048]{1,0:T(8,128)(2,1)S(1)}, bf16[640,2048]{1,0:T(8,128)(2,1)S(1)}, f32[8,128]{1,0:T(8,128)S(1)}) custom-call(s32[1,256]{1,0:T(1,128)S(1)} %sub.159.pos_row, bf16[640,256]{1,0:T(8,128)(2,1)S(1)} %get-tuple-element.118.cc_own, ...), custom_call_target="tpu_custom_call" | custom-call | flops 4000000000 | bytes 12288000 | tf_op jit(solution)/shard_map/cond/branch_1_fun/pallas_call | solution.py:373
  63.1 3.3 %branch_1_fun.18 = (f32[128,2048]{1,0:T(8,128)S(1)}, f32[128,2048]{1,0:T(8,128)S(1)}, f32[128,2048]{1,0:T(8,128)S(1)}, f32[8,256]{1,0:T(8,128)S(1)}) custom-call(bf16[384,128]{1,0:T(8,128)(2,1)S(1)} %copy-done.19, bf16[128,384]{1,0:T(8,128)(2,1)S(1)} %copy-done.26, bf16[128,2048]{1,0:T(8,128)(2,1)S(1)} %collective-permute-done.5.halo.halo_ref, ...), custom_call_target="tpu_custom_call" | custom-call | flops 600000000 | bytes 6144000 | tf_op jit(solution)/shard_map/cond/branch_1_fun/pallas_call | solution.py:436
  66.4 3.8 %collective-permute-start.8 = (f32[8,256]{1,0:T(8,128)S(1)}, f32[8,256]{1,0:T(8,128)S(1)}, u32[]{:S(2)}, u32[]{:S(2)}) collective-permute-start(f32[8,256]{1,0:T(8,128)S(1)} %get-tuple-element.129.s0), channel_id=1, source_target_pairs={{0,3},{1,0},{2,1},{3,2},{4,7},{5,4},{6,5},{7,6},{8,11},{9,8},{10,9... | collective-permute-start | bytes 24584 | tf_op jit(solution)/shard_map/cond/branch_1_fun/ppermute | solution.py:897
  70.2 0.7 collective-permute-start.6
  71.0 3.2 %collective-permute-done.7.s2 = f32[8,256]{1,0:T(8,128)S(1)} collective-permute-done((f32[8,256]{1,0:T(8,128)S(1)}, f32[8,256]{1,0:T(8,128)S(1)}, u32[]{:S(2)}, u32[]{:S(2)}) %collective-permute-start.7) | collective-permute-done | bytes 8224 | tf_op jit(solution)/shard_map/cond/branch_1_fun/ppermute | solution.py:897
  74.2 1.4 branch_1_fun.21
  75.7 3.6 %collective-permute-start.9 = (bf16[128,2048]{1,0:T(8,128)(2,1)}, bf16[128,2048]{1,0:T(8,128)(2,1)S(1)}, u32[]{:S(2)}, u32[]{:S(2)}) collective-permute-start(bf16[128,2048]{1,0:T(8,128)(2,1)} %branch_1_fun.21), channel_id=1, source_target_pairs={{4,0},{8,4},{12,8},{16,12},{20,16},{24,20},{28,24},{32,28},{36,32}... | collective-permute-start | bytes 1572872 | tf_op jit(solution)/shard_map/cond/branch_1_fun/ppermute | solution.py:834
  79.3 7.2 %branch_1_fun.19 = (bf16[256,2048]{1,0:T(8,128)(2,1)}, bf16[256,3328]{1,0:T(8,128)(2,1)}) custom-call(f32[8,256]{1,0:T(8,128)S(1)} %get-tuple-element.129.s0, f32[8,256]{1,0:T(8,128)S(1)} %collective-permute-done.6.s1, f32[8,256]{1,0:T(8,128)S(1)} %collective-permute-done.7.s2, f32[8,256]{1,0:T(8,128)S(1)} %collective-permute-done.8.s3, ...), custom_call_target="tpu_custom_call" | custom-call | flops 2000000000 | bytes 12288000 | tf_op jit(solution)/shard_map/cond/branch_1_fun/pallas_call | solution.py:598
  86.5 1.0 collective-permute-done.9.next_ref
  87.5 0.8 copy-done.16
  88.3 8.0 %all-to-all-start.4 = ((bf16[32,8,3328]{2,1,0:T(8,128)(2,1)}), bf16[32,8,3328]{2,1,0:T(8,128)(2,1)}, u32[]{:S(2)}, u32[]{:S(2)}) async-start(bf16[32,8,3328]{2,1,0:T(8,128)(2,1)} %bitcast.33), calls=%async_computation.4 | async-start | bytes 3407872 | tf_op jit(solution)/shard_map/cond/branch_1_fun/all_to_all | solution.py:827
  96.2 1.7 %copy-done.7 = bf16[640,2048]{1,0:T(8,128)(2,1)S(1)} copy-done((bf16[640,2048]{1,0:T(8,128)(2,1)S(1)}, bf16[640,2048]{1,0:T(8,128)(2,1)}, u32[]{:S(2)}) %copy-start.7) | copy-done | bytes 2621464 | tf_op jit(solution)/shard_map/cond
  98.0 1.2 copy-done.13
  99.2 1.0 copy-done.22
  100.2 6.0 %branch_1_fun.20 = (bf16[256,2048]{1,0:T(8,128)(2,1)}, bf16[256,2048]{1,0:T(8,128)(2,1)}, f32[256,2048]{1,0:T(8,128)}) custom-call(f32[8,256]{1,0:T(8,128)S(1)} %get-tuple-element.129.s0, f32[8,256]{1,0:T(8,128)S(1)} %collective-permute-done.6.s1, f32[8,256]{1,0:T(8,128)S(1)} %collective-permute-done.7.s2, f32[8,256]{1,0:T(8,128)S(1)} %collective-permute-done.8.s3, ...), custom_call_target="tpu_custom_call" | custom-call | flops 1342177280 | bytes 12288000 | tf_op jit(solution)/shard_map/cond/branch_1_fun/pallas_call | solution.py:639
  106.2 4.5 %branch_1_fun.23.rows_ref = bf16[256,2560]{1,0:T(8,128)(2,1)} custom-call(s32[1,256]{1,0:T(1,128)S(1)} %sub.159.pos_row, bf16[384,128]{1,0:T(8,128)(2,1)S(1)} %copy-done.34, bf16[128,384]{1,0:T(8,128)(2,1)S(1)} %copy-done.36, bf16[384,128]{1,0:T(8,128)(2,1)S(1)} %copy-done.38, f32[256,2048]{1,0:T(8,128)} %get-tuple-element.146.own_ref, ...), custom_call_target="tpu_custom_call" | custom-call | flops 268435456 | bytes 4915200 | tf_op jit(solution)/shard_map/cond/branch_1_fun/pallas_call | solution.py:677
  110.7 9.7 %all-to-all-done.4 = bf16[32,8,3328]{2,1,0:T(8,128)(2,1)} async-done(((bf16[32,8,3328]{2,1,0:T(8,128)(2,1)}), bf16[32,8,3328]{2,1,0:T(8,128)(2,1)}, u32[]{:S(2)}, u32[]{:S(2)}) %all-to-all-start.4) | async-done | bytes 1703968 | tf_op jit(solution)/shard_map/cond/branch_1_fun/all_to_all | solution.py:827
  120.4 2.3 %branch_1_fun.24 = (bf16[256,2560]{1,0:T(8,128)(2,1)}, f32[2,8,128]{2,1,0:T(8,128)}) custom-call(bf16[256,3328]{1,0:T(8,128)(2,1)} %bitcast.18.refs_0_.received_ref, bf16[256,2560]{1,0:T(8,128)(2,1)} %branch_1_fun.23.rows_ref), custom_call_target="tpu_custom_call", output_to_operand_aliasing={{0}: (1, {})} | custom-call | flops 131072 | bytes 524288 | tf_op jit(solution)/shard_map/cond/branch_1_fun/pallas_call | solution.py:719
  122.6 4.3 %all-to-all-start.5 = ((bf16[32,8,2560]{2,1,0:T(8,128)(2,1)}), bf16[32,8,2560]{2,1,0:T(8,128)(2,1)S(1)}, u32[]{:S(2)}, u32[]{:S(2)}) async-start(bf16[32,8,2560]{2,1,0:T(8,128)(2,1)} %bitcast.30), calls=%async_computation.5 | async-start | bytes 2621440 | tf_op jit(solution)/shard_map/cond/branch_1_fun/all_to_all | solution.py:827
  127.0 0.4 collective-permute-start.10
  127.4 19.5 %all-to-all-done.5 = bf16[32,8,2560]{2,1,0:T(8,128)(2,1)S(1)} async-done(((bf16[32,8,2560]{2,1,0:T(8,128)(2,1)}), bf16[32,8,2560]{2,1,0:T(8,128)(2,1)S(1)}, u32[]{:S(2)}, u32[]{:S(2)}) %all-to-all-start.5) | async-done | bytes 1310752 | tf_op jit(solution)/shard_map/cond/branch_1_fun/all_to_all | solution.py:827
  146.9 0.4 collective-permute-start.11
  147.2 3.8 %branch_1_fun.22 = bf16[384,2048]{1,0:T(8,128)(2,1)} custom-call(s32[8,384]{1,0:T(8,128)S(1)} %branch_1_fun.13.slots_ref, bf16[256,3328]{1,0:T(8,128)(2,1)} %bitcast.18.refs_0_.received_ref, bf16[256,3328]{1,0:T(8,128)(2,1)S(1)} %collective-permute-done.10.refs_1_), custom_call_target="tpu_custom_call" | custom-call | flops 805306368 | bytes 3670016 | tf_op jit(solution)/shard_map/cond/branch_1_fun/pallas_call | solution.py:763
  151.0 4.4 %branch_1_fun.25 = (bf16[384,2048]{1,0:T(8,128)(2,1)}, bf16[384,2048]{1,0:T(8,128)(2,1)}, f32[128,2048]{1,0:T(8,128)}) custom-call(s32[1]{0:T(128)} %bitcast.11.index_ref, s32[8,384]{1,0:T(8,128)S(1)} %branch_1_fun.13.slots_ref, bf16[384,2048]{1,0:T(8,128)(2,1)} %get-tuple-element.141.k_ref, bf16[384,2048]{1,0:T(8,128)(2,1)} %get-tuple-element.142.v_ref, ...), custom_call_target="tpu_custom_call" | custom-call | flops 402653184 | bytes 8912896 | tf_op jit(solution)/shard_map/cond/branch_1_fun/pallas_call | solution.py:807
  (73 shorter events, 0.4 us)
Async XLA Ops:
  0.6 4.4 %copy-start.49 = (s32[12288]{0:T(1024)S(1)}, s32[12288]{0:T(1024)}, u32[]{:S(2)}) copy-start(s32[12288]{0:T(1024)} %param.14) | copy-start | bytes 147460
  0.6 9.9 %copy-start.52 = (s32[8192]{0:T(1024)S(1)}, s32[8192]{0:T(1024)}, u32[]{:S(2)}) copy-start(s32[8192]{0:T(1024)} %param.15) | copy-start | bytes 98308
  3.6 4.7 %collective-permute-start.12 = (bf16[384,2048]{1,0:T(8,128)(2,1)}, bf16[384,2048]{1,0:T(8,128)(2,1)S(1)}, u32[]{:S(2)}, u32[]{:S(2)}) collective-permute-start(bf16[384,2048]{1,0:T(8,128)(2,1)} %shard_map.148), channel_id=1, source_target_pairs={{0,4},{4,0},{8,12},{12,8},{16,20},{20,16},{24,28},{28,24},{32,36},... | collective-permute-start | bytes 4718600 | tf_op jit(solution)/shard_map/ppermute | solution.py:838
  5.0 5.5 %collective-permute-start.13 = (bf16[384,2048]{1,0:T(8,128)(2,1)}, bf16[384,2048]{1,0:T(8,128)(2,1)S(1)}, u32[]{:S(2)}, u32[]{:S(2)}) collective-permute-start(bf16[384,2048]{1,0:T(8,128)(2,1)} %param.11), channel_id=1, source_target_pairs={{0,4},{4,0},{8,12},{12,8},{16,20},{20,16},{24,28},{28,24},{32,36},... | collective-permute-start | bytes 4718600 | tf_op jit(solution)/shard_map/ppermute | solution.py:838
  10.5 6.2 %copy-start.53 = (s32[8192]{0:T(1024)}, s32[8192]{0:T(1024)S(1)}, u32[]{:S(2)}) copy-start(s32[8192]{0:T(1024)S(1)} %get-tuple-element.104) | copy-start | bytes 98308 | tf_op jit(solution)/shard_map/cond
  16.7 8.1 %copy-start.54 = (s32[8192]{0:T(1024)S(1)}, s32[8192]{0:T(1024)}, u32[]{:S(2)}) copy-start(s32[8192]{0:T(1024)} %copy-done.53) | copy-start | bytes 98308 | tf_op jit(solution)/shard_map/cond
  16.7 36.0 %all-to-all-start.3 = ((bf16[32,8,4096]{2,1,0:T(8,128)(2,1)}), bf16[32,8,4096]{2,1,0:T(8,128)(2,1)S(1)}, u32[]{:S(2)}, u32[]{:S(2)}) async-start(bf16[32,8,4096]{2,1,0:T(8,128)(2,1)} %bitcast.31), calls=%async_computation.3 | async-start | bytes 4194304 | tf_op jit(solution)/shard_map/cond/branch_1_fun/all_to_all | solution.py:827
  29.6 0.6 copy-start.18
  30.2 0.7 copy-start.20
  31.0 0.7 copy-start.23
  31.6 0.6 copy-start.25
  32.3 0.6 copy-start.33
  32.9 0.6 copy-start.35
  33.6 0.7 copy-start.37
  34.2 0.7 copy-start.47
  34.9 21.2 %copy-start.51 = (f32[2048]{0:T(1024)S(1)}, f32[2048]{0:T(1024)}, u32[]{:S(2)}) copy-start(f32[2048]{0:T(1024)} %get-tuple-element.124) | copy-start | bytes 24580 | tf_op jit(solution)/shard_map/cond
  52.7 3.4 %copy-start.8 = (bf16[32,8,4096]{2,1,0:T(8,128)(2,1)}, bf16[32,8,4096]{2,1,0:T(8,128)(2,1)S(1)}, u32[]{:S(2)}) copy-start(bf16[32,8,4096]{2,1,0:T(8,128)(2,1)S(1)} %all-to-all-done.3) | copy-start | bytes 6291460 | tf_op jit(solution)/shard_map/cond
  52.7 3.4 %copy-start.21 = (bf16[256,640]{1,0:T(8,128)(2,1)S(1)}, bf16[256,640]{1,0:T(8,128)(2,1)}, u32[]{:S(2)}) copy-start(bf16[256,640]{1,0:T(8,128)(2,1)} %copy-done.20) | copy-start | bytes 983044 | tf_op jit(solution)/shard_map/cond
  52.7 3.4 %copy-start.48 = (bf16[640,128]{1,0:T(8,128)(2,1)S(1)}, bf16[640,128]{1,0:T(8,128)(2,1)}, u32[]{:S(2)}) copy-start(bf16[640,128]{1,0:T(8,128)(2,1)} %copy-done.47) | copy-start | bytes 491524 | tf_op jit(solution)/shard_map/cond
  53.9 9.1 %collective-permute-start.5 = (bf16[128,2048]{1,0:T(8,128)(2,1)}, bf16[128,2048]{1,0:T(8,128)(2,1)S(1)}, u32[]{:S(2)}, u32[]{:S(2)}) collective-permute-start(bf16[128,2048]{1,0:T(8,128)(2,1)} %branch_1_fun.16), channel_id=1, source_target_pairs={{0,4},{4,8},{8,12},{12,16},{16,20},{20,24},{24,28},{28,32},{32,36}... | collective-permute-start | bytes 1572872 | tf_op jit(solution)/shard_map/cond/branch_1_fun/ppermute | solution.py:834
  56.1 1.6 %copy-start.9 = (bf16[32,8,4096]{2,1,0:T(8,128)(2,1)S(1)}, bf16[32,8,4096]{2,1,0:T(8,128)(2,1)}, u32[]{:S(2)}) copy-start(bf16[32,8,4096]{2,1,0:T(8,128)(2,1)} %copy-done.8) | copy-start | bytes 6291460 | tf_op jit(solution)/shard_map/cond
  57.7 5.3 %copy-start.19 = (bf16[384,128]{1,0:T(8,128)(2,1)S(1)}, bf16[384,128]{1,0:T(8,128)(2,1)}, u32[]{:S(2)}) copy-start(bf16[384,128]{1,0:T(8,128)(2,1)} %copy-done.18) | copy-start | bytes 294916 | tf_op jit(solution)/shard_map/cond
  57.7 5.3 %copy-start.26 = (bf16[128,384]{1,0:T(8,128)(2,1)S(1)}, bf16[128,384]{1,0:T(8,128)(2,1)}, u32[]{:S(2)}) copy-start(bf16[128,384]{1,0:T(8,128)(2,1)} %copy-done.25) | copy-start | bytes 294916 | tf_op jit(solution)/shard_map/cond
  63.0 3.4 %copy-start.6 = (bf16[640,2048]{1,0:T(8,128)(2,1)}, bf16[640,2048]{1,0:T(8,128)(2,1)S(1)}, u32[]{:S(2)}) copy-start(bf16[640,2048]{1,0:T(8,128)(2,1)S(1)} %get-tuple-element.125.f_ref) | copy-start | bytes 7864324 | tf_op jit(solution)/shard_map/cond
  66.4 12.9 %copy-start.12 = (f32[128,2048]{1,0:T(8,128)}, f32[128,2048]{1,0:T(8,128)S(1)}, u32[]{:S(2)}) copy-start(f32[128,2048]{1,0:T(8,128)S(1)} %get-tuple-element.130.mix_head_ref) | copy-start | bytes 3145732 | tf_op jit(solution)/shard_map/cond
  66.4 4.6 %collective-permute-start.8 = (f32[8,256]{1,0:T(8,128)S(1)}, f32[8,256]{1,0:T(8,128)S(1)}, u32[]{:S(2)}, u32[]{:S(2)}) collective-permute-start(f32[8,256]{1,0:T(8,128)S(1)} %get-tuple-element.129.s0), channel_id=1, source_target_pairs={{0,3},{1,0},{2,1},{3,2},{4,7},{5,4},{6,5},{7,6},{8,11},{9,8},{10,9... | collective-permute-start | bytes 24584 | tf_op jit(solution)/shard_map/cond/branch_1_fun/ppermute | solution.py:897
  70.2 4.0 %collective-permute-start.7 = (f32[8,256]{1,0:T(8,128)S(1)}, f32[8,256]{1,0:T(8,128)S(1)}, u32[]{:S(2)}, u32[]{:S(2)}) collective-permute-start(f32[8,256]{1,0:T(8,128)S(1)} %get-tuple-element.129.s0), channel_id=1, source_target_pairs={{0,2},{1,3},{2,0},{3,1},{4,6},{5,7},{6,4},{7,5},{8,10},{9,11},{10,... | collective-permute-start | bytes 24584 | tf_op jit(solution)/shard_map/cond/branch_1_fun/ppermute | solution.py:897
  70.2 4.0 %collective-permute-start.6 = (f32[8,256]{1,0:T(8,128)S(1)}, f32[8,256]{1,0:T(8,128)S(1)}, u32[]{:S(2)}, u32[]{:S(2)}) collective-permute-start(f32[8,256]{1,0:T(8,128)S(1)} %get-tuple-element.129.s0), channel_id=1, source_target_pairs={{0,1},{1,2},{2,3},{3,0},{4,5},{5,6},{6,7},{7,4},{8,9},{9,10},{10,1... | collective-permute-start | bytes 24584 | tf_op jit(solution)/shard_map/cond/branch_1_fun/ppermute | solution.py:897
  74.2 5.1 %copy-start.24 = (bf16[128,640]{1,0:T(8,128)(2,1)S(1)}, bf16[128,640]{1,0:T(8,128)(2,1)}, u32[]{:S(2)}) copy-start(bf16[128,640]{1,0:T(8,128)(2,1)} %copy-done.23) | copy-start | bytes 491524 | tf_op jit(solution)/shard_map/cond
  75.7 11.8 %collective-permute-start.9 = (bf16[128,2048]{1,0:T(8,128)(2,1)}, bf16[128,2048]{1,0:T(8,128)(2,1)S(1)}, u32[]{:S(2)}, u32[]{:S(2)}) collective-permute-start(bf16[128,2048]{1,0:T(8,128)(2,1)} %branch_1_fun.21), channel_id=1, source_target_pairs={{4,0},{8,4},{12,8},{16,12},{20,16},{24,20},{28,24},{32,28},{36,32}... | collective-permute-start | bytes 1572872 | tf_op jit(solution)/shard_map/cond/branch_1_fun/ppermute | solution.py:834
  87.5 0.8 copy-start.16
  88.3 32.1 %all-to-all-start.4 = ((bf16[32,8,3328]{2,1,0:T(8,128)(2,1)}), bf16[32,8,3328]{2,1,0:T(8,128)(2,1)}, u32[]{:S(2)}, u32[]{:S(2)}) async-start(bf16[32,8,3328]{2,1,0:T(8,128)(2,1)} %bitcast.33), calls=%async_computation.4 | async-start | bytes 3407872 | tf_op jit(solution)/shard_map/cond/branch_1_fun/all_to_all | solution.py:827
  96.2 1.7 %copy-start.7 = (bf16[640,2048]{1,0:T(8,128)(2,1)S(1)}, bf16[640,2048]{1,0:T(8,128)(2,1)}, u32[]{:S(2)}) copy-start(bf16[640,2048]{1,0:T(8,128)(2,1)} %copy-done.6) | copy-start | bytes 7864324 | tf_op jit(solution)/shard_map/cond
  98.0 1.2 copy-start.13
  99.2 1.0 copy-start.22
  100.2 6.0 %copy-start.17 = (bf16[128,2048]{1,0:T(8,128)(2,1)S(1)}, bf16[128,2048]{1,0:T(8,128)(2,1)}, u32[]{:S(2)}) copy-start(bf16[128,2048]{1,0:T(8,128)(2,1)} %copy-done.16) | copy-start | bytes 1572868 | tf_op jit(solution)/shard_map/cond
  100.2 6.0 %copy-start.34 = (bf16[384,128]{1,0:T(8,128)(2,1)S(1)}, bf16[384,128]{1,0:T(8,128)(2,1)}, u32[]{:S(2)}) copy-start(bf16[384,128]{1,0:T(8,128)(2,1)} %copy-done.33) | copy-start | bytes 294916 | tf_op jit(solution)/shard_map/cond
  100.2 6.0 %copy-start.36 = (bf16[128,384]{1,0:T(8,128)(2,1)S(1)}, bf16[128,384]{1,0:T(8,128)(2,1)}, u32[]{:S(2)}) copy-start(bf16[128,384]{1,0:T(8,128)(2,1)} %copy-done.35) | copy-start | bytes 294916 | tf_op jit(solution)/shard_map/cond
  100.2 6.0 %copy-start.38 = (bf16[384,128]{1,0:T(8,128)(2,1)S(1)}, bf16[384,128]{1,0:T(8,128)(2,1)}, u32[]{:S(2)}) copy-start(bf16[384,128]{1,0:T(8,128)(2,1)} %copy-done.37) | copy-start | bytes 294916 | tf_op jit(solution)/shard_map/cond
  122.6 24.2 %all-to-all-start.5 = ((bf16[32,8,2560]{2,1,0:T(8,128)(2,1)}), bf16[32,8,2560]{2,1,0:T(8,128)(2,1)S(1)}, u32[]{:S(2)}, u32[]{:S(2)}) async-start(bf16[32,8,2560]{2,1,0:T(8,128)(2,1)} %bitcast.30), calls=%async_computation.5 | async-start | bytes 2621440 | tf_op jit(solution)/shard_map/cond/branch_1_fun/all_to_all | solution.py:827
  127.0 20.3 %collective-permute-start.10 = (bf16[256,3328]{1,0:T(8,128)(2,1)}, bf16[256,3328]{1,0:T(8,128)(2,1)S(1)}, u32[]{:S(2)}, u32[]{:S(2)}) collective-permute-start(bf16[256,3328]{1,0:T(8,128)(2,1)} %bitcast.18.refs_0_.received_ref), channel_id=1, source_target_pairs={{0,4},{4,0},{8,12},{12,8},{16,20},{20,16},{24,28},{28,24},{32,36},... | collective-permute-start | bytes 5111816 | tf_op jit(solution)/shard_map/cond/branch_1_fun/ppermute | solution.py:838
  146.9 4.2 %collective-permute-start.11 = (bf16[256,2560]{1,0:T(8,128)(2,1)S(1)}, bf16[256,2560]{1,0:T(8,128)(2,1)S(1)}, u32[]{:S(2)}, u32[]{:S(2)}) collective-permute-start(bf16[256,2560]{1,0:T(8,128)(2,1)S(1)} %bitcast.26), channel_id=1, source_target_pairs={{0,4},{4,0},{8,12},{12,8},{16,20},{20,16},{24,28},{28,24},{32,36},... | collective-permute-start | bytes 3932168 | tf_op jit(solution)/shard_map/cond/branch_1_fun/ppermute | solution.py:838

commit v7 on v6

--- a/solution.py
+++ b/solution.py
@@ -751,9 +751,9 @@
     def _():
         build_home(pair, slots_ref, homes)
 
-    piece = piece_cols(pair)
-    at = pl.ds(pl.multiple_of(pl.program_id(0) * piece, 128), WIDE)
-    rows = [ref.at[:, at] for ref in backs]
+    step = pl.program_id(0)
+    at = pl.ds(pl.multiple_of(step * piece_cols(pair), 128), WIDE)
+    rows = [backs[0].at[:, at]] + [ref.at[:, block_of(step, WIDE)] for ref in backs[1:]]
     out_ref[...] = homecoming(rows, homes).astype(BF)
 
 
@@ -908,10 +908,15 @@
     )
     rows = give_back(pair, pos_row, onward, own_grad, from_next, mr_filter)
     sent_dp, d_gain = reduce_parts(pair, back_q, rows, width)
+    sent_dp, back_q = lax.optimization_barrier((sent_dp, back_q))
     back_p = exchange(pair, sent_dp)
     backs_q, backs_p = [back_q], [back_p]
     if shared:
-        backs_q.append(swap(back_q))
+        pieces = range(0, back_q.shape[1], piece_cols(pair))
+        rows = jnp.concatenate([back_q[:, at : at + WIDE] for at in pieces], axis=1)
+        back_p, rows = lax.optimization_barrier((back_p, swap(rows)))
+        backs_p = [back_p]
+        backs_q.append(rows)
         backs_p.append(swap(back_p))
     d_q_in = home_rows(pair, slots, backs_q, width)
     d_k_in, d_v_in, d_filter = home_product(pair, my_index, slots, backs_p, k_in, v_in)

time: 156 us -> 155 us (level)
  Pallas kernels: 48.8 us -> 46.2 us
    ppermute x4, waiting for transfers between devices: 3.78 us -> 6.09 us  [swap(): return lax.ppermute(value, 'seq', [(i, i ^ 1) for i in range(SHARDS)])]
    cond x56 -> x58, local copies, waits for them, and re-layouts: 11.6 us -> 12.1 us
  transfers between devices with their start and end apart: 12 -> 12, of which waited for: 8 -> 9; matrix products, arithmetic and copies ran while one was open for 4% -> 4% of each run, Pallas kernels for 17% -> 17%
where the time goes in v7:
time: 155 us; the launch traced here: 154 us
  waiting for transfers between devices  55.9 us (36%)
  Pallas kernels  46.2 us (30%)
  starting transfers between devices  32.2 us (21%)
  local copies, waits for them, and re-layouts  12.9 us (8%)
  other arithmetic  4.9 us (3%)
    all_to_all x3, waiting for transfers between devices, exchange(): lax.all_to_all(shards, 'seq', split_axis=0, concat_axis=0, tiled=True)  46.1 us
    all_to_all x3, starting transfers between devices, exchange(): lax.all_to_all(shards, 'seq', split_axis=0, concat_axis=0, tiled=True)  19.7 us
    cond x58, local copies, waits for them, and re-layouts  12.1 us
    pallas_call x1, Pallas kernels, backward(): pl.pallas_call(functools.partial(backward_kernel, pair), grid=(steps,), i...  7.19 us
    ppermute x4, waiting for transfers between devices, swap(): return lax.ppermute(value, 'seq', [(i, i ^ 1) for i in range(SHARDS)])  6.09 us
    pallas_call x1, Pallas kernels, finish(): pl.pallas_call(finish_kernel, grid=(width // wide,), in_specs=[RESIDENT]...  6.01 us
    pallas_call x1, Pallas kernels, pack_arrivals(): pl.pallas_call(functools.partial(pack_kernel, halves, blocks), grid=(2 *...  5.8 us
    ppermute x2, starting transfers between devices, shift(): return lax.ppermute(value, 'seq', pairs)  5.75 us
  transfers between devices with their start and end apart: 12, of which 9 were waited for; matrix products, arithmetic and copies ran while one was open for 4% of the time, Pallas kernels for 17%

profile of v7, /device:TPU:1, one launch (start us, length us, event | category | flops | bytes accessed | tf_op | source)
XLA Modules:
  0.0 154.1 jit_solution(12825736192689003932)
XLA Ops:
  0.7 2.9 %shard_map.148 = bf16[384,2048]{1,0:T(8,128)(2,1)} custom-call(bf16[384,2048]{1,0:T(8,128)(2,1)} %k_ref.1, bf16[384,2048]{1,0:T(8,128)(2,1)} %v_ref.1), custom_call_target="tpu_custom_call" | custom-call | flops 786432 | bytes 4718592 | tf_op jit(solution)/shard_map/pallas_call | solution.py:207
  3.6 1.4 collective-permute-start.12
  5.1 0.4 convert_reduce_fusion.4
  5.4 0.6 reduce_max.9
  6.7 1.5 collective-permute-done.12
  8.3 2.2 %collective-permute-done.13 = bf16[384,2048]{1,0:T(8,128)(2,1)S(1)} collective-permute-done((bf16[384,2048]{1,0:T(8,128)(2,1)}, bf16[384,2048]{1,0:T(8,128)(2,1)S(1)}, u32[]{:S(2)}, u32[]{:S(2)}) %collective-permute-start.13) | collective-permute-done | bytes 1572896 | tf_op jit(solution)/shard_map/ppermute | solution.py:838
  10.5 143.6 %conditional.1 = (bf16[256,2048]{1,0:T(8,128)(2,1)}, bf16[256,2048]{1,0:T(8,128)(2,1)}, bf16[384,2048]{1,0:T(8,128)(2,1)}, bf16[384,2048]{1,0:T(8,128)(2,1)}, f3...) conditional(s32[]{:T(128)} %convert_element_type.91, (s32[12288]{0:T(1024)S(1)}, ...), branch_computations={%region_2.14_spmd, %region_14.26_spmd} | conditional | flops 11994341376 | bytes 193494464 | solution.py:938
  10.5 0.4 branch_1_fun.13.slots_ref
  11.0 5.8 %branch_1_fun.14 = bf16[256,4096]{1,0:T(8,128)(2,1)} custom-call(s32[8,384]{1,0:T(8,128)S(1)} %branch_1_fun.13.slots_ref, bf16[384,2048]{1,0:T(8,128)(2,1)} %get-tuple-element.99.refs_0_, bf16[384,2048]{1,0:T(8,128)(2,1)S(1)} %get-tuple-element.100.refs_1_, bf16[384,2048]{1,0:T(8,128)(2,1)} %get-tuple-element.101.refs_2_, ...), custom_call_target="tpu_custom_call" | custom-call | flops 1610612736 | bytes 8388608 | tf_op jit(solution)/shard_map/cond/branch_1_fun/pallas_call | solution.py:185
  16.8 7.7 %all-to-all-start.3 = ((bf16[32,8,4096]{2,1,0:T(8,128)(2,1)}), bf16[32,8,4096]{2,1,0:T(8,128)(2,1)S(1)}, u32[]{:S(2)}, u32[]{:S(2)}) async-start(bf16[32,8,4096]{2,1,0:T(8,128)(2,1)} %bitcast.34), calls=%async_computation.3 | async-start | bytes 4194304 | tf_op jit(solution)/shard_map/cond/branch_1_fun/all_to_all | solution.py:827
  24.5 0.1 multiply_add_fusion.4
  24.6 0.3 fusion.40
  24.9 0.1 fusion.69
  25.0 0.2 select_reduce_fusion.13
  25.2 0.1 select_reduce_fusion.17
  25.3 0.2 select_reduce_fusion.10
  25.5 0.4 select_reduce_fusion.9
  25.9 0.6 slice.32
  26.7 0.1 multiply_multiply_fusion.6
  26.8 0.4 select_multiply_fusion.3
  27.2 0.1 broadcast_compare_fusion.2
  27.4 0.9 multiply_add_fusion.3
  28.3 0.1 maximum_select_fusion.2.cc_ref
  28.4 0.7 slice_compare_fusion.2
  29.0 0.2 multiply_add_fusion.5
  29.2 0.1 fusion.48
  29.3 0.3 branch_1_fun.15
  29.6 0.7 copy-done.22
  30.3 0.6 copy-done.32
  30.9 0.6 copy-done.34
  31.6 21.1 %all-to-all-done.3 = bf16[32,8,4096]{2,1,0:T(8,128)(2,1)S(1)} async-done(((bf16[32,8,4096]{2,1,0:T(8,128)(2,1)}), bf16[32,8,4096]{2,1,0:T(8,128)(2,1)S(1)}, u32[]{:S(2)}, u32[]{:S(2)}) %all-to-all-start.3) | async-done | bytes 2097184 | tf_op jit(solution)/shard_map/cond/branch_1_fun/all_to_all | solution.py:827
  52.7 1.5 branch_1_fun.16
  54.2 2.1 %collective-permute-start.5 = (bf16[128,2048]{1,0:T(8,128)(2,1)}, bf16[128,2048]{1,0:T(8,128)(2,1)S(1)}, u32[]{:S(2)}, u32[]{:S(2)}) collective-permute-start(bf16[128,2048]{1,0:T(8,128)(2,1)} %branch_1_fun.16), channel_id=1, source_target_pairs={{0,4},{4,8},{8,12},{12,16},{16,20},{20,24},{24,28},{28,32},{32,36}... | collective-permute-start | bytes 1572872 | tf_op jit(solution)/shard_map/cond/branch_1_fun/ppermute | solution.py:834
  56.4 1.6 %copy-done.11 = bf16[32,8,4096]{2,1,0:T(8,128)(2,1)S(1)} copy-done((bf16[32,8,4096]{2,1,0:T(8,128)(2,1)S(1)}, bf16[32,8,4096]{2,1,0:T(8,128)(2,1)}, u32[]{:S(2)}) %copy-start.11) | copy-done | bytes 2097176 | tf_op jit(solution)/shard_map/cond
  58.0 0.9 copy-done.47
  58.9 5.3 %branch_1_fun.17 = (bf16[256,2048]{1,0:T(8,128)(2,1)S(1)}, f32[256,2048]{1,0:T(8,128)S(1)}, bf16[640,2048]{1,0:T(8,128)(2,1)S(1)}, bf16[640,2048]{1,0:T(8,128)(2,1)S(1)}, f32[8,128]{1,0:T(8,128)S(1)}) custom-call(s32[1,256]{1,0:T(1,128)S(1)} %sub.159.pos_row, bf16[640,256]{1,0:T(8,128)(2,1)S(1)} %get-tuple-element.120.cc_own, ...), custom_call_target="tpu_custom_call" | custom-call | flops 4000000000 | bytes 12288000 | tf_op jit(solution)/shard_map/cond/branch_1_fun/pallas_call | solution.py:373
  64.3 3.3 %branch_1_fun.18 = (f32[128,2048]{1,0:T(8,128)S(1)}, f32[128,2048]{1,0:T(8,128)S(1)}, f32[128,2048]{1,0:T(8,128)S(1)}, f32[8,256]{1,0:T(8,128)S(1)}) custom-call(bf16[384,128]{1,0:T(8,128)(2,1)S(1)} %get-tuple-element.116.cc_halo, bf16[128,384]{1,0:T(8,128)(2,1)S(1)} %copy-done.25, bf16[128,2048]{1,0:T(8,128)(2,1)S(1)} %collective-permute-done.5.halo.halo_ref, ...), custom_call_target="tpu_custom_call" | custom-call | flops 600000000 | bytes 6144000 | tf_op jit(solution)/shard_map/cond/branch_1_fun/pallas_call | solution.py:436
  67.6 3.8 %collective-permute-start.8 = (f32[8,256]{1,0:T(8,128)S(1)}, f32[8,256]{1,0:T(8,128)S(1)}, u32[]{:S(2)}, u32[]{:S(2)}) collective-permute-start(f32[8,256]{1,0:T(8,128)S(1)} %get-tuple-element.131.s0), channel_id=1, source_target_pairs={{0,3},{1,0},{2,1},{3,2},{4,7},{5,4},{6,5},{7,6},{8,11},{9,8},{10,9... | collective-permute-start | bytes 24584 | tf_op jit(solution)/shard_map/cond/branch_1_fun/ppermute | solution.py:897
  71.4 0.7 collective-permute-start.6
  72.1 0.1 collective-permute-done.8.s3
  72.2 3.2 %collective-permute-done.7.s2 = f32[8,256]{1,0:T(8,128)S(1)} collective-permute-done((f32[8,256]{1,0:T(8,128)S(1)}, f32[8,256]{1,0:T(8,128)S(1)}, u32[]{:S(2)}, u32[]{:S(2)}) %collective-permute-start.7) | collective-permute-done | bytes 8224 | tf_op jit(solution)/shard_map/cond/branch_1_fun/ppermute | solution.py:897
  75.4 1.4 branch_1_fun.21
  76.9 3.6 %collective-permute-start.9 = (bf16[128,2048]{1,0:T(8,128)(2,1)}, bf16[128,2048]{1,0:T(8,128)(2,1)S(1)}, u32[]{:S(2)}, u32[]{:S(2)}) collective-permute-start(bf16[128,2048]{1,0:T(8,128)(2,1)} %branch_1_fun.21), channel_id=1, source_target_pairs={{4,0},{8,4},{12,8},{16,12},{20,16},{24,20},{28,24},{32,28},{36,32}... | collective-permute-start | bytes 1572872 | tf_op jit(solution)/shard_map/cond/branch_1_fun/ppermute | solution.py:834
  80.5 7.2 %branch_1_fun.19 = (bf16[256,2048]{1,0:T(8,128)(2,1)}, bf16[256,3328]{1,0:T(8,128)(2,1)}) custom-call(f32[8,256]{1,0:T(8,128)S(1)} %get-tuple-element.131.s0, f32[8,256]{1,0:T(8,128)S(1)} %collective-permute-done.6.s1, f32[8,256]{1,0:T(8,128)S(1)} %collective-permute-done.7.s2, f32[8,256]{1,0:T(8,128)S(1)} %collective-permute-done.8.s3, ...), custom_call_target="tpu_custom_call" | custom-call | flops 2000000000 | bytes 12288000 | tf_op jit(solution)/shard_map/cond/branch_1_fun/pallas_call | solution.py:598
  87.7 0.4 collective-permute-done.9.next_ref
  88.2 0.8 copy-done.20
  89.0 7.6 %all-to-all-start.4 = ((bf16[32,8,3328]{2,1,0:T(8,128)(2,1)}), bf16[32,8,3328]{2,1,0:T(8,128)(2,1)S(1)}, u32[]{:S(2)}, u32[]{:S(2)}) async-start(bf16[32,8,3328]{2,1,0:T(8,128)(2,1)} %bitcast.36), calls=%async_computation.4 | async-start | bytes 3407872 | tf_op jit(solution)/shard_map/cond/branch_1_fun/all_to_all | solution.py:827
  96.6 1.6 %copy-done.3 = f32[256,2048]{1,0:T(8,128)S(1)} copy-done((f32[256,2048]{1,0:T(8,128)S(1)}, f32[256,2048]{1,0:T(8,128)}, u32[]{:S(2)}) %copy-start.3) | copy-done | bytes 2097176 | tf_op jit(solution)/shard_map/cond
  98.2 1.7 %copy-done.9 = bf16[640,2048]{1,0:T(8,128)(2,1)S(1)} copy-done((bf16[640,2048]{1,0:T(8,128)(2,1)S(1)}, bf16[640,2048]{1,0:T(8,128)(2,1)}, u32[]{:S(2)}) %copy-start.9) | copy-done | bytes 2621464 | tf_op jit(solution)/shard_map/cond
  99.9 1.2 copy-done.15
  101.2 6.0 %branch_1_fun.20 = (bf16[256,2048]{1,0:T(8,128)(2,1)}, bf16[256,2048]{1,0:T(8,128)(2,1)}, f32[256,2048]{1,0:T(8,128)}) custom-call(f32[8,256]{1,0:T(8,128)S(1)} %get-tuple-element.131.s0, f32[8,256]{1,0:T(8,128)S(1)} %collective-permute-done.6.s1, f32[8,256]{1,0:T(8,128)S(1)} %collective-permute-done.7.s2, f32[8,256]{1,0:T(8,128)S(1)} %collective-permute-done.8.s3, ...), custom_call_target="tpu_custom_call" | custom-call | flops 1342177280 | bytes 12288000 | tf_op jit(solution)/shard_map/cond/branch_1_fun/pallas_call | solution.py:639
  107.2 4.5 %branch_1_fun.22.rows_ref = bf16[256,2560]{1,0:T(8,128)(2,1)} custom-call(s32[1,256]{1,0:T(1,128)S(1)} %sub.159.pos_row, bf16[384,128]{1,0:T(8,128)(2,1)S(1)} %copy-done.33, bf16[128,384]{1,0:T(8,128)(2,1)S(1)} %copy-done.35, bf16[384,128]{1,0:T(8,128)(2,1)S(1)} %copy-done.37, f32[256,2048]{1,0:T(8,128)} %get-tuple-element.146.own_ref, ...), custom_call_target="tpu_custom_call" | custom-call | flops 268435456 | bytes 4915200 | tf_op jit(solution)/shard_map/cond/branch_1_fun/pallas_call | solution.py:677
  111.7 9.0 %all-to-all-done.4 = bf16[32,8,3328]{2,1,0:T(8,128)(2,1)S(1)} async-done(((bf16[32,8,3328]{2,1,0:T(8,128)(2,1)}), bf16[32,8,3328]{2,1,0:T(8,128)(2,1)S(1)}, u32[]{:S(2)}, u32[]{:S(2)}) %all-to-all-start.4) | async-done | bytes 1703968 | tf_op jit(solution)/shard_map/cond/branch_1_fun/all_to_all | solution.py:827
  120.7 0.8 branch_1_fun.23
  121.5 4.3 %all-to-all-start.5 = ((bf16[32,8,2560]{2,1,0:T(8,128)(2,1)}), bf16[32,8,2560]{2,1,0:T(8,128)(2,1)S(1)}, u32[]{:S(2)}, u32[]{:S(2)}) async-start(bf16[32,8,2560]{2,1,0:T(8,128)(2,1)} %bitcast.33), calls=%async_computation.5 | async-start | bytes 2621440 | tf_op jit(solution)/shard_map/cond/branch_1_fun/all_to_all | solution.py:827
  125.8 0.1 fusion.85
  126.1 0.4 collective-permute-start.10
  126.5 2.3 %collective-permute-done.10.refs_1_ = bf16[256,2048]{1,0:T(8,128)(2,1)S(1)} collective-permute-done((bf16[256,2048]{1,0:T(8,128)(2,1)S(1)}, bf16[256,2048]{1,0:T(8,128)(2,1)S(1)}, u32[]{:S(2)}, u32[]{:S(2)}) %collective-permute-start.10) | collective-permute-done | bytes 1048608 | tf_op jit(solution)/shard_map/cond/branch_1_fun/ppermute | solution.py:838
  128.8 1.0 copy-done.16
  129.8 15.9 %all-to-all-done.5 = bf16[32,8,2560]{2,1,0:T(8,128)(2,1)S(1)} async-done(((bf16[32,8,2560]{2,1,0:T(8,128)(2,1)}), bf16[32,8,2560]{2,1,0:T(8,128)(2,1)S(1)}, u32[]{:S(2)}, u32[]{:S(2)}) %all-to-all-start.5) | async-done | bytes 1310752 | tf_op jit(solution)/shard_map/cond/branch_1_fun/all_to_all | solution.py:827
  145.7 0.4 collective-permute-start.11
  146.1 1.2 copy-done.17
  147.3 2.3 %branch_1_fun.24 = bf16[384,2048]{1,0:T(8,128)(2,1)} custom-call(s32[8,384]{1,0:T(8,128)S(1)} %branch_1_fun.13.slots_ref, bf16[256,3328]{1,0:T(8,128)(2,1)S(1)} %bitcast.26, bf16[256,2048]{1,0:T(8,128)(2,1)S(1)} %copy-done.17), custom_call_target="tpu_custom_call" | custom-call | flops 805306368 | bytes 3670016 | tf_op jit(solution)/shard_map/cond/branch_1_fun/pallas_call | solution.py:763
  149.7 4.4 %branch_1_fun.25 = (bf16[384,2048]{1,0:T(8,128)(2,1)}, bf16[384,2048]{1,0:T(8,128)(2,1)}, f32[128,2048]{1,0:T(8,128)}) custom-call(s32[1]{0:T(128)} %bitcast.11.index_ref, s32[8,384]{1,0:T(8,128)S(1)} %branch_1_fun.13.slots_ref, bf16[384,2048]{1,0:T(8,128)(2,1)} %get-tuple-element.152.k_ref, bf16[384,2048]{1,0:T(8,128)(2,1)} %get-tuple-element.153.v_ref, ...), custom_call_target="tpu_custom_call" | custom-call | flops 402653184 | bytes 8912896 | tf_op jit(solution)/shard_map/cond/branch_1_fun/pallas_call | solution.py:807
  (77 shorter events, 0.5 us)
Async XLA Ops:
  0.6 4.4 %copy-start.48 = (s32[12288]{0:T(1024)S(1)}, s32[12288]{0:T(1024)}, u32[]{:S(2)}) copy-start(s32[12288]{0:T(1024)} %param.14) | copy-start | bytes 147460
  0.6 9.9 %copy-start.53 = (s32[8192]{0:T(1024)S(1)}, s32[8192]{0:T(1024)}, u32[]{:S(2)}) copy-start(s32[8192]{0:T(1024)} %param.15) | copy-start | bytes 98308
  3.6 4.7 %collective-permute-start.12 = (bf16[384,2048]{1,0:T(8,128)(2,1)}, bf16[384,2048]{1,0:T(8,128)(2,1)S(1)}, u32[]{:S(2)}, u32[]{:S(2)}) collective-permute-start(bf16[384,2048]{1,0:T(8,128)(2,1)} %shard_map.148), channel_id=1, source_target_pairs={{0,4},{4,0},{8,12},{12,8},{16,20},{20,16},{24,28},{28,24},{32,36},... | collective-permute-start | bytes 4718600 | tf_op jit(solution)/shard_map/ppermute | solution.py:838
  5.0 5.5 %collective-permute-start.13 = (bf16[384,2048]{1,0:T(8,128)(2,1)}, bf16[384,2048]{1,0:T(8,128)(2,1)S(1)}, u32[]{:S(2)}, u32[]{:S(2)}) collective-permute-start(bf16[384,2048]{1,0:T(8,128)(2,1)} %param.11), channel_id=1, source_target_pairs={{0,4},{4,0},{8,12},{12,8},{16,20},{20,16},{24,28},{28,24},{32,36},... | collective-permute-start | bytes 4718600 | tf_op jit(solution)/shard_map/ppermute | solution.py:838
  10.5 6.2 %copy-start.54 = (s32[8192]{0:T(1024)}, s32[8192]{0:T(1024)S(1)}, u32[]{:S(2)}) copy-start(s32[8192]{0:T(1024)S(1)} %get-tuple-element.106) | copy-start | bytes 98308 | tf_op jit(solution)/shard_map/cond
  16.8 8.1 %copy-start.55 = (s32[8192]{0:T(1024)S(1)}, s32[8192]{0:T(1024)}, u32[]{:S(2)}) copy-start(s32[8192]{0:T(1024)} %copy-done.54) | copy-start | bytes 98308 | tf_op jit(solution)/shard_map/cond
  16.8 36.0 %all-to-all-start.3 = ((bf16[32,8,4096]{2,1,0:T(8,128)(2,1)}), bf16[32,8,4096]{2,1,0:T(8,128)(2,1)S(1)}, u32[]{:S(2)}, u32[]{:S(2)}) async-start(bf16[32,8,4096]{2,1,0:T(8,128)(2,1)} %bitcast.34), calls=%async_computation.3 | async-start | bytes 4194304 | tf_op jit(solution)/shard_map/cond/branch_1_fun/all_to_all | solution.py:827
  29.6 0.7 copy-start.22
  30.3 0.6 copy-start.32
  30.9 0.6 copy-start.34
  31.6 24.8 %copy-start.24 = (bf16[128,384]{1,0:T(8,128)(2,1)}, bf16[128,384]{1,0:T(8,128)(2,1)S(1)}, u32[]{:S(2)}) copy-start(bf16[128,384]{1,0:T(8,128)(2,1)S(1)} %get-tuple-element.117.cc_head_t) | copy-start | bytes 294916 | tf_op jit(solution)/shard_map/cond
  31.6 24.8 %copy-start.36 = (bf16[384,128]{1,0:T(8,128)(2,1)}, bf16[384,128]{1,0:T(8,128)(2,1)S(1)}, u32[]{:S(2)}) copy-start(bf16[384,128]{1,0:T(8,128)(2,1)S(1)} %get-tuple-element.145.taps) | copy-start | bytes 294916 | tf_op jit(solution)/shard_map/cond
  31.6 24.8 %copy-start.46 = (bf16[640,128]{1,0:T(8,128)(2,1)}, bf16[640,128]{1,0:T(8,128)(2,1)S(1)}, u32[]{:S(2)}) copy-start(bf16[640,128]{1,0:T(8,128)(2,1)S(1)} %get-tuple-element.122.bb) | copy-start | bytes 491524 | tf_op jit(solution)/shard_map/cond
  31.6 24.8 %copy-start.50 = (f32[2048]{0:T(1024)S(1)}, f32[2048]{0:T(1024)}, u32[]{:S(2)}) copy-start(f32[2048]{0:T(1024)} %get-tuple-element.126) | copy-start | bytes 24580 | tf_op jit(solution)/shard_map/cond
  52.7 3.7 %copy-start.10 = (bf16[32,8,4096]{2,1,0:T(8,128)(2,1)}, bf16[32,8,4096]{2,1,0:T(8,128)(2,1)S(1)}, u32[]{:S(2)}) copy-start(bf16[32,8,4096]{2,1,0:T(8,128)(2,1)S(1)} %all-to-all-done.3) | copy-start | bytes 6291460 | tf_op jit(solution)/shard_map/cond
  54.2 10.0 %collective-permute-start.5 = (bf16[128,2048]{1,0:T(8,128)(2,1)}, bf16[128,2048]{1,0:T(8,128)(2,1)S(1)}, u32[]{:S(2)}, u32[]{:S(2)}) collective-permute-start(bf16[128,2048]{1,0:T(8,128)(2,1)} %branch_1_fun.16), channel_id=1, source_target_pairs={{0,4},{4,8},{8,12},{12,16},{16,20},{20,24},{24,28},{28,32},{32,36}... | collective-permute-start | bytes 1572872 | tf_op jit(solution)/shard_map/cond/branch_1_fun/ppermute | solution.py:834
  56.4 1.6 %copy-start.11 = (bf16[32,8,4096]{2,1,0:T(8,128)(2,1)S(1)}, bf16[32,8,4096]{2,1,0:T(8,128)(2,1)}, u32[]{:S(2)}) copy-start(bf16[32,8,4096]{2,1,0:T(8,128)(2,1)} %copy-done.10) | copy-start | bytes 6291460 | tf_op jit(solution)/shard_map/cond
  58.0 0.9 copy-start.47
  58.9 5.3 %copy-start.25 = (bf16[128,384]{1,0:T(8,128)(2,1)S(1)}, bf16[128,384]{1,0:T(8,128)(2,1)}, u32[]{:S(2)}) copy-start(bf16[128,384]{1,0:T(8,128)(2,1)} %copy-done.24) | copy-start | bytes 294916 | tf_op jit(solution)/shard_map/cond
  64.2 3.4 %copy-start.8 = (bf16[640,2048]{1,0:T(8,128)(2,1)}, bf16[640,2048]{1,0:T(8,128)(2,1)S(1)}, u32[]{:S(2)}) copy-start(bf16[640,2048]{1,0:T(8,128)(2,1)S(1)} %get-tuple-element.127.f_ref) | copy-start | bytes 7864324 | tf_op jit(solution)/shard_map/cond
  64.2 16.3 %copy-start.2 = (f32[256,2048]{1,0:T(8,128)}, f32[256,2048]{1,0:T(8,128)S(1)}, u32[]{:S(2)}) copy-start(f32[256,2048]{1,0:T(8,128)S(1)} %get-tuple-element.129.mix_ref) | copy-start | bytes 6291460 | tf_op jit(solution)/shard_map/cond
  67.6 12.9 %copy-start.14 = (f32[128,2048]{1,0:T(8,128)}, f32[128,2048]{1,0:T(8,128)S(1)}, u32[]{:S(2)}) copy-start(f32[128,2048]{1,0:T(8,128)S(1)} %get-tuple-element.132.mix_head_ref) | copy-start | bytes 3145732 | tf_op jit(solution)/shard_map/cond
  67.6 4.6 %collective-permute-start.8 = (f32[8,256]{1,0:T(8,128)S(1)}, f32[8,256]{1,0:T(8,128)S(1)}, u32[]{:S(2)}, u32[]{:S(2)}) collective-permute-start(f32[8,256]{1,0:T(8,128)S(1)} %get-tuple-element.131.s0), channel_id=1, source_target_pairs={{0,3},{1,0},{2,1},{3,2},{4,7},{5,4},{6,5},{7,6},{8,11},{9,8},{10,9... | collective-permute-start | bytes 24584 | tf_op jit(solution)/shard_map/cond/branch_1_fun/ppermute | solution.py:897
  71.4 4.0 %collective-permute-start.7 = (f32[8,256]{1,0:T(8,128)S(1)}, f32[8,256]{1,0:T(8,128)S(1)}, u32[]{:S(2)}, u32[]{:S(2)}) collective-permute-start(f32[8,256]{1,0:T(8,128)S(1)} %get-tuple-element.131.s0), channel_id=1, source_target_pairs={{0,2},{1,3},{2,0},{3,1},{4,6},{5,7},{6,4},{7,5},{8,10},{9,11},{10,... | collective-permute-start | bytes 24584 | tf_op jit(solution)/shard_map/cond/branch_1_fun/ppermute | solution.py:897
  71.4 4.0 %collective-permute-start.6 = (f32[8,256]{1,0:T(8,128)S(1)}, f32[8,256]{1,0:T(8,128)S(1)}, u32[]{:S(2)}, u32[]{:S(2)}) collective-permute-start(f32[8,256]{1,0:T(8,128)S(1)} %get-tuple-element.131.s0), channel_id=1, source_target_pairs={{0,1},{1,2},{2,3},{3,0},{4,5},{5,6},{6,7},{7,4},{8,9},{9,10},{10,1... | collective-permute-start | bytes 24584 | tf_op jit(solution)/shard_map/cond/branch_1_fun/ppermute | solution.py:897
  75.4 5.1 %copy-start.23 = (bf16[128,640]{1,0:T(8,128)(2,1)S(1)}, bf16[128,640]{1,0:T(8,128)(2,1)}, u32[]{:S(2)}) copy-start(bf16[128,640]{1,0:T(8,128)(2,1)} %copy-done.22) | copy-start | bytes 491524 | tf_op jit(solution)/shard_map/cond
  75.4 5.1 %copy-start.51 = (f32[2048]{0:T(1024)S(1)}, f32[2048]{0:T(1024)}, u32[]{:S(2)}) copy-start(f32[2048]{0:T(1024)} %get-tuple-element.126) | copy-start | bytes 24580 | tf_op jit(solution)/shard_map/cond
  76.9 11.3 %collective-permute-start.9 = (bf16[128,2048]{1,0:T(8,128)(2,1)}, bf16[128,2048]{1,0:T(8,128)(2,1)S(1)}, u32[]{:S(2)}, u32[]{:S(2)}) collective-permute-start(bf16[128,2048]{1,0:T(8,128)(2,1)} %branch_1_fun.21), channel_id=1, source_target_pairs={{4,0},{8,4},{12,8},{16,12},{20,16},{24,20},{28,24},{32,28},{36,32}... | collective-permute-start | bytes 1572872 | tf_op jit(solution)/shard_map/cond/branch_1_fun/ppermute | solution.py:834
  88.2 0.8 copy-start.20
  88.9 7.7 %copy-start.52 = (f32[2048]{0:T(1024)S(1)}, f32[2048]{0:T(1024)}, u32[]{:S(2)}) copy-start(f32[2048]{0:T(1024)} %get-tuple-element.126) | copy-start | bytes 24580 | tf_op jit(solution)/shard_map/cond
  89.0 31.7 %all-to-all-start.4 = ((bf16[32,8,3328]{2,1,0:T(8,128)(2,1)}), bf16[32,8,3328]{2,1,0:T(8,128)(2,1)S(1)}, u32[]{:S(2)}, u32[]{:S(2)}) async-start(bf16[32,8,3328]{2,1,0:T(8,128)(2,1)} %bitcast.36), calls=%async_computation.4 | async-start | bytes 3407872 | tf_op jit(solution)/shard_map/cond/branch_1_fun/all_to_all | solution.py:827
  96.6 1.6 %copy-start.3 = (f32[256,2048]{1,0:T(8,128)S(1)}, f32[256,2048]{1,0:T(8,128)}, u32[]{:S(2)}) copy-start(f32[256,2048]{1,0:T(8,128)} %copy-done.2) | copy-start | bytes 6291460 | tf_op jit(solution)/shard_map/cond
  98.2 1.7 %copy-start.9 = (bf16[640,2048]{1,0:T(8,128)(2,1)S(1)}, bf16[640,2048]{1,0:T(8,128)(2,1)}, u32[]{:S(2)}) copy-start(bf16[640,2048]{1,0:T(8,128)(2,1)} %copy-done.8) | copy-start | bytes 7864324 | tf_op jit(solution)/shard_map/cond
  99.9 1.2 copy-start.15
  101.2 6.0 %copy-start.21 = (bf16[128,2048]{1,0:T(8,128)(2,1)S(1)}, bf16[128,2048]{1,0:T(8,128)(2,1)}, u32[]{:S(2)}) copy-start(bf16[128,2048]{1,0:T(8,128)(2,1)} %copy-done.20) | copy-start | bytes 1572868 | tf_op jit(solution)/shard_map/cond
  101.2 6.0 %copy-start.33 = (bf16[384,128]{1,0:T(8,128)(2,1)S(1)}, bf16[384,128]{1,0:T(8,128)(2,1)}, u32[]{:S(2)}) copy-start(bf16[384,128]{1,0:T(8,128)(2,1)} %copy-done.32) | copy-start | bytes 294916 | tf_op jit(solution)/shard_map/cond
  101.2 6.0 %copy-start.35 = (bf16[128,384]{1,0:T(8,128)(2,1)S(1)}, bf16[128,384]{1,0:T(8,128)(2,1)}, u32[]{:S(2)}) copy-start(bf16[128,384]{1,0:T(8,128)(2,1)} %copy-done.34) | copy-start | bytes 294916 | tf_op jit(solution)/shard_map/cond
  101.2 6.0 %copy-start.37 = (bf16[384,128]{1,0:T(8,128)(2,1)S(1)}, bf16[384,128]{1,0:T(8,128)(2,1)}, u32[]{:S(2)}) copy-start(bf16[384,128]{1,0:T(8,128)(2,1)} %copy-done.36) | copy-start | bytes 294916 | tf_op jit(solution)/shard_map/cond
  121.5 24.2 %all-to-all-start.5 = ((bf16[32,8,2560]{2,1,0:T(8,128)(2,1)}), bf16[32,8,2560]{2,1,0:T(8,128)(2,1)S(1)}, u32[]{:S(2)}, u32[]{:S(2)}) async-start(bf16[32,8,2560]{2,1,0:T(8,128)(2,1)} %bitcast.33), calls=%async_computation.5 | async-start | bytes 2621440 | tf_op jit(solution)/shard_map/cond/branch_1_fun/all_to_all | solution.py:827
  126.1 2.7 %collective-permute-start.10 = (bf16[256,2048]{1,0:T(8,128)(2,1)S(1)}, bf16[256,2048]{1,0:T(8,128)(2,1)S(1)}, u32[]{:S(2)}, u32[]{:S(2)}) collective-permute-start(bf16[256,2048]{1,0:T(8,128)(2,1)S(1)} %pad_maximum_fusion.2), channel_id=1, source_target_pairs={{0,4},{4,0},{8,12},{12,8},{16,20},{20,16},{24,28},{28,24},{32,36},... | collective-permute-start | bytes 3145736 | tf_op jit(solution)/shard_map/cond/branch_1_fun/ppermute | solution.py:838
  128.8 1.0 copy-start.16
  145.7 3.9 %collective-permute-start.11 = (bf16[256,2560]{1,0:T(8,128)(2,1)S(1)}, bf16[256,2560]{1,0:T(8,128)(2,1)S(1)}, u32[]{:S(2)}, u32[]{:S(2)}) collective-permute-start(bf16[256,2560]{1,0:T(8,128)(2,1)S(1)} %bitcast.29), channel_id=1, source_target_pairs={{0,4},{4,0},{8,12},{12,8},{16,20},{20,16},{24,28},{28,24},{32,36},... | collective-permute-start | bytes 3932168 | tf_op jit(solution)/shard_map/cond/branch_1_fun/ppermute | solution.py:838
  146.1 1.2 copy-start.17

commit v8 on v7

--- a/solution.py
+++ b/solution.py
@@ -886,7 +886,7 @@
     received, pos_row, prepared = lax.optimization_barrier((received, pos_row, prepared))
     cc_own, cc_own_t, cc_halo, cc_head_t, bb, bb_t, *onward = prepared
 
-    halo = shift(place_tail(wide, pos_row, received, width), 1)
+    halo = shift(place_tail(2 * wide, pos_row, received, width), 1)
     q, mix, x, f, sums = forward(
         wide, pos_row, cc_own, cc_own_t, bb, received, mr_filter, residual, cotangent, gain
     )
@@ -896,7 +896,7 @@
     all_sums = [sums] + [
         lax.ppermute(sums, "mp", [(i, (i + k) % 4) for i in range(4)]) for k in (1, 2, 3)
     ]
-    head = head_grad(wide, all_sums, q, summed_head, scaled_head)
+    head = head_grad(2 * wide, all_sums, q, summed_head, scaled_head)
     d_mix, sent_dq = backward(
         pair, all_sums, pos_row, cc_own, cc_halo, bb_t, q, mix, mix_head, x, halo,
         residual, cotangent, gain,

time: 155 us -> 155 us (level)
  no operation moved by 1% of the time
where the time goes in v8:
time: 155 us; the launch traced here: 154 us
  waiting for transfers between devices  55.9 us (36%)
  Pallas kernels  46 us (30%)
  starting transfers between devices  32.2 us (21%)
  local copies, waits for them, and re-layouts  12.9 us (8%)
  other arithmetic  4.9 us (3%)
    all_to_all x3, waiting for transfers between devices, exchange(): lax.all_to_all(shards, 'seq', split_axis=0, concat_axis=0, tiled=True)  46.1 us
    all_to_all x3, starting transfers between devices, exchange(): lax.all_to_all(shards, 'seq', split_axis=0, concat_axis=0, tiled=True)  19.7 us
    cond x58, local copies, waits for them, and re-layouts  12 us
    pallas_call x1, Pallas kernels, backward(): pl.pallas_call(functools.partial(backward_kernel, pair), grid=(steps,), i...  7.18 us
    ppermute x4, waiting for transfers between devices, swap(): return lax.ppermute(value, 'seq', [(i, i ^ 1) for i in range(SHARDS)])  6.09 us
    pallas_call x1, Pallas kernels, finish(): pl.pallas_call(finish_kernel, grid=(width // wide,), in_specs=[RESIDENT]...  6.01 us
    pallas_call x1, Pallas kernels, pack_arrivals(): pl.pallas_call(functools.partial(pack_kernel, halves, blocks), grid=(2 *...  5.8 us
    ppermute x2, starting transfers between devices, shift(): return lax.ppermute(value, 'seq', pairs)  5.77 us
  transfers between devices with their start and end apart: 12, of which 9 were waited for; matrix products, arithmetic and copies ran while one was open for 4% of the time, Pallas kernels for 17%

profile of v8, /device:TPU:1, one launch (start us, length us, event | category | flops | bytes accessed | tf_op | source)
XLA Modules:
  0.0 153.8 jit_solution(147662566370138341)
XLA Ops:
  0.7 2.9 %shard_map.148 = bf16[384,2048]{1,0:T(8,128)(2,1)} custom-call(bf16[384,2048]{1,0:T(8,128)(2,1)} %k_ref.1, bf16[384,2048]{1,0:T(8,128)(2,1)} %v_ref.1), custom_call_target="tpu_custom_call" | custom-call | flops 786432 | bytes 4718592 | tf_op jit(solution)/shard_map/pallas_call | solution.py:207
  3.6 1.4 collective-permute-start.12
  5.1 0.4 convert_reduce_fusion.4
  5.4 0.6 reduce_max.9
  6.7 1.5 collective-permute-done.12
  8.3 2.2 %collective-permute-done.13 = bf16[384,2048]{1,0:T(8,128)(2,1)S(1)} collective-permute-done((bf16[384,2048]{1,0:T(8,128)(2,1)}, bf16[384,2048]{1,0:T(8,128)(2,1)S(1)}, u32[]{:S(2)}, u32[]{:S(2)}) %collective-permute-start.13) | collective-permute-done | bytes 1572896 | tf_op jit(solution)/shard_map/ppermute | solution.py:838
  10.5 143.3 %conditional.1 = (bf16[256,2048]{1,0:T(8,128)(2,1)}, bf16[256,2048]{1,0:T(8,128)(2,1)}, bf16[384,2048]{1,0:T(8,128)(2,1)}, bf16[384,2048]{1,0:T(8,128)(2,1)}, f3...) conditional(s32[]{:T(128)} %convert_element_type.91, (s32[12288]{0:T(1024)S(1)}, ...), branch_computations={%region_2.14_spmd, %region_14.26_spmd} | conditional | flops 11994341376 | bytes 193494464 | solution.py:938
  10.5 0.4 branch_1_fun.13.slots_ref
  11.0 5.8 %branch_1_fun.14 = bf16[256,4096]{1,0:T(8,128)(2,1)} custom-call(s32[8,384]{1,0:T(8,128)S(1)} %branch_1_fun.13.slots_ref, bf16[384,2048]{1,0:T(8,128)(2,1)} %get-tuple-element.99.refs_0_, bf16[384,2048]{1,0:T(8,128)(2,1)S(1)} %get-tuple-element.100.refs_1_, bf16[384,2048]{1,0:T(8,128)(2,1)} %get-tuple-element.101.refs_2_, ...), custom_call_target="tpu_custom_call" | custom-call | flops 1610612736 | bytes 8388608 | tf_op jit(solution)/shard_map/cond/branch_1_fun/pallas_call | solution.py:185
  16.8 7.7 %all-to-all-start.3 = ((bf16[32,8,4096]{2,1,0:T(8,128)(2,1)}), bf16[32,8,4096]{2,1,0:T(8,128)(2,1)S(1)}, u32[]{:S(2)}, u32[]{:S(2)}) async-start(bf16[32,8,4096]{2,1,0:T(8,128)(2,1)} %bitcast.34), calls=%async_computation.3 | async-start | bytes 4194304 | tf_op jit(solution)/shard_map/cond/branch_1_fun/all_to_all | solution.py:827
  24.5 0.1 multiply_add_fusion.4
  24.6 0.3 fusion.40
  24.9 0.1 fusion.69
  25.0 0.2 select_reduce_fusion.13
  25.2 0.1 select_reduce_fusion.17
  25.3 0.2 select_reduce_fusion.10
  25.5 0.4 select_reduce_fusion.9
  25.9 0.6 slice.32
  26.7 0.1 multiply_multiply_fusion.6
  26.8 0.4 select_multiply_fusion.3
  27.2 0.1 broadcast_compare_fusion.2
  27.4 0.9 multiply_add_fusion.3
  28.3 0.1 maximum_select_fusion.2.cc_ref
  28.4 0.7 slice_compare_fusion.2
  29.0 0.2 multiply_add_fusion.5
  29.2 0.1 fusion.48
  29.3 0.3 branch_1_fun.15
  29.6 0.7 copy-done.22
  30.3 0.6 copy-done.32
  30.9 0.6 copy-done.34
  31.6 21.1 %all-to-all-done.3 = bf16[32,8,4096]{2,1,0:T(8,128)(2,1)S(1)} async-done(((bf16[32,8,4096]{2,1,0:T(8,128)(2,1)}), bf16[32,8,4096]{2,1,0:T(8,128)(2,1)S(1)}, u32[]{:S(2)}, u32[]{:S(2)}) %all-to-all-start.3) | async-done | bytes 2097184 | tf_op jit(solution)/shard_map/cond/branch_1_fun/all_to_all | solution.py:827
  52.7 1.4 branch_1_fun.16
  54.1 2.1 %collective-permute-start.5 = (bf16[128,2048]{1,0:T(8,128)(2,1)}, bf16[128,2048]{1,0:T(8,128)(2,1)S(1)}, u32[]{:S(2)}, u32[]{:S(2)}) collective-permute-start(bf16[128,2048]{1,0:T(8,128)(2,1)} %branch_1_fun.16), channel_id=1, source_target_pairs={{0,4},{4,8},{8,12},{12,16},{16,20},{20,24},{24,28},{28,32},{32,36}... | collective-permute-start | bytes 1572872 | tf_op jit(solution)/shard_map/cond/branch_1_fun/ppermute | solution.py:834
  56.3 1.6 %copy-done.11 = bf16[32,8,4096]{2,1,0:T(8,128)(2,1)S(1)} copy-done((bf16[32,8,4096]{2,1,0:T(8,128)(2,1)S(1)}, bf16[32,8,4096]{2,1,0:T(8,128)(2,1)}, u32[]{:S(2)}) %copy-start.11) | copy-done | bytes 2097176 | tf_op jit(solution)/shard_map/cond
  57.9 0.9 copy-done.47
  58.9 5.3 %branch_1_fun.17 = (bf16[256,2048]{1,0:T(8,128)(2,1)S(1)}, f32[256,2048]{1,0:T(8,128)S(1)}, bf16[640,2048]{1,0:T(8,128)(2,1)S(1)}, bf16[640,2048]{1,0:T(8,128)(2,1)S(1)}, f32[8,128]{1,0:T(8,128)S(1)}) custom-call(s32[1,256]{1,0:T(1,128)S(1)} %sub.159.pos_row, bf16[640,256]{1,0:T(8,128)(2,1)S(1)} %get-tuple-element.120.cc_own, ...), custom_call_target="tpu_custom_call" | custom-call | flops 4000000000 | bytes 12288000 | tf_op jit(solution)/shard_map/cond/branch_1_fun/pallas_call | solution.py:373
  64.2 3.3 %branch_1_fun.18 = (f32[128,2048]{1,0:T(8,128)S(1)}, f32[128,2048]{1,0:T(8,128)S(1)}, f32[128,2048]{1,0:T(8,128)S(1)}, f32[8,256]{1,0:T(8,128)S(1)}) custom-call(bf16[384,128]{1,0:T(8,128)(2,1)S(1)} %get-tuple-element.116.cc_halo, bf16[128,384]{1,0:T(8,128)(2,1)S(1)} %copy-done.25, bf16[128,2048]{1,0:T(8,128)(2,1)S(1)} %collective-permute-done.5.halo.halo_ref, ...), custom_call_target="tpu_custom_call" | custom-call | flops 600000000 | bytes 6144000 | tf_op jit(solution)/shard_map/cond/branch_1_fun/pallas_call | solution.py:436
  67.5 3.8 %collective-permute-start.8 = (f32[8,256]{1,0:T(8,128)S(1)}, f32[8,256]{1,0:T(8,128)S(1)}, u32[]{:S(2)}, u32[]{:S(2)}) collective-permute-start(f32[8,256]{1,0:T(8,128)S(1)} %get-tuple-element.131.s0), channel_id=1, source_target_pairs={{0,3},{1,0},{2,1},{3,2},{4,7},{5,4},{6,5},{7,6},{8,11},{9,8},{10,9... | collective-permute-start | bytes 24584 | tf_op jit(solution)/shard_map/cond/branch_1_fun/ppermute | solution.py:897
  71.3 0.7 collective-permute-start.6
  72.0 0.1 collective-permute-done.8.s3
  72.1 3.2 %collective-permute-done.7.s2 = f32[8,256]{1,0:T(8,128)S(1)} collective-permute-done((f32[8,256]{1,0:T(8,128)S(1)}, f32[8,256]{1,0:T(8,128)S(1)}, u32[]{:S(2)}, u32[]{:S(2)}) %collective-permute-start.7) | collective-permute-done | bytes 8224 | tf_op jit(solution)/shard_map/cond/branch_1_fun/ppermute | solution.py:897
  75.3 1.3 branch_1_fun.21
  76.6 3.6 %collective-permute-start.9 = (bf16[128,2048]{1,0:T(8,128)(2,1)}, bf16[128,2048]{1,0:T(8,128)(2,1)S(1)}, u32[]{:S(2)}, u32[]{:S(2)}) collective-permute-start(bf16[128,2048]{1,0:T(8,128)(2,1)} %branch_1_fun.21), channel_id=1, source_target_pairs={{4,0},{8,4},{12,8},{16,12},{20,16},{24,20},{28,24},{32,28},{36,32}... | collective-permute-start | bytes 1572872 | tf_op jit(solution)/shard_map/cond/branch_1_fun/ppermute | solution.py:834
  80.3 7.2 %branch_1_fun.19 = (bf16[256,2048]{1,0:T(8,128)(2,1)}, bf16[256,3328]{1,0:T(8,128)(2,1)}) custom-call(f32[8,256]{1,0:T(8,128)S(1)} %get-tuple-element.131.s0, f32[8,256]{1,0:T(8,128)S(1)} %collective-permute-done.6.s1, f32[8,256]{1,0:T(8,128)S(1)} %collective-permute-done.7.s2, f32[8,256]{1,0:T(8,128)S(1)} %collective-permute-done.8.s3, ...), custom_call_target="tpu_custom_call" | custom-call | flops 2000000000 | bytes 12288000 | tf_op jit(solution)/shard_map/cond/branch_1_fun/pallas_call | solution.py:598
  87.5 0.4 collective-permute-done.9.next_ref
  87.9 0.8 copy-done.20
  88.7 7.7 %all-to-all-start.4 = ((bf16[32,8,3328]{2,1,0:T(8,128)(2,1)}), bf16[32,8,3328]{2,1,0:T(8,128)(2,1)S(1)}, u32[]{:S(2)}, u32[]{:S(2)}) async-start(bf16[32,8,3328]{2,1,0:T(8,128)(2,1)} %bitcast.36), calls=%async_computation.4 | async-start | bytes 3407872 | tf_op jit(solution)/shard_map/cond/branch_1_fun/all_to_all | solution.py:827
  96.4 1.6 %copy-done.3 = f32[256,2048]{1,0:T(8,128)S(1)} copy-done((f32[256,2048]{1,0:T(8,128)S(1)}, f32[256,2048]{1,0:T(8,128)}, u32[]{:S(2)}) %copy-start.3) | copy-done | bytes 2097176 | tf_op jit(solution)/shard_map/cond
  98.0 1.7 %copy-done.9 = bf16[640,2048]{1,0:T(8,128)(2,1)S(1)} copy-done((bf16[640,2048]{1,0:T(8,128)(2,1)S(1)}, bf16[640,2048]{1,0:T(8,128)(2,1)}, u32[]{:S(2)}) %copy-start.9) | copy-done | bytes 2621464 | tf_op jit(solution)/shard_map/cond
  99.7 1.2 copy-done.15
  100.9 6.0 %branch_1_fun.20 = (bf16[256,2048]{1,0:T(8,128)(2,1)}, bf16[256,2048]{1,0:T(8,128)(2,1)}, f32[256,2048]{1,0:T(8,128)}) custom-call(f32[8,256]{1,0:T(8,128)S(1)} %get-tuple-element.131.s0, f32[8,256]{1,0:T(8,128)S(1)} %collective-permute-done.6.s1, f32[8,256]{1,0:T(8,128)S(1)} %collective-permute-done.7.s2, f32[8,256]{1,0:T(8,128)S(1)} %collective-permute-done.8.s3, ...), custom_call_target="tpu_custom_call" | custom-call | flops 1342177280 | bytes 12288000 | tf_op jit(solution)/shard_map/cond/branch_1_fun/pallas_call | solution.py:639
  107.0 4.5 %branch_1_fun.22.rows_ref = bf16[256,2560]{1,0:T(8,128)(2,1)} custom-call(s32[1,256]{1,0:T(1,128)S(1)} %sub.159.pos_row, bf16[384,128]{1,0:T(8,128)(2,1)S(1)} %copy-done.33, bf16[128,384]{1,0:T(8,128)(2,1)S(1)} %copy-done.35, bf16[384,128]{1,0:T(8,128)(2,1)S(1)} %copy-done.37, f32[256,2048]{1,0:T(8,128)} %get-tuple-element.146.own_ref, ...), custom_call_target="tpu_custom_call" | custom-call | flops 268435456 | bytes 4915200 | tf_op jit(solution)/shard_map/cond/branch_1_fun/pallas_call | solution.py:677
  111.5 9.0 %all-to-all-done.4 = bf16[32,8,3328]{2,1,0:T(8,128)(2,1)S(1)} async-done(((bf16[32,8,3328]{2,1,0:T(8,128)(2,1)}), bf16[32,8,3328]{2,1,0:T(8,128)(2,1)S(1)}, u32[]{:S(2)}, u32[]{:S(2)}) %all-to-all-start.4) | async-done | bytes 1703968 | tf_op jit(solution)/shard_map/cond/branch_1_fun/all_to_all | solution.py:827
  120.4 0.8 branch_1_fun.23
  121.2 4.3 %all-to-all-start.5 = ((bf16[32,8,2560]{2,1,0:T(8,128)(2,1)}), bf16[32,8,2560]{2,1,0:T(8,128)(2,1)S(1)}, u32[]{:S(2)}, u32[]{:S(2)}) async-start(bf16[32,8,2560]{2,1,0:T(8,128)(2,1)} %bitcast.33), calls=%async_computation.5 | async-start | bytes 2621440 | tf_op jit(solution)/shard_map/cond/branch_1_fun/all_to_all | solution.py:827
  125.6 0.1 fusion.85
  125.8 0.4 collective-permute-start.10
  126.3 2.3 %collective-permute-done.10.refs_1_ = bf16[256,2048]{1,0:T(8,128)(2,1)S(1)} collective-permute-done((bf16[256,2048]{1,0:T(8,128)(2,1)S(1)}, bf16[256,2048]{1,0:T(8,128)(2,1)S(1)}, u32[]{:S(2)}, u32[]{:S(2)}) %collective-permute-start.10) | collective-permute-done | bytes 1048608 | tf_op jit(solution)/shard_map/cond/branch_1_fun/ppermute | solution.py:838
  128.6 1.0 copy-done.16
  129.5 15.9 %all-to-all-done.5 = bf16[32,8,2560]{2,1,0:T(8,128)(2,1)S(1)} async-done(((bf16[32,8,2560]{2,1,0:T(8,128)(2,1)}), bf16[32,8,2560]{2,1,0:T(8,128)(2,1)S(1)}, u32[]{:S(2)}, u32[]{:S(2)}) %all-to-all-start.5) | async-done | bytes 1310752 | tf_op jit(solution)/shard_map/cond/branch_1_fun/all_to_all | solution.py:827
  145.5 0.4 collective-permute-start.11
  145.9 1.2 copy-done.17
  147.1 2.3 %branch_1_fun.24 = bf16[384,2048]{1,0:T(8,128)(2,1)} custom-call(s32[8,384]{1,0:T(8,128)S(1)} %branch_1_fun.13.slots_ref, bf16[256,3328]{1,0:T(8,128)(2,1)S(1)} %bitcast.26, bf16[256,2048]{1,0:T(8,128)(2,1)S(1)} %copy-done.17), custom_call_target="tpu_custom_call" | custom-call | flops 805306368 | bytes 3670016 | tf_op jit(solution)/shard_map/cond/branch_1_fun/pallas_call | solution.py:763
  149.4 4.4 %branch_1_fun.25 = (bf16[384,2048]{1,0:T(8,128)(2,1)}, bf16[384,2048]{1,0:T(8,128)(2,1)}, f32[128,2048]{1,0:T(8,128)}) custom-call(s32[1]{0:T(128)} %bitcast.11.index_ref, s32[8,384]{1,0:T(8,128)S(1)} %branch_1_fun.13.slots_ref, bf16[384,2048]{1,0:T(8,128)(2,1)} %get-tuple-element.152.k_ref, bf16[384,2048]{1,0:T(8,128)(2,1)} %get-tuple-element.153.v_ref, ...), custom_call_target="tpu_custom_call" | custom-call | flops 402653184 | bytes 8912896 | tf_op jit(solution)/shard_map/cond/branch_1_fun/pallas_call | solution.py:807
  (77 shorter events, 0.5 us)
Async XLA Ops:
  0.6 4.4 %copy-start.48 = (s32[12288]{0:T(1024)S(1)}, s32[12288]{0:T(1024)}, u32[]{:S(2)}) copy-start(s32[12288]{0:T(1024)} %param.14) | copy-start | bytes 147460
  0.6 9.9 %copy-start.53 = (s32[8192]{0:T(1024)S(1)}, s32[8192]{0:T(1024)}, u32[]{:S(2)}) copy-start(s32[8192]{0:T(1024)} %param.15) | copy-start | bytes 98308
  3.6 4.7 %collective-permute-start.12 = (bf16[384,2048]{1,0:T(8,128)(2,1)}, bf16[384,2048]{1,0:T(8,128)(2,1)S(1)}, u32[]{:S(2)}, u32[]{:S(2)}) collective-permute-start(bf16[384,2048]{1,0:T(8,128)(2,1)} %shard_map.148), channel_id=1, source_target_pairs={{0,4},{4,0},{8,12},{12,8},{16,20},{20,16},{24,28},{28,24},{32,36},... | collective-permute-start | bytes 4718600 | tf_op jit(solution)/shard_map/ppermute | solution.py:838
  5.0 5.5 %collective-permute-start.13 = (bf16[384,2048]{1,0:T(8,128)(2,1)}, bf16[384,2048]{1,0:T(8,128)(2,1)S(1)}, u32[]{:S(2)}, u32[]{:S(2)}) collective-permute-start(bf16[384,2048]{1,0:T(8,128)(2,1)} %param.11), channel_id=1, source_target_pairs={{0,4},{4,0},{8,12},{12,8},{16,20},{20,16},{24,28},{28,24},{32,36},... | collective-permute-start | bytes 4718600 | tf_op jit(solution)/shard_map/ppermute | solution.py:838
  10.5 6.2 %copy-start.54 = (s32[8192]{0:T(1024)}, s32[8192]{0:T(1024)S(1)}, u32[]{:S(2)}) copy-start(s32[8192]{0:T(1024)S(1)} %get-tuple-element.106) | copy-start | bytes 98308 | tf_op jit(solution)/shard_map/cond
  16.8 8.1 %copy-start.55 = (s32[8192]{0:T(1024)S(1)}, s32[8192]{0:T(1024)}, u32[]{:S(2)}) copy-start(s32[8192]{0:T(1024)} %copy-done.54) | copy-start | bytes 98308 | tf_op jit(solution)/shard_map/cond
  16.8 36.0 %all-to-all-start.3 = ((bf16[32,8,4096]{2,1,0:T(8,128)(2,1)}), bf16[32,8,4096]{2,1,0:T(8,128)(2,1)S(1)}, u32[]{:S(2)}, u32[]{:S(2)}) async-start(bf16[32,8,4096]{2,1,0:T(8,128)(2,1)} %bitcast.34), calls=%async_computation.3 | async-start | bytes 4194304 | tf_op jit(solution)/shard_map/cond/branch_1_fun/all_to_all | solution.py:827
  29.6 0.7 copy-start.22
  30.3 0.6 copy-start.32
  30.9 0.6 copy-start.34
  31.6 24.7 %copy-start.24 = (bf16[128,384]{1,0:T(8,128)(2,1)}, bf16[128,384]{1,0:T(8,128)(2,1)S(1)}, u32[]{:S(2)}) copy-start(bf16[128,384]{1,0:T(8,128)(2,1)S(1)} %get-tuple-element.117.cc_head_t) | copy-start | bytes 294916 | tf_op jit(solution)/shard_map/cond
  31.6 24.7 %copy-start.36 = (bf16[384,128]{1,0:T(8,128)(2,1)}, bf16[384,128]{1,0:T(8,128)(2,1)S(1)}, u32[]{:S(2)}) copy-start(bf16[384,128]{1,0:T(8,128)(2,1)S(1)} %get-tuple-element.145.taps) | copy-start | bytes 294916 | tf_op jit(solution)/shard_map/cond
  31.6 24.7 %copy-start.46 = (bf16[640,128]{1,0:T(8,128)(2,1)}, bf16[640,128]{1,0:T(8,128)(2,1)S(1)}, u32[]{:S(2)}) copy-start(bf16[640,128]{1,0:T(8,128)(2,1)S(1)} %get-tuple-element.122.bb) | copy-start | bytes 491524 | tf_op jit(solution)/shard_map/cond
  31.6 24.7 %copy-start.50 = (f32[2048]{0:T(1024)S(1)}, f32[2048]{0:T(1024)}, u32[]{:S(2)}) copy-start(f32[2048]{0:T(1024)} %get-tuple-element.126) | copy-start | bytes 24580 | tf_op jit(solution)/shard_map/cond
  52.7 3.6 %copy-start.10 = (bf16[32,8,4096]{2,1,0:T(8,128)(2,1)}, bf16[32,8,4096]{2,1,0:T(8,128)(2,1)S(1)}, u32[]{:S(2)}) copy-start(bf16[32,8,4096]{2,1,0:T(8,128)(2,1)S(1)} %all-to-all-done.3) | copy-start | bytes 6291460 | tf_op jit(solution)/shard_map/cond
  54.1 10.0 %collective-permute-start.5 = (bf16[128,2048]{1,0:T(8,128)(2,1)}, bf16[128,2048]{1,0:T(8,128)(2,1)S(1)}, u32[]{:S(2)}, u32[]{:S(2)}) collective-permute-start(bf16[128,2048]{1,0:T(8,128)(2,1)} %branch_1_fun.16), channel_id=1, source_target_pairs={{0,4},{4,8},{8,12},{12,16},{16,20},{20,24},{24,28},{28,32},{32,36}... | collective-permute-start | bytes 1572872 | tf_op jit(solution)/shard_map/cond/branch_1_fun/ppermute | solution.py:834
  56.3 1.6 %copy-start.11 = (bf16[32,8,4096]{2,1,0:T(8,128)(2,1)S(1)}, bf16[32,8,4096]{2,1,0:T(8,128)(2,1)}, u32[]{:S(2)}) copy-start(bf16[32,8,4096]{2,1,0:T(8,128)(2,1)} %copy-done.10) | copy-start | bytes 6291460 | tf_op jit(solution)/shard_map/cond
  57.9 0.9 copy-start.47
  58.8 5.3 %copy-start.25 = (bf16[128,384]{1,0:T(8,128)(2,1)S(1)}, bf16[128,384]{1,0:T(8,128)(2,1)}, u32[]{:S(2)}) copy-start(bf16[128,384]{1,0:T(8,128)(2,1)} %copy-done.24) | copy-start | bytes 294916 | tf_op jit(solution)/shard_map/cond
  64.2 3.4 %copy-start.8 = (bf16[640,2048]{1,0:T(8,128)(2,1)}, bf16[640,2048]{1,0:T(8,128)(2,1)S(1)}, u32[]{:S(2)}) copy-start(bf16[640,2048]{1,0:T(8,128)(2,1)S(1)} %get-tuple-element.127.f_ref) | copy-start | bytes 7864324 | tf_op jit(solution)/shard_map/cond
  64.2 16.1 %copy-start.2 = (f32[256,2048]{1,0:T(8,128)}, f32[256,2048]{1,0:T(8,128)S(1)}, u32[]{:S(2)}) copy-start(f32[256,2048]{1,0:T(8,128)S(1)} %get-tuple-element.129.mix_ref) | copy-start | bytes 6291460 | tf_op jit(solution)/shard_map/cond
  67.5 12.8 %copy-start.14 = (f32[128,2048]{1,0:T(8,128)}, f32[128,2048]{1,0:T(8,128)S(1)}, u32[]{:S(2)}) copy-start(f32[128,2048]{1,0:T(8,128)S(1)} %get-tuple-element.132.mix_head_ref) | copy-start | bytes 3145732 | tf_op jit(solution)/shard_map/cond
  67.5 4.6 %collective-permute-start.8 = (f32[8,256]{1,0:T(8,128)S(1)}, f32[8,256]{1,0:T(8,128)S(1)}, u32[]{:S(2)}, u32[]{:S(2)}) collective-permute-start(f32[8,256]{1,0:T(8,128)S(1)} %get-tuple-element.131.s0), channel_id=1, source_target_pairs={{0,3},{1,0},{2,1},{3,2},{4,7},{5,4},{6,5},{7,6},{8,11},{9,8},{10,9... | collective-permute-start | bytes 24584 | tf_op jit(solution)/shard_map/cond/branch_1_fun/ppermute | solution.py:897
  71.3 4.0 %collective-permute-start.7 = (f32[8,256]{1,0:T(8,128)S(1)}, f32[8,256]{1,0:T(8,128)S(1)}, u32[]{:S(2)}, u32[]{:S(2)}) collective-permute-start(f32[8,256]{1,0:T(8,128)S(1)} %get-tuple-element.131.s0), channel_id=1, source_target_pairs={{0,2},{1,3},{2,0},{3,1},{4,6},{5,7},{6,4},{7,5},{8,10},{9,11},{10,... | collective-permute-start | bytes 24584 | tf_op jit(solution)/shard_map/cond/branch_1_fun/ppermute | solution.py:897
  71.3 4.0 %collective-permute-start.6 = (f32[8,256]{1,0:T(8,128)S(1)}, f32[8,256]{1,0:T(8,128)S(1)}, u32[]{:S(2)}, u32[]{:S(2)}) collective-permute-start(f32[8,256]{1,0:T(8,128)S(1)} %get-tuple-element.131.s0), channel_id=1, source_target_pairs={{0,1},{1,2},{2,3},{3,0},{4,5},{5,6},{6,7},{7,4},{8,9},{9,10},{10,1... | collective-permute-start | bytes 24584 | tf_op jit(solution)/shard_map/cond/branch_1_fun/ppermute | solution.py:897
  75.3 5.0 %copy-start.23 = (bf16[128,640]{1,0:T(8,128)(2,1)S(1)}, bf16[128,640]{1,0:T(8,128)(2,1)}, u32[]{:S(2)}) copy-start(bf16[128,640]{1,0:T(8,128)(2,1)} %copy-done.22) | copy-start | bytes 491524 | tf_op jit(solution)/shard_map/cond
  75.3 5.0 %copy-start.51 = (f32[2048]{0:T(1024)S(1)}, f32[2048]{0:T(1024)}, u32[]{:S(2)}) copy-start(f32[2048]{0:T(1024)} %get-tuple-element.126) | copy-start | bytes 24580 | tf_op jit(solution)/shard_map/cond
  76.6 11.3 %collective-permute-start.9 = (bf16[128,2048]{1,0:T(8,128)(2,1)}, bf16[128,2048]{1,0:T(8,128)(2,1)S(1)}, u32[]{:S(2)}, u32[]{:S(2)}) collective-permute-start(bf16[128,2048]{1,0:T(8,128)(2,1)} %branch_1_fun.21), channel_id=1, source_target_pairs={{4,0},{8,4},{12,8},{16,12},{20,16},{24,20},{28,24},{32,28},{36,32}... | collective-permute-start | bytes 1572872 | tf_op jit(solution)/shard_map/cond/branch_1_fun/ppermute | solution.py:834
  87.9 0.8 copy-start.20
  88.7 7.7 %copy-start.52 = (f32[2048]{0:T(1024)S(1)}, f32[2048]{0:T(1024)}, u32[]{:S(2)}) copy-start(f32[2048]{0:T(1024)} %get-tuple-element.126) | copy-start | bytes 24580 | tf_op jit(solution)/shard_map/cond
  88.7 31.8 %all-to-all-start.4 = ((bf16[32,8,3328]{2,1,0:T(8,128)(2,1)}), bf16[32,8,3328]{2,1,0:T(8,128)(2,1)S(1)}, u32[]{:S(2)}, u32[]{:S(2)}) async-start(bf16[32,8,3328]{2,1,0:T(8,128)(2,1)} %bitcast.36), calls=%async_computation.4 | async-start | bytes 3407872 | tf_op jit(solution)/shard_map/cond/branch_1_fun/all_to_all | solution.py:827
  96.4 1.6 %copy-start.3 = (f32[256,2048]{1,0:T(8,128)S(1)}, f32[256,2048]{1,0:T(8,128)}, u32[]{:S(2)}) copy-start(f32[256,2048]{1,0:T(8,128)} %copy-done.2) | copy-start | bytes 6291460 | tf_op jit(solution)/shard_map/cond
  98.0 1.7 %copy-start.9 = (bf16[640,2048]{1,0:T(8,128)(2,1)S(1)}, bf16[640,2048]{1,0:T(8,128)(2,1)}, u32[]{:S(2)}) copy-start(bf16[640,2048]{1,0:T(8,128)(2,1)} %copy-done.8) | copy-start | bytes 7864324 | tf_op jit(solution)/shard_map/cond
  99.7 1.2 copy-start.15
  100.9 6.0 %copy-start.21 = (bf16[128,2048]{1,0:T(8,128)(2,1)S(1)}, bf16[128,2048]{1,0:T(8,128)(2,1)}, u32[]{:S(2)}) copy-start(bf16[128,2048]{1,0:T(8,128)(2,1)} %copy-done.20) | copy-start | bytes 1572868 | tf_op jit(solution)/shard_map/cond
  100.9 6.0 %copy-start.33 = (bf16[384,128]{1,0:T(8,128)(2,1)S(1)}, bf16[384,128]{1,0:T(8,128)(2,1)}, u32[]{:S(2)}) copy-start(bf16[384,128]{1,0:T(8,128)(2,1)} %copy-done.32) | copy-start | bytes 294916 | tf_op jit(solution)/shard_map/cond
  100.9 6.0 %copy-start.35 = (bf16[128,384]{1,0:T(8,128)(2,1)S(1)}, bf16[128,384]{1,0:T(8,128)(2,1)}, u32[]{:S(2)}) copy-start(bf16[128,384]{1,0:T(8,128)(2,1)} %copy-done.34) | copy-start | bytes 294916 | tf_op jit(solution)/shard_map/cond
  100.9 6.0 %copy-start.37 = (bf16[384,128]{1,0:T(8,128)(2,1)S(1)}, bf16[384,128]{1,0:T(8,128)(2,1)}, u32[]{:S(2)}) copy-start(bf16[384,128]{1,0:T(8,128)(2,1)} %copy-done.36) | copy-start | bytes 294916 | tf_op jit(solution)/shard_map/cond
  121.2 24.2 %all-to-all-start.5 = ((bf16[32,8,2560]{2,1,0:T(8,128)(2,1)}), bf16[32,8,2560]{2,1,0:T(8,128)(2,1)S(1)}, u32[]{:S(2)}, u32[]{:S(2)}) async-start(bf16[32,8,2560]{2,1,0:T(8,128)(2,1)} %bitcast.33), calls=%async_computation.5 | async-start | bytes 2621440 | tf_op jit(solution)/shard_map/cond/branch_1_fun/all_to_all | solution.py:827
  125.8 2.7 %collective-permute-start.10 = (bf16[256,2048]{1,0:T(8,128)(2,1)S(1)}, bf16[256,2048]{1,0:T(8,128)(2,1)S(1)}, u32[]{:S(2)}, u32[]{:S(2)}) collective-permute-start(bf16[256,2048]{1,0:T(8,128)(2,1)S(1)} %pad_maximum_fusion.2), channel_id=1, source_target_pairs={{0,4},{4,0},{8,12},{12,8},{16,20},{20,16},{24,28},{28,24},{32,36},... | collective-permute-start | bytes 3145736 | tf_op jit(solution)/shard_map/cond/branch_1_fun/ppermute | solution.py:838
  128.6 1.0 copy-start.16
  145.5 3.9 %collective-permute-start.11 = (bf16[256,2560]{1,0:T(8,128)(2,1)S(1)}, bf16[256,2560]{1,0:T(8,128)(2,1)S(1)}, u32[]{:S(2)}, u32[]{:S(2)}) collective-permute-start(bf16[256,2560]{1,0:T(8,128)(2,1)S(1)} %bitcast.29), channel_id=1, source_target_pairs={{0,4},{4,0},{8,12},{12,8},{16,20},{20,16},{24,28},{28,24},{32,36},... | collective-permute-start | bytes 3932168 | tf_op jit(solution)/shard_map/cond/branch_1_fun/ppermute | solution.py:838
  145.9 1.2 copy-start.17
